TPU v7x, 32 devices: a whole 2x2x4 slice. The times are simulated.
32 devices in a mesh: group: 2 (over x), lon: 8 (over z, y), lat: 2 (over core).
Axes of the slice: x: 2, y: 2, z: 4, core: 2. Of those that a mesh axis runs over, the one named last changes fastest.
Arguments:
- tokens: bfloat16 [128, 256, 384], P(('group', 'lat'), 'lon'), parts along dimension 0, may hold values from -6 to 6
- visible: int32 [128, 256], P(('group', 'lat'), 'lon'), parts along dimension 0, may hold values 0 or 1
- mask_token: bfloat16 [384], replicated, may hold values from -4 to 4
- norm_gain_table: float32 [2, 384], replicated, may hold values from 0.25 to 1.75
- query_key_value_weight: bfloat16 [2, 384, 1152], replicated, may hold values from -0.3125 to 0.3125
- output_weight: bfloat16 [2, 384, 384], replicated, may hold values from -0.3125 to 0.3125
- cotangent: float32 [128, 256, 384], P(('group', 'lat'), 'lon'), parts along dimension 0, may hold values from -6 to 6
Outputs:
- grad_tokens: float32 [128, 256, 384], P(('group', 'lat'), 'lon'), parts along dimension 0
- grad_qkv: float32 [4, 384, 1152], P('group'), parts along dimension 0
- grad_out: float32 [4, 384, 384], P('group'), parts along dimension 0
- grad_gain: float32 [4, 384], P('group'), parts along dimension 0
There are 2 independent parts, one for each index of `group`. A program takes and returns all parts, laid end to end along the dimension named above; an argument that names none is the same for every part. Nothing has to cross between parts.
Inputs may be any that keep to these rules, and one draw needn't show every extreme that they name: 1 marks a visible token.
All inputs are finite; a program needn't handle non-finite values. No bound on the sum of `visible` on one device may be relied on, other than what follows from the above.
Results may differ from a plain program's by a relative error of at most 0.01.
Values may be sent and summed in bfloat16 or wider, within the bound.
No kernel may reach another device: no remote copies, remote signals or barrier semaphores. Data moves between devices by JAX's collectives and lax.ppermute only.
A program may use at most 320 MiB of HBM per device.

v0:
```python
import jax
import jax.numpy as jnp
from jax import lax
from jax.sharding import PartitionSpec as P

HEADS = 6


def partner(value, axis, stride):
    mask = 2**stride
    pairs = [(source, source ^ mask) for source in range(lax.axis_size(axis))]
    return lax.ppermute(value, axis, pairs)


def passed_along(value, axis, steps):
    count = lax.axis_size(axis)
    pairs = [(source, (source + steps) % count) for source in range(count)]
    return lax.ppermute(value, axis, pairs)


def extended_2(cells, sides, width):
    for axis, dim in sides:
        count = lax.axis_size(axis)
        head = lax.slice_in_dim(cells, 0, width, axis=dim)
        tail = lax.slice_in_dim(cells, cells.shape[dim] - width, cells.shape[dim], axis=dim)
        cells = jnp.concatenate(
            [
                lax.ppermute(tail, axis, [(i, (i + 1) % count) for i in range(count)]),
                cells,
                lax.ppermute(head, axis, [((i + 1) % count, i) for i in range(count)]),
            ],
            axis=dim,
        )
    return cells


def normed(values_in, gain_row):
    mean_value = jnp.mean(values_in, axis=-1, keepdims=True)
    centred = values_in - mean_value
    spread = jnp.mean(centred * centred, axis=-1, keepdims=True)
    return centred * lax.rsqrt(spread + 1e-05) * gain_row


def mix_heads(query_heads, key_list, value_list, mask_list):
    head_size = query_heads.shape[1]
    weights = []
    for key_one, mask_one in zip(key_list, mask_list):
        weight_one = jnp.exp(jnp.sum(query_heads * key_one, axis=1) * head_size ** (-0.5))
        if mask_one is not None:
            weight_one = weight_one * mask_one
        weights.append(weight_one)
    weight_sum = sum(weights)
    result = jnp.zeros_like(query_heads)
    for weight_one, value_one in zip(weights, value_list):
        result = result + (weight_one / weight_sum)[:, None, :] * value_one
    return result


def dilated_mix(query_flat, blocks):
    width = query_flat.shape[0]
    head_size = width // HEADS
    points = query_flat.shape[1]
    query_heads = query_flat.reshape(HEADS, head_size, points)
    key_list = [
        blocks[number, :width].reshape(HEADS, head_size, points)
        for number in range(blocks.shape[0])
    ]
    value_list = [
        blocks[number, width:].reshape(HEADS, head_size, points)
        for number in range(blocks.shape[0])
    ]
    mask_list = [None for number in range(blocks.shape[0])]
    return mix_heads(query_heads, key_list, value_list, mask_list).reshape(width, points)


def plain_mix(query_grid, padded, lat_masks, grid_rows, grid_cols, margin):
    width = query_grid.shape[0]
    head_size = width // HEADS
    points = grid_rows * grid_cols
    placed = jnp.pad(query_grid, ((0, 0), (1, 1), (1, 1))).reshape(HEADS, head_size, points)
    key_list = []
    value_list = []
    mask_list = []
    for lat_step in (-1, 0, 1):
        for lon_step in (-1, 0, 1):
            start_at = margin + lat_step * grid_cols + lon_step
            window = padded[:, start_at : start_at + points]
            key_list.append(window[:width].reshape(HEADS, head_size, points))
            value_list.append(window[width:].reshape(HEADS, head_size, points))
            mask_list.append(lat_masks[lat_step + 1])
    result = mix_heads(placed, key_list, value_list, mask_list).reshape(width, grid_rows, grid_cols)
    return result[:, 1 : grid_rows - 1, 1 : grid_cols - 1]


def surround(block_in):
    partner_block = partner(block_in, "lat", 0)
    pair_blocks = jnp.stack([block_in, partner_block])
    moved_blocks = [passed_along(pair_blocks, "lon", step_dir) for step_dir in (1, -1)]
    return jnp.concatenate([pair_blocks, moved_blocks[0], moved_blocks[1]], 0)


def gather_back(grad_blocks):
    pair_blocks = grad_blocks[0:2]
    for step_dir, rim_part in ((-1, grad_blocks[2:4]), (1, grad_blocks[4:6])):
        pair_blocks = pair_blocks + passed_along(
            rim_part.astype(jnp.bfloat16), "lon", step_dir
        ).astype(rim_part.dtype)
    return pair_blocks[0] + partner(pair_blocks[1].astype(jnp.bfloat16), "lat", 0).astype(
        jnp.float32
    )


def widen_plain(keyval_grid):
    row_count = keyval_grid.shape[1]
    is_upper = lax.axis_index("lat") == 0
    outgoing = jnp.where(is_upper, keyval_grid[:, row_count - 1 :], keyval_grid[:, :1])
    partner_row = partner(outgoing, "lat", 0)
    empty_row = jnp.zeros_like(partner_row)
    lat_band = jnp.where(
        is_upper,
        jnp.concatenate([empty_row, keyval_grid, partner_row], 1),
        jnp.concatenate([partner_row, keyval_grid, empty_row], 1),
    )
    return extended_2(lat_band, (("lon", 2),), 1)


def fold_plain(grad_grid):
    grid_rows = grad_grid.shape[1]
    grid_cols = grad_grid.shape[2]
    col_count = grid_cols - 2
    row_count = grid_rows - 2
    core_part = grad_grid[:, :, 1 : grid_cols - 1]
    for step_dir, rim_part in ((-1, grad_grid[:, :, :1]), (1, grad_grid[:, :, grid_cols - 1 :])):
        arrived = passed_along(rim_part.astype(jnp.bfloat16), "lon", step_dir).astype(
            rim_part.dtype
        )
        before = col_count - 1 if step_dir == -1 else 0
        core_part = core_part + jnp.pad(arrived, ((0, 0), (0, 0), (before, col_count - 1 - before)))
    is_upper = lax.axis_index("lat") == 0
    outgoing = jnp.where(is_upper, core_part[:, grid_rows - 1 :], core_part[:, :1])
    returned = partner(outgoing.astype(jnp.bfloat16), "lat", 0).astype(outgoing.dtype)
    own_part = core_part[:, 1 : grid_rows - 1]
    placed = jnp.where(
        is_upper,
        jnp.pad(returned, ((0, 0), (row_count - 1, 0), (0, 0))),
        jnp.pad(returned, ((0, 0), (0, row_count - 1), (0, 0))),
    )
    return own_part + placed


def project_features(normal_flat, weight_part):
    return jnp.einsum(
        "nd,de->en", normal_flat, weight_part, preferred_element_type=jnp.float32
    ).astype(jnp.bfloat16)


def forward_layer(layer_in, gain_row, weight_qkv, weight_out, dilated):
    row_count, col_count, width = layer_in.shape
    points = row_count * col_count
    normal_part, norm_pull = jax.vjp(normed, layer_in, gain_row)
    normal_half = normal_part.astype(jnp.bfloat16).reshape(points, width)
    query_flat = project_features(normal_half, weight_qkv[:, :width])
    grid_info = None
    if dilated:
        wide_input = normal_half
        blocks = surround(project_features(normal_half, weight_qkv[:, width:]))
        mixed_flat, attend_pull = jax.vjp(
            dilated_mix, query_flat.astype(jnp.float32), blocks.astype(jnp.float32)
        )
    else:
        wide_input = normal_half
        keyval_grid = project_features(normal_half, weight_qkv[:, width:]).reshape(
            2 * width, row_count, col_count
        )
        extended = widen_plain(keyval_grid)
        grid_rows = row_count + 2
        grid_cols = col_count + 2
        margin = grid_cols + 1
        grid_points = grid_rows * grid_cols
        padded = jnp.pad(extended.reshape(2 * width, grid_points), ((0, 0), (margin, margin)))
        row_index = jnp.arange(grid_points, dtype=jnp.int32) // grid_cols
        outside_row = jnp.where(lax.axis_index("lat") == 0, 0, grid_rows - 1)
        lat_masks = []
        for lat_step in (-1, 0, 1):
            target = row_index + lat_step
            lat_masks.append(
                jnp.where(
                    (target >= 0) & (target <= grid_rows - 1) & (target != outside_row), 1.0, 0.0
                ).astype(jnp.float32)
            )

        def local_mix(query_grid, padded_in):
            return plain_mix(query_grid, padded_in, lat_masks, grid_rows, grid_cols, margin)

        query_grid = query_flat.astype(jnp.float32).reshape(width, row_count, col_count)
        mixed_grid, attend_pull = jax.vjp(local_mix, query_grid, padded.astype(jnp.float32))
        mixed_flat = mixed_grid.reshape(width, points)
        grid_info = (grid_rows, grid_cols, margin)
    mixed_half = mixed_flat.astype(jnp.bfloat16)
    layer_out = layer_in.reshape(points, width) + jnp.einsum(
        "dn,de->ne", mixed_half, weight_out, preferred_element_type=jnp.float32
    )
    saved = (
        norm_pull,
        attend_pull,
        normal_half,
        wide_input,
        mixed_half,
        dilated,
        grid_info,
        (row_count, col_count),
    )
    return (layer_out.reshape(row_count, col_count, width), saved)


def backward_layer(grad_in, saved, weight_qkv, weight_out):
    norm_pull, attend_pull, normal_half, wide_input, mixed_half, dilated, grid_info, shape_info = (
        saved
    )
    row_count, col_count = shape_info
    points, width = normal_half.shape
    highest = lax.Precision.HIGHEST
    weight_full = weight_qkv.astype(jnp.float32)
    normal_full = normal_half.astype(jnp.float32)
    grad_mixed = jnp.einsum("ne,de->dn", grad_in, weight_out.astype(jnp.float32), precision=highest)
    grad_wout = jnp.einsum("dn,ne->de", mixed_half.astype(jnp.float32), grad_in, precision=highest)
    if dilated:
        grad_query, grad_blocks = attend_pull(grad_mixed)
    else:
        grad_query_grid, grad_padded = attend_pull(grad_mixed.reshape(width, row_count, col_count))
        grad_query = grad_query_grid.reshape(width, points)
        grid_rows, grid_cols, margin = grid_info
        grad_grid = grad_padded[:, margin : margin + grid_rows * grid_cols].reshape(
            2 * width, grid_rows, grid_cols
        )
        grad_blocks = fold_plain(grad_grid).reshape(2 * width, points)
    grad_normal = jnp.einsum("en,de->nd", grad_query, weight_full[:, :width], precision=highest)
    grad_wquery = jnp.einsum("nd,en->de", normal_full, grad_query, precision=highest)
    grad_kvown = gather_back(grad_blocks) if dilated else grad_blocks
    grad_wkv = jnp.einsum("nd,en->de", normal_full, grad_kvown, precision=highest)
    grad_normal = grad_normal + jnp.einsum(
        "en,de->nd", grad_kvown, weight_full[:, width:], precision=highest
    )
    grad_field, grad_gain = norm_pull(grad_normal.reshape(row_count, col_count, width))
    return (
        grad_in + grad_field.reshape(points, width),
        jnp.concatenate([grad_wquery, grad_wkv], axis=1),
        grad_wout,
        grad_gain,
    )


def local(
    tokens, visible, mask_token, norm_gain_table, query_key_value_weight, output_weight, cotangent
):
    row_count, col_count, width = tokens.shape
    lat_count = lax.axis_size("lat")
    lon_count = lax.axis_size("lon")
    shown = visible[..., None] == 1
    starting_tokens = jnp.where(
        shown, tokens.astype(jnp.float32), mask_token.astype(jnp.float32)[None, None, :]
    )
    between_tokens, saved_first = forward_layer(
        starting_tokens, norm_gain_table[0], query_key_value_weight[0], output_weight[0], True
    )
    middle_half = lax.optimization_barrier(between_tokens.astype(jnp.bfloat16)).astype(jnp.float32)
    unused_final, saved_second = forward_layer(
        middle_half, norm_gain_table[1], query_key_value_weight[1], output_weight[1], False
    )
    grad_final = cotangent.reshape(row_count * col_count, width)
    gradient_between, qkv_second, out_second, gain_second = backward_layer(
        grad_final, saved_second, query_key_value_weight[1], output_weight[1]
    )
    grad_start, qkv_first, out_first, gain_first = backward_layer(
        gradient_between, saved_first, query_key_value_weight[0], output_weight[0]
    )
    grad_tokens = jnp.where(shown, grad_start.reshape(row_count, col_count, width), 0.0)
    summed_qkv, summed_out, summed_gain = lax.psum(
        (
            jnp.stack([qkv_first, qkv_second]),
            jnp.stack([out_first, out_second]),
            jnp.stack([gain_first, gain_second]),
        ),
        ("lon", "lat"),
    )
    factor = (row_count * col_count * lat_count * lon_count) ** (-0.5)
    return (grad_tokens, summed_qkv * factor, summed_out * factor, summed_gain * factor)


def solution(mesh):
    return jax.shard_map(
        local,
        mesh=mesh,
        in_specs=(
            P(("group", "lat"), "lon", None),
            P(("group", "lat"), "lon"),
            P(),
            P(),
            P(),
            P(),
            P(("group", "lat"), "lon", None),
        ),
        out_specs=(
            P(("group", "lat"), "lon", None),
            P("group", None, None),
            P("group", None, None),
            P("group", None),
        ),
        check_vma=False,
    )
```

profile of v0, /device:TPU:0, one launch (start us, length us, event | category | flops | bytes accessed | tf_op | source)
XLA Modules:
  0.0 959.3 jit_solution(4182502671617775337)
XLA Ops:
  43.2 119.3 %collective-permute-done.1 = bf16[2,768,1024]{2,1,0:T(8,128)(2,1)} collective-permute-done((bf16[2,768,1024]{2,1,0:T(8,128)(2,1)}, bf16[2,768,1024]{2,1,0:T(8,128)(2,1)}, u32[]{:S(2)}, u32[]{:S(2)}) %collective-permute-start.1) | collective-permute-done | bytes 3145760 | tf_op jit(solution)/shard_map/ppermute | solution.py:18
  170.0 6.6 fusion.90
  176.6 5.4 copy-done
  182.1 6.0 multiply_reduce_fusion.26
  213.8 10.1 %fusion.92 = (f32[384,1156]{0,1:T(8,128)}, f32[384,1156]{0,1:T(8,128)}, f32[384,1156]{0,1:T(8,128)}, f32[384,1156]{0,1:T(8,128)}, f32[384,1156]{0,1:T(8,128)}, /...) fusion(f32[768,1226]{0,1:T(8,128)S(1)} %pad_convert_fusion), kind=kLoop, calls=%fused_computation.281 | loop fusion | bytes 63922176 | tf_op jit(solution)/shard_map/jvp()/slice | solution.py:88
  290.0 24.3 %multiply_reduce_fusion.17 = (f32[6,1156]{0,1:T(8,128)}, f32[6,1156]{0,1:T(8,128)S(1)}, f32[6,1156]{0,1:T(8,128)S(1)}, f32[6,1156]{0,1:T(8,128)}, f32[6,1156]{0,...) fusion(f32[6,64,1156]{1,0,2:T(8,128)} %reshape.1855, ...), kind=kLoop, calls=%fused_computation.21 | loop fusion | flops 7927848 | bytes 18005856 | tf_op jit(solution)/shard_map/transpose(jvp())/reduce_sum | solution.py:55
  391.4 24.1 %multiply_reduce_fusion.16 = (f32[6,1156]{0,1:T(8,128)}, f32[6,1156]{0,1:T(8,128)S(1)}, f32[6,1156]{0,1:T(8,128)S(1)}, f32[6,1156]{0,1:T(8,128)}, f32[6,1156]{0,...) fusion(f32[6,64,1156]{1,0,2:T(8,128)} %reshape.1864, ...), kind=kLoop, calls=%fused_computation.20 | loop fusion | flops 7927848 | bytes 18005856 | tf_op jit(solution)/shard_map/jvp()/reduce_sum | solution.py:48
  466.1 5.6 bitcast_multiply_fusion.29
  493.1 9.4 pad_add_fusion.13
  502.5 10.4 %pad_add_fusion.1 = f32[768,1156]{1,0:T(8,128)} fusion(f32[768,1156]{1,0:T(8,128)} %pad_add_fusion.7, f32[768,1156]{1,0:T(8,128)S(1)} %pad_add_fusion.8, f32[768,1156]{1,0:T(8,128)S(1)} %pad_add_fusion.9, f32[768,1156]{1,0:T(8,128)S(1)} %pad_add_fusion.10, f32[768,1156]{1,0:T(8,128)S(1)} %pad_add_fusion.11, f32[768,1156]{1,0:T(8,128)S(1)} %pad_add_fusion.12, ...), kind=kLoop, calls=%fused_computation.22 | loop fusion | flops 5326848 | bytes 28409856 | tf_op jit(solution)/shard_map/transpose(jvp())/add_any | solution.py:87
  512.9 5.3 copy.367
  531.9 5.1 broadcast_in_dim.184
  541.2 5.2 broadcast_in_dim.186
  550.4 5.2 broadcast_in_dim.182
  559.7 5.2 broadcast_in_dim.188
  568.9 5.2 broadcast_in_dim.190
  587.4 5.2 broadcast_in_dim.194
  606.2 5.2 broadcast_in_dim.198
  642.5 9.2 bitcast_multiply_fusion.10
  651.8 12.2 %fusion.89 = (bf16[6,768,1024]{2,1,0:T(8,128)(2,1)S(1)}, f32[6,768,1024]{2,1,0:T(8,128)}) fusion(f32[1,384,1024]{2,1,0:T(8,128)} %bitcast.394, f32[1,384,1024]{2,1,0:T(8,128)} %bitcast.395, f32[1,384,1024]{2,1,0:T(8,128)} %bitcast.396, f32[1,384,1024]{2,1,0:T(8,128)} %bitcast.397, f32[1,384,1024]{2,1,0:T(8,128)} %bitcast.398, ...), kind=kLoop, calls=%fused_computation.278 | loop fusion | flops 56623104 | bytes 47185920 | tf_op jit(solution)/shard_map/convert.12
  727.3 5.2 mul.2013
  736.5 5.1 mul.2015
  745.8 5.1 mul.2019
  755.0 5.1 mul.2021
  764.3 5.2 mul.2023
  773.5 5.1 mul.2025
  782.8 5.6 mul.2027
  800.9 9.7 %convolution_bitcast_fusion.1 = f32[1,384,384]{2,1,0:T(8,128)S(1)} fusion(f32[32,32,384]{2,1,0:T(8,128)S(1)} %copy-done.15, f32[384,34,34]{0,2,1:T(8,128)} %reshape.1907, f32[384,34,34]{0,2,1:T(8,128)} %mul.2027, f32[384,34,34]{0,2,1:T(8,128)} %reshape.1906, f32[384,34,34]{0,2,1:T(8,128)} %mul.2025, f32[384,34,34]{0,2,1:T(8,128)} %reshape.1905, ...), kind=kOutput, calls=%fused_computation.162 | convolution fusion | flops 1815871488 | bytes 17891328 | tf_op jit(solution)/shard_map/dn,ne->de/dot_general | solution.py:226
  812.1 6.3 fusion
  833.2 7.4 fusion.5
  846.7 30.4 %psum.23 = f32[2,384]{1,0:T(2,128)S(1)} all-reduce(f32[2,384]{1,0:T(2,128)S(1)} %pad_maximum_fusion.4), channel_id=1, replica_groups=mesh['group'=2,'lon'=8,'lat'=2] {'lon','lat'}, use_global_device_ids=true, to_apply=%region_42.43 | all-reduce | flops 768 | bytes 6144 | tf_op jit(solution)/shard_map/psum | solution.py:278
  880.6 66.4 %all-reduce.49.cloned.1.call-done = (f32[2,384,1152]{2,1,0:T(8,128)}, f32[2,384,384]{2,1,0:T(8,128)}) async-done(((f32[2,384,1152]{2,1,0:T(8,128)}, f32[2,384,384]{2,1,0:T(8,128)}), (f32[2,384,1152]{2,1,0:T(8,128)}, f32[2,384,384]{2,1,0:T(8,128)})) %all-reduce.49.cloned.1.call-update) | async-done | bytes 4718608 | tf_op jit(solution)/shard_map/psum | solution.py:278
  (595 shorter events, 502.2 us)
Async XLA Ops:
  7.2 939.8 %all-reduce.49.cloned.1.call-start = ((), (), s32[]{:S(2)}) async-start(), calls=%async_computation | async-start | bytes 9437184 | tf_op jit(solution)/shard_map/psum | solution.py:278
  13.3 178.8 %copy-start.176 = (f32[384]{0:T(512)}, f32[384]{0:T(512)S(1)}, u32[]{:S(2)}) copy-start(f32[384]{0:T(512)S(1)} %get-tuple-element.38) | copy-start | bytes 4612
  17.2 22.9 %copy-start.36 = (bf16[32,32,384]{2,1,0:T(8,128)(2,1)}, bf16[32,32,384]{2,1,0:T(8,128)(2,1)S(1)}, u32[]{:S(2)}) copy-start(bf16[32,32,384]{2,1,0:T(8,128)(2,1)S(1)} %get-tuple-element.114) | copy-start | bytes 2359300
  18.3 3.5 collective-permute-start
  24.2 138.3 %collective-permute-start.1 = (bf16[2,768,1024]{2,1,0:T(8,128)(2,1)}, bf16[2,768,1024]{2,1,0:T(8,128)(2,1)}, u32[]{:S(2)}, u32[]{:S(2)}) collective-permute-start(bf16[2,768,1024]{2,1,0:T(8,128)(2,1)} %pad_maximum_fusion.1), channel_id=1, source_target_pairs={{0,2},{2,4},{4,6},{6,8},{8,10},{10,12},{12,14},{14,0},{1,3},{3,5},... | collective-permute-start | bytes 9437192 | tf_op jit(solution)/shard_map/ppermute | solution.py:18
  27.1 138.1 %collective-permute-start.2 = (bf16[2,768,1024]{2,1,0:T(8,128)(2,1)}, bf16[2,768,1024]{2,1,0:T(8,128)(2,1)}, u32[]{:S(2)}, u32[]{:S(2)}) collective-permute-start(bf16[2,768,1024]{2,1,0:T(8,128)(2,1)} %pad_maximum_fusion.1), channel_id=1, source_target_pairs={{0,14},{2,0},{4,2},{6,4},{8,6},{10,8},{12,10},{14,12},{1,15},{3,1}... | collective-permute-start | bytes 9437192 | tf_op jit(solution)/shard_map/ppermute | solution.py:18
  170.0 12.1 %copy-start = (f32[6,768,1024]{2,1,0:T(8,128)}, f32[6,768,1024]{2,1,0:T(8,128)S(1)}, u32[]{:S(2)}) copy-start(f32[6,768,1024]{2,1,0:T(8,128)S(1)} %maximum_convert_fusion) | copy-start | bytes 56623108
  193.7 1.3 collective-permute-start.3
  195.4 12.1 %collective-permute-start.4 = (bf16[768,34,1]{0,2,1:T(2,128)(2,1)S(1)}, bf16[768,34,1]{0,2,1:T(2,128)(2,1)S(1)}, u32[]{:S(2)}, u32[]{:S(2)}) collective-permute-start(bf16[768,34,1]{0,2,1:T(2,128)(2,1)S(1)} %get-tuple-element.106), channel_id=1, source_target_pairs={{0,2},{2,4},{4,6},{6,8},{8,10},{10,12},{12,14},{14,0},{1,3},{3,5},... | collective-permute-start | bytes 156680 | tf_op jit(solution)/shard_map/ppermute | solution.py:28
  195.5 12.1 %collective-permute-start.5 = (bf16[768,34,1]{0,2,1:T(2,128)(2,1)S(1)}, bf16[768,34,1]{0,2,1:T(2,128)(2,1)S(1)}, u32[]{:S(2)}, u32[]{:S(2)}) collective-permute-start(bf16[768,34,1]{0,2,1:T(2,128)(2,1)S(1)} %get-tuple-element.107), channel_id=1, source_target_pairs={{2,0},{4,2},{6,4},{8,6},{10,8},{12,10},{14,12},{0,14},{3,1},{5,3},... | collective-permute-start | bytes 156680 | tf_op jit(solution)/shard_map/ppermute | solution.py:30
  317.4 109.0 %copy-start.131 = (f32[6,1156]{1,0:T(8,128)}, f32[6,1156]{1,0:T(8,128)S(1)}, u32[]{:S(2)}) copy-start(f32[6,1156]{1,0:T(8,128)S(1)} %copy.292) | copy-start | bytes 83236
  318.8 107.7 %copy-start.132 = (f32[6,1156]{1,0:T(8,128)}, f32[6,1156]{1,0:T(8,128)S(1)}, u32[]{:S(2)}) copy-start(f32[6,1156]{1,0:T(8,128)S(1)} %copy.295) | copy-start | bytes 83236
  325.2 101.3 %copy-start.133 = (f32[6,1156]{1,0:T(8,128)}, f32[6,1156]{1,0:T(8,128)S(1)}, u32[]{:S(2)}) copy-start(f32[6,1156]{1,0:T(8,128)S(1)} %copy.307) | copy-start | bytes 83236
  325.4 101.0 %copy-start.134 = (f32[6,1156]{1,0:T(8,128)}, f32[6,1156]{1,0:T(8,128)S(1)}, u32[]{:S(2)}) copy-start(f32[6,1156]{1,0:T(8,128)S(1)} %copy.310) | copy-start | bytes 83236
  325.7 100.8 %copy-start.135 = (f32[6,1156]{1,0:T(8,128)}, f32[6,1156]{1,0:T(8,128)S(1)}, u32[]{:S(2)}) copy-start(f32[6,1156]{1,0:T(8,128)S(1)} %copy.313) | copy-start | bytes 83236
  427.5 38.5 %copy-start.125 = (f32[6,1156]{1,0:T(8,128)}, f32[6,1156]{1,0:T(8,128)S(1)}, u32[]{:S(2)}) copy-start(f32[6,1156]{1,0:T(8,128)S(1)} %get-tuple-element.130) | copy-start | bytes 83236
  429.1 36.9 %copy-start.126 = (f32[6,1156]{1,0:T(8,128)}, f32[6,1156]{1,0:T(8,128)S(1)}, u32[]{:S(2)}) copy-start(f32[6,1156]{1,0:T(8,128)S(1)} %get-tuple-element.133) | copy-start | bytes 83236
  429.1 36.9 %copy-start.127 = (f32[6,1156]{1,0:T(8,128)}, f32[6,1156]{1,0:T(8,128)S(1)}, u32[]{:S(2)}) copy-start(f32[6,1156]{1,0:T(8,128)S(1)} %get-tuple-element.138) | copy-start | bytes 83236
  525.5 101.2 %collective-permute-start.6 = (bf16[768,34,1]{0,2,1:T(2,128)(2,1)S(1)}, bf16[768,34,1]{0,2,1:T(2,128)(2,1)S(1)}, u32[]{:S(2)}, u32[]{:S(2)}) collective-permute-start(bf16[768,34,1]{0,2,1:T(2,128)(2,1)S(1)} %get-tuple-element.84), channel_id=1, source_target_pairs={{0,14},{2,0},{4,2},{6,4},{8,6},{10,8},{12,10},{14,12},{1,15},{3,1}... | collective-permute-start | bytes 156680 | tf_op jit(solution)/shard_map/ppermute | solution.py:18
  525.8 101.0 %collective-permute-start.7 = (bf16[768,34,1]{0,2,1:T(2,128)(2,1)S(1)}, bf16[768,34,1]{0,2,1:T(2,128)(2,1)S(1)}, u32[]{:S(2)}, u32[]{:S(2)}) collective-permute-start(bf16[768,34,1]{0,2,1:T(2,128)(2,1)S(1)} %get-tuple-element.85), channel_id=1, source_target_pairs={{0,2},{2,4},{4,6},{6,8},{8,10},{10,12},{12,14},{14,0},{1,3},{3,5},... | collective-permute-start | bytes 156680 | tf_op jit(solution)/shard_map/ppermute | solution.py:18
  627.4 2.7 collective-permute-start.8
  636.3 182.4 %copy-start.7 = (f32[32,32,384]{2,1,0:T(8,128)}, f32[32,32,384]{2,1,0:T(8,128)S(1)}, u32[]{:S(2)}) copy-start(f32[32,32,384]{2,1,0:T(8,128)S(1)} %add_add_fusion.2) | copy-start | bytes 4718596
  667.4 12.2 %copy-start.12 = (f32[384,1156]{0,1:T(8,128)S(1)}, f32[384,1156]{0,1:T(8,128)}, u32[]{:S(2)}) copy-start(f32[384,1156]{0,1:T(8,128)} %get-tuple-element.67) | copy-start | bytes 5326852
  667.4 144.6 %collective-permute-start.10 = (bf16[2,768,1024]{2,1,0:T(8,128)(2,1)}, bf16[2,768,1024]{2,1,0:T(8,128)(2,1)}, u32[]{:S(2)}, u32[]{:S(2)}) collective-permute-start(bf16[2,768,1024]{2,1,0:T(8,128)(2,1)} %get-tuple-element.65), channel_id=1, source_target_pairs={{0,2},{2,4},{4,6},{6,8},{8,10},{10,12},{12,14},{14,0},{1,3},{3,5},... | collective-permute-start | bytes 9437192 | tf_op jit(solution)/shard_map/ppermute | solution.py:18
  667.5 144.6 %collective-permute-start.9 = (bf16[2,768,1024]{2,1,0:T(8,128)(2,1)}, bf16[2,768,1024]{2,1,0:T(8,128)(2,1)}, u32[]{:S(2)}, u32[]{:S(2)}) collective-permute-start(bf16[2,768,1024]{2,1,0:T(8,128)(2,1)} %get-tuple-element.64), channel_id=1, source_target_pairs={{0,14},{2,0},{4,2},{6,4},{8,6},{10,8},{12,10},{14,12},{1,15},{3,1}... | collective-permute-start | bytes 9437192 | tf_op jit(solution)/shard_map/ppermute | solution.py:18
  800.9 9.9 %copy-start.31 = (f32[1,384,1024]{2,1,0:T(8,128)S(1)}, f32[1,384,1024]{2,1,0:T(8,128)}, u32[]{:S(2)}) copy-start(f32[1,384,1024]{2,1,0:T(8,128)} %get-tuple-element.61) | copy-start | bytes 4718596
  800.9 9.9 %copy-start.32 = (f32[1,384,1024]{2,1,0:T(8,128)S(1)}, f32[1,384,1024]{2,1,0:T(8,128)}, u32[]{:S(2)}) copy-start(f32[1,384,1024]{2,1,0:T(8,128)} %get-tuple-element.62) | copy-start | bytes 4718596
  800.9 9.9 %copy-start.33 = (f32[1,384,1024]{2,1,0:T(8,128)S(1)}, f32[1,384,1024]{2,1,0:T(8,128)}, u32[]{:S(2)}) copy-start(f32[1,384,1024]{2,1,0:T(8,128)} %get-tuple-element.63) | copy-start | bytes 4718596
  800.9 9.9 %copy-start.139 = (f32[6,1024]{1,0:T(8,128)S(1)}, f32[6,1024]{1,0:T(8,128)}, u32[]{:S(2)}) copy-start(f32[6,1024]{1,0:T(8,128)} %copy-done.138) | copy-start | bytes 73732
  800.9 9.9 %copy-start.141 = (f32[6,1024]{1,0:T(8,128)S(1)}, f32[6,1024]{1,0:T(8,128)}, u32[]{:S(2)}) copy-start(f32[6,1024]{1,0:T(8,128)} %copy-done.140) | copy-start | bytes 73732
  800.9 9.9 %copy-start.143 = (f32[6,1024]{1,0:T(8,128)S(1)}, f32[6,1024]{1,0:T(8,128)}, u32[]{:S(2)}) copy-start(f32[6,1024]{1,0:T(8,128)} %copy-done.142) | copy-start | bytes 73732
  818.7 8.4 collective-permute-start.11
  (159 other events, 600.4 us)
Sparse Core Ops, SparseCore 0:
  832.2 114.7 all-reduce.48
where the time goes:
time: 967 us; the launch traced here: 959 us
  local copies, waits for them, and re-layouts  465 us (48%)
  waiting for transfers between devices  192 us (20%)
  other arithmetic  190 us (20%)
  matrix products  46.3 us (5%)
  blocking collectives  30.4 us (3%)
  starting transfers between devices  18.9 us (2%)
  between operations  16.3 us (2%)
    ppermute x6, waiting for transfers between devices, passed_along(): return lax.ppermute(value, axis, pairs)  122 us
    mul x18, local copies, waits for them, and re-layouts, mix_heads(): result = result + (weight_one / weight_sum)[:, None, :] * value_one  84.1 us
    broadcast_in_dim x18, local copies, waits for them, and re-layouts, mix_heads(): jnp.sum(query_heads * key_one, axis=1) * head_size ** (-0.5)  83.7 us
    psum x1, waiting for transfers between devices, local(): lax.psum((jnp.stack([qkv_first, qkv_second]), jnp.stack([out_first, out_s...  66.4 us
    reshape x18, local copies, waits for them, and re-layouts, plain_mix(): key_list.append(window[:width].reshape(HEADS, head_size, points))  63.9 us
    reshape x18, local copies, waits for them, and re-layouts, plain_mix(): value_list.append(window[width:].reshape(HEADS, head_size, points))  59.8 us
    unnamed x365, local copies, waits for them, and re-layouts  39.3 us
    slice x10, local copies, waits for them, and re-layouts, plain_mix(): key_list.append(window[:width].reshape(HEADS, head_size, points))  35.1 us
  transfers between devices with their start and end apart: 13, of which 5 were waited for; matrix products, arithmetic and copies ran while one was open for 29% of the time, Pallas kernels for 0%

commit v1 on v0

v1 whole, which is shorter than its diff:
```python
import jax
import jax.numpy as jnp
from jax import lax
from jax.experimental import pallas as pl
from jax.experimental.pallas import tpu as pltpu
from jax.sharding import PartitionSpec as P

HEADS = 6
EPS = 1e-05
F32 = jnp.float32
BF16 = jnp.bfloat16
VMEM_BYTES = 56 * 1024 * 1024
HALO = 128
COLS_AT = 32
RIGHT_AT = 72
HALO_COLS = 80


def nn(a, b):
    return lax.dot_general(a, b, (((1,), (0,)), ((), ())), preferred_element_type=F32)


def nt(a, b):
    return lax.dot_general(a, b, (((1,), (1,)), ((), ())), preferred_element_type=F32)


def tn(a, b):
    return lax.dot_general(a, b, (((0,), (0,)), ((), ())), preferred_element_type=F32)


def iota(shape, dim):
    return lax.broadcasted_iota(jnp.int32, shape, dim)


def one_hot(condition):
    return jnp.where(condition, 1.0, 0.0).astype(BF16)


def permuted(value, axis, target):
    count = lax.axis_size(axis)
    return lax.ppermute(value, axis, [(i, target(i) % count) for i in range(count)])


def lat_swap(value):
    return permuted(value, "lat", lambda i: i ^ 1)


def lon_swap(value):
    return permuted(value, "lon", lambda i: i ^ 1)


def lon_forward(value):
    return permuted(value, "lon", lambda i: i + 2 if i % 2 == 0 else i - 2)


def lon_backward(value):
    return permuted(value, "lon", lambda i: i - 2 if i % 2 == 0 else i + 2)


def from_left(value):
    return permuted(value, "lon", lambda i: i + 1)


def from_right(value):
    return permuted(value, "lon", lambda i: i - 1)


def around(pack):
    left, right = from_left(pack), from_right(pack)
    return [lat_swap(pack), left, right, lat_swap(left), lat_swap(right)]


def norm_parts(x):
    mean = jnp.mean(x, axis=-1, keepdims=True)
    centred = x - mean
    spread = jnp.mean(centred * centred, axis=-1, keepdims=True)
    rstd = lax.rsqrt(spread + EPS)
    return centred * rstd, rstd


def norm_back(x, gain, grad_normal):
    xhat, rstd = norm_parts(x)
    g = grad_normal * gain
    return rstd * (
        g - jnp.mean(g, axis=-1, keepdims=True) - xhat * jnp.mean(g * xhat, axis=-1, keepdims=True)
    )


def visible_columns(visible):
    side = visible.shape[1]
    eye = jnp.where(iota((side, side), 0) == iota((side, side), 1), 1.0, 0.0)
    return nt(eye, visible.astype(F32))


def start_kernel(tok_ref, vis_ref, mask_ref, gain_ref, start_ref, normal_ref):
    rows, cols, width = tok_ref.shape
    shown = visible_columns(vis_ref[...])
    mask_row = mask_ref[...].astype(F32)
    gain = gain_ref[...]
    for r in range(rows):
        x = jnp.where(shown[:, r : r + 1] > 0.5, tok_ref[r].astype(F32), mask_row)
        start_ref[r] = x.astype(BF16)
        xhat, _ = norm_parts(x)
        normal_ref[r] = (xhat * gain).astype(BF16)


def first_kernel(
    lat_ref, n0, n1, n2, n3, n4, n5, start_ref, wt_ref, wo_ref, gain_ref,
    q_ref, kv_ref, p_ref, mixed_ref, h_ref, normal_ref, pack_ref,
    w_s, pack_s,
):
    width, tile = q_ref.shape
    head = width // HEADS
    blocks = (n0, n1, n2, n3, n4, n5)
    q_ref[...] = nt(wt_ref[0:width], n0[...]).astype(BF16)
    for b, ref in enumerate(blocks):
        kv_ref[b] = nt(wt_ref[width : 3 * width], ref[...]).astype(BF16)
    for h in range(HEADS):
        lo, hi = h * head, (h + 1) * head
        q = q_ref[lo:hi, :].astype(F32) * (head**-0.5)
        total = jnp.zeros((1, tile), F32)
        out = jnp.zeros((head, tile), F32)
        for b in range(len(blocks)):
            k = kv_ref[b, lo:hi, :].astype(F32)
            w = jnp.exp(jnp.sum(q * k, axis=0, keepdims=True))
            w_s[b, h : h + 1, :] = w
            total = total + w
            out = out + w * kv_ref[b, width + lo : width + hi, :].astype(F32)
        inverse = 1.0 / total
        for b in range(len(blocks)):
            p_ref[b, h : h + 1, :] = w_s[b, h : h + 1, :] * inverse
        mixed_ref[lo:hi, :] = (out * inverse).astype(BF16)
    h1 = start_ref[...].astype(F32) + tn(mixed_ref[...], wo_ref[...])
    h1 = h1.astype(BF16)
    h_ref[...] = h1
    xhat, _ = norm_parts(h1.astype(F32))
    normal = (xhat * gain_ref[...]).astype(BF16)
    normal_ref[...] = normal
    step = pl.program_id(0)
    brow = jnp.where(lat_ref[0] == 0, 31, 0)
    slot = iota((HALO, tile), 0)
    token = step * tile + iota((HALO, tile), 1)
    r, c = token // 32, token % 32
    pick = one_hot(
        ((slot < 32) & (r == brow) & (c == slot))
        | ((slot >= 32) & (slot < 64) & (c == 0) & (r == slot - 32))
        | ((slot >= 64) & (slot < 96) & (c == 31) & (r == slot - 64))
    )

    @pl.when(step == 0)
    def _():
        pack_s[...] = jnp.zeros_like(pack_s)

    pack_s[...] += nn(pick, normal)

    @pl.when(step == pl.num_programs(0) - 1)
    def _():
        pack_ref[...] = pack_s[...].astype(BF16)


def second_kernel(
    lat_ref, n_ref, pv, pl_, pr, pdl, pdr, w_ref, wo_ref, cot_ref,
    dn_ref, back_ref, dw_ref, dwo_ref,
    q_s, k_s, v_s, kc_s, vc_s, dq_s, dk_s, dv_s, dkc_s, dvc_s, do_s, mixed_s, halo_s, mask_s,
):
    points, width = n_ref.shape
    head = width // HEADS
    lat = lat_ref[0]
    upper = lat == 0
    a, b = iota((HALO, HALO), 0), iota((HALO, HALO), 1)
    corner = jnp.where(upper, 33, 0)
    halo = nn(one_hot((a < 32) & (a == b)), pv[...])
    halo += nn(one_hot((b >= 64) & (b < 96) & (a == COLS_AT + 1 + b - 64)), pl_[...])
    halo += nn(one_hot((b >= 32) & (b < 64) & (a == RIGHT_AT + 1 + b - 32)), pr[...])
    halo += nn(one_hot((b == 31) & (a == COLS_AT + corner)), pdl[...])
    halo += nn(one_hot((b == 0) & (a == RIGHT_AT + corner)), pdr[...])
    halo = halo.astype(BF16)
    halo_s[...] = halo

    normal = n_ref[...]
    scale = head**-0.5
    q_s[...] = (nn(normal, w_ref[:, 0:width]).astype(BF16).astype(F32) * scale).astype(BF16)
    k_s[32 : 32 + points, :] = nn(normal, w_ref[:, width : 2 * width]).astype(BF16)
    v_s[32 : 32 + points, :] = nn(normal, w_ref[:, 2 * width : 3 * width]).astype(BF16)
    kh = nn(halo, w_ref[:, width : 2 * width]).astype(BF16)
    vh = nn(halo, w_ref[:, 2 * width : 3 * width]).astype(BF16)
    for at in (0, 32 + points):
        k_s[at : at + 32, :] = kh[0:32]
        v_s[at : at + 32, :] = vh[0:32]
    kc_s[...] = kh[COLS_AT : COLS_AT + HALO_COLS]
    vc_s[...] = vh[COLS_AT : COLS_AT + HALO_COLS]
    dk_s[...] = jnp.zeros_like(dk_s)
    dv_s[...] = jnp.zeros_like(dv_s)
    dkc_s[...] = jnp.zeros_like(dkc_s)
    dvc_s[...] = jnp.zeros_like(dvc_s)
    cot = cot_ref[...].astype(BF16)
    do_s[...] = nt(cot, wo_ref[...]).astype(BF16)

    key, query = iota((192, 256), 0), iota((192, 256), 1) % 128
    drow = key // 32 - 1 - query // 32
    dcol = key % 32 - query % 32
    mask_s[...] = jnp.where((jnp.abs(drow) <= 1) & (jnp.abs(dcol) <= 1), 1.0, 0.0)

    tiles = points // 128

    def tile_step(t, carry):
        base = pl.multiple_of(t * 128, 128)
        key = iota((192, 256), 0)
        first = jnp.where(upper & (t == 0), 32, 0)
        last = jnp.where(jnp.logical_not(upper) & (t == tiles - 1), 160, 192)
        mask1 = (mask_s[...] > 0.5) & (key >= first) & (key < last)
        e, query = iota((HALO_COLS, 256), 0), iota((HALO_COLS, 256), 1) % 128
        is_right = e >= 40
        ext = jnp.where(is_right, e - 40, e)
        near = jnp.abs(ext - 1 - (4 * t + query // 32)) <= 1
        side = query % 32 == jnp.where(is_right, 31, 0)
        real = (ext < 34) & (ext != jnp.where(upper, 0, 33))
        mask2 = near & side & real
        lane = iota((128, 128), 1)
        even = lane < 64
        for pair in range(HEADS // 2):
            lanes = slice(pair * 128, pair * 128 + 128)
            win = pl.ds(base, 192)
            here = pl.ds(base, 128)
            q = q_s[here, lanes]
            do = do_s[here, lanes]
            zero = jnp.zeros_like(q)
            qm = jnp.concatenate([jnp.where(even, q, zero), jnp.where(even, zero, q)], 0)
            dom = jnp.concatenate([jnp.where(even, do, zero), jnp.where(even, zero, do)], 0)
            k1, v1 = k_s[win, lanes], v_s[win, lanes]
            k2, v2 = kc_s[:, lanes], vc_s[:, lanes]
            w1 = jnp.where(mask1, jnp.exp(nt(k1, qm)), 0.0)
            w2 = jnp.where(mask2, jnp.exp(nt(k2, qm)), 0.0)
            total = jnp.sum(w1, axis=0, keepdims=True) + jnp.sum(w2, axis=0, keepdims=True)
            inverse = 1.0 / total
            p1, p2 = w1 * inverse, w2 * inverse
            dp1, dp2 = nt(v1, dom), nt(v2, dom)
            delta = jnp.sum(p1 * dp1, axis=0, keepdims=True) + jnp.sum(
                p2 * dp2, axis=0, keepdims=True
            )
            ds1, ds2 = (p1 * (dp1 - delta)).astype(BF16), (p2 * (dp2 - delta)).astype(BF16)
            p1, p2 = p1.astype(BF16), p2.astype(BF16)
            out = tn(p1, v1) + tn(p2, v2)
            mixed_s[here, lanes] = jnp.where(even, out[0:128], out[128:256]).astype(BF16)
            dq = (tn(ds1, k1) + tn(ds2, k2)) * scale
            dq_s[here, lanes] = jnp.where(even, dq[0:128], dq[128:256]).astype(BF16)
            dk_s[win, lanes] += nn(ds1, qm)
            dv_s[win, lanes] += nn(p1, dom)
            dkc_s[:, lanes] += nn(ds2, qm)
            dvc_s[:, lanes] += nn(p2, dom)
        return carry

    lax.fori_loop(0, tiles, tile_step, 0)

    dwo_ref[...] = tn(mixed_s[...], cot).astype(BF16)
    row_at = pl.multiple_of(jnp.where(upper, 32 + points, 0), 32)
    pad = jnp.zeros((HALO - COLS_AT - HALO_COLS, width), F32)
    dkh = jnp.concatenate([dk_s[pl.ds(row_at, 32), :], dkc_s[...], pad], 0).astype(BF16)
    dvh = jnp.concatenate([dv_s[pl.ds(row_at, 32), :], dvc_s[...], pad], 0).astype(BF16)
    dq = dq_s[...]
    dk = dk_s[32 : 32 + points, :].astype(BF16)
    dv = dv_s[32 : 32 + points, :].astype(BF16)
    halo = halo_s[...]
    wq, wk, wv = (w_ref[:, i * width : (i + 1) * width] for i in range(3))
    dn_ref[...] = nt(dq, wq) + nt(dk, wk) + nt(dv, wv)
    back_ref[...] = (nt(dkh, wk) + nt(dvh, wv)).astype(BF16)
    dw_ref[:, 0:width] = tn(normal, dq).astype(BF16)
    dw_ref[:, width : 2 * width] = (tn(normal, dk) + tn(halo, dkh)).astype(BF16)
    dw_ref[:, 2 * width : 3 * width] = (tn(normal, dv) + tn(halo, dvh)).astype(BF16)


def third_kernel(
    lat_ref, n0, n1, n2, n3, n4, n5, q_ref, kv_ref, p_ref, mixed_ref, h_ref, dn1_ref, cot_ref,
    packs_ref, wt_ref, wo_ref, gain_ref,
    dh_ref, d0, d1, d2, d3, d4, d5, dw_ref, dwo_ref,
    dw_s, dwo_s, dmix_s, dkv_s, dq_s, dp_s,
):
    width, tile = q_ref.shape
    head = width // HEADS
    scale = head**-0.5
    blocks = (n0, n1, n2, n3, n4, n5)
    outs = (d0, d1, d2, d3, d4, d5)
    step = pl.program_id(0)

    @pl.when(step == 0)
    def _():
        dw_s[...] = jnp.zeros_like(dw_s)
        dwo_s[...] = jnp.zeros_like(dwo_s)

    upper = lat_ref[0] == 0
    brow = jnp.where(upper, 31, 0)
    corner = jnp.where(upper, 0, 33)
    shape = (tile, 5 * HALO)
    token = step * tile + iota(shape, 0)
    r, c = token // 32, token % 32
    which, slot = iota(shape, 1) // HALO, iota(shape, 1) % HALO
    border = r == brow
    place = one_hot(
        ((which == 0) & border & (slot < 32) & (slot == c))
        | ((which == 1) & (c == 0) & (slot == RIGHT_AT + 1 + r))
        | ((which == 2) & (c == 31) & (slot == COLS_AT + 1 + r))
        | ((which == 3) & border & (c == 0) & (slot == RIGHT_AT + corner))
        | ((which == 4) & border & (c == 31) & (slot == COLS_AT + corner))
    )
    dn = dn1_ref[...] + nn(place, packs_ref[...])
    dh = cot_ref[...] + norm_back(h_ref[...].astype(F32), gain_ref[...], dn)
    dh_ref[...] = dh
    dhb = dh.astype(BF16)
    dmix_s[...] = nt(wo_ref[...], dhb)
    dwo_s[...] += nn(mixed_ref[...], dhb)
    for h in range(HEADS):
        lo, hi = h * head, (h + 1) * head
        dmix = dmix_s[lo:hi, :]
        delta = jnp.zeros((1, tile), F32)
        for b in range(len(blocks)):
            dp = jnp.sum(
                dmix * kv_ref[b, width + lo : width + hi, :].astype(F32), axis=0, keepdims=True
            )
            dp_s[b : b + 1, :] = dp
            delta = delta + p_ref[b, h : h + 1, :] * dp
        q = q_ref[lo:hi, :].astype(F32)
        dq = jnp.zeros((head, tile), F32)
        for b in range(len(blocks)):
            p = p_ref[b, h : h + 1, :]
            ds = p * (dp_s[b : b + 1, :] - delta) * scale
            dq = dq + ds * kv_ref[b, lo:hi, :].astype(F32)
            dkv_s[b, lo:hi, :] = (ds * q).astype(BF16)
            dkv_s[b, width + lo : width + hi, :] = (p * dmix).astype(BF16)
        dq_s[lo:hi, :] = dq.astype(BF16)
    dq = dq_s[...]
    dw_s[0:width, :] += nn(dq, n0[...])
    for b, (ref, out) in enumerate(zip(blocks, outs)):
        dkv = dkv_s[b]
        grad = tn(dkv, wt_ref[width : 3 * width])
        if b == 0:
            grad = grad + tn(dq, wt_ref[0:width])
        out[...] = grad.astype(out.dtype)
        dw_s[width : 3 * width, :] += nn(dkv, ref[...])

    @pl.when(step == pl.num_programs(0) - 1)
    def _():
        dw_ref[...] = dw_s[...].astype(BF16)
        dwo_ref[...] = dwo_s[...].astype(BF16)


def last_kernel(start_ref, vis_ref, gain_ref, dh_ref, own_ref, far_ref, out_ref):
    rows, cols, width = start_ref.shape
    shown = visible_columns(vis_ref[...])
    gain = gain_ref[...]
    for r in range(rows):
        dn = own_ref[r] + far_ref[r].astype(F32)
        grad = dh_ref[r] + norm_back(start_ref[r].astype(F32), gain, dn)
        out_ref[r] = jnp.where(shown[:, r : r + 1] > 0.5, grad, 0.0)


def call(kernel, out_shape, scratch=(), grid=None, in_specs=None, out_specs=None):
    return pl.pallas_call(
        kernel,
        out_shape=out_shape,
        grid_spec=pltpu.PrefetchScalarGridSpec(
            num_scalar_prefetch=0,
            grid=grid or (),
            in_specs=in_specs,
            out_specs=out_specs,
            scratch_shapes=list(scratch),
        ),
        compiler_params=pltpu.CompilerParams(vmem_limit_bytes=VMEM_BYTES),
    )


def whole():
    return pl.BlockSpec(memory_space=pltpu.VMEM)


def scalar():
    return pl.BlockSpec(memory_space=pltpu.SMEM)


def fixed(shape):
    return pl.BlockSpec(shape, lambda i: (0,) * len(shape))


def local(
    tokens, visible, mask_token, norm_gain_table, query_key_value_weight, output_weight, cotangent
):
    rows, cols, width = tokens.shape
    points = rows * cols
    lat_count, lon_count = lax.axis_size("lat"), lax.axis_size("lon")
    lat = lax.axis_index("lat").astype(jnp.int32).reshape(1)
    gain0, gain1 = norm_gain_table[0:1], norm_gain_table[1:2]
    w0, w1 = query_key_value_weight[0], query_key_value_weight[1]
    wo0, wo1 = output_weight[0], output_weight[1]
    wt0 = w0.T
    struct = jax.ShapeDtypeStruct

    start, normal0 = call(
        start_kernel,
        (struct((rows, cols, width), BF16), struct((rows, cols, width), BF16)),
        in_specs=[whole()] * 4,
        out_specs=(whole(), whole()),
    )(tokens, visible, mask_token.reshape(1, width), gain0)
    flat = lambda x: x.reshape(points, width)

    own = flat(normal0)
    swapped = lon_swap(own)
    beyond = lon_forward(swapped)
    blocks = [own, lat_swap(own), swapped, beyond, lat_swap(swapped), lat_swap(beyond)]

    tile = 256
    steps = points // tile
    tok_spec = pl.BlockSpec((tile, width), lambda i: (i, 0))
    feat_spec = pl.BlockSpec((width, tile), lambda i: (0, i))
    kv_spec = pl.BlockSpec((6, 2 * width, tile), lambda i: (0, 0, i))
    p_spec = pl.BlockSpec((6, 8, tile), lambda i: (0, 0, i))
    q0, kv0, p0, mixed0, h1, normal1, pack = call(
        first_kernel,
        (
            struct((width, points), BF16),
            struct((6, 2 * width, points), BF16),
            struct((6, 8, points), F32),
            struct((width, points), BF16),
            struct((points, width), BF16),
            struct((points, width), BF16),
            struct((HALO, width), BF16),
        ),
        grid=(steps,),
        in_specs=[scalar()]
        + [tok_spec] * 7
        + [fixed((3 * width, width)), fixed((width, width)), fixed((1, width))],
        out_specs=(
            feat_spec, kv_spec, p_spec, feat_spec, tok_spec, tok_spec, fixed((HALO, width)),
        ),
        scratch=[pltpu.VMEM((6, 8, tile), F32), pltpu.VMEM((HALO, width), F32)],
    )(lat, *blocks, flat(start), wt0, wo0, gain1)

    halos = around(pack)
    cot = flat(cotangent)
    ext = points + 64
    dn1, back, dw1, dwo1 = call(
        second_kernel,
        (
            struct((points, width), F32),
            struct((HALO, width), BF16),
            struct((width, 3 * width), BF16),
            struct((width, width), BF16),
        ),
        in_specs=[scalar()] + [whole()] * 9,
        out_specs=(whole(),) * 4,
        scratch=[
            pltpu.VMEM((points, width), BF16),
            pltpu.VMEM((ext, width), BF16),
            pltpu.VMEM((ext, width), BF16),
            pltpu.VMEM((HALO_COLS, width), BF16),
            pltpu.VMEM((HALO_COLS, width), BF16),
            pltpu.VMEM((points, width), BF16),
            pltpu.VMEM((ext, width), F32),
            pltpu.VMEM((ext, width), F32),
            pltpu.VMEM((HALO_COLS, width), F32),
            pltpu.VMEM((HALO_COLS, width), F32),
            pltpu.VMEM((points, width), BF16),
            pltpu.VMEM((points, width), BF16),
            pltpu.VMEM((HALO, width), BF16),
            pltpu.VMEM((192, 256), F32),
        ],
    )(lat, normal1, *halos, w1, wo1, cot)

    packs = jnp.concatenate(around(back), 0)
    dh1, d0, d1, d2, d3, d4, d5, dw0t, dwo0 = call(
        third_kernel,
        (
            struct((points, width), F32),
            struct((points, width), F32),
            *[struct((points, width), BF16)] * 5,
            struct((3 * width, width), BF16),
            struct((width, width), BF16),
        ),
        grid=(steps,),
        in_specs=[scalar()]
        + [tok_spec] * 6
        + [feat_spec, kv_spec, p_spec, feat_spec, tok_spec, tok_spec, tok_spec]
        + [
            fixed((5 * HALO, width)),
            fixed((3 * width, width)),
            fixed((width, width)),
            fixed((1, width)),
        ],
        out_specs=(
            *[tok_spec] * 7, fixed((3 * width, width)), fixed((width, width)),
        ),
        scratch=[
            pltpu.VMEM((3 * width, width), F32),
            pltpu.VMEM((width, width), F32),
            pltpu.VMEM((width, tile), F32),
            pltpu.VMEM((6, 2 * width, tile), BF16),
            pltpu.VMEM((width, tile), BF16),
            pltpu.VMEM((8, tile), F32),
        ],
    )(lat, *blocks, q0, kv0, p0, mixed0, h1, dn1, cot, packs, wt0, wo0, gain1)

    def plus(a, b):
        return (a.astype(F32) + b.astype(F32)).astype(BF16)

    d3 = plus(d3, lat_swap(d5))
    d2 = plus(d2, lat_swap(d4))
    d2 = plus(d2, lon_backward(d3))
    far = plus(lon_swap(d2), lat_swap(d1))

    cube = lambda x: x.reshape(rows, cols, width)
    grad_tokens = call(
        last_kernel,
        struct((rows, cols, width), F32),
        in_specs=[whole()] * 6,
        out_specs=whole(),
    )(start, visible, gain0, cube(dh1), cube(d0), cube(far))

    factor = (points * lat_count * lon_count) ** (-0.5)
    s1, so1 = lax.psum((dw1.astype(F32), dwo1.astype(F32)), ("lon", "lat"))
    s0, so0 = lax.psum((dw0t.astype(F32), dwo0.astype(F32)), ("lon", "lat"))
    g_qkv = jnp.stack([s0.T, s1]) * factor
    g_out = jnp.stack([so0, so1]) * factor
    g_gain = (
        jnp.sum(query_key_value_weight.astype(F32) * g_qkv, axis=-1) / norm_gain_table
    )
    return grad_tokens, g_qkv, g_out, g_gain


def solution(mesh):
    return jax.shard_map(
        local,
        mesh=mesh,
        in_specs=(
            P(("group", "lat"), "lon", None),
            P(("group", "lat"), "lon"),
            P(),
            P(),
            P(),
            P(),
            P(("group", "lat"), "lon", None),
        ),
        out_specs=(
            P(("group", "lat"), "lon", None),
            P("group", None, None),
            P("group", None, None),
            P("group", None),
        ),
        check_vma=False,
    )
```

time: 967 us -> 310 us (0.32)
  local copies, waits for them, and re-layouts: 465 us -> 17.4 us
  other arithmetic: 190 us -> 15.3 us
  Pallas kernels: 0 us -> 75.7 us
  matrix products: 46.3 us -> 0 us
  blocking collectives: 30.4 us -> 0 us
  waiting for transfers between devices: 192 us -> 174 us
    reshape x44 -> x1, local copies, waits for them, and re-layouts: 144 us -> 1.24 us  [local(): mask_token.reshape(1, width)]
    mul x18 -> x0, local copies, waits for them, and re-layouts: 84.1 us -> none  [mix_heads(): result = result + (weight_one / weight_sum)[:, None, :] * value_one]
    broadcast_in_dim x19 -> x0, local copies, waits for them, and re-layouts: 83.8 us -> none  [the longest x18 83.7 us: mix_heads(): jnp.sum(query_heads * key_one, axis=1) * head_size ** (-0.5)]
    pallas_call x0 -> x5, Pallas kernels: none -> 75.7 us  [the longest x1 22.9 us: local(): call(third_kernel, (struct((points, width), F32), struct((points, width),...]
    slice x25 -> x1, local copies, waits for them, and re-layouts: 77.1 us -> 1.35 us  [local(): gain0, gain1 = (norm_gain_table[0:1], norm_gain_table[1:2])]
    reduce_sum x12 -> x1, other arithmetic: 63 us -> 3.02 us  [local(): jnp.sum(query_key_value_weight.astype(F32) * g_qkv, axis=-1)]
    dot_general x17 -> x0, matrix products: 46.3 us -> none  [the longest x2 11.2 us: backward_layer(): jnp.einsum('dn,ne->de', mixed_half.astype(jnp.float32), grad_in, precisio...]
    ppermute x12 -> x20, waiting for transfers between devices: 126 us -> 82.3 us  [permuted(): lax.ppermute(value, axis, [(i, target(i) % count) for i in range(count)])]
  transfers between devices with their start and end apart: 13 -> 21, of which waited for: 5 -> 10; matrix products, arithmetic and copies ran while one was open for 29% -> 8% of each run, Pallas kernels for 0% -> 0%
where the time goes in v1:
time: 310 us
  waiting for transfers between devices  174 us (56%)
  Pallas kernels  75.7 us (24%)
  local copies, waits for them, and re-layouts  17.4 us (6%)
  other arithmetic  15.3 us (5%)
  between operations  14.2 us (5%)
  starting transfers between devices  13.3 us (4%)
    psum x1, waiting for transfers between devices, local(): s1, so1 = lax.psum((dw1.astype(F32), dwo1.astype(F32)), ('lon', 'lat'))  91.5 us
    ppermute x20, waiting for transfers between devices, permuted(): lax.ppermute(value, axis, [(i, target(i) % count) for i in range(count)])  82.3 us
    pallas_call x1, Pallas kernels, local(): call(third_kernel, (struct((points, width), F32), struct((points, width),...  22.9 us
    pallas_call x1, Pallas kernels, local(): call(second_kernel, (struct((points, width), F32), struct((HALO, width),...  22.6 us
    pallas_call x1, Pallas kernels, local(): call(first_kernel, (struct((width, points), BF16), struct((6, 2 * width,...  13.5 us
    ppermute x20, starting transfers between devices, permuted(): lax.ppermute(value, axis, [(i, target(i) % count) for i in range(count)])  13.3 us
    pallas_call x1, Pallas kernels, local(): call(last_kernel, struct((rows, cols, width), F32), in_specs=[whole()] *...  9.94 us
    unnamed x38, local copies, waits for them, and re-layouts  8.62 us
  transfers between devices with their start and end apart: 21, of which 10 were waited for; matrix products, arithmetic and copies ran while one was open for 8% of the time, Pallas kernels for 0%

profile of v1, /device:TPU:0, one launch (start us, length us, event | category | flops | bytes accessed | tf_op | source)
XLA Modules:
  0.0 309.9 jit_solution(2142987820642225284)
XLA Ops:
  7.2 1.2 reshape.32.mask_ref
  8.5 1.3 fusion
  9.8 6.8 %shard_map.102 = (bf16[32,32,384]{2,1,0:T(8,128)(2,1)}, bf16[32,32,384]{2,1,0:T(8,128)(2,1)}) custom-call(bf16[32,32,384]{2,1,0:T(8,128)(2,1)} %tok_ref.1, s32[32,32]{1,0:T(8,128)} %vis_ref.3, bf16[1,384]{1,0:T(2,128)(2,1)} %reshape.32.mask_ref, f32[1,384]{1,0:T(1,128)} %get-tuple-element.61.gain_ref), custom_call_target="tpu_custom_call" | custom-call | tf_op jit(solution)/shard_map/pallas_call | solution.py:396
  16.6 3.0 collective-permute-start.1
  19.6 17.7 %collective-permute-done.1.n2 = bf16[1024,384]{1,0:T(8,128)(2,1)S(1)} collective-permute-done((bf16[1024,384]{1,0:T(8,128)(2,1)}, bf16[1024,384]{1,0:T(8,128)(2,1)S(1)}, u32[]{:S(2)}, u32[]{:S(2)}) %collective-permute-start.1) | collective-permute-done | bytes 786464 | tf_op jit(solution)/shard_map/ppermute | solution.py:41
  37.3 1.8 collective-permute-start.2
  39.7 18.2 %collective-permute-done.2.n3 = bf16[1024,384]{1,0:T(8,128)(2,1)S(1)} collective-permute-done((bf16[1024,384]{1,0:T(8,128)(2,1)S(1)}, bf16[1024,384]{1,0:T(8,128)(2,1)S(1)}, u32[]{:S(2)}, u32[]{:S(2)}) %collective-permute-start.2) | collective-permute-done | bytes 786464 | tf_op jit(solution)/shard_map/ppermute | solution.py:41
  57.9 3.0 copy.11
  61.0 2.4 slice_bitcast_fusion.2
  64.4 13.5 %shard_map.103 = (bf16[384,1024]{1,0:T(8,128)(2,1)}, bf16[6,768,1024]{2,1,0:T(8,128)(2,1)}, f32[6,8,1024]{2,1,0:T(8,128)}, bf16[384,1024]{1,0:T(8,128)(2,1)}, bf...) custom-call(s32[1]{0:T(128)} %bitcast.lat_ref, bf16[1024,384]{1,0:T(8,128)(2,1)} %bitcast.34, ...), custom_call_target="tpu_custom_call" | custom-call | tf_op jit(solution)/shard_map/pallas_call | solution.py:415
  77.9 4.5 %collective-permute-start.7 = (bf16[128,384]{1,0:T(8,128)(2,1)}, bf16[128,384]{1,0:T(8,128)(2,1)S(1)}, u32[]{:S(2)}, u32[]{:S(2)}) collective-permute-start(bf16[128,384]{1,0:T(8,128)(2,1)} %get-tuple-element.34), channel_id=1, source_target_pairs={{0,14},{2,0},{4,2},{6,4},{8,6},{10,8},{12,10},{14,12},{1,15},{3,1}... | collective-permute-start | bytes 294920 | tf_op jit(solution)/shard_map/ppermute | solution.py:41
  82.4 2.7 collective-permute-done.7.pr
  85.2 4.8 %collective-permute-done.6.pl_ = bf16[128,384]{1,0:T(8,128)(2,1)S(1)} collective-permute-done((bf16[128,384]{1,0:T(8,128)(2,1)}, bf16[128,384]{1,0:T(8,128)(2,1)S(1)}, u32[]{:S(2)}, u32[]{:S(2)}) %collective-permute-start.6) | collective-permute-done | bytes 98336 | tf_op jit(solution)/shard_map/ppermute | solution.py:41
  90.0 1.0 slice_bitcast_fusion.1.w_ref
  91.9 22.6 %shard_map.104 = (f32[1024,384]{1,0:T(8,128)}, bf16[128,384]{1,0:T(8,128)(2,1)}, bf16[384,1152]{1,0:T(8,128)(2,1)}, bf16[384,384]{1,0:T(8,128)(2,1)}) custom-call(s32[1]{0:T(128)} %bitcast.lat_ref, bf16[1024,384]{1,0:T(8,128)(2,1)} %get-tuple-element.33.n_ref, bf16[128,384]{1,0:T(8,128)(2,1)} %copy-done.11, bf16[128,384]{1,0:T(8,128)(2,1)} %copy-done.10, ...), custom_call_target="tpu_custom_call" | custom-call | tf_op jit(solution)/shard_map/pallas_call | solution.py:439
  115.1 1.4 collective-permute-start.11
  116.5 1.7 copy.12
  118.3 1.3 bitcast_convert_fusion
  121.0 1.7 collective-permute-done.11
  122.8 1.2 collective-permute-done.13
  124.9 22.9 %shard_map.105 = (f32[1024,384]{1,0:T(8,128)}, f32[1024,384]{1,0:T(8,128)}, bf16[1024,384]{1,0:T(8,128)(2,1)}, bf16[1024,384]{1,0:T(8,128)(2,1)}, bf16[1024,384]...) custom-call(s32[1]{0:T(128)} %bitcast.lat_ref, ...), custom_call_target="tpu_custom_call" | custom-call | tf_op jit(solution)/shard_map/pallas_call | solution.py:468
  148.0 2.5 convert_bitcast_fusion
  151.4 1.1 copy-done.15
  153.4 1.4 collective-permute-done.15
  154.7 34.2 %collective-permute-done.17 = bf16[1024,384]{1,0:T(8,128)(2,1)S(1)} collective-permute-done((bf16[1024,384]{1,0:T(8,128)(2,1)S(1)}, bf16[1024,384]{1,0:T(8,128)(2,1)S(1)}, u32[]{:S(2)}, u32[]{:S(2)}) %collective-permute-start.17) | collective-permute-done | bytes 786464 | tf_op jit(solution)/shard_map/ppermute | solution.py:41
  189.0 1.2 add_convert_fusion.1
  190.2 91.5 %all-reduce.3.cloned.1.call-done = (f32[1,384,1152]{1,2,0:T(8,128)}, f32[1,384,1152]{1,2,0:T(8,128)}, f32[1,384,384]{2,1,0:T(8,128)}, f32[1,384,384]{2,1,0:T(8,128)}) async-done(((f32[1,384,1152]{1,2,0:T(8,128)}, f32[1,384,1152]{1,2,0:T(8,128)}, f32[1,384,384]{2,1,0:T(8,128)}, f32[1,384,384]{2,1,0:T(8,128)}), (f32[1,384,1152]{1,2,0:T(8,128)}, f32[1,384,1152]{1,2,0:T(8,128)}, f32[1,384,384]{2,1,0:T(8,128)}, ...) | async-done | bytes 4718608 | tf_op jit(solution)/shard_map/psum | solution.py:517
  281.7 3.0 multiply_reduce_fusion
  285.4 2.9 copy.14
  288.3 2.3 maximum_multiply_fusion.1
  290.6 2.5 add_convert_fusion
  293.1 9.9 %shard_map.106 = f32[32,32,384]{2,1,0:T(8,128)} custom-call(bf16[32,32,384]{2,1,0:T(8,128)(2,1)} %get-tuple-element.26.start_ref, s32[32,32]{1,0:T(8,128)} %vis_ref.3, f32[1,384]{1,0:T(1,128)} %get-tuple-element.61.gain_ref, f32[32,32,384]{2,1,0:T(8,128)} %bitcast.38, f32[32,32,384]{2,1,0:T(8,128)} %bitcast.39, bf16[32,32,384]{2,1,0:T(8,128)(2,1)} %bitcast.37), custom_call_target="tpu_custom_call" | custom-call | tf_op jit(solution)/shard_map/pallas_call | solution.py:509
  (71 shorter events, 8.0 us)
Async XLA Ops:
  7.2 274.6 %all-reduce.3.cloned.1.call-start = ((), (), s32[]{:S(2)}) async-start(), calls=%async_computation | async-start | bytes 9437184 | tf_op jit(solution)/shard_map/psum | solution.py:517
  16.6 20.7 %collective-permute-start.1 = (bf16[1024,384]{1,0:T(8,128)(2,1)}, bf16[1024,384]{1,0:T(8,128)(2,1)S(1)}, u32[]{:S(2)}, u32[]{:S(2)}) collective-permute-start(bf16[1024,384]{1,0:T(8,128)(2,1)} %bitcast.32), channel_id=1, source_target_pairs={{0,2},{2,0},{4,6},{6,4},{8,10},{10,8},{12,14},{14,12},{1,3},{3,1},... | collective-permute-start | bytes 2359304 | tf_op jit(solution)/shard_map/ppermute | solution.py:41
  37.3 23.6 %copy-start.2 = (bf16[1024,384]{1,0:T(8,128)(2,1)}, bf16[1024,384]{1,0:T(8,128)(2,1)S(1)}, u32[]{:S(2)}) copy-start(bf16[1024,384]{1,0:T(8,128)(2,1)S(1)} %collective-permute-done.1.n2) | copy-start | bytes 2359300
  37.3 20.5 %collective-permute-start.2 = (bf16[1024,384]{1,0:T(8,128)(2,1)S(1)}, bf16[1024,384]{1,0:T(8,128)(2,1)S(1)}, u32[]{:S(2)}, u32[]{:S(2)}) collective-permute-start(bf16[1024,384]{1,0:T(8,128)(2,1)S(1)} %collective-permute-done.1.n2), channel_id=1, source_target_pairs={{0,4},{2,14},{4,8},{6,2},{8,12},{10,6},{12,0},{14,10},{1,5},{3,15}... | collective-permute-start | bytes 2359304 | tf_op jit(solution)/shard_map/ppermute | solution.py:41
  39.1 25.2 %collective-permute-start = (bf16[1024,384]{1,0:T(8,128)(2,1)}, bf16[1024,384]{1,0:T(8,128)(2,1)}, u32[]{:S(2)}, u32[]{:S(2)}) collective-permute-start(bf16[1024,384]{1,0:T(8,128)(2,1)} %bitcast.33), channel_id=1, source_target_pairs={{0,1},{1,0},{2,3},{3,2},{4,5},{5,4},{6,7},{7,6},{8,9},{9,8},{10,11... | collective-permute-start | bytes 2359304 | tf_op jit(solution)/shard_map/ppermute | solution.py:41
  39.1 25.2 %collective-permute-start.3 = (bf16[1024,384]{1,0:T(8,128)(2,1)S(1)}, bf16[1024,384]{1,0:T(8,128)(2,1)}, u32[]{:S(2)}, u32[]{:S(2)}) collective-permute-start(bf16[1024,384]{1,0:T(8,128)(2,1)S(1)} %collective-permute-done.1.n2), channel_id=1, source_target_pairs={{0,1},{1,0},{2,3},{3,2},{4,5},{5,4},{6,7},{7,6},{8,9},{9,8},{10,11... | collective-permute-start | bytes 2359304 | tf_op jit(solution)/shard_map/ppermute | solution.py:41
  57.9 3.1 copy-start.3
  57.9 6.5 %collective-permute-start.4 = (bf16[1024,384]{1,0:T(8,128)(2,1)S(1)}, bf16[1024,384]{1,0:T(8,128)(2,1)}, u32[]{:S(2)}, u32[]{:S(2)}) collective-permute-start(bf16[1024,384]{1,0:T(8,128)(2,1)S(1)} %collective-permute-done.2.n3), channel_id=1, source_target_pairs={{0,1},{1,0},{2,3},{3,2},{4,5},{5,4},{6,7},{7,6},{8,9},{9,8},{10,11... | collective-permute-start | bytes 2359304 | tf_op jit(solution)/shard_map/ppermute | solution.py:41
  60.9 16.9 %copy-start = (bf16[2,384,1152]{1,2,0:T(8,128)(2,1)}, bf16[2,384,1152]{1,2,0:T(8,128)(2,1)S(1)}, u32[]{:S(2)}) copy-start(bf16[2,384,1152]{1,2,0:T(8,128)(2,1)S(1)} %copy.11) | copy-start | bytes 5308420
  64.3 25.6 %copy-start.1 = (bf16[2,384,1152]{2,1,0:T(8,128)(2,1)S(1)}, bf16[2,384,1152]{2,1,0:T(8,128)(2,1)}, u32[]{:S(2)}) copy-start(bf16[2,384,1152]{2,1,0:T(8,128)(2,1)} %param.11) | copy-start | bytes 5308420
  77.9 7.3 %collective-permute-start.7 = (bf16[128,384]{1,0:T(8,128)(2,1)}, bf16[128,384]{1,0:T(8,128)(2,1)S(1)}, u32[]{:S(2)}, u32[]{:S(2)}) collective-permute-start(bf16[128,384]{1,0:T(8,128)(2,1)} %get-tuple-element.34), channel_id=1, source_target_pairs={{0,14},{2,0},{4,2},{6,4},{8,6},{10,8},{12,10},{14,12},{1,15},{3,1}... | collective-permute-start | bytes 294920 | tf_op jit(solution)/shard_map/ppermute | solution.py:41
  82.4 7.5 %collective-permute-start.6 = (bf16[128,384]{1,0:T(8,128)(2,1)}, bf16[128,384]{1,0:T(8,128)(2,1)S(1)}, u32[]{:S(2)}, u32[]{:S(2)}) collective-permute-start(bf16[128,384]{1,0:T(8,128)(2,1)} %get-tuple-element.34), channel_id=1, source_target_pairs={{0,2},{2,4},{4,6},{6,8},{8,10},{10,12},{12,14},{14,0},{1,3},{3,5},... | collective-permute-start | bytes 294920 | tf_op jit(solution)/shard_map/ppermute | solution.py:41
  82.4 8.6 %collective-permute-start.5 = (bf16[128,384]{1,0:T(8,128)(2,1)}, bf16[128,384]{1,0:T(8,128)(2,1)S(1)}, u32[]{:S(2)}, u32[]{:S(2)}) collective-permute-start(bf16[128,384]{1,0:T(8,128)(2,1)} %get-tuple-element.34), channel_id=1, source_target_pairs={{0,1},{1,0},{2,3},{3,2},{4,5},{5,4},{6,7},{7,6},{8,9},{9,8},{10,11... | collective-permute-start | bytes 294920 | tf_op jit(solution)/shard_map/ppermute | solution.py:41
  85.2 6.1 %copy-start.9 = (bf16[128,384]{1,0:T(8,128)(2,1)}, bf16[128,384]{1,0:T(8,128)(2,1)S(1)}, u32[]{:S(2)}) copy-start(bf16[128,384]{1,0:T(8,128)(2,1)S(1)} %collective-permute-done.7.pr) | copy-start | bytes 294916
  85.2 5.8 %collective-permute-start.9 = (bf16[128,384]{1,0:T(8,128)(2,1)S(1)}, bf16[128,384]{1,0:T(8,128)(2,1)S(1)}, u32[]{:S(2)}, u32[]{:S(2)}) collective-permute-start(bf16[128,384]{1,0:T(8,128)(2,1)S(1)} %collective-permute-done.7.pr), channel_id=1, source_target_pairs={{0,1},{1,0},{2,3},{3,2},{4,5},{5,4},{6,7},{7,6},{8,9},{9,8},{10,11... | collective-permute-start | bytes 294920 | tf_op jit(solution)/shard_map/ppermute | solution.py:41
  90.0 1.3 copy-start.10
  90.0 1.3 collective-permute-start.8
  114.5 6.0 %collective-permute-start.12 = (bf16[128,384]{1,0:T(8,128)(2,1)}, bf16[128,384]{1,0:T(8,128)(2,1)S(1)}, u32[]{:S(2)}, u32[]{:S(2)}) collective-permute-start(bf16[128,384]{1,0:T(8,128)(2,1)} %get-tuple-element.36), channel_id=1, source_target_pairs={{0,14},{2,0},{4,2},{6,4},{8,6},{10,8},{12,10},{14,12},{1,15},{3,1}... | collective-permute-start | bytes 294920 | tf_op jit(solution)/shard_map/ppermute | solution.py:41
  115.1 7.6 %collective-permute-start.11 = (bf16[128,384]{1,0:T(8,128)(2,1)}, bf16[128,384]{1,0:T(8,128)(2,1)S(1)}, u32[]{:S(2)}, u32[]{:S(2)}) collective-permute-start(bf16[128,384]{1,0:T(8,128)(2,1)} %get-tuple-element.36), channel_id=1, source_target_pairs={{0,2},{2,4},{4,6},{6,8},{8,10},{10,12},{12,14},{14,0},{1,3},{3,5},... | collective-permute-start | bytes 294920 | tf_op jit(solution)/shard_map/ppermute | solution.py:41
  116.5 6.2 %collective-permute-start.10 = (bf16[128,384]{1,0:T(8,128)(2,1)}, bf16[128,384]{1,0:T(8,128)(2,1)S(1)}, u32[]{:S(2)}, u32[]{:S(2)}) collective-permute-start(bf16[128,384]{1,0:T(8,128)(2,1)} %get-tuple-element.36), channel_id=1, source_target_pairs={{0,1},{1,0},{2,3},{3,2},{4,5},{5,4},{6,7},{7,6},{8,9},{9,8},{10,11... | collective-permute-start | bytes 294920 | tf_op jit(solution)/shard_map/ppermute | solution.py:41
  118.3 1.3 copy-start.8
  120.5 3.6 %collective-permute-start.14 = (bf16[128,384]{1,0:T(8,128)(2,1)S(1)}, bf16[128,384]{1,0:T(8,128)(2,1)S(1)}, u32[]{:S(2)}, u32[]{:S(2)}) collective-permute-start(bf16[128,384]{1,0:T(8,128)(2,1)S(1)} %collective-permute-done.12), channel_id=1, source_target_pairs={{0,1},{1,0},{2,3},{3,2},{4,5},{5,4},{6,7},{7,6},{8,9},{9,8},{10,11... | collective-permute-start | bytes 294920 | tf_op jit(solution)/shard_map/ppermute | solution.py:41
  122.7 1.3 collective-permute-start.13
  147.7 2.7 copy-start.7
  147.7 5.1 %collective-permute-start.16 = (bf16[1024,384]{1,0:T(8,128)(2,1)}, bf16[1024,384]{1,0:T(8,128)(2,1)S(1)}, u32[]{:S(2)}, u32[]{:S(2)}) collective-permute-start(bf16[1024,384]{1,0:T(8,128)(2,1)} %get-tuple-element.42), channel_id=1, source_target_pairs={{0,1},{1,0},{2,3},{3,2},{4,5},{5,4},{6,7},{7,6},{8,9},{9,8},{10,11... | collective-permute-start | bytes 2359304 | tf_op jit(solution)/shard_map/ppermute | solution.py:41
  151.3 1.5 copy-start.5
  151.4 37.6 %copy-start.4 = (bf16[1024,384]{1,0:T(8,128)(2,1)S(1)}, bf16[1024,384]{1,0:T(8,128)(2,1)}, u32[]{:S(2)}) copy-start(bf16[1024,384]{1,0:T(8,128)(2,1)} %get-tuple-element.39) | copy-start | bytes 2359300
  152.5 2.3 collective-permute-start.15
  153.0 36.0 %collective-permute-start.17 = (bf16[1024,384]{1,0:T(8,128)(2,1)S(1)}, bf16[1024,384]{1,0:T(8,128)(2,1)S(1)}, u32[]{:S(2)}, u32[]{:S(2)}) collective-permute-start(bf16[1024,384]{1,0:T(8,128)(2,1)S(1)} %add_convert_fusion.2), channel_id=1, source_target_pairs={{0,12},{2,6},{4,0},{6,10},{8,4},{10,14},{12,8},{14,2},{1,13},{3,7}... | collective-permute-start | bytes 2359304 | tf_op jit(solution)/shard_map/ppermute | solution.py:41
  153.1 137.5 %collective-permute-start.19 = (bf16[1024,384]{1,0:T(8,128)(2,1)}, bf16[1024,384]{1,0:T(8,128)(2,1)}, u32[]{:S(2)}, u32[]{:S(2)}) collective-permute-start(bf16[1024,384]{1,0:T(8,128)(2,1)} %get-tuple-element.43), channel_id=1, source_target_pairs={{0,1},{1,0},{2,3},{3,2},{4,5},{5,4},{6,7},{7,6},{8,9},{9,8},{10,11... | collective-permute-start | bytes 2359304 | tf_op jit(solution)/shard_map/ppermute | solution.py:41
  190.2 100.4 %collective-permute-start.18 = (bf16[1024,384]{1,0:T(8,128)(2,1)}, bf16[1024,384]{1,0:T(8,128)(2,1)}, u32[]{:S(2)}, u32[]{:S(2)}) collective-permute-start(bf16[1024,384]{1,0:T(8,128)(2,1)} %add_convert_fusion.1), channel_id=1, source_target_pairs={{0,2},{2,0},{4,6},{6,4},{8,10},{10,8},{12,14},{14,12},{1,3},{3,1},... | collective-permute-start | bytes 2359304 | tf_op jit(solution)/shard_map/ppermute | solution.py:41
  281.7 3.0 copy-start.14
  (5 other events, 3.9 us)
Sparse Core Ops, SparseCore 0:
  151.5 130.2 all-reduce.2

commit v2 on v1

v2 whole, which is shorter than its diff:
```python
import functools

import jax
import jax.numpy as jnp
from jax import lax
from jax.experimental import pallas as pl
from jax.experimental.pallas import tpu as pltpu
from jax.sharding import PartitionSpec as P

HEADS = 6
EPS = 1e-05
F32 = jnp.float32
BF16 = jnp.bfloat16
VMEM_BYTES = 56 * 1024 * 1024
HALO = 112
CORNER = 96
RETURNED = 224


def nn(a, b):
    return lax.dot_general(a, b, (((1,), (0,)), ((), ())), preferred_element_type=F32)


def nt(a, b):
    return lax.dot_general(a, b, (((1,), (1,)), ((), ())), preferred_element_type=F32)


def tn(a, b):
    return lax.dot_general(a, b, (((0,), (0,)), ((), ())), preferred_element_type=F32)


def iota(shape, dim):
    return lax.broadcasted_iota(jnp.int32, shape, dim)


def one_hot(condition):
    return jnp.where(condition, 1.0, 0.0).astype(BF16)


def permuted(value, axis, target):
    count = lax.axis_size(axis)
    return lax.ppermute(value, axis, [(i, target(i) % count) for i in range(count)])


def lat_swap(value):
    return permuted(value, "lat", lambda i: i ^ 1)


def lon_swap(value):
    return permuted(value, "lon", lambda i: i ^ 1)


def lon_forward(value):
    return permuted(value, "lon", lambda i: i + 2 if i % 2 == 0 else i - 2)


def lon_backward(value):
    return permuted(value, "lon", lambda i: i - 2 if i % 2 == 0 else i + 2)


def from_left(value):
    return permuted(value, "lon", lambda i: i + 1)


def from_right(value):
    return permuted(value, "lon", lambda i: i - 1)


def chained(value, after):
    return lax.optimization_barrier((value, after))


def exchanged(parts, axis_stride, factor):
    count = lax.axis_size("lon")
    digit = (lax.axis_index("lon") // axis_stride) % factor
    moved = []
    for d in range(1, factor):
        pairs = [(i, shifted(i, axis_stride, factor, d)) for i in range(count)]
        moved.append(lax.ppermute(parts(lax.rem(digit + d, factor)), "lon", pairs))
    total = parts(digit).astype(F32)
    for piece in moved:
        total = total + piece.astype(F32)
    return total.astype(BF16)


def shifted(i, stride, factor, d):
    digit = (i // stride) % factor
    return i + ((digit + d) % factor - digit) * stride


def spread(value, axis_stride, factor):
    count = lax.axis_size("lon")
    digit = (lax.axis_index("lon") // axis_stride) % factor
    rows = value.shape[0]
    full = jnp.zeros((factor * rows,) + value.shape[1:], value.dtype)
    full = lax.dynamic_update_slice(full, value, (digit * rows, 0))
    for d in range(1, factor):
        pairs = [(i, shifted(i, axis_stride, factor, d)) for i in range(count)]
        got = lax.ppermute(value, "lon", pairs)
        at = lax.rem(digit - d + factor, factor) * rows
        full = lax.dynamic_update_slice(full, got, (at, 0))
    return full


def lon_factors():
    left = lax.axis_size("lon")
    stride, out = 1, []
    for factor in [2] + [4] * 10:
        if left == 1:
            break
        factor = min(factor, left)
        out.append((stride, factor))
        stride, left = stride * factor, left // factor
    return out


def summed(value):
    lat = lax.axis_index("lat")
    half = value.shape[0] // 2
    mine = lax.dynamic_slice_in_dim(value, lat * half, half, 0)
    other = lat_swap(lax.dynamic_slice_in_dim(value, (1 - lat) * half, half, 0))
    value = (mine.astype(F32) + other.astype(F32)).astype(BF16)
    factors = lon_factors()
    for stride, factor in factors:
        size = value.shape[0] // factor
        take = lambda k, v=value, n=size: lax.dynamic_slice_in_dim(v, k * n, n, 0)
        value = exchanged(take, stride, factor)
    for stride, factor in factors[::-1]:
        value = spread(value, stride, factor)
    other = lat_swap(value)
    return jnp.where(
        lat == 0, jnp.concatenate([value, other], 0), jnp.concatenate([other, value], 0)
    )


def norm_parts(x):
    mean = jnp.mean(x, axis=-1, keepdims=True)
    centred = x - mean
    spread = jnp.mean(centred * centred, axis=-1, keepdims=True)
    rstd = lax.rsqrt(spread + EPS)
    return centred * rstd, rstd


def norm_back(x, gain, grad_normal):
    xhat, rstd = norm_parts(x)
    g = grad_normal * gain
    return rstd * (
        g - jnp.mean(g, axis=-1, keepdims=True) - xhat * jnp.mean(g * xhat, axis=-1, keepdims=True)
    )


def shown_column(visible, base, tile):
    rows, cols = visible.shape
    token = base + iota((tile, rows), 0)
    of_row = nn(one_hot(token // cols == iota((tile, rows), 1)), visible.astype(F32).astype(BF16))
    token = base + iota((tile, cols), 0)
    mine = token % cols == iota((tile, cols), 1)
    return jnp.sum(jnp.where(mine, of_row, 0.0), axis=1, keepdims=True)


def start_kernel(first, tok_ref, vis_ref, mask_ref, gain_ref, start_ref, normal_ref):
    tile, width = tok_ref.shape
    base = first + pl.program_id(0) * tile
    shown = shown_column(vis_ref[...], base, tile)
    x = jnp.where(shown > 0.5, tok_ref[...].astype(F32), mask_ref[...].astype(F32))
    start_ref[...] = x.astype(BF16)
    xhat, _ = norm_parts(x)
    normal_ref[...] = (xhat * gain_ref[...]).astype(BF16)


def first_kernel(
    first, lat_ref, n0, n1, n2, n3, n4, n5, start_ref, row_in, left_in, right_in,
    wt_ref, wo_ref, gain_ref,
    q_ref, kv_ref, p_ref, mixed_ref, h_ref, normal_ref, row_ref, left_ref, right_ref,
    w_s, pack_s,
):
    width, tile = q_ref.shape
    head = width // HEADS
    blocks = (n0, n1, n2, n3, n4, n5)
    q_ref[...] = nt(wt_ref[0:width], n0[...]).astype(BF16)
    for b, ref in enumerate(blocks):
        kv_ref[b] = nt(wt_ref[width : 3 * width], ref[...]).astype(BF16)
    for h in range(HEADS):
        lo, hi = h * head, (h + 1) * head
        q = q_ref[lo:hi, :].astype(F32) * (head**-0.5)
        total = jnp.zeros((1, tile), F32)
        out = jnp.zeros((head, tile), F32)
        for b in range(len(blocks)):
            k = kv_ref[b, lo:hi, :].astype(F32)
            w = jnp.exp(jnp.sum(q * k, axis=0, keepdims=True))
            w_s[b, h : h + 1, :] = w
            total = total + w
            out = out + w * kv_ref[b, width + lo : width + hi, :].astype(F32)
        inverse = 1.0 / total
        for b in range(len(blocks)):
            p_ref[b, h : h + 1, :] = w_s[b, h : h + 1, :] * inverse
        mixed_ref[lo:hi, :] = (out * inverse).astype(BF16)
    h1 = start_ref[...].astype(F32) + tn(mixed_ref[...], wo_ref[...])
    h1 = h1.astype(BF16)
    h_ref[...] = h1
    xhat, _ = norm_parts(h1.astype(F32))
    normal = (xhat * gain_ref[...]).astype(BF16)
    normal_ref[...] = normal
    step = pl.program_id(0)
    brow = jnp.where(lat_ref[0] == 0, 31, 0)
    slot = iota((96, tile), 0)
    token = first + step * tile + iota((96, tile), 1)
    r, c = token // 32, token % 32
    pick = one_hot(
        ((slot < 32) & (r == brow) & (c == slot))
        | ((slot >= 32) & (slot < 64) & (c == 0) & (r == slot - 32))
        | ((slot >= 64) & (c == 31) & (r == slot - 64))
    )

    @pl.when(step == 0)
    def _():
        for i, ref in enumerate((row_in, left_in, right_in)):
            pack_s[i * 32 : i * 32 + 32, :] = ref[...].astype(F32)

    pack_s[...] += nn(pick, normal)

    @pl.when(step == pl.num_programs(0) - 1)
    def _():
        for i, ref in enumerate((row_ref, left_ref, right_ref)):
            ref[...] = pack_s[i * 32 : i * 32 + 32, :].astype(BF16)


def second_kernel(
    lat_ref, na_ref, nb_ref, row_ref, left_ref, right_ref, dleft_ref, dright_ref,
    w_ref, wo_ref, cot_ref,
    dn_ref, brow_ref, bleft_ref, bright_ref, dw_ref,
    q_s, k_s, v_s, kc_s, vc_s, dq_s, dk_s, dv_s, dkc_s, dvc_s, do_s, mixed_s, halo_s, mask_s, normal_s,
):
    points, width = cot_ref.shape
    head = width // HEADS
    upper = lat_ref[0] == 0
    halo_s[0:32, :] = row_ref[...]
    halo_s[32:64, :] = left_ref[...]
    halo_s[64:96, :] = right_ref[...]
    a, b = iota((16, 32), 0), iota((16, 32), 1)
    sent = b == jnp.where(upper, 0, 31)
    corners = nn(one_hot(sent & (a == 0)), dleft_ref[...])
    corners += nn(one_hot(sent & (a == 1)), dright_ref[...])
    halo_s[CORNER:HALO, :] = corners.astype(BF16)
    halo = halo_s[...]
    normal_s[0 : points // 2, :] = na_ref[...]
    normal_s[points // 2 : points, :] = nb_ref[...]
    normal = normal_s[...]
    scale = head**-0.5
    q_s[...] = (nn(normal, w_ref[:, 0:width]).astype(BF16).astype(F32) * scale).astype(BF16)
    k_s[32 : 32 + points, :] = nn(normal, w_ref[:, width : 2 * width]).astype(BF16)
    v_s[32 : 32 + points, :] = nn(normal, w_ref[:, 2 * width : 3 * width]).astype(BF16)
    kh = nn(halo, w_ref[:, width : 2 * width]).astype(BF16)
    vh = nn(halo, w_ref[:, 2 * width : 3 * width]).astype(BF16)
    for at in (0, 32 + points):
        k_s[at : at + 32, :] = kh[0:32]
        v_s[at : at + 32, :] = vh[0:32]
    kc_s[...] = kh[32:HALO]
    vc_s[...] = vh[32:HALO]
    dk_s[...] = jnp.zeros_like(dk_s)
    dv_s[...] = jnp.zeros_like(dv_s)
    dkc_s[...] = jnp.zeros_like(dkc_s)
    dvc_s[...] = jnp.zeros_like(dvc_s)
    cot = cot_ref[...].astype(BF16)
    do_s[...] = nt(cot, wo_ref[...]).astype(BF16)

    key, query = iota((192, 256), 0), iota((192, 256), 1) % 128
    drow = key // 32 - 1 - query // 32
    dcol = key % 32 - query % 32
    mask_s[...] = jnp.where((jnp.abs(drow) <= 1) & (jnp.abs(dcol) <= 1), 1.0, 0.0)

    tiles = points // 128

    def tile_step(t, carry):
        base = pl.multiple_of(t * 128, 128)
        key = iota((192, 256), 0)
        first = jnp.where(upper & (t == 0), 32, 0)
        last = jnp.where(jnp.logical_not(upper) & (t == tiles - 1), 160, 192)
        mask1 = (mask_s[...] > 0.5) & (key >= first) & (key < last)
        e, query = iota((HALO - 32, 256), 0), iota((HALO - 32, 256), 1) % 128
        corner = e >= 64
        key_row = jnp.where(corner, jnp.where(upper, 32, -1), e % 32)
        is_left = (e < 32) | (e == 64)
        near = jnp.abs(key_row - (4 * t + query // 32)) <= 1
        side = query % 32 == jnp.where(is_left, 0, 31)
        mask2 = near & side & (e < 66)
        lane = iota((128, 128), 1)
        even = lane < 64
        for pair in range(HEADS // 2):
            lanes = slice(pair * 128, pair * 128 + 128)
            win = pl.ds(base, 192)
            here = pl.ds(base, 128)
            q = q_s[here, lanes]
            do = do_s[here, lanes]
            zero = jnp.zeros_like(q)
            qm = jnp.concatenate([jnp.where(even, q, zero), jnp.where(even, zero, q)], 0)
            dom = jnp.concatenate([jnp.where(even, do, zero), jnp.where(even, zero, do)], 0)
            k1, v1 = k_s[win, lanes], v_s[win, lanes]
            k2, v2 = kc_s[:, lanes], vc_s[:, lanes]
            w1 = jnp.where(mask1, jnp.exp(nt(k1, qm)), 0.0)
            w2 = jnp.where(mask2, jnp.exp(nt(k2, qm)), 0.0)
            total = jnp.sum(w1, axis=0, keepdims=True) + jnp.sum(w2, axis=0, keepdims=True)
            inverse = 1.0 / total
            p1, p2 = w1 * inverse, w2 * inverse
            dp1, dp2 = nt(v1, dom), nt(v2, dom)
            delta = jnp.sum(p1 * dp1, axis=0, keepdims=True) + jnp.sum(
                p2 * dp2, axis=0, keepdims=True
            )
            ds1, ds2 = (p1 * (dp1 - delta)).astype(BF16), (p2 * (dp2 - delta)).astype(BF16)
            p1, p2 = p1.astype(BF16), p2.astype(BF16)
            out = tn(p1, v1) + tn(p2, v2)
            mixed_s[here, lanes] = jnp.where(even, out[0:128], out[128:256]).astype(BF16)
            dq = (tn(ds1, k1) + tn(ds2, k2)) * scale
            dq_s[here, lanes] = jnp.where(even, dq[0:128], dq[128:256]).astype(BF16)
            dk_s[win, lanes] += nn(ds1, qm)
            dv_s[win, lanes] += nn(p1, dom)
            dkc_s[:, lanes] += nn(ds2, qm)
            dvc_s[:, lanes] += nn(p2, dom)
        return carry

    lax.fori_loop(0, tiles, tile_step, 0)

    row_at = pl.multiple_of(jnp.where(upper, 32 + points, 0), 32)
    dkh = jnp.concatenate([dk_s[pl.ds(row_at, 32), :], dkc_s[...]], 0).astype(BF16)
    dvh = jnp.concatenate([dv_s[pl.ds(row_at, 32), :], dvc_s[...]], 0).astype(BF16)
    dq = dq_s[...]
    dk = dk_s[32 : 32 + points, :].astype(BF16)
    dv = dv_s[32 : 32 + points, :].astype(BF16)
    wq, wk, wv = (w_ref[:, i * width : (i + 1) * width] for i in range(3))
    dn_ref[...] = nt(dq, wq) + nt(dk, wk) + nt(dv, wv)
    back = (nt(dkh, wk) + nt(dvh, wv)).astype(BF16)
    brow_ref[...] = back[0:32]
    for ref, at in ((bleft_ref, 32), (bright_ref, 64)):
        ref[0:32, :] = back[at : at + 32]
        ref[32:48, :] = back[CORNER:HALO]
    dw_ref[0:width, :] = tn(dq, normal).astype(BF16)
    dw_ref[width : 2 * width, :] = (tn(dk, normal) + tn(dkh, halo)).astype(BF16)
    dw_ref[2 * width : 3 * width, :] = (tn(dv, normal) + tn(dvh, halo)).astype(BF16)
    dw_ref[3 * width : 4 * width, :] = tn(mixed_s[...], cot).astype(BF16)


def third_kernel(
    first, lat_ref, n0, n1, n2, n3, n4, n5, q_ref, kv_ref, p_ref, mixed_ref, h_ref, dn1_ref, cot_ref,
    packs_ref, wt_ref, wo_ref, gain_ref, dw_in,
    dh_ref, d0, d1, d2, d3, d4, d5, dw_ref,
    dw_s, dmix_s, dkv_s, dq_s, dp_s,
):
    width, tile = q_ref.shape
    head = width // HEADS
    scale = head**-0.5
    blocks = (n0, n1, n2, n3, n4, n5)
    outs = (d0, d1, d2, d3, d4, d5)
    step = pl.program_id(0)

    @pl.when(step == 0)
    def _():
        dw_s[...] = jnp.zeros_like(dw_s) if dw_in is None else dw_in[...]

    brow = jnp.where(lat_ref[0] == 0, 31, 0)
    shape = (tile, RETURNED)
    token = first + step * tile + iota(shape, 0)
    r, c, slot = token // 32, token % 32, iota(shape, 1)
    border = r == brow
    place = one_hot(
        (border & (slot < 32) & (slot == c))
        | ((c == 0) & (slot < 64) & (slot == 32 + r))
        | ((c == 31) & (slot < 112) & (slot == 80 + r))
        | (border & (c == 0) & (slot == 128 + 33))
        | (border & (c == 31) & (slot == 176 + 32))
    )
    dn = dn1_ref[...] + nn(place, packs_ref[...])
    dh = cot_ref[...] + norm_back(h_ref[...].astype(F32), gain_ref[...], dn)
    dh_ref[...] = dh
    dhb = dh.astype(BF16)
    dmix_s[...] = nt(wo_ref[...], dhb)
    dw_s[3 * width : 4 * width, :] += nn(mixed_ref[...], dhb)
    for h in range(HEADS):
        lo, hi = h * head, (h + 1) * head
        dmix = dmix_s[lo:hi, :]
        delta = jnp.zeros((1, tile), F32)
        for b in range(len(blocks)):
            dp = jnp.sum(
                dmix * kv_ref[b, width + lo : width + hi, :].astype(F32), axis=0, keepdims=True
            )
            dp_s[b : b + 1, :] = dp
            delta = delta + p_ref[b, h : h + 1, :] * dp
        q = q_ref[lo:hi, :].astype(F32)
        dq = jnp.zeros((head, tile), F32)
        for b in range(len(blocks)):
            p = p_ref[b, h : h + 1, :]
            ds = p * (dp_s[b : b + 1, :] - delta) * scale
            dq = dq + ds * kv_ref[b, lo:hi, :].astype(F32)
            dkv_s[b, lo:hi, :] = (ds * q).astype(BF16)
            dkv_s[b, width + lo : width + hi, :] = (p * dmix).astype(BF16)
        dq_s[lo:hi, :] = dq.astype(BF16)
    dq = dq_s[...]
    dw_s[0:width, :] += nn(dq, n0[...])
    for b, (ref, out) in enumerate(zip(blocks, outs)):
        dkv = dkv_s[b]
        grad = tn(dkv, wt_ref[width : 3 * width])
        if b == 0:
            grad = grad + tn(dq, wt_ref[0:width])
        out[...] = grad.astype(out.dtype)
        dw_s[width : 3 * width, :] += nn(dkv, ref[...])

    @pl.when(step == pl.num_programs(0) - 1)
    def _():
        dw_ref[...] = dw_s[...].astype(dw_ref.dtype)


def last_kernel(
    first, start_ref, vis_ref, gain_ref, dh_ref, own_ref, far_ref, near_ref, prev_ref, out_ref
):
    tile, width = start_ref.shape
    shown = shown_column(vis_ref[...], first + pl.program_id(0) * tile, tile)
    dn = own_ref[...] + far_ref[...].astype(F32) + near_ref[...].astype(F32)
    grad = dh_ref[...] + norm_back(start_ref[...].astype(F32), gain_ref[...], dn)
    out_ref[...] = jnp.where(shown > 0.5, grad, 0.0)


def weights_kernel(factor, r0_ref, r1_ref, wt_ref, gain_ref, qkv_ref, out_ref, gain_out_ref):
    width = r0_ref.shape[1]
    for layer, ref in enumerate((r0_ref, r1_ref)):
        acc = jnp.zeros((1, width), F32)
        for i in range(3):
            lo, hi = i * width, (i + 1) * width
            grad = ref[lo:hi, :].astype(F32) * factor
            weight = wt_ref[layer, lo:hi, :].astype(F32)
            acc = acc + jnp.sum(weight * grad, axis=0, keepdims=True)
            qkv_ref[layer, :, lo:hi] = grad.T
        out_ref[layer] = ref[3 * width : 4 * width, :].astype(F32) * factor
        gain_out_ref[layer : layer + 1, :] = acc / gain_ref[layer : layer + 1, :]


def call(
    kernel, out_shape, scratch=(), grid=None, in_specs=None, out_specs=None, us=1, aliases=None
):
    return pl.pallas_call(
        kernel,
        out_shape=out_shape,
        grid_spec=pltpu.PrefetchScalarGridSpec(
            num_scalar_prefetch=0,
            grid=grid or (),
            in_specs=in_specs,
            out_specs=out_specs,
            scratch_shapes=list(scratch),
        ),
        input_output_aliases=aliases or {},
        cost_estimate=pl.CostEstimate(
            flops=int(us * 1e6 * 800), bytes_accessed=int(us * 1e6), transcendentals=0
        ),
        compiler_params=pltpu.CompilerParams(vmem_limit_bytes=VMEM_BYTES),
    )


def whole():
    return pl.BlockSpec(memory_space=pltpu.VMEM)


def scalar():
    return pl.BlockSpec(memory_space=pltpu.SMEM)


def fixed(shape):
    return pl.BlockSpec(shape, lambda i: (0,) * len(shape))


def token_spec(tile, width, first=0):
    at = first // tile
    return pl.BlockSpec((tile, width), lambda i: (i + at, 0))


CHUNKS = 2


def local(
    tokens, visible, mask_token, norm_gain_table, query_key_value_weight, output_weight, cotangent
):
    rows, cols, width = tokens.shape
    points = rows * cols
    size = points // CHUNKS
    firsts = [c * size for c in range(CHUNKS)]
    lat_count, lon_count = lax.axis_size("lat"), lax.axis_size("lon")
    lat = lax.axis_index("lat").astype(jnp.int32).reshape(1)
    gain0, gain1 = norm_gain_table[0:1], norm_gain_table[1:2]
    w1 = query_key_value_weight[1]
    wo0, wo1 = output_weight[0], output_weight[1]
    wt = jnp.swapaxes(query_key_value_weight, 1, 2)
    wt0 = wt[0]
    struct = jax.ShapeDtypeStruct
    tokens = tokens.reshape(points, width)
    cot = cotangent.reshape(points, width)
    mask_row = mask_token.reshape(1, width)
    part = struct((size, width), BF16)

    small = 128
    starts, normals = [], []
    for first in firsts:
        start, normal = call(
            functools.partial(start_kernel, first),
            (part, part),
            grid=(size // small,),
            in_specs=[
                token_spec(small, width, first),
                fixed((rows, cols)),
                fixed((1, width)),
                fixed((1, width)),
            ],
            out_specs=(token_spec(small, width),) * 2,
            us=2,
        )(tokens, visible, mask_row, gain0)
        starts.append(start)
        normals.append(normal)

    blocks = []
    before = None
    for c in range(CHUNKS):
        own = normals[c]
        if before is not None:
            own, before = chained(own, before)
        swapped = lon_swap(own)
        beyond = lon_forward(swapped)
        before = swapped
        blocks.append(
            [own, lat_swap(own), swapped, beyond, lat_swap(swapped), lat_swap(beyond)]
        )

    tile = 256
    steps = size // tile
    tok_spec = token_spec(tile, width)
    feat_spec = pl.BlockSpec((width, tile), lambda i: (0, i))
    kv_spec = pl.BlockSpec((6, 2 * width, tile), lambda i: (0, 0, i))
    p_spec = pl.BlockSpec((6, 8, tile), lambda i: (0, 0, i))
    packs = [jnp.zeros((32, width), BF16)] * 3
    kept = []
    for c in range(CHUNKS):
        *keep, normal1, row, left, right = call(
            functools.partial(first_kernel, firsts[c]),
            (
                struct((width, size), BF16),
                struct((6, 2 * width, size), BF16),
                struct((6, 8, size), F32),
                struct((width, size), BF16),
                part,
                part,
                *[struct((32, width), BF16)] * 3,
            ),
            grid=(steps,),
            in_specs=[scalar()]
            + [tok_spec] * 7
            + [fixed((32, width))] * 3
            + [fixed((3 * width, width)), fixed((width, width)), fixed((1, width))],
            out_specs=(
                feat_spec, kv_spec, p_spec, feat_spec, tok_spec, tok_spec,
                *[fixed((32, width))] * 3,
            ),
            scratch=[pltpu.VMEM((6, 8, tile), F32), pltpu.VMEM((96, width), F32)],
            us=7,
        )(lat, *blocks[c], starts[c], *packs, wt0, wo0, gain1)
        packs = [row, left, right]
        kept.append((keep, normal1))

    row, left, right = packs
    from_l, from_r = from_left(right), from_right(left)
    ext = points + 64
    halo_cols = HALO - 32
    dn1, brow, bleft, bright, dw1 = call(
        second_kernel,
        (
            struct((points, width), F32),
            struct((32, width), BF16),
            struct((48, width), BF16),
            struct((48, width), BF16),
            struct((4 * width, width), BF16),
        ),
        in_specs=[scalar()] + [whole()] * 10,
        out_specs=(whole(),) * 5,
        scratch=[
            pltpu.VMEM((points, width), BF16),
            pltpu.VMEM((ext, width), BF16),
            pltpu.VMEM((ext, width), BF16),
            pltpu.VMEM((halo_cols, width), BF16),
            pltpu.VMEM((halo_cols, width), BF16),
            pltpu.VMEM((points, width), BF16),
            pltpu.VMEM((ext, width), F32),
            pltpu.VMEM((ext, width), F32),
            pltpu.VMEM((halo_cols, width), F32),
            pltpu.VMEM((halo_cols, width), F32),
            pltpu.VMEM((points, width), BF16),
            pltpu.VMEM((points, width), BF16),
            pltpu.VMEM((HALO, width), BF16),
            pltpu.VMEM((192, 256), F32),
            pltpu.VMEM((points, width), BF16),
        ],
        us=22,
    )(
        lat, kept[0][1], kept[1][1], lat_swap(row), from_l, from_r, lat_swap(from_l),
        lat_swap(from_r), w1, wo1, cot,
    )

    sum1 = summed(dw1)

    from_l, from_r = from_left(bright), from_right(bleft)
    packs = jnp.concatenate(
        [lat_swap(brow), from_l, from_r, lat_swap(from_l), lat_swap(from_r)], 0
    )
    weights = None
    backs = []
    for c in range(CHUNKS):
        q0, kv0, p0, mixed0, h1 = kept[c][0]
        final = c == CHUNKS - 1
        kernel = functools.partial(third_kernel, firsts[c])
        extra = [] if weights is None else [weights]
        if weights is None:
            kernel = functools.partial(without_weights, kernel)
        *back, weights = call(
            kernel,
            (
                struct((size, width), F32),
                struct((size, width), F32),
                *[part] * 5,
                struct((4 * width, width), BF16 if final else F32),
            ),
            grid=(steps,),
            in_specs=[scalar()]
            + [tok_spec] * 6
            + [feat_spec, kv_spec, p_spec, feat_spec, tok_spec]
            + [token_spec(tile, width, firsts[c])] * 2
            + [
                fixed((RETURNED, width)),
                fixed((3 * width, width)),
                fixed((width, width)),
                fixed((1, width)),
            ]
            + [fixed((4 * width, width))] * len(extra),
            out_specs=(*[tok_spec] * 7, fixed((4 * width, width))),
            scratch=[
                pltpu.VMEM((4 * width, width), F32),
                pltpu.VMEM((width, tile), F32),
                pltpu.VMEM((6, 2 * width, tile), BF16),
                pltpu.VMEM((width, tile), BF16),
                pltpu.VMEM((8, tile), F32),
            ],
            us=11,
        )(
            lat, *blocks[c], q0, kv0, p0, mixed0, h1, dn1, cot, packs, wt0, wo0, gain1, *extra
        )
        backs.append(back)

    sum0 = summed(weights)

    def plus(a, b):
        return (a.astype(F32) + b.astype(F32)).astype(BF16)

    grad_tokens = None
    for c in range(CHUNKS):
        dh1, d0, d1, d2, d3, d4, d5 = backs[c]
        d3 = plus(d3, lat_swap(d5))
        d2 = plus(d2, lat_swap(d4))
        d2 = plus(d2, lon_backward(d3))
        extra = [] if grad_tokens is None else [grad_tokens]
        kernel = functools.partial(last_kernel, firsts[c])
        grad_tokens = call(
            kernel if extra else functools.partial(without_previous, kernel),
            struct((points, width), F32),
            grid=(size // small,),
            in_specs=[
                token_spec(small, width),
                fixed((rows, cols)),
                fixed((1, width)),
                *[token_spec(small, width)] * 4,
            ]
            + [pl.BlockSpec(memory_space=pl.ANY)] * len(extra),
            out_specs=token_spec(small, width, firsts[c]),
            aliases={7: 0} if extra else {},
            us=2,
        )(starts[c], visible, gain0, dh1, d0, lon_swap(d2), lat_swap(d1), *extra)

    factor = (points * lat_count * lon_count) ** (-0.5)
    g_qkv, g_out, g_gain = call(
        functools.partial(weights_kernel, factor),
        (
            struct((2, width, 3 * width), F32),
            struct((2, width, width), F32),
            struct((2, width), F32),
        ),
        in_specs=[whole()] * 4,
        out_specs=(whole(),) * 3,
        us=4,
    )(sum0, sum1, wt, norm_gain_table)
    return grad_tokens.reshape(rows, cols, width), g_qkv, g_out, g_gain


def without_weights(kernel, *refs):
    kernel(*refs[:18], None, *refs[18:])


def without_previous(kernel, *refs):
    kernel(*refs[:7], None, *refs[7:])


def solution(mesh):
    return jax.shard_map(
        local,
        mesh=mesh,
        in_specs=(
            P(("group", "lat"), "lon", None),
            P(("group", "lat"), "lon"),
            P(),
            P(),
            P(),
            P(),
            P(("group", "lat"), "lon", None),
        ),
        out_specs=(
            P(("group", "lat"), "lon", None),
            P("group", None, None),
            P("group", None, None),
            P("group", None),
        ),
        check_vma=False,
    )
```

time: 310 us -> 232 us (0.75)
  waiting for transfers between devices: 174 us -> 65.9 us
  starting transfers between devices: 13.3 us -> 58.9 us
  Pallas kernels: 75.7 us -> 88.8 us
  between operations: 14.2 us -> 1.19 us
  other arithmetic: 15.3 us -> 3.94 us
  local copies, waits for them, and re-layouts: 17.4 us -> 12.9 us
    psum x1 -> x0, waiting for transfers between devices: 91.5 us -> none  [local(): s1, so1 = lax.psum((dw1.astype(F32), dwo1.astype(F32)), ('lon', 'lat'))]
    ppermute x20 -> x34, waiting for transfers between devices: 82.3 us -> 39.1 us  [permuted(): lax.ppermute(value, axis, [(i, target(i) % count) for i in range(count)])]
    ppermute x0 -> x16, starting transfers between devices: none -> 28.8 us  [the longest x8 19.1 us: spread(): got = lax.ppermute(value, 'lon', pairs)]
    ppermute x0 -> x16, waiting for transfers between devices: none -> 26.8 us  [the longest x8 18.6 us: spread(): got = lax.ppermute(value, 'lon', pairs)]
    ppermute x20 -> x34, starting transfers between devices: 13.3 us -> 30.1 us  [permuted(): lax.ppermute(value, axis, [(i, target(i) % count) for i in range(count)])]
    pallas_call x5 -> x10, Pallas kernels: 75.7 us -> 88.8 us  [the longest x2 27.6 us: local(): call(kernel, (struct((size, width), F32), struct((size, width), F32), *[p...]
    another operation x4 -> x0, other arithmetic: 5.54 us -> none  [the longest x2 3.82 us: local(): g_qkv = jnp.stack([s0.T, s1]) * factor]
    unnamed x38 -> x55, local copies, waits for them, and re-layouts: 8.62 us -> 4.5 us
  transfers between devices with their start and end apart: 21 -> 50, of which waited for: 10 -> 26; matrix products, arithmetic and copies ran while one was open for 8% -> 4% of each run, Pallas kernels for 0% -> 9%
where the time goes in v2:
time: 232 us
  Pallas kernels  88.8 us (38%)
  waiting for transfers between devices  65.9 us (28%)
  starting transfers between devices  58.9 us (25%)
  local copies, waits for them, and re-layouts  12.9 us (6%)
  other arithmetic  3.94 us (2%)
    ppermute x34, waiting for transfers between devices, permuted(): lax.ppermute(value, axis, [(i, target(i) % count) for i in range(count)])  39.1 us
    ppermute x34, starting transfers between devices, permuted(): lax.ppermute(value, axis, [(i, target(i) % count) for i in range(count)])  30.1 us
    pallas_call x2, Pallas kernels, local(): call(kernel, (struct((size, width), F32), struct((size, width), F32), *[p...  27.6 us
    pallas_call x1, Pallas kernels, local(): call(second_kernel, (struct((points, width), F32), struct((32, width), BF...  22.3 us
    ppermute x8, starting transfers between devices, spread(): got = lax.ppermute(value, 'lon', pairs)  19.1 us
    ppermute x8, waiting for transfers between devices, spread(): got = lax.ppermute(value, 'lon', pairs)  18.6 us
    pallas_call x2, Pallas kernels, local(): call(functools.partial(first_kernel, firsts[c]), (struct((width, size), B...  17 us
    ppermute x8, starting transfers between devices, exchanged(): moved.append(lax.ppermute(parts(lax.rem(digit + d, factor)), 'lon', pairs))  9.71 us
  transfers between devices with their start and end apart: 50, of which 26 were waited for; matrix products, arithmetic and copies ran while one was open for 4% of the time, Pallas kernels for 9%

profile of v2, /device:TPU:0, one launch (start us, length us, event | category | flops | bytes accessed | tf_op | source)
XLA Modules:
  0.0 231.7 jit_solution(15966900342058426537)
XLA Ops:
  3.2 3.9 %shard_map.103 = (bf16[512,384]{1,0:T(8,128)(2,1)}, bf16[512,384]{1,0:T(8,128)(2,1)}) custom-call(bf16[1024,384]{1,0:T(8,128)(2,1)} %bitcast.18, s32[32,32]{1,0:T(8,128)} %vis_ref.5, bf16[1,384]{1,0:T(2,128)(2,1)} %reshape.24.mask_ref, f32[1,384]{1,0:T(1,128)} %get-tuple-element.111.gain_ref.refs_2_), custom_call_target="tpu_custom_call" | custom-call | flops 1600000000 | bytes 2000000 | tf_op jit(solution)/shard_map/pallas_call | solution.py:499
  7.1 3.0 %collective-permute-start = (bf16[512,384]{1,0:T(8,128)(2,1)}, bf16[512,384]{1,0:T(8,128)(2,1)}, u32[]{:S(2)}, u32[]{:S(2)}) collective-permute-start(bf16[512,384]{1,0:T(8,128)(2,1)} %get-tuple-element.53.n0.refs_1_), channel_id=1, source_target_pairs={{0,2},{2,0},{4,6},{6,4},{8,10},{10,8},{12,14},{14,12},{1,3},{3,1},... | collective-permute-start | bytes 1179656 | tf_op jit(solution)/shard_map/ppermute | solution.py:42
  10.1 4.0 %shard_map.102 = (bf16[512,384]{1,0:T(8,128)(2,1)}, bf16[512,384]{1,0:T(8,128)(2,1)}) custom-call(bf16[1024,384]{1,0:T(8,128)(2,1)} %bitcast.19, s32[32,32]{1,0:T(8,128)} %vis_ref.5, bf16[1,384]{1,0:T(2,128)(2,1)} %reshape.24.mask_ref, f32[1,384]{1,0:T(1,128)} %get-tuple-element.111.gain_ref.refs_2_), custom_call_target="tpu_custom_call" | custom-call | flops 1600000000 | bytes 2000000 | tf_op jit(solution)/shard_map/pallas_call | solution.py:499
  14.1 5.4 %collective-permute-done.n2.refs_3_ = bf16[512,384]{1,0:T(8,128)(2,1)} collective-permute-done((bf16[512,384]{1,0:T(8,128)(2,1)}, bf16[512,384]{1,0:T(8,128)(2,1)}, u32[]{:S(2)}, u32[]{:S(2)}) %collective-permute-start) | collective-permute-done | bytes 393248 | tf_op jit(solution)/shard_map/ppermute | solution.py:42
  24.0 2.4 %slice_bitcast_fusion.2 = (bf16[384,384]{1,0:T(8,128)(2,1)}, bf16[384,384]{1,0:T(8,128)(2,1)}) fusion(bf16[2,384,384]{2,1,0:T(8,128)(2,1)} %param.12), kind=kLoop, calls=%fused_computation.14 | loop fusion | bytes 1179648 | tf_op jit(solution)/shard_map/squeeze | solution.py:487
  26.9 3.2 %collective-permute-done.2.n2 = bf16[512,384]{1,0:T(8,128)(2,1)} collective-permute-done((bf16[512,384]{1,0:T(8,128)(2,1)}, bf16[512,384]{1,0:T(8,128)(2,1)}, u32[]{:S(2)}, u32[]{:S(2)}) %collective-permute-start.2) | collective-permute-done | bytes 393248 | tf_op jit(solution)/shard_map/ppermute | solution.py:42
  34.8 6.7 %collective-permute-done.3.n3 = bf16[512,384]{1,0:T(8,128)(2,1)S(1)} collective-permute-done((bf16[512,384]{1,0:T(8,128)(2,1)}, bf16[512,384]{1,0:T(8,128)(2,1)S(1)}, u32[]{:S(2)}, u32[]{:S(2)}) %collective-permute-start.3) | collective-permute-done | bytes 393248 | tf_op jit(solution)/shard_map/ppermute | solution.py:42
  42.5 8.5 %shard_map.104 = (bf16[384,512]{1,0:T(8,128)(2,1)}, bf16[6,768,512]{2,1,0:T(8,128)(2,1)}, f32[6,8,512]{2,1,0:T(8,128)}, bf16[384,512]{1,0:T(8,128)(2,1)}, bf16[5...) custom-call(s32[1]{0:T(128)} %bitcast.1.lat_ref.refs_0_, ...), custom_call_target="tpu_custom_call" | custom-call | flops 5600000000 | bytes 7000000 | tf_op jit(solution)/shard_map/pallas_call | solution.py:537
  52.1 8.5 %shard_map.105 = (bf16[384,512]{1,0:T(8,128)(2,1)}, bf16[6,768,512]{2,1,0:T(8,128)(2,1)}, f32[6,8,512]{2,1,0:T(8,128)}, bf16[384,512]{1,0:T(8,128)(2,1)}, bf16[5...) custom-call(s32[1]{0:T(128)} %bitcast.1.lat_ref.refs_0_, ...), custom_call_target="tpu_custom_call" | custom-call | flops 5600000000 | bytes 7000000 | tf_op jit(solution)/shard_map/pallas_call | solution.py:537
  61.1 4.2 %collective-permute-start.12 = (bf16[32,384]{1,0:T(8,128)(2,1)}, bf16[32,384]{1,0:T(8,128)(2,1)S(1)}, u32[]{:S(2)}, u32[]{:S(2)}) collective-permute-start(bf16[32,384]{1,0:T(8,128)(2,1)} %get-tuple-element.68), channel_id=1, source_target_pairs={{0,14},{2,0},{4,2},{6,4},{8,6},{10,8},{12,10},{14,12},{1,15},{3,1}... | collective-permute-start | bytes 73736 | tf_op jit(solution)/shard_map/ppermute | solution.py:42
  69.5 22.3 %shard_map.106 = (f32[1024,384]{1,0:T(8,128)}, bf16[32,384]{1,0:T(8,128)(2,1)}, bf16[48,384]{1,0:T(8,128)(2,1)}, bf16[48,384]{1,0:T(8,128)(2,1)}, bf16[1536,384]{1,0:T(8,128)(2,1)}) custom-call(s32[1]{0:T(128)} %bitcast.1.lat_ref.refs_0_, bf16[512,384]{1,0:T(8,128)(2,1)} %get-tuple-element.64.na_ref, bf16[512,384]{1,0:T(8,128)(2,1)} %get-tuple-element.65.nb_ref, ...), custom_call_target="tpu_custom_call" | custom-call | flops 17600000000 | bytes 22000000 | tf_op jit(solution)/shard_map/pallas_call | solution.py:567
  92.0 4.7 %collective-permute-start.17 = (bf16[48,384]{1,0:T(8,128)(2,1)}, bf16[48,384]{1,0:T(8,128)(2,1)S(1)}, u32[]{:S(2)}, u32[]{:S(2)}) collective-permute-start(bf16[48,384]{1,0:T(8,128)(2,1)} %get-tuple-element.72), channel_id=1, source_target_pairs={{0,14},{2,0},{4,2},{6,4},{8,6},{10,8},{12,10},{14,12},{1,15},{3,1}... | collective-permute-start | bytes 110600 | tf_op jit(solution)/shard_map/ppermute | solution.py:42
  101.0 13.5 %shard_map.107 = (f32[512,384]{1,0:T(8,128)}, f32[512,384]{1,0:T(8,128)}, bf16[512,384]{1,0:T(8,128)(2,1)}, bf16[512,384]{1,0:T(8,128)(2,1)}, bf16[512,384]{1,0:...) custom-call(s32[1]{0:T(128)} %bitcast.1.lat_ref.refs_0_, ...), custom_call_target="tpu_custom_call" | custom-call | flops 8800000000 | bytes 11000000 | tf_op jit(solution)/shard_map/pallas_call | solution.py:616
  114.6 14.1 %shard_map.108 = (f32[512,384]{1,0:T(8,128)}, f32[512,384]{1,0:T(8,128)}, bf16[512,384]{1,0:T(8,128)(2,1)}, bf16[512,384]{1,0:T(8,128)(2,1)}, bf16[512,384]{1,0:...) custom-call(s32[1]{0:T(128)} %bitcast.1.lat_ref.refs_0_, ...), custom_call_target="tpu_custom_call" | custom-call | flops 8800000000 | bytes 11000000 | tf_op jit(solution)/shard_map/pallas_call | solution.py:616
  137.5 6.6 %collective-permute-done.27 = bf16[512,384]{1,0:T(8,128)(2,1)S(1)} collective-permute-done((bf16[512,384]{1,0:T(8,128)(2,1)S(1)}, bf16[512,384]{1,0:T(8,128)(2,1)S(1)}, u32[]{:S(2)}, u32[]{:S(2)}) %collective-permute-start.27) | collective-permute-done | bytes 393248 | tf_op jit(solution)/shard_map/ppermute | solution.py:42
  145.2 3.0 %collective-permute-start.44 = (bf16[96,384]{1,0:T(8,128)(2,1)S(1)}, bf16[96,384]{1,0:T(8,128)(2,1)S(1)}, u32[]{:S(2)}, u32[]{:S(2)}) collective-permute-start(bf16[96,384]{1,0:T(8,128)(2,1)S(1)} %get-tuple-element.105), channel_id=1, source_target_pairs={{0,12},{2,14},{4,0},{6,2},{8,4},{10,6},{12,8},{14,10},{1,13},{3,15... | collective-permute-start | bytes 221192 | tf_op jit(solution)/shard_map/ppermute | solution.py:79
  150.6 4.3 %collective-permute-start.34 = (bf16[96,384]{1,0:T(8,128)(2,1)S(1)}, bf16[96,384]{1,0:T(8,128)(2,1)S(1)}, u32[]{:S(2)}, u32[]{:S(2)}) collective-permute-start(bf16[96,384]{1,0:T(8,128)(2,1)S(1)} %get-tuple-element.108), channel_id=1, source_target_pairs={{0,12},{2,14},{4,0},{6,2},{8,4},{10,6},{12,8},{14,10},{1,13},{3,15... | collective-permute-start | bytes 221192 | tf_op jit(solution)/shard_map/ppermute | solution.py:79
  155.0 2.2 collective-permute-done.42
  157.3 3.9 %collective-permute-start.22 = (bf16[512,384]{1,0:T(8,128)(2,1)S(1)}, bf16[512,384]{1,0:T(8,128)(2,1)S(1)}, u32[]{:S(2)}, u32[]{:S(2)}) collective-permute-start(bf16[512,384]{1,0:T(8,128)(2,1)S(1)} %add_convert_fusion.6), channel_id=1, source_target_pairs={{0,12},{2,6},{4,0},{6,10},{8,4},{10,14},{12,8},{14,2},{1,13},{3,7}... | collective-permute-start | bytes 1179656 | tf_op jit(solution)/shard_map/ppermute | solution.py:42
  161.7 2.5 %collective-permute-done.32 = bf16[96,384]{1,0:T(8,128)(2,1)S(1)} collective-permute-done((bf16[96,384]{1,0:T(8,128)(2,1)S(1)}, bf16[96,384]{1,0:T(8,128)(2,1)S(1)}, u32[]{:S(2)}, u32[]{:S(2)}) %collective-permute-start.32) | collective-permute-done | bytes 73760 | tf_op jit(solution)/shard_map/ppermute | solution.py:79
  164.2 8.6 %collective-permute-start.46 = (bf16[96,384]{1,0:T(8,128)(2,1)S(1)}, bf16[96,384]{1,0:T(8,128)(2,1)S(1)}, u32[]{:S(2)}, u32[]{:S(2)}) collective-permute-start(bf16[96,384]{1,0:T(8,128)(2,1)S(1)} %get-tuple-element.99), channel_id=1, source_target_pairs={{0,8},{2,10},{4,12},{6,14},{8,0},{10,2},{12,4},{14,6},{1,9},{3,11}... | collective-permute-start | bytes 221192 | tf_op jit(solution)/shard_map/ppermute | solution.py:99
  173.0 2.9 %collective-permute-done.46 = bf16[96,384]{1,0:T(8,128)(2,1)S(1)} collective-permute-done((bf16[96,384]{1,0:T(8,128)(2,1)S(1)}, bf16[96,384]{1,0:T(8,128)(2,1)S(1)}, u32[]{:S(2)}, u32[]{:S(2)}) %collective-permute-start.46) | collective-permute-done | bytes 73760 | tf_op jit(solution)/shard_map/ppermute | solution.py:99
  177.3 2.3 collective-permute-start.36
  179.7 2.4 %collective-permute-done.35 = bf16[96,384]{1,0:T(8,128)(2,1)S(1)} collective-permute-done((bf16[96,384]{1,0:T(8,128)(2,1)S(1)}, bf16[96,384]{1,0:T(8,128)(2,1)S(1)}, u32[]{:S(2)}, u32[]{:S(2)}) %collective-permute-start.35) | collective-permute-done | bytes 73760 | tf_op jit(solution)/shard_map/ppermute | solution.py:99
  182.1 6.2 %collective-permute-start.48 = (bf16[384,384]{1,0:T(8,128)(2,1)S(1)}, bf16[384,384]{1,0:T(8,128)(2,1)S(1)}, u32[]{:S(2)}, u32[]{:S(2)}) collective-permute-start(bf16[384,384]{1,0:T(8,128)(2,1)S(1)} %constant_dynamic-update-slice_fusion.7), channel_id=1, source_target_pairs={{0,2},{2,0},{4,6},{6,4},{8,10},{10,8},{12,14},{14,12},{1,3},{3,1},... | collective-permute-start | bytes 884744 | tf_op jit(solution)/shard_map/ppermute | solution.py:99
  188.4 4.3 %collective-permute-done.37 = bf16[96,384]{1,0:T(8,128)(2,1)S(1)} collective-permute-done((bf16[96,384]{1,0:T(8,128)(2,1)S(1)}, bf16[96,384]{1,0:T(8,128)(2,1)S(1)}, u32[]{:S(2)}, u32[]{:S(2)}) %collective-permute-start.37) | collective-permute-done | bytes 73760 | tf_op jit(solution)/shard_map/ppermute | solution.py:99
  195.4 7.4 %collective-permute-done.38 = bf16[384,384]{1,0:T(8,128)(2,1)S(1)} collective-permute-done((bf16[384,384]{1,0:T(8,128)(2,1)S(1)}, bf16[384,384]{1,0:T(8,128)(2,1)S(1)}, u32[]{:S(2)}, u32[]{:S(2)}) %collective-permute-start.38) | collective-permute-done | bytes 294944 | tf_op jit(solution)/shard_map/ppermute | solution.py:99
  205.8 5.5 %collective-permute-done.28.refs_5_ = bf16[512,384]{1,0:T(8,128)(2,1)} collective-permute-done((bf16[512,384]{1,0:T(8,128)(2,1)S(1)}, bf16[512,384]{1,0:T(8,128)(2,1)}, u32[]{:S(2)}, u32[]{:S(2)}) %collective-permute-start.28) | collective-permute-done | bytes 393248 | tf_op jit(solution)/shard_map/ppermute | solution.py:42
  211.3 4.3 %shard_map.109.prev_ref = f32[1024,384]{1,0:T(8,128)} custom-call(bf16[512,384]{1,0:T(8,128)(2,1)} %get-tuple-element.55.start_ref.refs_0_, s32[32,32]{1,0:T(8,128)} %vis_ref.5, f32[1,384]{1,0:T(1,128)} %get-tuple-element.111.gain_ref.refs_2_, f32[512,384]{1,0:T(8,128)} %get-tuple-element.86.refs_3_, f32[512,384]{1,0:T(8,128)} %get-tuple-element.87.refs_4_, ...), custom_call_target="tpu_custom_call" | custom-call | flops 1600000000 | bytes 2000000 | tf_op jit(solution)/shard_map/pallas_call | solution.py:663
  215.6 3.6 %collective-permute-done.23.far_ref = bf16[512,384]{1,0:T(8,128)(2,1)} collective-permute-done((bf16[512,384]{1,0:T(8,128)(2,1)S(1)}, bf16[512,384]{1,0:T(8,128)(2,1)}, u32[]{:S(2)}, u32[]{:S(2)}) %collective-permute-start.23) | collective-permute-done | bytes 393248 | tf_op jit(solution)/shard_map/ppermute | solution.py:42
  219.2 4.3 %shard_map.110 = f32[1024,384]{1,0:T(8,128)} custom-call(bf16[512,384]{1,0:T(8,128)(2,1)} %get-tuple-element.51.start_ref, s32[32,32]{1,0:T(8,128)} %vis_ref.5, f32[1,384]{1,0:T(1,128)} %get-tuple-element.111.gain_ref.refs_2_, f32[512,384]{1,0:T(8,128)} %get-tuple-element.79.dh_ref, ...), custom_call_target="tpu_custom_call", output_to_operand_aliasing={{}: (7, {})} | custom-call | flops 1600000000 | bytes 2000000 | tf_op jit(solution)/shard_map/pallas_call | solution.py:663
  226.3 5.4 %shard_map.111 = (f32[2,384,1152]{2,1,0:T(8,128)}, f32[2,384,384]{2,1,0:T(8,128)}, f32[2,384]{1,0:T(2,128)}) custom-call(bf16[1536,384]{1,0:T(8,128)(2,1)} %maximum_select_fusion.r0_ref, bf16[1536,384]{1,0:T(8,128)(2,1)} %maximum_select_fusion.1.r1_ref, bf16[2,1152,384]{2,1,0:T(8,128)(2,1)} %bitcast.14, f32[2,384]{1,0:T(2,128)} %gain_ref.1), custom_call_target="tpu_custom_call" | custom-call | flops 3200000000 | bytes 4000000 | tf_op jit(solution)/shard_map/pallas_call | solution.py:680
  (172 shorter events, 46.5 us)
Async XLA Ops:
  7.1 12.4 %collective-permute-start = (bf16[512,384]{1,0:T(8,128)(2,1)}, bf16[512,384]{1,0:T(8,128)(2,1)}, u32[]{:S(2)}, u32[]{:S(2)}) collective-permute-start(bf16[512,384]{1,0:T(8,128)(2,1)} %get-tuple-element.53.n0.refs_1_), channel_id=1, source_target_pairs={{0,2},{2,0},{4,6},{6,4},{8,10},{10,8},{12,14},{14,12},{1,3},{3,1},... | collective-permute-start | bytes 1179656 | tf_op jit(solution)/shard_map/ppermute | solution.py:42
  19.5 10.6 %collective-permute-start.2 = (bf16[512,384]{1,0:T(8,128)(2,1)}, bf16[512,384]{1,0:T(8,128)(2,1)}, u32[]{:S(2)}, u32[]{:S(2)}) collective-permute-start(bf16[512,384]{1,0:T(8,128)(2,1)} %get-tuple-element.54.n0), channel_id=1, source_target_pairs={{0,2},{2,0},{4,6},{6,4},{8,10},{10,8},{12,14},{14,12},{1,3},{3,1},... | collective-permute-start | bytes 1179656 | tf_op jit(solution)/shard_map/ppermute | solution.py:42
  21.3 11.9 %collective-permute-start.7 = (bf16[512,384]{1,0:T(8,128)(2,1)}, bf16[512,384]{1,0:T(8,128)(2,1)}, u32[]{:S(2)}, u32[]{:S(2)}) collective-permute-start(bf16[512,384]{1,0:T(8,128)(2,1)} %collective-permute-done.n2.refs_3_), channel_id=1, source_target_pairs={{0,4},{2,14},{4,8},{6,2},{8,12},{10,6},{12,0},{14,10},{1,5},{3,15}... | collective-permute-start | bytes 1179656 | tf_op jit(solution)/shard_map/ppermute | solution.py:42
  22.8 11.9 %collective-permute-start.6 = (bf16[512,384]{1,0:T(8,128)(2,1)}, bf16[512,384]{1,0:T(8,128)(2,1)}, u32[]{:S(2)}, u32[]{:S(2)}) collective-permute-start(bf16[512,384]{1,0:T(8,128)(2,1)} %get-tuple-element.53.n0.refs_1_), channel_id=1, source_target_pairs={{0,1},{1,0},{2,3},{3,2},{4,5},{5,4},{6,7},{7,6},{8,9},{9,8},{10,11... | collective-permute-start | bytes 1179656 | tf_op jit(solution)/shard_map/ppermute | solution.py:42
  26.4 15.1 %collective-permute-start.8 = (bf16[512,384]{1,0:T(8,128)(2,1)}, bf16[512,384]{1,0:T(8,128)(2,1)S(1)}, u32[]{:S(2)}, u32[]{:S(2)}) collective-permute-start(bf16[512,384]{1,0:T(8,128)(2,1)} %collective-permute-done.n2.refs_3_), channel_id=1, source_target_pairs={{0,1},{1,0},{2,3},{3,2},{4,5},{5,4},{6,7},{7,6},{8,9},{9,8},{10,11... | collective-permute-start | bytes 1179656 | tf_op jit(solution)/shard_map/ppermute | solution.py:42
  30.1 11.4 %collective-permute-start.3 = (bf16[512,384]{1,0:T(8,128)(2,1)}, bf16[512,384]{1,0:T(8,128)(2,1)S(1)}, u32[]{:S(2)}, u32[]{:S(2)}) collective-permute-start(bf16[512,384]{1,0:T(8,128)(2,1)} %collective-permute-done.2.n2), channel_id=1, source_target_pairs={{0,4},{2,14},{4,8},{6,2},{8,12},{10,6},{12,0},{14,10},{1,5},{3,15}... | collective-permute-start | bytes 1179656 | tf_op jit(solution)/shard_map/ppermute | solution.py:42
  33.1 8.4 %collective-permute-start.9 = (bf16[512,384]{1,0:T(8,128)(2,1)}, bf16[512,384]{1,0:T(8,128)(2,1)S(1)}, u32[]{:S(2)}, u32[]{:S(2)}) collective-permute-start(bf16[512,384]{1,0:T(8,128)(2,1)} %collective-permute-done.7.n3.refs_4_), channel_id=1, source_target_pairs={{0,1},{1,0},{2,3},{3,2},{4,5},{5,4},{6,7},{7,6},{8,9},{9,8},{10,11... | collective-permute-start | bytes 1179656 | tf_op jit(solution)/shard_map/ppermute | solution.py:42
  34.2 16.8 %collective-permute-start.1 = (bf16[512,384]{1,0:T(8,128)(2,1)S(1)}, bf16[512,384]{1,0:T(8,128)(2,1)S(1)}, u32[]{:S(2)}, u32[]{:S(2)}) collective-permute-start(bf16[512,384]{1,0:T(8,128)(2,1)S(1)} %copy-done.12), channel_id=1, source_target_pairs={{0,1},{1,0},{2,3},{3,2},{4,5},{5,4},{6,7},{7,6},{8,9},{9,8},{10,11... | collective-permute-start | bytes 1179656 | tf_op jit(solution)/shard_map/ppermute | solution.py:42
  34.7 16.3 %collective-permute-start.4 = (bf16[512,384]{1,0:T(8,128)(2,1)}, bf16[512,384]{1,0:T(8,128)(2,1)S(1)}, u32[]{:S(2)}, u32[]{:S(2)}) collective-permute-start(bf16[512,384]{1,0:T(8,128)(2,1)} %collective-permute-done.2.n2), channel_id=1, source_target_pairs={{0,1},{1,0},{2,3},{3,2},{4,5},{5,4},{6,7},{7,6},{8,9},{9,8},{10,11... | collective-permute-start | bytes 1179656 | tf_op jit(solution)/shard_map/ppermute | solution.py:42
  41.5 9.5 %collective-permute-start.5 = (bf16[512,384]{1,0:T(8,128)(2,1)S(1)}, bf16[512,384]{1,0:T(8,128)(2,1)S(1)}, u32[]{:S(2)}, u32[]{:S(2)}) collective-permute-start(bf16[512,384]{1,0:T(8,128)(2,1)S(1)} %collective-permute-done.3.n3), channel_id=1, source_target_pairs={{0,1},{1,0},{2,3},{3,2},{4,5},{5,4},{6,7},{7,6},{8,9},{9,8},{10,11... | collective-permute-start | bytes 1179656 | tf_op jit(solution)/shard_map/ppermute | solution.py:42
  60.6 6.8 %collective-permute-start.11 = (bf16[32,384]{1,0:T(8,128)(2,1)}, bf16[32,384]{1,0:T(8,128)(2,1)S(1)}, u32[]{:S(2)}, u32[]{:S(2)}) collective-permute-start(bf16[32,384]{1,0:T(8,128)(2,1)} %get-tuple-element.67), channel_id=1, source_target_pairs={{0,2},{2,4},{4,6},{6,8},{8,10},{10,12},{12,14},{14,0},{1,3},{3,5},... | collective-permute-start | bytes 73736 | tf_op jit(solution)/shard_map/ppermute | solution.py:42
  92.0 6.9 %collective-permute-start.16 = (bf16[48,384]{1,0:T(8,128)(2,1)}, bf16[48,384]{1,0:T(8,128)(2,1)S(1)}, u32[]{:S(2)}, u32[]{:S(2)}) collective-permute-start(bf16[48,384]{1,0:T(8,128)(2,1)} %get-tuple-element.71), channel_id=1, source_target_pairs={{0,2},{2,4},{4,6},{6,8},{8,10},{10,12},{12,14},{14,0},{1,3},{3,5},... | collective-permute-start | bytes 110600 | tf_op jit(solution)/shard_map/ppermute | solution.py:42
  92.0 6.9 %collective-permute-start.17 = (bf16[48,384]{1,0:T(8,128)(2,1)}, bf16[48,384]{1,0:T(8,128)(2,1)S(1)}, u32[]{:S(2)}, u32[]{:S(2)}) collective-permute-start(bf16[48,384]{1,0:T(8,128)(2,1)} %get-tuple-element.72), channel_id=1, source_target_pairs={{0,14},{2,0},{4,2},{6,4},{8,6},{10,8},{12,10},{14,12},{1,15},{3,1}... | collective-permute-start | bytes 110600 | tf_op jit(solution)/shard_map/ppermute | solution.py:42
  129.7 65.3 %collective-permute-start.20 = (bf16[512,384]{1,0:T(8,128)(2,1)}, bf16[512,384]{1,0:T(8,128)(2,1)S(1)}, u32[]{:S(2)}, u32[]{:S(2)}) collective-permute-start(bf16[512,384]{1,0:T(8,128)(2,1)} %get-tuple-element.82), channel_id=1, source_target_pairs={{0,1},{1,0},{2,3},{3,2},{4,5},{5,4},{6,7},{7,6},{8,9},{9,8},{10,11... | collective-permute-start | bytes 1179656 | tf_op jit(solution)/shard_map/ppermute | solution.py:42
  129.9 85.7 %collective-permute-start.24 = (bf16[512,384]{1,0:T(8,128)(2,1)}, bf16[512,384]{1,0:T(8,128)(2,1)S(1)}, u32[]{:S(2)}, u32[]{:S(2)}) collective-permute-start(bf16[512,384]{1,0:T(8,128)(2,1)} %get-tuple-element.85), channel_id=1, source_target_pairs={{0,1},{1,0},{2,3},{3,2},{4,5},{5,4},{6,7},{7,6},{8,9},{9,8},{10,11... | collective-permute-start | bytes 1179656 | tf_op jit(solution)/shard_map/ppermute | solution.py:42
  132.7 11.4 %collective-permute-start.27 = (bf16[512,384]{1,0:T(8,128)(2,1)S(1)}, bf16[512,384]{1,0:T(8,128)(2,1)S(1)}, u32[]{:S(2)}, u32[]{:S(2)}) collective-permute-start(bf16[512,384]{1,0:T(8,128)(2,1)S(1)} %add_convert_fusion.3), channel_id=1, source_target_pairs={{0,12},{2,6},{4,0},{6,10},{8,4},{10,14},{12,8},{14,2},{1,13},{3,7}... | collective-permute-start | bytes 1179656 | tf_op jit(solution)/shard_map/ppermute | solution.py:42
  135.1 10.0 %collective-permute-start.41 = (bf16[384,384]{1,0:T(8,128)(2,1)S(1)}, bf16[384,384]{1,0:T(8,128)(2,1)S(1)}, u32[]{:S(2)}, u32[]{:S(2)}) collective-permute-start(bf16[384,384]{1,0:T(8,128)(2,1)S(1)} %constant_dynamic-slice_fusion.3), channel_id=1, source_target_pairs={{0,2},{2,0},{4,6},{6,4},{8,10},{10,8},{12,14},{14,12},{1,3},{3,1},... | collective-permute-start | bytes 884744 | tf_op jit(solution)/shard_map/ppermute | solution.py:79
  135.4 14.9 %collective-permute-start.31 = (bf16[384,384]{1,0:T(8,128)(2,1)S(1)}, bf16[384,384]{1,0:T(8,128)(2,1)S(1)}, u32[]{:S(2)}, u32[]{:S(2)}) collective-permute-start(bf16[384,384]{1,0:T(8,128)(2,1)S(1)} %constant_dynamic-slice_fusion.8), channel_id=1, source_target_pairs={{0,2},{2,0},{4,6},{6,4},{8,10},{10,8},{12,14},{14,12},{1,3},{3,1},... | collective-permute-start | bytes 884744 | tf_op jit(solution)/shard_map/ppermute | solution.py:79
  150.3 6.9 %collective-permute-start.42 = (bf16[96,384]{1,0:T(8,128)(2,1)S(1)}, bf16[96,384]{1,0:T(8,128)(2,1)S(1)}, u32[]{:S(2)}, u32[]{:S(2)}) collective-permute-start(bf16[96,384]{1,0:T(8,128)(2,1)S(1)} %get-tuple-element.104), channel_id=1, source_target_pairs={{0,4},{2,6},{4,8},{6,10},{8,12},{10,14},{12,0},{14,2},{1,5},{3,7},... | collective-permute-start | bytes 221192 | tf_op jit(solution)/shard_map/ppermute | solution.py:79
  154.8 6.9 %collective-permute-start.33 = (bf16[96,384]{1,0:T(8,128)(2,1)S(1)}, bf16[96,384]{1,0:T(8,128)(2,1)S(1)}, u32[]{:S(2)}, u32[]{:S(2)}) collective-permute-start(bf16[96,384]{1,0:T(8,128)(2,1)S(1)} %get-tuple-element.109), channel_id=1, source_target_pairs={{0,8},{2,10},{4,12},{6,14},{8,0},{10,2},{12,4},{14,6},{1,9},{3,11}... | collective-permute-start | bytes 221192 | tf_op jit(solution)/shard_map/ppermute | solution.py:79
  157.2 7.0 %collective-permute-start.32 = (bf16[96,384]{1,0:T(8,128)(2,1)S(1)}, bf16[96,384]{1,0:T(8,128)(2,1)S(1)}, u32[]{:S(2)}, u32[]{:S(2)}) collective-permute-start(bf16[96,384]{1,0:T(8,128)(2,1)S(1)} %get-tuple-element.107), channel_id=1, source_target_pairs={{0,4},{2,6},{4,8},{6,10},{8,12},{10,14},{12,0},{14,2},{1,5},{3,7},... | collective-permute-start | bytes 221192 | tf_op jit(solution)/shard_map/ppermute | solution.py:79
  157.3 37.8 %collective-permute-start.22 = (bf16[512,384]{1,0:T(8,128)(2,1)S(1)}, bf16[512,384]{1,0:T(8,128)(2,1)S(1)}, u32[]{:S(2)}, u32[]{:S(2)}) collective-permute-start(bf16[512,384]{1,0:T(8,128)(2,1)S(1)} %add_convert_fusion.6), channel_id=1, source_target_pairs={{0,12},{2,6},{4,0},{6,10},{8,4},{10,14},{12,8},{14,2},{1,13},{3,7}... | collective-permute-start | bytes 1179656 | tf_op jit(solution)/shard_map/ppermute | solution.py:42
  161.7 11.2 %collective-permute-start.45 = (bf16[96,384]{1,0:T(8,128)(2,1)S(1)}, bf16[96,384]{1,0:T(8,128)(2,1)S(1)}, u32[]{:S(2)}, u32[]{:S(2)}) collective-permute-start(bf16[96,384]{1,0:T(8,128)(2,1)S(1)} %get-tuple-element.99), channel_id=1, source_target_pairs={{0,4},{2,6},{4,8},{6,10},{8,12},{10,14},{12,0},{14,2},{1,5},{3,7},... | collective-permute-start | bytes 221192 | tf_op jit(solution)/shard_map/ppermute | solution.py:99
  164.2 11.7 %collective-permute-start.46 = (bf16[96,384]{1,0:T(8,128)(2,1)S(1)}, bf16[96,384]{1,0:T(8,128)(2,1)S(1)}, u32[]{:S(2)}, u32[]{:S(2)}) collective-permute-start(bf16[96,384]{1,0:T(8,128)(2,1)S(1)} %get-tuple-element.99), channel_id=1, source_target_pairs={{0,8},{2,10},{4,12},{6,14},{8,0},{10,2},{12,4},{14,6},{1,9},{3,11}... | collective-permute-start | bytes 221192 | tf_op jit(solution)/shard_map/ppermute | solution.py:99
  177.3 11.0 %collective-permute-start.36 = (bf16[96,384]{1,0:T(8,128)(2,1)S(1)}, bf16[96,384]{1,0:T(8,128)(2,1)S(1)}, u32[]{:S(2)}, u32[]{:S(2)}) collective-permute-start(bf16[96,384]{1,0:T(8,128)(2,1)S(1)} %get-tuple-element.101), channel_id=1, source_target_pairs={{0,8},{2,10},{4,12},{6,14},{8,0},{10,2},{12,4},{14,6},{1,9},{3,11}... | collective-permute-start | bytes 221192 | tf_op jit(solution)/shard_map/ppermute | solution.py:99
  182.1 10.9 %collective-permute-start.48 = (bf16[384,384]{1,0:T(8,128)(2,1)S(1)}, bf16[384,384]{1,0:T(8,128)(2,1)S(1)}, u32[]{:S(2)}, u32[]{:S(2)}) collective-permute-start(bf16[384,384]{1,0:T(8,128)(2,1)S(1)} %constant_dynamic-update-slice_fusion.7), channel_id=1, source_target_pairs={{0,2},{2,0},{4,6},{6,4},{8,10},{10,8},{12,14},{14,12},{1,3},{3,1},... | collective-permute-start | bytes 884744 | tf_op jit(solution)/shard_map/ppermute | solution.py:99
  192.7 12.4 %collective-permute-start.29 = (bf16[512,384]{1,0:T(8,128)(2,1)S(1)}, bf16[512,384]{1,0:T(8,128)(2,1)S(1)}, u32[]{:S(2)}, u32[]{:S(2)}) collective-permute-start(bf16[512,384]{1,0:T(8,128)(2,1)S(1)} %copy-done.9), channel_id=1, source_target_pairs={{0,1},{1,0},{2,3},{3,2},{4,5},{5,4},{6,7},{7,6},{8,9},{9,8},{10,11... | collective-permute-start | bytes 1179656 | tf_op jit(solution)/shard_map/ppermute | solution.py:42
  193.0 9.8 %collective-permute-start.38 = (bf16[384,384]{1,0:T(8,128)(2,1)S(1)}, bf16[384,384]{1,0:T(8,128)(2,1)S(1)}, u32[]{:S(2)}, u32[]{:S(2)}) collective-permute-start(bf16[384,384]{1,0:T(8,128)(2,1)S(1)} %constant_dynamic-update-slice_fusion.13), channel_id=1, source_target_pairs={{0,2},{2,0},{4,6},{6,4},{8,10},{10,8},{12,14},{14,12},{1,3},{3,1},... | collective-permute-start | bytes 884744 | tf_op jit(solution)/shard_map/ppermute | solution.py:99
  195.1 16.3 %collective-permute-start.28 = (bf16[512,384]{1,0:T(8,128)(2,1)S(1)}, bf16[512,384]{1,0:T(8,128)(2,1)}, u32[]{:S(2)}, u32[]{:S(2)}) collective-permute-start(bf16[512,384]{1,0:T(8,128)(2,1)S(1)} %add_convert_fusion.2), channel_id=1, source_target_pairs={{0,2},{2,0},{4,6},{6,4},{8,10},{10,8},{12,14},{14,12},{1,3},{3,1},... | collective-permute-start | bytes 1179656 | tf_op jit(solution)/shard_map/ppermute | solution.py:42
  195.1 28.3 %collective-permute-start.49 = (bf16[768,384]{1,0:T(8,128)(2,1)S(1)}, bf16[768,384]{1,0:T(8,128)(2,1)S(1)}, u32[]{:S(2)}, u32[]{:S(2)}) collective-permute-start(bf16[768,384]{1,0:T(8,128)(2,1)S(1)} %constant_dynamic-update-slice_fusion.5), channel_id=1, source_target_pairs={{0,1},{1,0},{2,3},{3,2},{4,5},{5,4},{6,7},{7,6},{8,9},{9,8},{10,11... | collective-permute-start | bytes 1769480 | tf_op jit(solution)/shard_map/ppermute | solution.py:42
  202.8 16.4 %collective-permute-start.23 = (bf16[512,384]{1,0:T(8,128)(2,1)S(1)}, bf16[512,384]{1,0:T(8,128)(2,1)}, u32[]{:S(2)}, u32[]{:S(2)}) collective-permute-start(bf16[512,384]{1,0:T(8,128)(2,1)S(1)} %add_convert_fusion.5), channel_id=1, source_target_pairs={{0,2},{2,0},{4,6},{6,4},{8,10},{10,8},{12,14},{14,12},{1,3},{3,1},... | collective-permute-start | bytes 1179656 | tf_op jit(solution)/shard_map/ppermute | solution.py:42
  205.8 19.1 %collective-permute-start.39 = (bf16[768,384]{1,0:T(8,128)(2,1)S(1)}, bf16[768,384]{1,0:T(8,128)(2,1)S(1)}, u32[]{:S(2)}, u32[]{:S(2)}) collective-permute-start(bf16[768,384]{1,0:T(8,128)(2,1)S(1)} %constant_dynamic-update-slice_fusion.11), channel_id=1, source_target_pairs={{0,1},{1,0},{2,3},{3,2},{4,5},{5,4},{6,7},{7,6},{8,9},{9,8},{10,11... | collective-permute-start | bytes 1769480 | tf_op jit(solution)/shard_map/ppermute | solution.py:42
  (43 other events, 193.7 us)

commit v3 on v2

--- a/solution.py
+++ b/solution.py
@@ -114,22 +114,19 @@
     return out
 
 
-def summed(value):
+def halves_summed(value):
     lat = lax.axis_index("lat")
     half = value.shape[0] // 2
     mine = lax.dynamic_slice_in_dim(value, lat * half, half, 0)
     other = lat_swap(lax.dynamic_slice_in_dim(value, (1 - lat) * half, half, 0))
-    value = (mine.astype(F32) + other.astype(F32)).astype(BF16)
-    factors = lon_factors()
-    for stride, factor in factors:
-        size = value.shape[0] // factor
-        take = lambda k, v=value, n=size: lax.dynamic_slice_in_dim(v, k * n, n, 0)
-        value = exchanged(take, stride, factor)
-    for stride, factor in factors[::-1]:
-        value = spread(value, stride, factor)
-    other = lat_swap(value)
-    return jnp.where(
-        lat == 0, jnp.concatenate([value, other], 0), jnp.concatenate([other, value], 0)
+    return (mine.astype(F32) + other.astype(F32)).astype(BF16)
+
+
+def stage_summed(value, stage):
+    stride, factor = stage
+    size = value.shape[0] // factor
+    return exchanged(
+        lambda k: lax.dynamic_slice_in_dim(value, k * size, size, 0), stride, factor
     )
 
 
@@ -162,10 +159,10 @@
     tile, width = tok_ref.shape
     base = first + pl.program_id(0) * tile
     shown = shown_column(vis_ref[...], base, tile)
-    x = jnp.where(shown > 0.5, tok_ref[...].astype(F32), mask_ref[...].astype(F32))
+    x = jnp.where(shown > 0.5, tok_ref[...].astype(F32), mask_ref[...].astype(F32).reshape(1, width))
     start_ref[...] = x.astype(BF16)
     xhat, _ = norm_parts(x)
-    normal_ref[...] = (xhat * gain_ref[...]).astype(BF16)
+    normal_ref[...] = (xhat * gain_ref[0:1, :]).astype(BF16)
 
 
 def first_kernel(
@@ -199,7 +196,7 @@
     h1 = h1.astype(BF16)
     h_ref[...] = h1
     xhat, _ = norm_parts(h1.astype(F32))
-    normal = (xhat * gain_ref[...]).astype(BF16)
+    normal = (xhat * gain_ref[1:2, :]).astype(BF16)
     normal_ref[...] = normal
     step = pl.program_id(0)
     brow = jnp.where(lat_ref[0] == 0, 31, 0)
@@ -215,7 +212,8 @@
     @pl.when(step == 0)
     def _():
         for i, ref in enumerate((row_in, left_in, right_in)):
-            pack_s[i * 32 : i * 32 + 32, :] = ref[...].astype(F32)
+            known = jnp.zeros((32, width), F32) if ref is None else ref[...].astype(F32)
+            pack_s[i * 32 : i * 32 + 32, :] = known
 
     pack_s[...] += nn(pick, normal)
 
@@ -227,12 +225,13 @@
 
 def second_kernel(
     lat_ref, na_ref, nb_ref, row_ref, left_ref, right_ref, dleft_ref, dright_ref,
-    w_ref, wo_ref, cot_ref,
-    dn_ref, brow_ref, bleft_ref, bright_ref, dw_ref,
-    q_s, k_s, v_s, kc_s, vc_s, dq_s, dk_s, dv_s, dkc_s, dvc_s, do_s, mixed_s, halo_s, mask_s, normal_s,
+    w_all, wo_all, cot_ref,
+    dq_ref, dk_ref, dv_ref, mixed_s, dkh_ref, dvh_ref, halo_s, brow_ref, bleft_ref, bright_ref,
+    q_s, k_s, v_s, kc_s, vc_s, dk_s, dv_s, dkc_s, dvc_s, do_s, mask_s, normal_s,
 ):
     points, width = cot_ref.shape
     head = width // HEADS
+    w_ref, wo_ref = w_all.at[1], wo_all.at[1]
     upper = lat_ref[0] == 0
     halo_s[0:32, :] = row_ref[...]
     halo_s[32:64, :] = left_ref[...]
@@ -311,7 +310,7 @@
             out = tn(p1, v1) + tn(p2, v2)
             mixed_s[here, lanes] = jnp.where(even, out[0:128], out[128:256]).astype(BF16)
             dq = (tn(ds1, k1) + tn(ds2, k2)) * scale
-            dq_s[here, lanes] = jnp.where(even, dq[0:128], dq[128:256]).astype(BF16)
+            dq_ref[here, lanes] = jnp.where(even, dq[0:128], dq[128:256]).astype(BF16)
             dk_s[win, lanes] += nn(ds1, qm)
             dv_s[win, lanes] += nn(p1, dom)
             dkc_s[:, lanes] += nn(ds2, qm)
@@ -323,20 +322,34 @@
     row_at = pl.multiple_of(jnp.where(upper, 32 + points, 0), 32)
     dkh = jnp.concatenate([dk_s[pl.ds(row_at, 32), :], dkc_s[...]], 0).astype(BF16)
     dvh = jnp.concatenate([dv_s[pl.ds(row_at, 32), :], dvc_s[...]], 0).astype(BF16)
-    dq = dq_s[...]
-    dk = dk_s[32 : 32 + points, :].astype(BF16)
-    dv = dv_s[32 : 32 + points, :].astype(BF16)
-    wq, wk, wv = (w_ref[:, i * width : (i + 1) * width] for i in range(3))
-    dn_ref[...] = nt(dq, wq) + nt(dk, wk) + nt(dv, wv)
+    dkh_ref[...] = dkh
+    dvh_ref[...] = dvh
+    dk_ref[...] = dk_s[32 : 32 + points, :].astype(BF16)
+    dv_ref[...] = dv_s[32 : 32 + points, :].astype(BF16)
+    wk, wv = (w_ref[:, i * width : (i + 1) * width] for i in (1, 2))
     back = (nt(dkh, wk) + nt(dvh, wv)).astype(BF16)
     brow_ref[...] = back[0:32]
     for ref, at in ((bleft_ref, 32), (bright_ref, 64)):
         ref[0:32, :] = back[at : at + 32]
         ref[32:48, :] = back[CORNER:HALO]
-    dw_ref[0:width, :] = tn(dq, normal).astype(BF16)
-    dw_ref[width : 2 * width, :] = (tn(dk, normal) + tn(dkh, halo)).astype(BF16)
-    dw_ref[2 * width : 3 * width, :] = (tn(dv, normal) + tn(dvh, halo)).astype(BF16)
-    dw_ref[3 * width : 4 * width, :] = tn(mixed_s[...], cot).astype(BF16)
+
+
+def second_weights_kernel(
+    na_ref, nb_ref, halo_ref, dq_ref, dk_ref, dv_ref, mixed_ref, dkh_ref, dvh_ref,
+    w_all, cot_ref, dn_ref, dw_ref, normal_s,
+):
+    points, width = cot_ref.shape
+    normal_s[0 : points // 2, :] = na_ref[...]
+    normal_s[points // 2 : points, :] = nb_ref[...]
+    normal, halo = normal_s[...], halo_ref[...]
+    wq, wk, wv = (w_all[1, :, i * width : (i + 1) * width] for i in range(3))
+    dw_ref[0:width, :] = tn(dq_ref[...], normal).astype(BF16)
+    dw_ref[width : 2 * width, :] = (tn(dk_ref[...], normal) + tn(dkh_ref[...], halo)).astype(BF16)
+    dw_ref[2 * width : 3 * width, :] = (
+        tn(dv_ref[...], normal) + tn(dvh_ref[...], halo)
+    ).astype(BF16)
+    dw_ref[3 * width : 4 * width, :] = tn(mixed_ref[...], cot_ref[...].astype(BF16)).astype(BF16)
+    dn_ref[...] = nt(dq_ref[...], wq) + nt(dk_ref[...], wk) + nt(dv_ref[...], wv)
 
 
 def third_kernel(
@@ -369,7 +382,7 @@
         | (border & (c == 31) & (slot == 176 + 32))
     )
     dn = dn1_ref[...] + nn(place, packs_ref[...])
-    dh = cot_ref[...] + norm_back(h_ref[...].astype(F32), gain_ref[...], dn)
+    dh = cot_ref[...] + norm_back(h_ref[...].astype(F32), gain_ref[1:2, :], dn)
     dh_ref[...] = dh
     dhb = dh.astype(BF16)
     dmix_s[...] = nt(wo_ref[...], dhb)
@@ -414,21 +427,32 @@
     tile, width = start_ref.shape
     shown = shown_column(vis_ref[...], first + pl.program_id(0) * tile, tile)
     dn = own_ref[...] + far_ref[...].astype(F32) + near_ref[...].astype(F32)
-    grad = dh_ref[...] + norm_back(start_ref[...].astype(F32), gain_ref[...], dn)
+    grad = dh_ref[...] + norm_back(start_ref[...].astype(F32), gain_ref[0:1, :], dn)
     out_ref[...] = jnp.where(shown > 0.5, grad, 0.0)
 
 
-def weights_kernel(factor, r0_ref, r1_ref, wt_ref, gain_ref, qkv_ref, out_ref, gain_out_ref):
-    width = r0_ref.shape[1]
-    for layer, ref in enumerate((r0_ref, r1_ref)):
+def weights_kernel(
+    factor, pieces, lat_ref, mine_ref, other_ref, wt_ref, gain_ref,
+    qkv_ref, out_ref, gain_out_ref, rows_s,
+):
+    total, width = mine_ref.shape
+    piece = total // pieces // 2
+    lat = lat_ref[0]
+    for ref, band in ((mine_ref, lat), (other_ref, 1 - lat)):
+        for k in range(pieces):
+            at = pl.multiple_of(band * (total // 2) + k * piece, 8)
+            for layer in range(2):
+                lo = (2 * k + layer) * piece
+                rows_s[layer, pl.ds(at, piece), :] = ref[lo : lo + piece, :].astype(F32) * factor
+    for layer in range(2):
         acc = jnp.zeros((1, width), F32)
         for i in range(3):
             lo, hi = i * width, (i + 1) * width
-            grad = ref[lo:hi, :].astype(F32) * factor
+            grad = rows_s[layer, lo:hi, :]
             weight = wt_ref[layer, lo:hi, :].astype(F32)
             acc = acc + jnp.sum(weight * grad, axis=0, keepdims=True)
             qkv_ref[layer, :, lo:hi] = grad.T
-        out_ref[layer] = ref[3 * width : 4 * width, :].astype(F32) * factor
+        out_ref[layer] = rows_s[layer, 3 * width : 4 * width, :]
         gain_out_ref[layer : layer + 1, :] = acc / gain_ref[layer : layer + 1, :]
 
 
@@ -470,6 +494,10 @@
     return pl.BlockSpec((tile, width), lambda i: (i + at, 0))
 
 
+def layer_spec(layer, rows, width):
+    return pl.BlockSpec((None, rows, width), lambda i: (layer, 0, 0))
+
+
 CHUNKS = 2
 
 
@@ -482,18 +510,16 @@
     firsts = [c * size for c in range(CHUNKS)]
     lat_count, lon_count = lax.axis_size("lat"), lax.axis_size("lon")
     lat = lax.axis_index("lat").astype(jnp.int32).reshape(1)
-    gain0, gain1 = norm_gain_table[0:1], norm_gain_table[1:2]
-    w1 = query_key_value_weight[1]
-    wo0, wo1 = output_weight[0], output_weight[1]
     wt = jnp.swapaxes(query_key_value_weight, 1, 2)
-    wt0 = wt[0]
     struct = jax.ShapeDtypeStruct
     tokens = tokens.reshape(points, width)
     cot = cotangent.reshape(points, width)
-    mask_row = mask_token.reshape(1, width)
     part = struct((size, width), BF16)
-
-    small = 128
+    every = struct((points, width), BF16)
+    gain_spec = fixed((2, width))
+    wt_spec, wo_spec = layer_spec(0, 3 * width, width), layer_spec(0, width, width)
+
+    small = 256
     starts, normals = [], []
     for first in firsts:
         start, normal = call(
@@ -503,27 +529,25 @@
             in_specs=[
                 token_spec(small, width, first),
                 fixed((rows, cols)),
-                fixed((1, width)),
-                fixed((1, width)),
+                fixed((width,)),
+                gain_spec,
             ],
             out_specs=(token_spec(small, width),) * 2,
             us=2,
-        )(tokens, visible, mask_row, gain0)
+        )(tokens, visible, mask_token, norm_gain_table)
         starts.append(start)
         normals.append(normal)
 
-    blocks = []
-    before = None
-    for c in range(CHUNKS):
-        own = normals[c]
-        if before is not None:
-            own, before = chained(own, before)
-        swapped = lon_swap(own)
-        beyond = lon_forward(swapped)
-        before = swapped
-        blocks.append(
-            [own, lat_swap(own), swapped, beyond, lat_swap(swapped), lat_swap(beyond)]
-        )
+    swapped0 = lon_swap(normals[0])
+    own1, swapped0 = chained(normals[1], swapped0)
+    swapped1 = lon_swap(own1)
+    beyond0, beyond1 = lon_forward(swapped0), lon_forward(swapped1)
+    near0, near1 = lat_swap(normals[0]), lat_swap(own1)
+
+    def blocks_of(own, near, swapped, beyond):
+        return [own, near, swapped, beyond, lat_swap(swapped), lat_swap(beyond)]
+
+    blocks = [blocks_of(normals[0], near0, swapped0, beyond0), None]
 
     tile = 256
     steps = size // tile
@@ -531,11 +555,12 @@
     feat_spec = pl.BlockSpec((width, tile), lambda i: (0, i))
     kv_spec = pl.BlockSpec((6, 2 * width, tile), lambda i: (0, 0, i))
     p_spec = pl.BlockSpec((6, 8, tile), lambda i: (0, 0, i))
-    packs = [jnp.zeros((32, width), BF16)] * 3
+    packs = []
     kept = []
     for c in range(CHUNKS):
+        kernel = functools.partial(first_kernel, firsts[c])
         *keep, normal1, row, left, right = call(
-            functools.partial(first_kernel, firsts[c]),
+            kernel if packs else functools.partial(without, kernel, 8, 3),
             (
                 struct((width, size), BF16),
                 struct((6, 2 * width, size), BF16),
@@ -548,62 +573,80 @@
             grid=(steps,),
             in_specs=[scalar()]
             + [tok_spec] * 7
-            + [fixed((32, width))] * 3
-            + [fixed((3 * width, width)), fixed((width, width)), fixed((1, width))],
+            + [fixed((32, width))] * len(packs)
+            + [wt_spec, wo_spec, gain_spec],
             out_specs=(
                 feat_spec, kv_spec, p_spec, feat_spec, tok_spec, tok_spec,
                 *[fixed((32, width))] * 3,
             ),
             scratch=[pltpu.VMEM((6, 8, tile), F32), pltpu.VMEM((96, width), F32)],
-            us=7,
-        )(lat, *blocks[c], starts[c], *packs, wt0, wo0, gain1)
+            us=8,
+        )(lat, *blocks[c], starts[c], *packs, wt, output_weight, norm_gain_table)
         packs = [row, left, right]
         kept.append((keep, normal1))
+        if c == 0:
+            beyond1, row, left, right = lax.optimization_barrier((beyond1, *packs))
+            packs = [row, left, right]
+            blocks[1] = blocks_of(own1, near1, swapped1, beyond1)
 
     row, left, right = packs
     from_l, from_r = from_left(right), from_right(left)
     ext = points + 64
     halo_cols = HALO - 32
-    dn1, brow, bleft, bright, dw1 = call(
+    halo_struct = struct((HALO, width), BF16)
+    dq1, dk1, dv1, mixed1, dkh, dvh, halo, brow, bleft, bright = call(
         second_kernel,
         (
-            struct((points, width), F32),
+            every, every, every, every, halo_struct, halo_struct, halo_struct,
             struct((32, width), BF16),
             struct((48, width), BF16),
             struct((48, width), BF16),
-            struct((4 * width, width), BF16),
         ),
         in_specs=[scalar()] + [whole()] * 10,
-        out_specs=(whole(),) * 5,
+        out_specs=(whole(),) * 10,
         scratch=[
             pltpu.VMEM((points, width), BF16),
             pltpu.VMEM((ext, width), BF16),
             pltpu.VMEM((ext, width), BF16),
             pltpu.VMEM((halo_cols, width), BF16),
             pltpu.VMEM((halo_cols, width), BF16),
-            pltpu.VMEM((points, width), BF16),
             pltpu.VMEM((ext, width), F32),
             pltpu.VMEM((ext, width), F32),
             pltpu.VMEM((halo_cols, width), F32),
             pltpu.VMEM((halo_cols, width), F32),
             pltpu.VMEM((points, width), BF16),
-            pltpu.VMEM((points, width), BF16),
-            pltpu.VMEM((HALO, width), BF16),
             pltpu.VMEM((192, 256), F32),
             pltpu.VMEM((points, width), BF16),
         ],
-        us=22,
+        us=17,
     )(
         lat, kept[0][1], kept[1][1], lat_swap(row), from_l, from_r, lat_swap(from_l),
-        lat_swap(from_r), w1, wo1, cot,
-    )
-
-    sum1 = summed(dw1)
+        lat_swap(from_r), query_key_value_weight, output_weight, cot,
+    )
+
+    dn1, dw1 = call(
+        second_weights_kernel,
+        (struct((points, width), F32), struct((4 * width, width), BF16)),
+        in_specs=[whole()] * 11,
+        out_specs=(whole(),) * 2,
+        scratch=[pltpu.VMEM((points, width), BF16)],
+        us=5,
+    )(
+        kept[0][1], kept[1][1], halo, dq1, dk1, dv1, mixed1, dkh, dvh,
+        query_key_value_weight, cot,
+    )
 
     from_l, from_r = from_left(bright), from_right(bleft)
     packs = jnp.concatenate(
         [lat_swap(brow), from_l, from_r, lat_swap(from_l), lat_swap(from_r)], 0
     )
+    stages = lon_factors()
+    sum1 = halves_summed(dw1)
+    packs, sum1 = chained(packs, sum1)
+
+    def plus(a, b):
+        return (a.astype(F32) + b.astype(F32)).astype(BF16)
+
     weights = None
     backs = []
     for c in range(CHUNKS):
@@ -612,8 +655,8 @@
         kernel = functools.partial(third_kernel, firsts[c])
         extra = [] if weights is None else [weights]
         if weights is None:
-            kernel = functools.partial(without_weights, kernel)
-        *back, weights = call(
+            kernel = functools.partial(without, kernel, 18, 1)
+        dh1, d0, d1, d2, d3, d4, d5, weights = call(
             kernel,
             (
                 struct((size, width), F32),
@@ -626,12 +669,7 @@
             + [tok_spec] * 6
             + [feat_spec, kv_spec, p_spec, feat_spec, tok_spec]
             + [token_spec(tile, width, firsts[c])] * 2
-            + [
-                fixed((RETURNED, width)),
-                fixed((3 * width, width)),
-                fixed((width, width)),
-                fixed((1, width)),
-            ]
+            + [fixed((RETURNED, width)), wt_spec, wo_spec, gain_spec]
             + [fixed((4 * width, width))] * len(extra),
             out_specs=(*[tok_spec] * 7, fixed((4 * width, width))),
             scratch=[
@@ -641,62 +679,69 @@
                 pltpu.VMEM((width, tile), BF16),
                 pltpu.VMEM((8, tile), F32),
             ],
-            us=11,
+            us=13,
         )(
-            lat, *blocks[c], q0, kv0, p0, mixed0, h1, dn1, cot, packs, wt0, wo0, gain1, *extra
+            lat, *blocks[c], q0, kv0, p0, mixed0, h1, dn1, cot, packs, wt, output_weight,
+            norm_gain_table, *extra,
         )
-        backs.append(back)
-
-    sum0 = summed(weights)
-
-    def plus(a, b):
-        return (a.astype(F32) + b.astype(F32)).astype(BF16)
+        d3 = plus(d3, lat_swap(d5))
+        d2 = plus(d2, lat_swap(d4))
+        d1 = lat_swap(d1)
+        if c == 0:
+            sum1 = stage_summed(sum1, stages[0])
+            weights, sum1, d1, d2, d3 = lax.optimization_barrier((weights, sum1, d1, d2, d3))
+            for stage in stages[1:]:
+                sum1 = stage_summed(sum1, stage)
+        d2 = plus(d2, lon_backward(d3))
+        if c == 0:
+            held = d2
+        backs.append((dh1, d0, d1, d2))
+
+    weights, sum1, held = lax.optimization_barrier((weights, sum1, held))
+    backs[0] = backs[0][:3] + (held,)
+    sum0 = halves_summed(weights)
+    for stage in stages:
+        sum0 = stage_summed(sum0, stage)
+    sums = jnp.concatenate([sum0, sum1], 0)
+    for stage in stages[::-1]:
+        sums = spread(sums, *stage)
+    other = lat_swap(sums)
 
     grad_tokens = None
     for c in range(CHUNKS):
-        dh1, d0, d1, d2, d3, d4, d5 = backs[c]
-        d3 = plus(d3, lat_swap(d5))
-        d2 = plus(d2, lat_swap(d4))
-        d2 = plus(d2, lon_backward(d3))
+        dh1, d0, d1, d2 = backs[c]
         extra = [] if grad_tokens is None else [grad_tokens]
         kernel = functools.partial(last_kernel, firsts[c])
         grad_tokens = call(
-            kernel if extra else functools.partial(without_previous, kernel),
+            kernel if extra else functools.partial(without, kernel, 7, 1),
             struct((points, width), F32),
             grid=(size // small,),
-            in_specs=[
-                token_spec(small, width),
-                fixed((rows, cols)),
-                fixed((1, width)),
-                *[token_spec(small, width)] * 4,
-            ]
+            in_specs=[token_spec(small, width), fixed((rows, cols)), gain_spec]
+            + [token_spec(small, width)] * 4
             + [pl.BlockSpec(memory_space=pl.ANY)] * len(extra),
             out_specs=token_spec(small, width, firsts[c]),
             aliases={7: 0} if extra else {},
-            us=2,
-        )(starts[c], visible, gain0, dh1, d0, lon_swap(d2), lat_swap(d1), *extra)
+            us=4,
+        )(starts[c], visible, norm_gain_table, dh1, d0, lon_swap(d2), d1, *extra)
 
     factor = (points * lat_count * lon_count) ** (-0.5)
     g_qkv, g_out, g_gain = call(
-        functools.partial(weights_kernel, factor),
+        functools.partial(weights_kernel, factor, lon_count),
         (
             struct((2, width, 3 * width), F32),
             struct((2, width, width), F32),
             struct((2, width), F32),
         ),
-        in_specs=[whole()] * 4,
+        in_specs=[scalar()] + [whole()] * 4,
         out_specs=(whole(),) * 3,
-        us=4,
-    )(sum0, sum1, wt, norm_gain_table)
+        scratch=[pltpu.VMEM((2, 4 * width, width), F32)],
+        us=5,
+    )(lat, sums, other, wt, norm_gain_table)
     return grad_tokens.reshape(rows, cols, width), g_qkv, g_out, g_gain
 
 
-def without_weights(kernel, *refs):
-    kernel(*refs[:18], None, *refs[18:])
-
-
-def without_previous(kernel, *refs):
-    kernel(*refs[:7], None, *refs[7:])
+def without(kernel, at, count, *refs):
+    kernel(*refs[:at], *[None] * count, *refs[at:])
 
 
 def solution(mesh):

time: 232 us -> 222 us (0.957)
  starting transfers between devices: 58.9 us -> 45.6 us
  waiting for transfers between devices: 65.9 us -> 75.3 us
  local copies, waits for them, and re-layouts: 12.9 us -> 9.64 us
  other arithmetic: 3.94 us -> 1.16 us
    ppermute x8 -> x4, starting transfers between devices: 19.1 us -> 4.91 us  [spread(): got = lax.ppermute(value, 'lon', pairs)]
    ppermute x8, waiting for transfers between devices: 8.18 us -> 14.3 us  [exchanged(): moved.append(lax.ppermute(parts(lax.rem(digit + d, factor)), 'lon', pairs))]
    squeeze x3 -> x0, local copies, waits for them, and re-layouts: 4.43 us -> none  [the longest x1 2.38 us: local(): wo0, wo1 = (output_weight[0], output_weight[1])]
    unnamed x55 -> x71, local copies, waits for them, and re-layouts: 4.5 us -> 7.77 us
    ppermute x34 -> x33, waiting for transfers between devices: 39.1 us -> 42.2 us  [permuted(): lax.ppermute(value, axis, [(i, target(i) % count) for i in range(count)])]
    pallas_call x6 -> x7, Pallas kernels: 53.3 us -> 56.4 us  [the longest x1 19.8 us: local(): call(second_kernel, (every, every, every, every, halo_struct, halo_struct...]
    select_n x2 -> x0, other arithmetic: 2.85 us -> none  [summed(): jnp.where(lat == 0, jnp.concatenate([value, other], 0), jnp.concatenate([...]
    pallas_call x2, Pallas kernels: 7.94 us -> 5.3 us  [local(): call(functools.partial(start_kernel, first), (part, part), grid=(size //...]
  transfers between devices with their start and end apart: 50 -> 45, of which waited for: 26 -> 22; matrix products, arithmetic and copies ran while one was open for 4% -> 1% of each run, Pallas kernels for 9% -> 20%
where the time goes in v3:
time: 222 us
  Pallas kernels  89.2 us (40%)
  waiting for transfers between devices  75.3 us (34%)
  starting transfers between devices  45.6 us (21%)
  local copies, waits for them, and re-layouts  9.64 us (4%)
    ppermute x33, waiting for transfers between devices, permuted(): lax.ppermute(value, axis, [(i, target(i) % count) for i in range(count)])  42.2 us
    ppermute x33, starting transfers between devices, permuted(): lax.ppermute(value, axis, [(i, target(i) % count) for i in range(count)])  31.5 us
    pallas_call x2, Pallas kernels, local(): call(kernel, (struct((size, width), F32), struct((size, width), F32), *[p...  27.5 us
    pallas_call x1, Pallas kernels, local(): call(second_kernel, (every, every, every, every, halo_struct, halo_struct...  19.8 us
    ppermute x4, waiting for transfers between devices, spread(): got = lax.ppermute(value, 'lon', pairs)  18.8 us
    pallas_call x2, Pallas kernels, local(): call(kernel if packs else functools.partial(without, kernel, 8, 3), (stru...  17 us
    ppermute x8, waiting for transfers between devices, exchanged(): moved.append(lax.ppermute(parts(lax.rem(digit + d, factor)), 'lon', pairs))  14.3 us
    ppermute x8, starting transfers between devices, exchanged(): moved.append(lax.ppermute(parts(lax.rem(digit + d, factor)), 'lon', pairs))  9.2 us
  transfers between devices with their start and end apart: 45, of which 22 were waited for; matrix products, arithmetic and copies ran while one was open for 1% of the time, Pallas kernels for 20%

profile of v3, /device:TPU:0, one launch (start us, length us, event | category | flops | bytes accessed | tf_op | source)
XLA Modules:
  0.0 222.0 jit_solution(14788540831290870676)
XLA Ops:
  0.6 2.6 %shard_map.103 = (bf16[512,384]{1,0:T(8,128)(2,1)}, bf16[512,384]{1,0:T(8,128)(2,1)}) custom-call(bf16[1024,384]{1,0:T(8,128)(2,1)} %bitcast.14, s32[32,32]{1,0:T(8,128)} %vis_ref.5, bf16[384]{0:T(512)(128)(2,1)} %mask_ref.3, f32[2,384]{1,0:T(2,128)} %gain_ref.11), custom_call_target="tpu_custom_call" | custom-call | flops 1600000000 | bytes 2000000 | tf_op jit(solution)/shard_map/pallas_call | solution.py:525
  3.2 3.0 %collective-permute-start = (bf16[512,384]{1,0:T(8,128)(2,1)}, bf16[512,384]{1,0:T(8,128)(2,1)S(1)}, u32[]{:S(2)}, u32[]{:S(2)}) collective-permute-start(bf16[512,384]{1,0:T(8,128)(2,1)} %get-tuple-element.75.refs_1_), channel_id=1, source_target_pairs={{0,2},{2,0},{4,6},{6,4},{8,10},{10,8},{12,14},{14,12},{1,3},{3,1},... | collective-permute-start | bytes 1179656 | tf_op jit(solution)/shard_map/ppermute | solution.py:42
  6.2 2.7 %shard_map.102 = (bf16[512,384]{1,0:T(8,128)(2,1)}, bf16[512,384]{1,0:T(8,128)(2,1)}) custom-call(bf16[1024,384]{1,0:T(8,128)(2,1)} %bitcast.15, s32[32,32]{1,0:T(8,128)} %vis_ref.5, bf16[384]{0:T(512)(128)(2,1)} %mask_ref.3, f32[2,384]{1,0:T(2,128)} %gain_ref.11), custom_call_target="tpu_custom_call" | custom-call | flops 1600000000 | bytes 2000000 | tf_op jit(solution)/shard_map/pallas_call | solution.py:525
  8.9 6.7 %collective-permute-done.refs_3_ = bf16[512,384]{1,0:T(8,128)(2,1)S(1)} collective-permute-done((bf16[512,384]{1,0:T(8,128)(2,1)}, bf16[512,384]{1,0:T(8,128)(2,1)S(1)}, u32[]{:S(2)}, u32[]{:S(2)}) %collective-permute-start) | collective-permute-done | bytes 393248 | tf_op jit(solution)/shard_map/ppermute | solution.py:42
  17.3 3.5 %collective-permute-start.2 = (bf16[512,384]{1,0:T(8,128)(2,1)}, bf16[512,384]{1,0:T(8,128)(2,1)S(1)}, u32[]{:S(2)}, u32[]{:S(2)}) collective-permute-start(bf16[512,384]{1,0:T(8,128)(2,1)} %get-tuple-element.76.n0), channel_id=1, source_target_pairs={{0,2},{2,0},{4,6},{6,4},{8,10},{10,8},{12,14},{14,12},{1,3},{3,1},... | collective-permute-start | bytes 1179656 | tf_op jit(solution)/shard_map/ppermute | solution.py:42
  21.4 6.4 %collective-permute-done.5.refs_4_ = bf16[512,384]{1,0:T(8,128)(2,1)} collective-permute-done((bf16[512,384]{1,0:T(8,128)(2,1)S(1)}, bf16[512,384]{1,0:T(8,128)(2,1)}, u32[]{:S(2)}, u32[]{:S(2)}) %collective-permute-start.5) | collective-permute-done | bytes 393248 | tf_op jit(solution)/shard_map/ppermute | solution.py:42
  27.8 2.3 %copy.12 = bf16[2,384,1152]{1,2,0:T(8,128)(2,1)} copy(bf16[2,384,1152]{2,1,0:T(8,128)(2,1)S(1)} %copy-done) | data formatting | bytes 3538944 | tf_op args[4]
  30.7 8.5 %shard_map.104 = (bf16[384,512]{1,0:T(8,128)(2,1)}, bf16[6,768,512]{2,1,0:T(8,128)(2,1)}, f32[6,8,512]{2,1,0:T(8,128)}, bf16[384,512]{1,0:T(8,128)(2,1)}, bf16[5...) custom-call(s32[1]{0:T(128)} %bitcast.1.refs_0_.lat_ref, ...), custom_call_target="tpu_custom_call" | custom-call | flops 6400000000 | bytes 8000000 | tf_op jit(solution)/shard_map/pallas_call | solution.py:562
  39.2 4.2 %collective-permute-done.3.n3 = bf16[512,384]{1,0:T(8,128)(2,1)S(1)} collective-permute-done((bf16[512,384]{1,0:T(8,128)(2,1)S(1)}, bf16[512,384]{1,0:T(8,128)(2,1)S(1)}, u32[]{:S(2)}, u32[]{:S(2)}) %collective-permute-start.3) | collective-permute-done | bytes 393248 | tf_op jit(solution)/shard_map/ppermute | solution.py:42
  45.9 8.5 %shard_map.105 = (bf16[384,512]{1,0:T(8,128)(2,1)}, bf16[6,768,512]{2,1,0:T(8,128)(2,1)}, f32[6,8,512]{2,1,0:T(8,128)}, bf16[384,512]{1,0:T(8,128)(2,1)}, bf16[5...) custom-call(s32[1]{0:T(128)} %bitcast.1.refs_0_.lat_ref, ...), custom_call_target="tpu_custom_call" | custom-call | flops 6400000000 | bytes 8000000 | tf_op jit(solution)/shard_map/pallas_call | solution.py:562
  55.3 3.9 %collective-permute-start.12 = (bf16[32,384]{1,0:T(8,128)(2,1)}, bf16[32,384]{1,0:T(8,128)(2,1)S(1)}, u32[]{:S(2)}, u32[]{:S(2)}) collective-permute-start(bf16[32,384]{1,0:T(8,128)(2,1)} %get-tuple-element.95), channel_id=1, source_target_pairs={{0,14},{2,0},{4,2},{6,4},{8,6},{10,8},{12,10},{14,12},{1,15},{3,1}... | collective-permute-start | bytes 73736 | tf_op jit(solution)/shard_map/ppermute | solution.py:42
  59.2 2.0 collective-permute-done.11.left_ref
  63.2 19.8 %shard_map.106 = (bf16[1024,384]{1,0:T(8,128)(2,1)}, bf16[1024,384]{1,0:T(8,128)(2,1)}, bf16[1024,384]{1,0:T(8,128)(2,1)}, bf16[1024,384]{1,0:T(8,128)(2,1)}, bf...) custom-call(s32[1]{0:T(128)} %bitcast.1.refs_0_.lat_ref, ...), custom_call_target="tpu_custom_call" | custom-call | flops 13600000000 | bytes 17000000 | tf_op jit(solution)/shard_map/pallas_call | solution.py:597
  83.1 7.8 %shard_map.107 = (f32[1024,384]{1,0:T(8,128)}, bf16[1536,384]{1,0:T(8,128)(2,1)}) custom-call(bf16[512,384]{1,0:T(8,128)(2,1)} %get-tuple-element.91.na_ref, bf16[512,384]{1,0:T(8,128)(2,1)} %get-tuple-element.92.nb_ref, bf16[112,384]{1,0:T(8,128)(2,1)} %get-tuple-element.96.halo_ref, bf16[1024,384]{1,0:T(8,128)(2,1)} %get-tuple-element.97.dq_ref, ...), custom_call_target="tpu_custom_call" | custom-call | flops 4000000000 | bytes 5000000 | tf_op jit(solution)/shard_map/pallas_call | solution.py:627
  92.7 4.8 %collective-permute-start.17 = (bf16[48,384]{1,0:T(8,128)(2,1)S(1)}, bf16[48,384]{1,0:T(8,128)(2,1)S(1)}, u32[]{:S(2)}, u32[]{:S(2)}) collective-permute-start(bf16[48,384]{1,0:T(8,128)(2,1)S(1)} %copy-done.25), channel_id=1, source_target_pairs={{0,14},{2,0},{4,2},{6,4},{8,6},{10,8},{12,10},{14,12},{1,15},{3,1}... | collective-permute-start | bytes 110600 | tf_op jit(solution)/shard_map/ppermute | solution.py:42
  101.4 13.5 %shard_map.108 = (f32[512,384]{1,0:T(8,128)}, f32[512,384]{1,0:T(8,128)}, bf16[512,384]{1,0:T(8,128)(2,1)}, bf16[512,384]{1,0:T(8,128)(2,1)}, bf16[512,384]{1,0:...) custom-call(s32[1]{0:T(128)} %bitcast.1.refs_0_.lat_ref, ...), custom_call_target="tpu_custom_call" | custom-call | flops 10400000000 | bytes 13000000 | tf_op jit(solution)/shard_map/pallas_call | solution.py:659
  118.3 5.3 %collective-permute-start.32 = (bf16[96,384]{1,0:T(8,128)(2,1)S(1)}, bf16[96,384]{1,0:T(8,128)(2,1)S(1)}, u32[]{:S(2)}, u32[]{:S(2)}) collective-permute-start(bf16[96,384]{1,0:T(8,128)(2,1)S(1)} %get-tuple-element.146), channel_id=1, source_target_pairs={{0,12},{2,14},{4,0},{6,2},{8,4},{10,6},{12,8},{14,10},{1,13},{3,15... | collective-permute-start | bytes 221192 | tf_op jit(solution)/shard_map/ppermute | solution.py:79
  124.2 3.2 %collective-permute-start.33 = (bf16[512,384]{1,0:T(8,128)(2,1)S(1)}, bf16[512,384]{1,0:T(8,128)(2,1)S(1)}, u32[]{:S(2)}, u32[]{:S(2)}) collective-permute-start(bf16[512,384]{1,0:T(8,128)(2,1)S(1)} %add_convert_fusion.6), channel_id=1, source_target_pairs={{0,12},{2,6},{4,0},{6,10},{8,4},{10,14},{12,8},{14,2},{1,13},{3,7}... | collective-permute-start | bytes 1179656 | tf_op jit(solution)/shard_map/ppermute | solution.py:42
  127.4 14.0 %shard_map.109 = (f32[512,384]{1,0:T(8,128)}, f32[512,384]{1,0:T(8,128)}, bf16[512,384]{1,0:T(8,128)(2,1)}, bf16[512,384]{1,0:T(8,128)(2,1)}, bf16[512,384]{1,0:...) custom-call(s32[1]{0:T(128)} %bitcast.1.refs_0_.lat_ref, ...), custom_call_target="tpu_custom_call" | custom-call | flops 10400000000 | bytes 13000000 | tf_op jit(solution)/shard_map/pallas_call | solution.py:659
  142.8 2.0 collective-permute-done.35
  145.1 9.0 %collective-permute-done.36 = bf16[384,384]{1,0:T(8,128)(2,1)S(1)} collective-permute-done((bf16[384,384]{1,0:T(8,128)(2,1)S(1)}, bf16[384,384]{1,0:T(8,128)(2,1)S(1)}, u32[]{:S(2)}, u32[]{:S(2)}) %collective-permute-start.36) | collective-permute-done | bytes 294944 | tf_op jit(solution)/shard_map/ppermute | solution.py:79
  159.2 3.5 %collective-permute-done.38 = bf16[96,384]{1,0:T(8,128)(2,1)S(1)} collective-permute-done((bf16[96,384]{1,0:T(8,128)(2,1)S(1)}, bf16[96,384]{1,0:T(8,128)(2,1)S(1)}, u32[]{:S(2)}, u32[]{:S(2)}) %collective-permute-start.38) | collective-permute-done | bytes 73760 | tf_op jit(solution)/shard_map/ppermute | solution.py:79
  164.7 2.5 %collective-permute-start.42 = (bf16[192,384]{1,0:T(8,128)(2,1)S(1)}, bf16[192,384]{1,0:T(8,128)(2,1)S(1)}, u32[]{:S(2)}, u32[]{:S(2)}) collective-permute-start(bf16[192,384]{1,0:T(8,128)(2,1)S(1)} %get-tuple-element.148), channel_id=1, source_target_pairs={{0,12},{2,14},{4,0},{6,2},{8,4},{10,6},{12,8},{14,10},{1,13},{3,15... | collective-permute-start | bytes 442376 | tf_op jit(solution)/shard_map/ppermute | solution.py:99
  167.2 4.4 %collective-permute-done.40 = bf16[192,384]{1,0:T(8,128)(2,1)S(1)} collective-permute-done((bf16[192,384]{1,0:T(8,128)(2,1)S(1)}, bf16[192,384]{1,0:T(8,128)(2,1)S(1)}, u32[]{:S(2)}, u32[]{:S(2)}) %collective-permute-start.40) | collective-permute-done | bytes 147488 | tf_op jit(solution)/shard_map/ppermute | solution.py:99
  171.6 3.6 %collective-permute-done.41 = bf16[192,384]{1,0:T(8,128)(2,1)S(1)} collective-permute-done((bf16[192,384]{1,0:T(8,128)(2,1)S(1)}, bf16[192,384]{1,0:T(8,128)(2,1)S(1)}, u32[]{:S(2)}, u32[]{:S(2)}) %collective-permute-start.41) | collective-permute-done | bytes 147488 | tf_op jit(solution)/shard_map/ppermute | solution.py:99
  176.7 4.3 %collective-permute-start.27 = (bf16[512,384]{1,0:T(8,128)(2,1)S(1)}, bf16[512,384]{1,0:T(8,128)(2,1)S(1)}, u32[]{:S(2)}, u32[]{:S(2)}) collective-permute-start(bf16[512,384]{1,0:T(8,128)(2,1)S(1)} %add_convert_fusion.4), channel_id=1, source_target_pairs={{0,12},{2,6},{4,0},{6,10},{8,4},{10,14},{12,8},{14,2},{1,13},{3,7}... | collective-permute-start | bytes 1179656 | tf_op jit(solution)/shard_map/ppermute | solution.py:42
  181.3 10.1 %collective-permute-done.43 = bf16[768,384]{1,0:T(8,128)(2,1)S(1)} collective-permute-done((bf16[768,384]{1,0:T(8,128)(2,1)S(1)}, bf16[768,384]{1,0:T(8,128)(2,1)S(1)}, u32[]{:S(2)}, u32[]{:S(2)}) %collective-permute-start.43) | collective-permute-done | bytes 589856 | tf_op jit(solution)/shard_map/ppermute | solution.py:99
  194.0 9.5 %collective-permute-done.34.refs_5_ = bf16[512,384]{1,0:T(8,128)(2,1)S(1)} collective-permute-done((bf16[512,384]{1,0:T(8,128)(2,1)S(1)}, bf16[512,384]{1,0:T(8,128)(2,1)S(1)}, u32[]{:S(2)}, u32[]{:S(2)}) %collective-permute-start.34) | collective-permute-done | bytes 393248 | tf_op jit(solution)/shard_map/ppermute | solution.py:42
  204.3 3.1 %shard_map.110.prev_ref = f32[1024,384]{1,0:T(8,128)} custom-call(bf16[512,384]{1,0:T(8,128)(2,1)} %get-tuple-element.78.refs_7_.refs_0_, s32[32,32]{1,0:T(8,128)} %vis_ref.5, f32[2,384]{1,0:T(2,128)} %gain_ref.11, f32[512,384]{1,0:T(8,128)} %get-tuple-element.129.refs_3_, f32[512,384]{1,0:T(8,128)} %get-tuple-element.130.refs_4_, ...), custom_call_target="tpu_custom_call" | custom-call | flops 3200000000 | bytes 4000000 | tf_op jit(solution)/shard_map/pallas_call | solution.py:715
  207.3 4.2 %collective-permute-done.28.far_ref = bf16[512,384]{1,0:T(8,128)(2,1)S(1)} collective-permute-done((bf16[512,384]{1,0:T(8,128)(2,1)S(1)}, bf16[512,384]{1,0:T(8,128)(2,1)S(1)}, u32[]{:S(2)}, u32[]{:S(2)}) %collective-permute-start.28) | collective-permute-done | bytes 393248 | tf_op jit(solution)/shard_map/ppermute | solution.py:42
  212.2 3.0 %shard_map.111 = f32[1024,384]{1,0:T(8,128)} custom-call(bf16[512,384]{1,0:T(8,128)(2,1)} %get-tuple-element.73.start_ref, s32[32,32]{1,0:T(8,128)} %vis_ref.5, f32[2,384]{1,0:T(2,128)} %gain_ref.11, f32[512,384]{1,0:T(8,128)} %get-tuple-element.122.dh_ref, f32[512,384]{1,0:T(8,128)} %get-tuple-element.123.own_ref, ...), custom_call_target="tpu_custom_call", output_to_operand_aliasing={{}: (7, {})} | custom-call | flops 3200000000 | bytes 4000000 | tf_op jit(solution)/shard_map/pallas_call | solution.py:715
  216.3 5.7 %shard_map.112 = (f32[2,384,1152]{2,1,0:T(8,128)}, f32[2,384,384]{2,1,0:T(8,128)}, f32[2,384]{1,0:T(2,128)}) custom-call(s32[1]{0:T(128)} %bitcast.1.refs_0_.lat_ref, bf16[1536,384]{1,0:T(8,128)(2,1)} %copy-done.1, bf16[1536,384]{1,0:T(8,128)(2,1)} %copy-done.9, bf16[2,1152,384]{2,1,0:T(8,128)(2,1)} %bitcast.9, f32[2,384]{1,0:T(2,128)} %gain_ref.11), custom_call_target="tpu_custom_call" | custom-call | flops 4000000000 | bytes 5000000 | tf_op jit(solution)/shard_map/pallas_call | solution.py:728
  (166 shorter events, 33.4 us)
Async XLA Ops:
  3.2 12.4 %collective-permute-start = (bf16[512,384]{1,0:T(8,128)(2,1)}, bf16[512,384]{1,0:T(8,128)(2,1)S(1)}, u32[]{:S(2)}, u32[]{:S(2)}) collective-permute-start(bf16[512,384]{1,0:T(8,128)(2,1)} %get-tuple-element.75.refs_1_), channel_id=1, source_target_pairs={{0,2},{2,0},{4,6},{6,4},{8,10},{10,8},{12,14},{14,12},{1,3},{3,1},... | collective-permute-start | bytes 1179656 | tf_op jit(solution)/shard_map/ppermute | solution.py:42
  15.6 12.2 %collective-permute-start.5 = (bf16[512,384]{1,0:T(8,128)(2,1)S(1)}, bf16[512,384]{1,0:T(8,128)(2,1)}, u32[]{:S(2)}, u32[]{:S(2)}) collective-permute-start(bf16[512,384]{1,0:T(8,128)(2,1)S(1)} %collective-permute-done.refs_3_), channel_id=1, source_target_pairs={{0,4},{2,14},{4,8},{6,2},{8,12},{10,6},{12,0},{14,10},{1,5},{3,15}... | collective-permute-start | bytes 1179656 | tf_op jit(solution)/shard_map/ppermute | solution.py:42
  17.3 13.2 %collective-permute-start.2 = (bf16[512,384]{1,0:T(8,128)(2,1)}, bf16[512,384]{1,0:T(8,128)(2,1)S(1)}, u32[]{:S(2)}, u32[]{:S(2)}) collective-permute-start(bf16[512,384]{1,0:T(8,128)(2,1)} %get-tuple-element.76.n0), channel_id=1, source_target_pairs={{0,2},{2,0},{4,6},{6,4},{8,10},{10,8},{12,14},{14,12},{1,3},{3,1},... | collective-permute-start | bytes 1179656 | tf_op jit(solution)/shard_map/ppermute | solution.py:42
  20.9 9.7 %collective-permute-start.4 = (bf16[512,384]{1,0:T(8,128)(2,1)S(1)}, bf16[512,384]{1,0:T(8,128)(2,1)}, u32[]{:S(2)}, u32[]{:S(2)}) collective-permute-start(bf16[512,384]{1,0:T(8,128)(2,1)S(1)} %copy-done.17), channel_id=1, source_target_pairs={{0,1},{1,0},{2,3},{3,2},{4,5},{5,4},{6,7},{7,6},{8,9},{9,8},{10,11... | collective-permute-start | bytes 1179656 | tf_op jit(solution)/shard_map/ppermute | solution.py:42
  20.9 9.9 %collective-permute-start.6 = (bf16[512,384]{1,0:T(8,128)(2,1)S(1)}, bf16[512,384]{1,0:T(8,128)(2,1)}, u32[]{:S(2)}, u32[]{:S(2)}) collective-permute-start(bf16[512,384]{1,0:T(8,128)(2,1)S(1)} %collective-permute-done.refs_3_), channel_id=1, source_target_pairs={{0,1},{1,0},{2,3},{3,2},{4,5},{5,4},{6,7},{7,6},{8,9},{9,8},{10,11... | collective-permute-start | bytes 1179656 | tf_op jit(solution)/shard_map/ppermute | solution.py:42
  30.1 13.4 %collective-permute-start.1 = (bf16[512,384]{1,0:T(8,128)(2,1)S(1)}, bf16[512,384]{1,0:T(8,128)(2,1)S(1)}, u32[]{:S(2)}, u32[]{:S(2)}) collective-permute-start(bf16[512,384]{1,0:T(8,128)(2,1)S(1)} %copy-done.10), channel_id=1, source_target_pairs={{0,1},{1,0},{2,3},{3,2},{4,5},{5,4},{6,7},{7,6},{8,9},{9,8},{10,11... | collective-permute-start | bytes 1179656 | tf_op jit(solution)/shard_map/ppermute | solution.py:42
  30.6 12.9 %collective-permute-start.3 = (bf16[512,384]{1,0:T(8,128)(2,1)S(1)}, bf16[512,384]{1,0:T(8,128)(2,1)S(1)}, u32[]{:S(2)}, u32[]{:S(2)}) collective-permute-start(bf16[512,384]{1,0:T(8,128)(2,1)S(1)} %collective-permute-done.2.n2), channel_id=1, source_target_pairs={{0,4},{2,14},{4,8},{6,2},{8,12},{10,6},{12,0},{14,10},{1,5},{3,15}... | collective-permute-start | bytes 1179656 | tf_op jit(solution)/shard_map/ppermute | solution.py:42
  30.6 12.9 %collective-permute-start.8 = (bf16[512,384]{1,0:T(8,128)(2,1)S(1)}, bf16[512,384]{1,0:T(8,128)(2,1)S(1)}, u32[]{:S(2)}, u32[]{:S(2)}) collective-permute-start(bf16[512,384]{1,0:T(8,128)(2,1)S(1)} %collective-permute-done.2.n2), channel_id=1, source_target_pairs={{0,1},{1,0},{2,3},{3,2},{4,5},{5,4},{6,7},{7,6},{8,9},{9,8},{10,11... | collective-permute-start | bytes 1179656 | tf_op jit(solution)/shard_map/ppermute | solution.py:42
  54.4 6.8 %collective-permute-start.11 = (bf16[32,384]{1,0:T(8,128)(2,1)}, bf16[32,384]{1,0:T(8,128)(2,1)S(1)}, u32[]{:S(2)}, u32[]{:S(2)}) collective-permute-start(bf16[32,384]{1,0:T(8,128)(2,1)} %get-tuple-element.94), channel_id=1, source_target_pairs={{0,2},{2,4},{4,6},{6,8},{8,10},{10,12},{12,14},{14,0},{1,3},{3,5},... | collective-permute-start | bytes 73736 | tf_op jit(solution)/shard_map/ppermute | solution.py:42
  55.3 6.0 %collective-permute-start.12 = (bf16[32,384]{1,0:T(8,128)(2,1)}, bf16[32,384]{1,0:T(8,128)(2,1)S(1)}, u32[]{:S(2)}, u32[]{:S(2)}) collective-permute-start(bf16[32,384]{1,0:T(8,128)(2,1)} %get-tuple-element.95), channel_id=1, source_target_pairs={{0,14},{2,0},{4,2},{6,4},{8,6},{10,8},{12,10},{14,12},{1,15},{3,1}... | collective-permute-start | bytes 73736 | tf_op jit(solution)/shard_map/ppermute | solution.py:42
  92.1 8.6 %collective-permute-start.20 = (bf16[768,384]{1,0:T(8,128)(2,1)S(1)}, bf16[768,384]{1,0:T(8,128)(2,1)S(1)}, u32[]{:S(2)}, u32[]{:S(2)}) collective-permute-start(bf16[768,384]{1,0:T(8,128)(2,1)S(1)} %constant_dynamic-slice_fusion.9), channel_id=1, source_target_pairs={{0,1},{1,0},{2,3},{3,2},{4,5},{5,4},{6,7},{7,6},{8,9},{9,8},{10,11... | collective-permute-start | bytes 1769480 | tf_op jit(solution)/shard_map/ppermute | solution.py:42
  92.7 6.7 %collective-permute-start.16 = (bf16[48,384]{1,0:T(8,128)(2,1)S(1)}, bf16[48,384]{1,0:T(8,128)(2,1)S(1)}, u32[]{:S(2)}, u32[]{:S(2)}) collective-permute-start(bf16[48,384]{1,0:T(8,128)(2,1)S(1)} %copy-done.26), channel_id=1, source_target_pairs={{0,2},{2,4},{4,6},{6,8},{8,10},{10,12},{12,14},{14,0},{1,3},{3,5},... | collective-permute-start | bytes 110600 | tf_op jit(solution)/shard_map/ppermute | solution.py:42
  92.7 6.7 %collective-permute-start.17 = (bf16[48,384]{1,0:T(8,128)(2,1)S(1)}, bf16[48,384]{1,0:T(8,128)(2,1)S(1)}, u32[]{:S(2)}, u32[]{:S(2)}) collective-permute-start(bf16[48,384]{1,0:T(8,128)(2,1)S(1)} %copy-done.25), channel_id=1, source_target_pairs={{0,14},{2,0},{4,2},{6,4},{8,6},{10,8},{12,10},{14,12},{1,15},{3,1}... | collective-permute-start | bytes 110600 | tf_op jit(solution)/shard_map/ppermute | solution.py:42
  101.4 14.5 %collective-permute-start.21 = (bf16[384,384]{1,0:T(8,128)(2,1)S(1)}, bf16[384,384]{1,0:T(8,128)(2,1)S(1)}, u32[]{:S(2)}, u32[]{:S(2)}) collective-permute-start(bf16[384,384]{1,0:T(8,128)(2,1)S(1)} %constant_dynamic-slice_fusion.8), channel_id=1, source_target_pairs={{0,2},{2,0},{4,6},{6,4},{8,10},{10,8},{12,14},{14,12},{1,3},{3,1},... | collective-permute-start | bytes 884744 | tf_op jit(solution)/shard_map/ppermute | solution.py:79
  118.3 23.1 %collective-permute-start.32 = (bf16[96,384]{1,0:T(8,128)(2,1)S(1)}, bf16[96,384]{1,0:T(8,128)(2,1)S(1)}, u32[]{:S(2)}, u32[]{:S(2)}) collective-permute-start(bf16[96,384]{1,0:T(8,128)(2,1)S(1)} %get-tuple-element.146), channel_id=1, source_target_pairs={{0,12},{2,14},{4,0},{6,2},{8,4},{10,6},{12,8},{14,10},{1,13},{3,15... | collective-permute-start | bytes 221192 | tf_op jit(solution)/shard_map/ppermute | solution.py:79
  123.6 17.8 %collective-permute-start.31 = (bf16[96,384]{1,0:T(8,128)(2,1)S(1)}, bf16[96,384]{1,0:T(8,128)(2,1)S(1)}, u32[]{:S(2)}, u32[]{:S(2)}) collective-permute-start(bf16[96,384]{1,0:T(8,128)(2,1)S(1)} %get-tuple-element.147), channel_id=1, source_target_pairs={{0,8},{2,10},{4,12},{6,14},{8,0},{10,2},{12,4},{14,6},{1,9},{3,11}... | collective-permute-start | bytes 221192 | tf_op jit(solution)/shard_map/ppermute | solution.py:79
  123.6 17.8 %collective-permute-start.30 = (bf16[96,384]{1,0:T(8,128)(2,1)S(1)}, bf16[96,384]{1,0:T(8,128)(2,1)S(1)}, u32[]{:S(2)}, u32[]{:S(2)}) collective-permute-start(bf16[96,384]{1,0:T(8,128)(2,1)S(1)} %get-tuple-element.145), channel_id=1, source_target_pairs={{0,4},{2,6},{4,8},{6,10},{8,12},{10,14},{12,0},{14,2},{1,5},{3,7},... | collective-permute-start | bytes 221192 | tf_op jit(solution)/shard_map/ppermute | solution.py:79
  124.2 17.3 %collective-permute-start.33 = (bf16[512,384]{1,0:T(8,128)(2,1)S(1)}, bf16[512,384]{1,0:T(8,128)(2,1)S(1)}, u32[]{:S(2)}, u32[]{:S(2)}) collective-permute-start(bf16[512,384]{1,0:T(8,128)(2,1)S(1)} %add_convert_fusion.6), channel_id=1, source_target_pairs={{0,12},{2,6},{4,0},{6,10},{8,4},{10,14},{12,8},{14,2},{1,13},{3,7}... | collective-permute-start | bytes 1179656 | tf_op jit(solution)/shard_map/ppermute | solution.py:42
  145.0 9.1 %collective-permute-start.36 = (bf16[384,384]{1,0:T(8,128)(2,1)S(1)}, bf16[384,384]{1,0:T(8,128)(2,1)S(1)}, u32[]{:S(2)}, u32[]{:S(2)}) collective-permute-start(bf16[384,384]{1,0:T(8,128)(2,1)S(1)} %constant_dynamic-slice_fusion.3), channel_id=1, source_target_pairs={{0,2},{2,0},{4,6},{6,4},{8,10},{10,8},{12,14},{14,12},{1,3},{3,1},... | collective-permute-start | bytes 884744 | tf_op jit(solution)/shard_map/ppermute | solution.py:79
  154.9 7.8 %collective-permute-start.38 = (bf16[96,384]{1,0:T(8,128)(2,1)S(1)}, bf16[96,384]{1,0:T(8,128)(2,1)S(1)}, u32[]{:S(2)}, u32[]{:S(2)}) collective-permute-start(bf16[96,384]{1,0:T(8,128)(2,1)S(1)} %get-tuple-element.144), channel_id=1, source_target_pairs={{0,8},{2,10},{4,12},{6,14},{8,0},{10,2},{12,4},{14,6},{1,9},{3,11}... | collective-permute-start | bytes 221192 | tf_op jit(solution)/shard_map/ppermute | solution.py:79
  155.5 7.2 %collective-permute-start.37 = (bf16[96,384]{1,0:T(8,128)(2,1)S(1)}, bf16[96,384]{1,0:T(8,128)(2,1)S(1)}, u32[]{:S(2)}, u32[]{:S(2)}) collective-permute-start(bf16[96,384]{1,0:T(8,128)(2,1)S(1)} %get-tuple-element.142), channel_id=1, source_target_pairs={{0,4},{2,6},{4,8},{6,10},{8,12},{10,14},{12,0},{14,2},{1,5},{3,7},... | collective-permute-start | bytes 221192 | tf_op jit(solution)/shard_map/ppermute | solution.py:79
  162.8 8.7 %collective-permute-start.40 = (bf16[192,384]{1,0:T(8,128)(2,1)S(1)}, bf16[192,384]{1,0:T(8,128)(2,1)S(1)}, u32[]{:S(2)}, u32[]{:S(2)}) collective-permute-start(bf16[192,384]{1,0:T(8,128)(2,1)S(1)} %get-tuple-element.148), channel_id=1, source_target_pairs={{0,4},{2,6},{4,8},{6,10},{8,12},{10,14},{12,0},{14,2},{1,5},{3,7},... | collective-permute-start | bytes 442376 | tf_op jit(solution)/shard_map/ppermute | solution.py:99
  162.9 12.2 %collective-permute-start.41 = (bf16[192,384]{1,0:T(8,128)(2,1)S(1)}, bf16[192,384]{1,0:T(8,128)(2,1)S(1)}, u32[]{:S(2)}, u32[]{:S(2)}) collective-permute-start(bf16[192,384]{1,0:T(8,128)(2,1)S(1)} %get-tuple-element.148), channel_id=1, source_target_pairs={{0,8},{2,10},{4,12},{6,14},{8,0},{10,2},{12,4},{14,6},{1,9},{3,11}... | collective-permute-start | bytes 442376 | tf_op jit(solution)/shard_map/ppermute | solution.py:99
  164.7 11.9 %collective-permute-start.26 = (bf16[512,384]{1,0:T(8,128)(2,1)S(1)}, bf16[512,384]{1,0:T(8,128)(2,1)S(1)}, u32[]{:S(2)}, u32[]{:S(2)}) collective-permute-start(bf16[512,384]{1,0:T(8,128)(2,1)S(1)} %copy-done.21), channel_id=1, source_target_pairs={{0,1},{1,0},{2,3},{3,2},{4,5},{5,4},{6,7},{7,6},{8,9},{9,8},{10,11... | collective-permute-start | bytes 1179656 | tf_op jit(solution)/shard_map/ppermute | solution.py:42
  164.7 11.3 %collective-permute-start.42 = (bf16[192,384]{1,0:T(8,128)(2,1)S(1)}, bf16[192,384]{1,0:T(8,128)(2,1)S(1)}, u32[]{:S(2)}, u32[]{:S(2)}) collective-permute-start(bf16[192,384]{1,0:T(8,128)(2,1)S(1)} %get-tuple-element.148), channel_id=1, source_target_pairs={{0,12},{2,14},{4,0},{6,2},{8,4},{10,6},{12,8},{14,10},{1,13},{3,15... | collective-permute-start | bytes 442376 | tf_op jit(solution)/shard_map/ppermute | solution.py:99
  176.0 15.3 %collective-permute-start.43 = (bf16[768,384]{1,0:T(8,128)(2,1)S(1)}, bf16[768,384]{1,0:T(8,128)(2,1)S(1)}, u32[]{:S(2)}, u32[]{:S(2)}) collective-permute-start(bf16[768,384]{1,0:T(8,128)(2,1)S(1)} %constant_dynamic-update-slice_fusion.7), channel_id=1, source_target_pairs={{0,2},{2,0},{4,6},{6,4},{8,10},{10,8},{12,14},{14,12},{1,3},{3,1},... | collective-permute-start | bytes 1769480 | tf_op jit(solution)/shard_map/ppermute | solution.py:99
  176.6 15.7 %collective-permute-start.25 = (bf16[512,384]{1,0:T(8,128)(2,1)S(1)}, bf16[512,384]{1,0:T(8,128)(2,1)S(1)}, u32[]{:S(2)}, u32[]{:S(2)}) collective-permute-start(bf16[512,384]{1,0:T(8,128)(2,1)S(1)} %copy-done.20), channel_id=1, source_target_pairs={{0,1},{1,0},{2,3},{3,2},{4,5},{5,4},{6,7},{7,6},{8,9},{9,8},{10,11... | collective-permute-start | bytes 1179656 | tf_op jit(solution)/shard_map/ppermute | solution.py:42
  176.7 15.6 %collective-permute-start.27 = (bf16[512,384]{1,0:T(8,128)(2,1)S(1)}, bf16[512,384]{1,0:T(8,128)(2,1)S(1)}, u32[]{:S(2)}, u32[]{:S(2)}) collective-permute-start(bf16[512,384]{1,0:T(8,128)(2,1)S(1)} %add_convert_fusion.4), channel_id=1, source_target_pairs={{0,12},{2,6},{4,0},{6,10},{8,4},{10,14},{12,8},{14,2},{1,13},{3,7}... | collective-permute-start | bytes 1179656 | tf_op jit(solution)/shard_map/ppermute | solution.py:42
  191.4 23.8 %collective-permute-start.44 = (bf16[1536,384]{1,0:T(8,128)(2,1)S(1)}, bf16[1536,384]{1,0:T(8,128)(2,1)S(1)}, u32[]{:S(2)}, u32[]{:S(2)}) collective-permute-start(bf16[1536,384]{1,0:T(8,128)(2,1)S(1)} %constant_dynamic-update-slice_fusion.5.mine_ref), channel_id=1, source_target_pairs={{0,1},{1,0},{2,3},{3,2},{4,5},{5,4},{6,7},{7,6},{8,9},{9,8},{10,11... | collective-permute-start | bytes 3538952 | tf_op jit(solution)/shard_map/ppermute | solution.py:42
  191.5 12.0 %collective-permute-start.34 = (bf16[512,384]{1,0:T(8,128)(2,1)S(1)}, bf16[512,384]{1,0:T(8,128)(2,1)S(1)}, u32[]{:S(2)}, u32[]{:S(2)}) collective-permute-start(bf16[512,384]{1,0:T(8,128)(2,1)S(1)} %add_convert_fusion.2), channel_id=1, source_target_pairs={{0,2},{2,0},{4,6},{6,4},{8,10},{10,8},{12,14},{14,12},{1,3},{3,1},... | collective-permute-start | bytes 1179656 | tf_op jit(solution)/shard_map/ppermute | solution.py:42
  192.1 15.2 %collective-permute-start.29 = (bf16[512,384]{1,0:T(8,128)(2,1)S(1)}, bf16[512,384]{1,0:T(8,128)(2,1)S(1)}, u32[]{:S(2)}, u32[]{:S(2)}) collective-permute-start(bf16[512,384]{1,0:T(8,128)(2,1)S(1)} %copy-done.19), channel_id=1, source_target_pairs={{0,1},{1,0},{2,3},{3,2},{4,5},{5,4},{6,7},{7,6},{8,9},{9,8},{10,11... | collective-permute-start | bytes 1179656 | tf_op jit(solution)/shard_map/ppermute | solution.py:42
  192.5 19.0 %collective-permute-start.28 = (bf16[512,384]{1,0:T(8,128)(2,1)S(1)}, bf16[512,384]{1,0:T(8,128)(2,1)S(1)}, u32[]{:S(2)}, u32[]{:S(2)}) collective-permute-start(bf16[512,384]{1,0:T(8,128)(2,1)S(1)} %add_convert_fusion.3), channel_id=1, source_target_pairs={{0,2},{2,0},{4,6},{6,4},{8,10},{10,8},{12,14},{14,12},{1,3},{3,1},... | collective-permute-start | bytes 1179656 | tf_op jit(solution)/shard_map/ppermute | solution.py:42
  (46 other events, 277.3 us)

commit v4 on v3

--- a/solution.py
+++ b/solution.py
@@ -226,7 +226,8 @@
 def second_kernel(
     lat_ref, na_ref, nb_ref, row_ref, left_ref, right_ref, dleft_ref, dright_ref,
     w_all, wo_all, cot_ref,
-    dq_ref, dk_ref, dv_ref, mixed_s, dkh_ref, dvh_ref, halo_s, brow_ref, bleft_ref, bright_ref,
+    dn_ref, dw_ref, brow_ref, bleft_ref, bright_ref,
+    dq_ref, dk_ref, dv_ref, mixed_s, dkh_ref, dvh_ref, halo_s,
     q_s, k_s, v_s, kc_s, vc_s, dk_s, dv_s, dkc_s, dvc_s, do_s, mask_s, normal_s,
 ):
     points, width = cot_ref.shape
@@ -332,23 +333,13 @@
     for ref, at in ((bleft_ref, 32), (bright_ref, 64)):
         ref[0:32, :] = back[at : at + 32]
         ref[32:48, :] = back[CORNER:HALO]
-
-
-def second_weights_kernel(
-    na_ref, nb_ref, halo_ref, dq_ref, dk_ref, dv_ref, mixed_ref, dkh_ref, dvh_ref,
-    w_all, cot_ref, dn_ref, dw_ref, normal_s,
-):
-    points, width = cot_ref.shape
-    normal_s[0 : points // 2, :] = na_ref[...]
-    normal_s[points // 2 : points, :] = nb_ref[...]
-    normal, halo = normal_s[...], halo_ref[...]
     wq, wk, wv = (w_all[1, :, i * width : (i + 1) * width] for i in range(3))
     dw_ref[0:width, :] = tn(dq_ref[...], normal).astype(BF16)
     dw_ref[width : 2 * width, :] = (tn(dk_ref[...], normal) + tn(dkh_ref[...], halo)).astype(BF16)
     dw_ref[2 * width : 3 * width, :] = (
         tn(dv_ref[...], normal) + tn(dvh_ref[...], halo)
     ).astype(BF16)
-    dw_ref[3 * width : 4 * width, :] = tn(mixed_ref[...], cot_ref[...].astype(BF16)).astype(BF16)
+    dw_ref[3 * width : 4 * width, :] = tn(mixed_s[...], cot).astype(BF16)
     dn_ref[...] = nt(dq_ref[...], wq) + nt(dk_ref[...], wk) + nt(dv_ref[...], wv)
 
 
@@ -515,7 +506,6 @@
     tokens = tokens.reshape(points, width)
     cot = cotangent.reshape(points, width)
     part = struct((size, width), BF16)
-    every = struct((points, width), BF16)
     gain_spec = fixed((2, width))
     wt_spec, wo_spec = layer_spec(0, 3 * width, width), layer_spec(0, width, width)
 
@@ -593,18 +583,21 @@
     from_l, from_r = from_left(right), from_right(left)
     ext = points + 64
     halo_cols = HALO - 32
-    halo_struct = struct((HALO, width), BF16)
-    dq1, dk1, dv1, mixed1, dkh, dvh, halo, brow, bleft, bright = call(
+    every, halo_struct = pltpu.VMEM((points, width), BF16), pltpu.VMEM((HALO, width), BF16)
+    dn1, dw1, brow, bleft, bright = call(
         second_kernel,
         (
-            every, every, every, every, halo_struct, halo_struct, halo_struct,
+            struct((points, width), F32),
+            struct((4 * width, width), BF16),
             struct((32, width), BF16),
             struct((48, width), BF16),
             struct((48, width), BF16),
         ),
         in_specs=[scalar()] + [whole()] * 10,
-        out_specs=(whole(),) * 10,
+        out_specs=(whole(),) * 5,
         scratch=[
+            *[every] * 4,
+            *[halo_struct] * 3,
             pltpu.VMEM((points, width), BF16),
             pltpu.VMEM((ext, width), BF16),
             pltpu.VMEM((ext, width), BF16),
@@ -618,27 +611,15 @@
             pltpu.VMEM((192, 256), F32),
             pltpu.VMEM((points, width), BF16),
         ],
-        us=17,
+        us=22,
     )(
         lat, kept[0][1], kept[1][1], lat_swap(row), from_l, from_r, lat_swap(from_l),
         lat_swap(from_r), query_key_value_weight, output_weight, cot,
     )
 
-    dn1, dw1 = call(
-        second_weights_kernel,
-        (struct((points, width), F32), struct((4 * width, width), BF16)),
-        in_specs=[whole()] * 11,
-        out_specs=(whole(),) * 2,
-        scratch=[pltpu.VMEM((points, width), BF16)],
-        us=5,
-    )(
-        kept[0][1], kept[1][1], halo, dq1, dk1, dv1, mixed1, dkh, dvh,
-        query_key_value_weight, cot,
-    )
-
-    from_l, from_r = from_left(bright), from_right(bleft)
+    from_l, from_r, brow = from_left(bright), from_right(bleft), lat_swap(brow)
     packs = jnp.concatenate(
-        [lat_swap(brow), from_l, from_r, lat_swap(from_l), lat_swap(from_r)], 0
+        [brow, from_l, from_r, lat_swap(from_l), lat_swap(from_r)], 0
     )
     stages = lon_factors()
     sum1 = halves_summed(dw1)
@@ -692,24 +673,34 @@
             weights, sum1, d1, d2, d3 = lax.optimization_barrier((weights, sum1, d1, d2, d3))
             for stage in stages[1:]:
                 sum1 = stage_summed(sum1, stage)
-        d2 = plus(d2, lon_backward(d3))
-        if c == 0:
-            held = d2
-        backs.append((dh1, d0, d1, d2))
-
-    weights, sum1, held = lax.optimization_barrier((weights, sum1, held))
-    backs[0] = backs[0][:3] + (held,)
+            d2 = plus(d2, lon_backward(d3))
+        backs.append((dh1, d0, d1, d2, d3))
+
+    d2_0, (d1_1, d2_1, d3_1) = backs[0][3], backs[1][2:]
     sum0 = halves_summed(weights)
-    for stage in stages:
+    sum0, sum1, d2_0, d1_1, d2_1, d3_1 = lax.optimization_barrier(
+        (sum0, sum1, d2_0, d1_1, d2_1, d3_1)
+    )
+    back_1 = lon_backward(d3_1)
+    sum0 = stage_summed(sum0, stages[0])
+    sum0, d2_0, back_1 = lax.optimization_barrier((sum0, d2_0, back_1))
+    far_0 = lon_swap(d2_0)
+    d2_1 = plus(d2_1, back_1)
+    for stage in stages[1:]:
         sum0 = stage_summed(sum0, stage)
+    sum0, d2_1, far_0 = lax.optimization_barrier((sum0, d2_1, far_0))
+    far_1 = lon_swap(d2_1)
     sums = jnp.concatenate([sum0, sum1], 0)
-    for stage in stages[::-1]:
+    for stage in stages[:0:-1]:
         sums = spread(sums, *stage)
+    sums, far_1 = chained(sums, far_1)
+    sums = spread(sums, *stages[0])
     other = lat_swap(sums)
+    ends = [(*backs[0][:3], far_0), (*backs[1][:2], d1_1, far_1)]
 
     grad_tokens = None
     for c in range(CHUNKS):
-        dh1, d0, d1, d2 = backs[c]
+        dh1, d0, near, far = ends[c]
         extra = [] if grad_tokens is None else [grad_tokens]
         kernel = functools.partial(last_kernel, firsts[c])
         grad_tokens = call(
@@ -722,7 +713,7 @@
             out_specs=token_spec(small, width, firsts[c]),
             aliases={7: 0} if extra else {},
             us=4,
-        )(starts[c], visible, norm_gain_table, dh1, d0, lon_swap(d2), d1, *extra)
+        )(starts[c], visible, norm_gain_table, dh1, d0, far, near, *extra)
 
     factor = (points * lat_count * lon_count) ** (-0.5)
     g_qkv, g_out, g_gain = call(

time: 222 us -> 208 us (0.937)
  waiting for transfers between devices: 75.3 us -> 64.2 us
  Pallas kernels: 89.2 us -> 84.8 us
    ppermute x33, waiting for transfers between devices: 42.2 us -> 36.3 us  [permuted(): lax.ppermute(value, axis, [(i, target(i) % count) for i in range(count)])]
    pallas_call x2 -> x1, Pallas kernels: 27.6 us -> 22.9 us  [local(): call(second_kernel, (struct((points, width), F32), struct((4 * width, wid...]
    ppermute x4, waiting for transfers between devices: 18.8 us -> 16.1 us  [spread(): got = lax.ppermute(value, 'lon', pairs)]
    ppermute x4, starting transfers between devices: 4.91 us -> 7.36 us  [spread(): got = lax.ppermute(value, 'lon', pairs)]
    ppermute x8, waiting for transfers between devices: 14.3 us -> 11.9 us  [exchanged(): moved.append(lax.ppermute(parts(lax.rem(digit + d, factor)), 'lon', pairs))]
    unnamed x71 -> x68, local copies, waits for them, and re-layouts: 7.77 us -> 5.8 us
  transfers between devices with their start and end apart: 45 -> 45, of which waited for: 22 -> 22; matrix products, arithmetic and copies ran while one was open for 1% -> 2% of each run, Pallas kernels for 20% -> 22%
where the time goes in v4:
time: 208 us; the launch traced here: 207 us
  Pallas kernels  84.8 us (41%)
  waiting for transfers between devices  64.2 us (31%)
  starting transfers between devices  46.7 us (22%)
  local copies, waits for them, and re-layouts  8.89 us (4%)
    ppermute x33, waiting for transfers between devices, permuted(): lax.ppermute(value, axis, [(i, target(i) % count) for i in range(count)])  36.3 us
    ppermute x33, starting transfers between devices, permuted(): lax.ppermute(value, axis, [(i, target(i) % count) for i in range(count)])  30.5 us
    pallas_call x2, Pallas kernels, local(): call(kernel, (struct((size, width), F32), struct((size, width), F32), *[p...  27.5 us
    pallas_call x1, Pallas kernels, local(): call(second_kernel, (struct((points, width), F32), struct((4 * width, wid...  22.9 us
    pallas_call x2, Pallas kernels, local(): call(kernel if packs else functools.partial(without, kernel, 8, 3), (stru...  17 us
    ppermute x4, waiting for transfers between devices, spread(): got = lax.ppermute(value, 'lon', pairs)  16.1 us
    ppermute x8, waiting for transfers between devices, exchanged(): moved.append(lax.ppermute(parts(lax.rem(digit + d, factor)), 'lon', pairs))  11.9 us
    ppermute x8, starting transfers between devices, exchanged(): moved.append(lax.ppermute(parts(lax.rem(digit + d, factor)), 'lon', pairs))  8.88 us
  transfers between devices with their start and end apart: 45, of which 22 were waited for; matrix products, arithmetic and copies ran while one was open for 2% of the time, Pallas kernels for 22%

profile of v4, /device:TPU:0, one launch (start us, length us, event | category | flops | bytes accessed | tf_op | source)
XLA Modules:
  0.0 206.9 jit_solution(12225155944961617734)
XLA Ops:
  0.6 2.6 %shard_map.103 = (bf16[512,384]{1,0:T(8,128)(2,1)}, bf16[512,384]{1,0:T(8,128)(2,1)}) custom-call(bf16[1024,384]{1,0:T(8,128)(2,1)} %bitcast.13, s32[32,32]{1,0:T(8,128)} %vis_ref.5, bf16[384]{0:T(512)(128)(2,1)} %mask_ref.3, f32[2,384]{1,0:T(2,128)} %gain_ref.11), custom_call_target="tpu_custom_call" | custom-call | flops 1600000000 | bytes 2000000 | tf_op jit(solution)/shard_map/pallas_call | solution.py:515
  3.2 3.0 %collective-permute-start = (bf16[512,384]{1,0:T(8,128)(2,1)}, bf16[512,384]{1,0:T(8,128)(2,1)S(1)}, u32[]{:S(2)}, u32[]{:S(2)}) collective-permute-start(bf16[512,384]{1,0:T(8,128)(2,1)} %get-tuple-element.79.refs_1_), channel_id=1, source_target_pairs={{0,2},{2,0},{4,6},{6,4},{8,10},{10,8},{12,14},{14,12},{1,3},{3,1},... | collective-permute-start | bytes 1179656 | tf_op jit(solution)/shard_map/ppermute | solution.py:42
  6.2 2.7 %shard_map.102 = (bf16[512,384]{1,0:T(8,128)(2,1)}, bf16[512,384]{1,0:T(8,128)(2,1)}) custom-call(bf16[1024,384]{1,0:T(8,128)(2,1)} %bitcast.14, s32[32,32]{1,0:T(8,128)} %vis_ref.5, bf16[384]{0:T(512)(128)(2,1)} %mask_ref.3, f32[2,384]{1,0:T(2,128)} %gain_ref.11), custom_call_target="tpu_custom_call" | custom-call | flops 1600000000 | bytes 2000000 | tf_op jit(solution)/shard_map/pallas_call | solution.py:515
  8.9 6.7 %collective-permute-done.refs_3_ = bf16[512,384]{1,0:T(8,128)(2,1)S(1)} collective-permute-done((bf16[512,384]{1,0:T(8,128)(2,1)}, bf16[512,384]{1,0:T(8,128)(2,1)S(1)}, u32[]{:S(2)}, u32[]{:S(2)}) %collective-permute-start) | collective-permute-done | bytes 393248 | tf_op jit(solution)/shard_map/ppermute | solution.py:42
  17.3 3.5 %collective-permute-start.2 = (bf16[512,384]{1,0:T(8,128)(2,1)}, bf16[512,384]{1,0:T(8,128)(2,1)S(1)}, u32[]{:S(2)}, u32[]{:S(2)}) collective-permute-start(bf16[512,384]{1,0:T(8,128)(2,1)} %get-tuple-element.80.n0), channel_id=1, source_target_pairs={{0,2},{2,0},{4,6},{6,4},{8,10},{10,8},{12,14},{14,12},{1,3},{3,1},... | collective-permute-start | bytes 1179656 | tf_op jit(solution)/shard_map/ppermute | solution.py:42
  21.4 6.4 %collective-permute-done.5.refs_4_ = bf16[512,384]{1,0:T(8,128)(2,1)} collective-permute-done((bf16[512,384]{1,0:T(8,128)(2,1)S(1)}, bf16[512,384]{1,0:T(8,128)(2,1)}, u32[]{:S(2)}, u32[]{:S(2)}) %collective-permute-start.5) | collective-permute-done | bytes 393248 | tf_op jit(solution)/shard_map/ppermute | solution.py:42
  27.8 2.3 %copy.12 = bf16[2,384,1152]{1,2,0:T(8,128)(2,1)} copy(bf16[2,384,1152]{2,1,0:T(8,128)(2,1)S(1)} %copy-done) | data formatting | bytes 3538944 | tf_op args[4]
  30.7 8.5 %shard_map.104 = (bf16[384,512]{1,0:T(8,128)(2,1)}, bf16[6,768,512]{2,1,0:T(8,128)(2,1)}, f32[6,8,512]{2,1,0:T(8,128)}, bf16[384,512]{1,0:T(8,128)(2,1)}, bf16[5...) custom-call(s32[1]{0:T(128)} %bitcast.1.refs_0_.lat_ref, ...), custom_call_target="tpu_custom_call" | custom-call | flops 6400000000 | bytes 8000000 | tf_op jit(solution)/shard_map/pallas_call | solution.py:552
  39.2 4.2 %collective-permute-done.3.n3 = bf16[512,384]{1,0:T(8,128)(2,1)S(1)} collective-permute-done((bf16[512,384]{1,0:T(8,128)(2,1)S(1)}, bf16[512,384]{1,0:T(8,128)(2,1)S(1)}, u32[]{:S(2)}, u32[]{:S(2)}) %collective-permute-start.3) | collective-permute-done | bytes 393248 | tf_op jit(solution)/shard_map/ppermute | solution.py:42
  45.9 8.5 %shard_map.105 = (bf16[384,512]{1,0:T(8,128)(2,1)}, bf16[6,768,512]{2,1,0:T(8,128)(2,1)}, f32[6,8,512]{2,1,0:T(8,128)}, bf16[384,512]{1,0:T(8,128)(2,1)}, bf16[5...) custom-call(s32[1]{0:T(128)} %bitcast.1.refs_0_.lat_ref, ...), custom_call_target="tpu_custom_call" | custom-call | flops 6400000000 | bytes 8000000 | tf_op jit(solution)/shard_map/pallas_call | solution.py:552
  55.3 3.9 %collective-permute-start.12 = (bf16[32,384]{1,0:T(8,128)(2,1)}, bf16[32,384]{1,0:T(8,128)(2,1)S(1)}, u32[]{:S(2)}, u32[]{:S(2)}) collective-permute-start(bf16[32,384]{1,0:T(8,128)(2,1)} %get-tuple-element.99), channel_id=1, source_target_pairs={{0,14},{2,0},{4,2},{6,4},{8,6},{10,8},{12,10},{14,12},{1,15},{3,1}... | collective-permute-start | bytes 73736 | tf_op jit(solution)/shard_map/ppermute | solution.py:42
  59.3 2.0 collective-permute-done.11.left_ref
  63.2 22.9 %shard_map.106 = (f32[1024,384]{1,0:T(8,128)}, bf16[1536,384]{1,0:T(8,128)(2,1)}, bf16[32,384]{1,0:T(8,128)(2,1)}, bf16[48,384]{1,0:T(8,128)(2,1)}, bf16[48,384]{1,0:T(8,128)(2,1)}) custom-call(s32[1]{0:T(128)} %bitcast.1.refs_0_.lat_ref, bf16[512,384]{1,0:T(8,128)(2,1)} %get-tuple-element.95.na_ref, bf16[512,384]{1,0:T(8,128)(2,1)} %get-tuple-element.96.nb_ref, ...), custom_call_target="tpu_custom_call" | custom-call | flops 17600000000 | bytes 22000000 | tf_op jit(solution)/shard_map/pallas_call | solution.py:587
  88.0 4.7 %collective-permute-start.17 = (bf16[48,384]{1,0:T(8,128)(2,1)S(1)}, bf16[48,384]{1,0:T(8,128)(2,1)S(1)}, u32[]{:S(2)}, u32[]{:S(2)}) collective-permute-start(bf16[48,384]{1,0:T(8,128)(2,1)S(1)} %copy-done.25), channel_id=1, source_target_pairs={{0,14},{2,0},{4,2},{6,4},{8,6},{10,8},{12,10},{14,12},{1,15},{3,1}... | collective-permute-start | bytes 110600 | tf_op jit(solution)/shard_map/ppermute | solution.py:42
  92.7 2.1 %collective-permute-done.16 = bf16[48,384]{1,0:T(8,128)(2,1)S(1)} collective-permute-done((bf16[48,384]{1,0:T(8,128)(2,1)}, bf16[48,384]{1,0:T(8,128)(2,1)S(1)}, u32[]{:S(2)}, u32[]{:S(2)}) %collective-permute-start.16) | collective-permute-done | bytes 36896 | tf_op jit(solution)/shard_map/ppermute | solution.py:42
  96.9 13.5 %shard_map.107 = (f32[512,384]{1,0:T(8,128)}, f32[512,384]{1,0:T(8,128)}, bf16[512,384]{1,0:T(8,128)(2,1)}, bf16[512,384]{1,0:T(8,128)(2,1)}, bf16[512,384]{1,0:...) custom-call(s32[1]{0:T(128)} %bitcast.1.refs_0_.lat_ref, ...), custom_call_target="tpu_custom_call" | custom-call | flops 10400000000 | bytes 13000000 | tf_op jit(solution)/shard_map/pallas_call | solution.py:640
  113.8 5.0 %collective-permute-start.28 = (bf16[96,384]{1,0:T(8,128)(2,1)S(1)}, bf16[96,384]{1,0:T(8,128)(2,1)S(1)}, u32[]{:S(2)}, u32[]{:S(2)}) collective-permute-start(bf16[96,384]{1,0:T(8,128)(2,1)S(1)} %get-tuple-element.154), channel_id=1, source_target_pairs={{0,12},{2,14},{4,0},{6,2},{8,4},{10,6},{12,8},{14,10},{1,13},{3,15... | collective-permute-start | bytes 221192 | tf_op jit(solution)/shard_map/ppermute | solution.py:79
  119.4 3.2 %collective-permute-start.29 = (bf16[512,384]{1,0:T(8,128)(2,1)S(1)}, bf16[512,384]{1,0:T(8,128)(2,1)S(1)}, u32[]{:S(2)}, u32[]{:S(2)}) collective-permute-start(bf16[512,384]{1,0:T(8,128)(2,1)S(1)} %add_convert_fusion.6), channel_id=1, source_target_pairs={{0,12},{2,6},{4,0},{6,10},{8,4},{10,14},{12,8},{14,2},{1,13},{3,7}... | collective-permute-start | bytes 1179656 | tf_op jit(solution)/shard_map/ppermute | solution.py:42
  122.6 14.0 %shard_map.108 = (f32[512,384]{1,0:T(8,128)}, f32[512,384]{1,0:T(8,128)}, bf16[512,384]{1,0:T(8,128)(2,1)}, bf16[512,384]{1,0:T(8,128)(2,1)}, bf16[512,384]{1,0:...) custom-call(s32[1]{0:T(128)} %bitcast.1.refs_0_.lat_ref, ...), custom_call_target="tpu_custom_call" | custom-call | flops 10400000000 | bytes 13000000 | tf_op jit(solution)/shard_map/pallas_call | solution.py:640
  143.2 8.4 %collective-permute-done.33 = bf16[384,384]{1,0:T(8,128)(2,1)S(1)} collective-permute-done((bf16[384,384]{1,0:T(8,128)(2,1)S(1)}, bf16[384,384]{1,0:T(8,128)(2,1)S(1)}, u32[]{:S(2)}, u32[]{:S(2)}) %collective-permute-start.33) | collective-permute-done | bytes 294944 | tf_op jit(solution)/shard_map/ppermute | solution.py:79
  151.7 2.1 %collective-permute-done.34 = bf16[512,384]{1,0:T(8,128)(2,1)S(1)} collective-permute-done((bf16[512,384]{1,0:T(8,128)(2,1)S(1)}, bf16[512,384]{1,0:T(8,128)(2,1)S(1)}, u32[]{:S(2)}, u32[]{:S(2)}) %collective-permute-start.34) | collective-permute-done | bytes 393248 | tf_op jit(solution)/shard_map/ppermute | solution.py:42
  153.8 2.4 %collective-permute-start.37 = (bf16[96,384]{1,0:T(8,128)(2,1)S(1)}, bf16[96,384]{1,0:T(8,128)(2,1)S(1)}, u32[]{:S(2)}, u32[]{:S(2)}) collective-permute-start(bf16[96,384]{1,0:T(8,128)(2,1)S(1)} %get-tuple-element.151), channel_id=1, source_target_pairs={{0,12},{2,14},{4,0},{6,2},{8,4},{10,6},{12,8},{14,10},{1,13},{3,15... | collective-permute-start | bytes 221192 | tf_op jit(solution)/shard_map/ppermute | solution.py:79
  157.0 2.4 %collective-permute-start.38 = (bf16[512,384]{1,0:T(8,128)(2,1)S(1)}, bf16[512,384]{1,0:T(8,128)(2,1)S(1)}, u32[]{:S(2)}, u32[]{:S(2)}) collective-permute-start(bf16[512,384]{1,0:T(8,128)(2,1)S(1)} %add_convert_fusion.5), channel_id=1, source_target_pairs={{0,2},{2,0},{4,6},{6,4},{8,10},{10,8},{12,14},{14,12},{1,3},{3,1},... | collective-permute-start | bytes 1179656 | tf_op jit(solution)/shard_map/ppermute | solution.py:42
  159.5 3.5 %collective-permute-done.36 = bf16[96,384]{1,0:T(8,128)(2,1)S(1)} collective-permute-done((bf16[96,384]{1,0:T(8,128)(2,1)S(1)}, bf16[96,384]{1,0:T(8,128)(2,1)S(1)}, u32[]{:S(2)}, u32[]{:S(2)}) %collective-permute-start.36) | collective-permute-done | bytes 73760 | tf_op jit(solution)/shard_map/ppermute | solution.py:79
  163.0 4.1 %collective-permute-done.38.refs_5_ = bf16[512,384]{1,0:T(8,128)(2,1)S(1)} collective-permute-done((bf16[512,384]{1,0:T(8,128)(2,1)S(1)}, bf16[512,384]{1,0:T(8,128)(2,1)S(1)}, u32[]{:S(2)}, u32[]{:S(2)}) %collective-permute-start.38) | collective-permute-done | bytes 393248 | tf_op jit(solution)/shard_map/ppermute | solution.py:42
  167.1 2.2 %collective-permute-start.39 = (bf16[192,384]{1,0:T(8,128)(2,1)S(1)}, bf16[192,384]{1,0:T(8,128)(2,1)S(1)}, u32[]{:S(2)}, u32[]{:S(2)}) collective-permute-start(bf16[192,384]{1,0:T(8,128)(2,1)S(1)} %constant_dynamic-update-slice_fusion.5), channel_id=1, source_target_pairs={{0,4},{2,6},{4,8},{6,10},{8,12},{10,14},{12,0},{14,2},{1,5},{3,7},... | collective-permute-start | bytes 442376 | tf_op jit(solution)/shard_map/ppermute | solution.py:99
  170.5 2.3 %collective-permute-start.41 = (bf16[192,384]{1,0:T(8,128)(2,1)S(1)}, bf16[192,384]{1,0:T(8,128)(2,1)S(1)}, u32[]{:S(2)}, u32[]{:S(2)}) collective-permute-start(bf16[192,384]{1,0:T(8,128)(2,1)S(1)} %constant_dynamic-update-slice_fusion.5), channel_id=1, source_target_pairs={{0,12},{2,14},{4,0},{6,2},{8,4},{10,6},{12,8},{14,10},{1,13},{3,15... | collective-permute-start | bytes 442376 | tf_op jit(solution)/shard_map/ppermute | solution.py:99
  175.8 3.8 %collective-permute-done.40 = bf16[192,384]{1,0:T(8,128)(2,1)S(1)} collective-permute-done((bf16[192,384]{1,0:T(8,128)(2,1)S(1)}, bf16[192,384]{1,0:T(8,128)(2,1)S(1)}, u32[]{:S(2)}, u32[]{:S(2)}) %collective-permute-start.40) | collective-permute-done | bytes 147488 | tf_op jit(solution)/shard_map/ppermute | solution.py:99
  182.5 11.1 %collective-permute-done.43 = bf16[768,384]{1,0:T(8,128)(2,1)S(1)} collective-permute-done((bf16[768,384]{1,0:T(8,128)(2,1)S(1)}, bf16[768,384]{1,0:T(8,128)(2,1)S(1)}, u32[]{:S(2)}, u32[]{:S(2)}) %collective-permute-start.43) | collective-permute-done | bytes 589856 | tf_op jit(solution)/shard_map/ppermute | solution.py:99
  193.8 3.4 %shard_map.109.prev_ref = f32[1024,384]{1,0:T(8,128)} custom-call(bf16[512,384]{1,0:T(8,128)(2,1)} %get-tuple-element.82.refs_7_.refs_0_, s32[32,32]{1,0:T(8,128)} %vis_ref.5, f32[2,384]{1,0:T(2,128)} %gain_ref.11, f32[512,384]{1,0:T(8,128)} %get-tuple-element.142.refs_3_, f32[512,384]{1,0:T(8,128)} %get-tuple-element.143.refs_4_, ...), custom_call_target="tpu_custom_call" | custom-call | flops 3200000000 | bytes 4000000 | tf_op jit(solution)/shard_map/pallas_call | solution.py:706
  197.2 3.0 %shard_map.110 = f32[1024,384]{1,0:T(8,128)} custom-call(bf16[512,384]{1,0:T(8,128)(2,1)} %get-tuple-element.77.start_ref, s32[32,32]{1,0:T(8,128)} %vis_ref.5, f32[2,384]{1,0:T(2,128)} %gain_ref.11, f32[512,384]{1,0:T(8,128)} %get-tuple-element.119.dh_ref, f32[512,384]{1,0:T(8,128)} %get-tuple-element.120.own_ref, ...), custom_call_target="tpu_custom_call", output_to_operand_aliasing={{}: (7, {})} | custom-call | flops 3200000000 | bytes 4000000 | tf_op jit(solution)/shard_map/pallas_call | solution.py:706
  201.3 5.7 %shard_map.111 = (f32[2,384,1152]{2,1,0:T(8,128)}, f32[2,384,384]{2,1,0:T(8,128)}, f32[2,384]{1,0:T(2,128)}) custom-call(s32[1]{0:T(128)} %bitcast.1.refs_0_.lat_ref, bf16[1536,384]{1,0:T(8,128)(2,1)} %copy-done.1, bf16[1536,384]{1,0:T(8,128)(2,1)} %copy-done.9, bf16[2,1152,384]{2,1,0:T(8,128)(2,1)} %bitcast.9, f32[2,384]{1,0:T(2,128)} %gain_ref.11), custom_call_target="tpu_custom_call" | custom-call | flops 4000000000 | bytes 5000000 | tf_op jit(solution)/shard_map/pallas_call | solution.py:719
  (164 shorter events, 31.8 us)
Async XLA Ops:
  3.2 12.4 %collective-permute-start = (bf16[512,384]{1,0:T(8,128)(2,1)}, bf16[512,384]{1,0:T(8,128)(2,1)S(1)}, u32[]{:S(2)}, u32[]{:S(2)}) collective-permute-start(bf16[512,384]{1,0:T(8,128)(2,1)} %get-tuple-element.79.refs_1_), channel_id=1, source_target_pairs={{0,2},{2,0},{4,6},{6,4},{8,10},{10,8},{12,14},{14,12},{1,3},{3,1},... | collective-permute-start | bytes 1179656 | tf_op jit(solution)/shard_map/ppermute | solution.py:42
  15.6 12.2 %collective-permute-start.5 = (bf16[512,384]{1,0:T(8,128)(2,1)S(1)}, bf16[512,384]{1,0:T(8,128)(2,1)}, u32[]{:S(2)}, u32[]{:S(2)}) collective-permute-start(bf16[512,384]{1,0:T(8,128)(2,1)S(1)} %collective-permute-done.refs_3_), channel_id=1, source_target_pairs={{0,4},{2,14},{4,8},{6,2},{8,12},{10,6},{12,0},{14,10},{1,5},{3,15}... | collective-permute-start | bytes 1179656 | tf_op jit(solution)/shard_map/ppermute | solution.py:42
  17.3 13.3 %collective-permute-start.2 = (bf16[512,384]{1,0:T(8,128)(2,1)}, bf16[512,384]{1,0:T(8,128)(2,1)S(1)}, u32[]{:S(2)}, u32[]{:S(2)}) collective-permute-start(bf16[512,384]{1,0:T(8,128)(2,1)} %get-tuple-element.80.n0), channel_id=1, source_target_pairs={{0,2},{2,0},{4,6},{6,4},{8,10},{10,8},{12,14},{14,12},{1,3},{3,1},... | collective-permute-start | bytes 1179656 | tf_op jit(solution)/shard_map/ppermute | solution.py:42
  20.9 9.7 %collective-permute-start.4 = (bf16[512,384]{1,0:T(8,128)(2,1)S(1)}, bf16[512,384]{1,0:T(8,128)(2,1)}, u32[]{:S(2)}, u32[]{:S(2)}) collective-permute-start(bf16[512,384]{1,0:T(8,128)(2,1)S(1)} %copy-done.17), channel_id=1, source_target_pairs={{0,1},{1,0},{2,3},{3,2},{4,5},{5,4},{6,7},{7,6},{8,9},{9,8},{10,11... | collective-permute-start | bytes 1179656 | tf_op jit(solution)/shard_map/ppermute | solution.py:42
  20.9 9.9 %collective-permute-start.6 = (bf16[512,384]{1,0:T(8,128)(2,1)S(1)}, bf16[512,384]{1,0:T(8,128)(2,1)}, u32[]{:S(2)}, u32[]{:S(2)}) collective-permute-start(bf16[512,384]{1,0:T(8,128)(2,1)S(1)} %collective-permute-done.refs_3_), channel_id=1, source_target_pairs={{0,1},{1,0},{2,3},{3,2},{4,5},{5,4},{6,7},{7,6},{8,9},{9,8},{10,11... | collective-permute-start | bytes 1179656 | tf_op jit(solution)/shard_map/ppermute | solution.py:42
  30.1 13.4 %collective-permute-start.1 = (bf16[512,384]{1,0:T(8,128)(2,1)S(1)}, bf16[512,384]{1,0:T(8,128)(2,1)S(1)}, u32[]{:S(2)}, u32[]{:S(2)}) collective-permute-start(bf16[512,384]{1,0:T(8,128)(2,1)S(1)} %copy-done.10), channel_id=1, source_target_pairs={{0,1},{1,0},{2,3},{3,2},{4,5},{5,4},{6,7},{7,6},{8,9},{9,8},{10,11... | collective-permute-start | bytes 1179656 | tf_op jit(solution)/shard_map/ppermute | solution.py:42
  30.6 12.9 %collective-permute-start.3 = (bf16[512,384]{1,0:T(8,128)(2,1)S(1)}, bf16[512,384]{1,0:T(8,128)(2,1)S(1)}, u32[]{:S(2)}, u32[]{:S(2)}) collective-permute-start(bf16[512,384]{1,0:T(8,128)(2,1)S(1)} %collective-permute-done.2.n2), channel_id=1, source_target_pairs={{0,4},{2,14},{4,8},{6,2},{8,12},{10,6},{12,0},{14,10},{1,5},{3,15}... | collective-permute-start | bytes 1179656 | tf_op jit(solution)/shard_map/ppermute | solution.py:42
  30.6 12.9 %collective-permute-start.8 = (bf16[512,384]{1,0:T(8,128)(2,1)S(1)}, bf16[512,384]{1,0:T(8,128)(2,1)S(1)}, u32[]{:S(2)}, u32[]{:S(2)}) collective-permute-start(bf16[512,384]{1,0:T(8,128)(2,1)S(1)} %collective-permute-done.2.n2), channel_id=1, source_target_pairs={{0,1},{1,0},{2,3},{3,2},{4,5},{5,4},{6,7},{7,6},{8,9},{9,8},{10,11... | collective-permute-start | bytes 1179656 | tf_op jit(solution)/shard_map/ppermute | solution.py:42
  54.5 6.8 %collective-permute-start.11 = (bf16[32,384]{1,0:T(8,128)(2,1)}, bf16[32,384]{1,0:T(8,128)(2,1)S(1)}, u32[]{:S(2)}, u32[]{:S(2)}) collective-permute-start(bf16[32,384]{1,0:T(8,128)(2,1)} %get-tuple-element.98), channel_id=1, source_target_pairs={{0,2},{2,4},{4,6},{6,8},{8,10},{10,12},{12,14},{14,0},{1,3},{3,5},... | collective-permute-start | bytes 73736 | tf_op jit(solution)/shard_map/ppermute | solution.py:42
  55.3 5.9 %collective-permute-start.12 = (bf16[32,384]{1,0:T(8,128)(2,1)}, bf16[32,384]{1,0:T(8,128)(2,1)S(1)}, u32[]{:S(2)}, u32[]{:S(2)}) collective-permute-start(bf16[32,384]{1,0:T(8,128)(2,1)} %get-tuple-element.99), channel_id=1, source_target_pairs={{0,14},{2,0},{4,2},{6,4},{8,6},{10,8},{12,10},{14,12},{1,15},{3,1}... | collective-permute-start | bytes 73736 | tf_op jit(solution)/shard_map/ppermute | solution.py:42
  87.4 8.8 %collective-permute-start.20 = (bf16[768,384]{1,0:T(8,128)(2,1)S(1)}, bf16[768,384]{1,0:T(8,128)(2,1)S(1)}, u32[]{:S(2)}, u32[]{:S(2)}) collective-permute-start(bf16[768,384]{1,0:T(8,128)(2,1)S(1)} %constant_dynamic-slice_fusion.9), channel_id=1, source_target_pairs={{0,1},{1,0},{2,3},{3,2},{4,5},{5,4},{6,7},{7,6},{8,9},{9,8},{10,11... | collective-permute-start | bytes 1769480 | tf_op jit(solution)/shard_map/ppermute | solution.py:42
  87.8 4.9 %collective-permute-start.15 = (bf16[32,384]{1,0:T(8,128)(2,1)}, bf16[32,384]{1,0:T(8,128)(2,1)S(1)}, u32[]{:S(2)}, u32[]{:S(2)}) collective-permute-start(bf16[32,384]{1,0:T(8,128)(2,1)} %get-tuple-element.101), channel_id=1, source_target_pairs={{0,1},{1,0},{2,3},{3,2},{4,5},{5,4},{6,7},{7,6},{8,9},{9,8},{10,11... | collective-permute-start | bytes 73736 | tf_op jit(solution)/shard_map/ppermute | solution.py:42
  88.0 6.9 %collective-permute-start.16 = (bf16[48,384]{1,0:T(8,128)(2,1)}, bf16[48,384]{1,0:T(8,128)(2,1)S(1)}, u32[]{:S(2)}, u32[]{:S(2)}) collective-permute-start(bf16[48,384]{1,0:T(8,128)(2,1)} %get-tuple-element.102), channel_id=1, source_target_pairs={{0,2},{2,4},{4,6},{6,8},{8,10},{10,12},{12,14},{14,0},{1,3},{3,5},... | collective-permute-start | bytes 110600 | tf_op jit(solution)/shard_map/ppermute | solution.py:42
  88.0 6.9 %collective-permute-start.17 = (bf16[48,384]{1,0:T(8,128)(2,1)S(1)}, bf16[48,384]{1,0:T(8,128)(2,1)S(1)}, u32[]{:S(2)}, u32[]{:S(2)}) collective-permute-start(bf16[48,384]{1,0:T(8,128)(2,1)S(1)} %copy-done.25), channel_id=1, source_target_pairs={{0,14},{2,0},{4,2},{6,4},{8,6},{10,8},{12,10},{14,12},{1,15},{3,1}... | collective-permute-start | bytes 110600 | tf_op jit(solution)/shard_map/ppermute | solution.py:42
  96.9 14.5 %collective-permute-start.21 = (bf16[384,384]{1,0:T(8,128)(2,1)S(1)}, bf16[384,384]{1,0:T(8,128)(2,1)S(1)}, u32[]{:S(2)}, u32[]{:S(2)}) collective-permute-start(bf16[384,384]{1,0:T(8,128)(2,1)S(1)} %constant_dynamic-slice_fusion.8), channel_id=1, source_target_pairs={{0,2},{2,0},{4,6},{6,4},{8,10},{10,8},{12,14},{14,12},{1,3},{3,1},... | collective-permute-start | bytes 884744 | tf_op jit(solution)/shard_map/ppermute | solution.py:79
  113.8 24.1 %collective-permute-start.28 = (bf16[96,384]{1,0:T(8,128)(2,1)S(1)}, bf16[96,384]{1,0:T(8,128)(2,1)S(1)}, u32[]{:S(2)}, u32[]{:S(2)}) collective-permute-start(bf16[96,384]{1,0:T(8,128)(2,1)S(1)} %get-tuple-element.154), channel_id=1, source_target_pairs={{0,12},{2,14},{4,0},{6,2},{8,4},{10,6},{12,8},{14,10},{1,13},{3,15... | collective-permute-start | bytes 221192 | tf_op jit(solution)/shard_map/ppermute | solution.py:79
  118.7 19.7 %collective-permute-start.27 = (bf16[96,384]{1,0:T(8,128)(2,1)S(1)}, bf16[96,384]{1,0:T(8,128)(2,1)S(1)}, u32[]{:S(2)}, u32[]{:S(2)}) collective-permute-start(bf16[96,384]{1,0:T(8,128)(2,1)S(1)} %get-tuple-element.155), channel_id=1, source_target_pairs={{0,8},{2,10},{4,12},{6,14},{8,0},{10,2},{12,4},{14,6},{1,9},{3,11}... | collective-permute-start | bytes 221192 | tf_op jit(solution)/shard_map/ppermute | solution.py:79
  118.7 19.8 %collective-permute-start.26 = (bf16[96,384]{1,0:T(8,128)(2,1)S(1)}, bf16[96,384]{1,0:T(8,128)(2,1)S(1)}, u32[]{:S(2)}, u32[]{:S(2)}) collective-permute-start(bf16[96,384]{1,0:T(8,128)(2,1)S(1)} %get-tuple-element.153), channel_id=1, source_target_pairs={{0,4},{2,6},{4,8},{6,10},{8,12},{10,14},{12,0},{14,2},{1,5},{3,7},... | collective-permute-start | bytes 221192 | tf_op jit(solution)/shard_map/ppermute | solution.py:79
  119.4 19.6 %collective-permute-start.29 = (bf16[512,384]{1,0:T(8,128)(2,1)S(1)}, bf16[512,384]{1,0:T(8,128)(2,1)S(1)}, u32[]{:S(2)}, u32[]{:S(2)}) collective-permute-start(bf16[512,384]{1,0:T(8,128)(2,1)S(1)} %add_convert_fusion.6), channel_id=1, source_target_pairs={{0,12},{2,6},{4,0},{6,10},{8,4},{10,14},{12,8},{14,2},{1,13},{3,7}... | collective-permute-start | bytes 1179656 | tf_op jit(solution)/shard_map/ppermute | solution.py:42
  137.9 4.5 %collective-permute-start.30 = (bf16[512,384]{1,0:T(8,128)(2,1)S(1)}, bf16[512,384]{1,0:T(8,128)(2,1)S(1)}, u32[]{:S(2)}, u32[]{:S(2)}) collective-permute-start(bf16[512,384]{1,0:T(8,128)(2,1)S(1)} %copy-done.22), channel_id=1, source_target_pairs={{0,1},{1,0},{2,3},{3,2},{4,5},{5,4},{6,7},{7,6},{8,9},{9,8},{10,11... | collective-permute-start | bytes 1179656 | tf_op jit(solution)/shard_map/ppermute | solution.py:42
  142.5 9.1 %collective-permute-start.33 = (bf16[384,384]{1,0:T(8,128)(2,1)S(1)}, bf16[384,384]{1,0:T(8,128)(2,1)S(1)}, u32[]{:S(2)}, u32[]{:S(2)}) collective-permute-start(bf16[384,384]{1,0:T(8,128)(2,1)S(1)} %constant_dynamic-slice_fusion.3), channel_id=1, source_target_pairs={{0,2},{2,0},{4,6},{6,4},{8,10},{10,8},{12,14},{14,12},{1,3},{3,1},... | collective-permute-start | bytes 884744 | tf_op jit(solution)/shard_map/ppermute | solution.py:79
  142.6 11.2 %collective-permute-start.34 = (bf16[512,384]{1,0:T(8,128)(2,1)S(1)}, bf16[512,384]{1,0:T(8,128)(2,1)S(1)}, u32[]{:S(2)}, u32[]{:S(2)}) collective-permute-start(bf16[512,384]{1,0:T(8,128)(2,1)S(1)} %add_convert_fusion.3), channel_id=1, source_target_pairs={{0,12},{2,6},{4,0},{6,10},{8,4},{10,14},{12,8},{14,2},{1,13},{3,7}... | collective-permute-start | bytes 1179656 | tf_op jit(solution)/shard_map/ppermute | solution.py:42
  153.8 5.7 %collective-permute-start.37 = (bf16[96,384]{1,0:T(8,128)(2,1)S(1)}, bf16[96,384]{1,0:T(8,128)(2,1)S(1)}, u32[]{:S(2)}, u32[]{:S(2)}) collective-permute-start(bf16[96,384]{1,0:T(8,128)(2,1)S(1)} %get-tuple-element.151), channel_id=1, source_target_pairs={{0,12},{2,14},{4,0},{6,2},{8,4},{10,6},{12,8},{14,10},{1,13},{3,15... | collective-permute-start | bytes 221192 | tf_op jit(solution)/shard_map/ppermute | solution.py:79
  156.2 6.7 %collective-permute-start.36 = (bf16[96,384]{1,0:T(8,128)(2,1)S(1)}, bf16[96,384]{1,0:T(8,128)(2,1)S(1)}, u32[]{:S(2)}, u32[]{:S(2)}) collective-permute-start(bf16[96,384]{1,0:T(8,128)(2,1)S(1)} %get-tuple-element.152), channel_id=1, source_target_pairs={{0,8},{2,10},{4,12},{6,14},{8,0},{10,2},{12,4},{14,6},{1,9},{3,11}... | collective-permute-start | bytes 221192 | tf_op jit(solution)/shard_map/ppermute | solution.py:79
  156.2 6.7 %collective-permute-start.35 = (bf16[96,384]{1,0:T(8,128)(2,1)S(1)}, bf16[96,384]{1,0:T(8,128)(2,1)S(1)}, u32[]{:S(2)}, u32[]{:S(2)}) collective-permute-start(bf16[96,384]{1,0:T(8,128)(2,1)S(1)} %get-tuple-element.150), channel_id=1, source_target_pairs={{0,4},{2,6},{4,8},{6,10},{8,12},{10,14},{12,0},{14,2},{1,5},{3,7},... | collective-permute-start | bytes 221192 | tf_op jit(solution)/shard_map/ppermute | solution.py:79
  157.0 10.1 %collective-permute-start.38 = (bf16[512,384]{1,0:T(8,128)(2,1)S(1)}, bf16[512,384]{1,0:T(8,128)(2,1)S(1)}, u32[]{:S(2)}, u32[]{:S(2)}) collective-permute-start(bf16[512,384]{1,0:T(8,128)(2,1)S(1)} %add_convert_fusion.5), channel_id=1, source_target_pairs={{0,2},{2,0},{4,6},{6,4},{8,10},{10,8},{12,14},{14,12},{1,3},{3,1},... | collective-permute-start | bytes 1179656 | tf_op jit(solution)/shard_map/ppermute | solution.py:42
  167.1 8.7 %collective-permute-start.39 = (bf16[192,384]{1,0:T(8,128)(2,1)S(1)}, bf16[192,384]{1,0:T(8,128)(2,1)S(1)}, u32[]{:S(2)}, u32[]{:S(2)}) collective-permute-start(bf16[192,384]{1,0:T(8,128)(2,1)S(1)} %constant_dynamic-update-slice_fusion.5), channel_id=1, source_target_pairs={{0,4},{2,6},{4,8},{6,10},{8,12},{10,14},{12,0},{14,2},{1,5},{3,7},... | collective-permute-start | bytes 442376 | tf_op jit(solution)/shard_map/ppermute | solution.py:99
  169.3 10.3 %collective-permute-start.40 = (bf16[192,384]{1,0:T(8,128)(2,1)S(1)}, bf16[192,384]{1,0:T(8,128)(2,1)S(1)}, u32[]{:S(2)}, u32[]{:S(2)}) collective-permute-start(bf16[192,384]{1,0:T(8,128)(2,1)S(1)} %constant_dynamic-update-slice_fusion.5), channel_id=1, source_target_pairs={{0,8},{2,10},{4,12},{6,14},{8,0},{10,2},{12,4},{14,6},{1,9},{3,11}... | collective-permute-start | bytes 442376 | tf_op jit(solution)/shard_map/ppermute | solution.py:99
  170.5 9.1 %collective-permute-start.41 = (bf16[192,384]{1,0:T(8,128)(2,1)S(1)}, bf16[192,384]{1,0:T(8,128)(2,1)S(1)}, u32[]{:S(2)}, u32[]{:S(2)}) collective-permute-start(bf16[192,384]{1,0:T(8,128)(2,1)S(1)} %constant_dynamic-update-slice_fusion.5), channel_id=1, source_target_pairs={{0,12},{2,14},{4,0},{6,2},{8,4},{10,6},{12,8},{14,10},{1,13},{3,15... | collective-permute-start | bytes 442376 | tf_op jit(solution)/shard_map/ppermute | solution.py:99
  172.7 7.8 %collective-permute-start.42 = (bf16[512,384]{1,0:T(8,128)(2,1)S(1)}, bf16[512,384]{1,0:T(8,128)(2,1)S(1)}, u32[]{:S(2)}, u32[]{:S(2)}) collective-permute-start(bf16[512,384]{1,0:T(8,128)(2,1)S(1)} %add_convert_fusion.2), channel_id=1, source_target_pairs={{0,2},{2,0},{4,6},{6,4},{8,10},{10,8},{12,14},{14,12},{1,3},{3,1},... | collective-permute-start | bytes 1179656 | tf_op jit(solution)/shard_map/ppermute | solution.py:42
  180.5 13.1 %collective-permute-start.43 = (bf16[768,384]{1,0:T(8,128)(2,1)S(1)}, bf16[768,384]{1,0:T(8,128)(2,1)S(1)}, u32[]{:S(2)}, u32[]{:S(2)}) collective-permute-start(bf16[768,384]{1,0:T(8,128)(2,1)S(1)} %constant_dynamic-update-slice_fusion.9), channel_id=1, source_target_pairs={{0,2},{2,0},{4,6},{6,4},{8,10},{10,8},{12,14},{14,12},{1,3},{3,1},... | collective-permute-start | bytes 1769480 | tf_op jit(solution)/shard_map/ppermute | solution.py:99
  193.7 6.5 %collective-permute-start.44 = (bf16[1536,384]{1,0:T(8,128)(2,1)S(1)}, bf16[1536,384]{1,0:T(8,128)(2,1)S(1)}, u32[]{:S(2)}, u32[]{:S(2)}) collective-permute-start(bf16[1536,384]{1,0:T(8,128)(2,1)S(1)} %constant_dynamic-update-slice_fusion.7.mine_ref), channel_id=1, source_target_pairs={{0,1},{1,0},{2,3},{3,2},{4,5},{5,4},{6,7},{7,6},{8,9},{9,8},{10,11... | collective-permute-start | bytes 3538952 | tf_op jit(solution)/shard_map/ppermute | solution.py:42
  (44 other events, 197.5 us)

commit v5 on v4

--- a/solution.py
+++ b/solution.py
@@ -11,7 +11,7 @@
 EPS = 1e-05
 F32 = jnp.float32
 BF16 = jnp.bfloat16
-VMEM_BYTES = 56 * 1024 * 1024
+VMEM_BYTES = 26 * 1024 * 1024
 HALO = 112
 CORNER = 96
 RETURNED = 224
@@ -76,7 +76,7 @@
     moved = []
     for d in range(1, factor):
         pairs = [(i, shifted(i, axis_stride, factor, d)) for i in range(count)]
-        moved.append(lax.ppermute(parts(lax.rem(digit + d, factor)), "lon", pairs))
+        moved.append(lax.ppermute(parts(digit ^ d), "lon", pairs))
     total = parts(digit).astype(F32)
     for piece in moved:
         total = total + piece.astype(F32)
@@ -85,7 +85,7 @@
 
 def shifted(i, stride, factor, d):
     digit = (i // stride) % factor
-    return i + ((digit + d) % factor - digit) * stride
+    return i + ((digit ^ d) - digit) * stride
 
 
 def spread(value, axis_stride, factor):
@@ -97,7 +97,7 @@
     for d in range(1, factor):
         pairs = [(i, shifted(i, axis_stride, factor, d)) for i in range(count)]
         got = lax.ppermute(value, "lon", pairs)
-        at = lax.rem(digit - d + factor, factor) * rows
+        at = (digit ^ d) * rows
         full = lax.dynamic_update_slice(full, got, (at, 0))
     return full
 
@@ -490,6 +490,139 @@
 
 
 CHUNKS = 2
+FORWARD_TILE = 256
+BACKWARD_TILE = 256
+
+
+def run_first(first, lat, blocks, start, packs, wt, output_weight, norm_gain_table):
+    size, width = start.shape
+    tile = min(FORWARD_TILE, size)
+    struct = jax.ShapeDtypeStruct
+    part = struct((size, width), BF16)
+    tok_spec = token_spec(tile, width)
+    feat_spec = pl.BlockSpec((width, tile), lambda i: (0, i))
+    kernel = functools.partial(first_kernel, first)
+    return call(
+        kernel if packs else functools.partial(without, kernel, 8, 3),
+        (
+            struct((width, size), BF16),
+            struct((6, 2 * width, size), BF16),
+            struct((6, 8, size), F32),
+            struct((width, size), BF16),
+            part,
+            part,
+            *[struct((32, width), BF16)] * 3,
+        ),
+        grid=(size // tile,),
+        in_specs=[scalar()]
+        + [tok_spec] * 7
+        + [fixed((32, width))] * len(packs)
+        + [
+            layer_spec(0, 3 * width, width),
+            layer_spec(0, width, width),
+            fixed((2, width)),
+        ],
+        out_specs=(
+            feat_spec,
+            pl.BlockSpec((6, 2 * width, tile), lambda i: (0, 0, i)),
+            pl.BlockSpec((6, 8, tile), lambda i: (0, 0, i)),
+            feat_spec,
+            tok_spec,
+            tok_spec,
+            *[fixed((32, width))] * 3,
+        ),
+        scratch=[pltpu.VMEM((6, 8, tile), F32), pltpu.VMEM((96, width), F32)],
+        us=8,
+    )(lat, *blocks, start, *packs, wt, output_weight, norm_gain_table)
+
+
+def run_second(lat, normals, halos, query_key_value_weight, output_weight, cot):
+    points, width = cot.shape
+    struct = jax.ShapeDtypeStruct
+    ext, halo_cols = points + 64, HALO - 32
+    every, halo = pltpu.VMEM((points, width), BF16), pltpu.VMEM((HALO, width), BF16)
+    return call(
+        second_kernel,
+        (
+            struct((points, width), F32),
+            struct((4 * width, width), BF16),
+            struct((32, width), BF16),
+            struct((48, width), BF16),
+            struct((48, width), BF16),
+        ),
+        in_specs=[scalar()] + [whole()] * 10,
+        out_specs=(whole(),) * 5,
+        scratch=[
+            *[every] * 4,
+            *[halo] * 3,
+            every,
+            pltpu.VMEM((ext, width), BF16),
+            pltpu.VMEM((ext, width), BF16),
+            pltpu.VMEM((halo_cols, width), BF16),
+            pltpu.VMEM((halo_cols, width), BF16),
+            pltpu.VMEM((ext, width), F32),
+            pltpu.VMEM((ext, width), F32),
+            pltpu.VMEM((halo_cols, width), F32),
+            pltpu.VMEM((halo_cols, width), F32),
+            every,
+            pltpu.VMEM((192, 256), F32),
+            every,
+        ],
+        us=22,
+    )(lat, *normals, *halos, query_key_value_weight, output_weight, cot)
+
+
+def run_third(
+    first, lat, blocks, kept, dn1, cot, packs, wt, output_weight, norm_gain_table, weights, final
+):
+    q0, kv0, p0, mixed0, h1 = kept
+    size, width = h1.shape
+    tile = min(BACKWARD_TILE, size)
+    struct = jax.ShapeDtypeStruct
+    part = struct((size, width), BF16)
+    tok_spec = token_spec(tile, width)
+    feat_spec = pl.BlockSpec((width, tile), lambda i: (0, i))
+    kernel = functools.partial(third_kernel, first)
+    extra = [] if weights is None else [weights]
+    return call(
+        kernel if extra else functools.partial(without, kernel, 18, 1),
+        (
+            struct((size, width), F32),
+            struct((size, width), F32),
+            *[part] * 5,
+            struct((4 * width, width), BF16 if final else F32),
+        ),
+        grid=(size // tile,),
+        in_specs=[scalar()]
+        + [tok_spec] * 6
+        + [
+            feat_spec,
+            pl.BlockSpec((6, 2 * width, tile), lambda i: (0, 0, i)),
+            pl.BlockSpec((6, 8, tile), lambda i: (0, 0, i)),
+            feat_spec,
+            tok_spec,
+        ]
+        + [token_spec(tile, width, first)] * 2
+        + [
+            fixed((RETURNED, width)),
+            layer_spec(0, 3 * width, width),
+            layer_spec(0, width, width),
+            fixed((2, width)),
+        ]
+        + [fixed((4 * width, width))] * len(extra),
+        out_specs=(*[tok_spec] * 7, fixed((4 * width, width))),
+        scratch=[
+            pltpu.VMEM((4 * width, width), F32),
+            pltpu.VMEM((width, tile), F32),
+            pltpu.VMEM((6, 2 * width, tile), BF16),
+            pltpu.VMEM((width, tile), BF16),
+            pltpu.VMEM((8, tile), F32),
+        ],
+        us=13,
+    )(
+        lat, *blocks, q0, kv0, p0, mixed0, h1, dn1, cot, packs, wt, output_weight,
+        norm_gain_table, *extra,
+    )
 
 
 def local(
@@ -539,39 +672,12 @@
 
     blocks = [blocks_of(normals[0], near0, swapped0, beyond0), None]
 
-    tile = 256
-    steps = size // tile
-    tok_spec = token_spec(tile, width)
-    feat_spec = pl.BlockSpec((width, tile), lambda i: (0, i))
-    kv_spec = pl.BlockSpec((6, 2 * width, tile), lambda i: (0, 0, i))
-    p_spec = pl.BlockSpec((6, 8, tile), lambda i: (0, 0, i))
     packs = []
     kept = []
     for c in range(CHUNKS):
-        kernel = functools.partial(first_kernel, firsts[c])
-        *keep, normal1, row, left, right = call(
-            kernel if packs else functools.partial(without, kernel, 8, 3),
-            (
-                struct((width, size), BF16),
-                struct((6, 2 * width, size), BF16),
-                struct((6, 8, size), F32),
-                struct((width, size), BF16),
-                part,
-                part,
-                *[struct((32, width), BF16)] * 3,
-            ),
-            grid=(steps,),
-            in_specs=[scalar()]
-            + [tok_spec] * 7
-            + [fixed((32, width))] * len(packs)
-            + [wt_spec, wo_spec, gain_spec],
-            out_specs=(
-                feat_spec, kv_spec, p_spec, feat_spec, tok_spec, tok_spec,
-                *[fixed((32, width))] * 3,
-            ),
-            scratch=[pltpu.VMEM((6, 8, tile), F32), pltpu.VMEM((96, width), F32)],
-            us=8,
-        )(lat, *blocks[c], starts[c], *packs, wt, output_weight, norm_gain_table)
+        *keep, normal1, row, left, right = run_first(
+            firsts[c], lat, blocks[c], starts[c], packs, wt, output_weight, norm_gain_table
+        )
         packs = [row, left, right]
         kept.append((keep, normal1))
         if c == 0:
@@ -581,40 +687,9 @@
 
     row, left, right = packs
     from_l, from_r = from_left(right), from_right(left)
-    ext = points + 64
-    halo_cols = HALO - 32
-    every, halo_struct = pltpu.VMEM((points, width), BF16), pltpu.VMEM((HALO, width), BF16)
-    dn1, dw1, brow, bleft, bright = call(
-        second_kernel,
-        (
-            struct((points, width), F32),
-            struct((4 * width, width), BF16),
-            struct((32, width), BF16),
-            struct((48, width), BF16),
-            struct((48, width), BF16),
-        ),
-        in_specs=[scalar()] + [whole()] * 10,
-        out_specs=(whole(),) * 5,
-        scratch=[
-            *[every] * 4,
-            *[halo_struct] * 3,
-            pltpu.VMEM((points, width), BF16),
-            pltpu.VMEM((ext, width), BF16),
-            pltpu.VMEM((ext, width), BF16),
-            pltpu.VMEM((halo_cols, width), BF16),
-            pltpu.VMEM((halo_cols, width), BF16),
-            pltpu.VMEM((ext, width), F32),
-            pltpu.VMEM((ext, width), F32),
-            pltpu.VMEM((halo_cols, width), F32),
-            pltpu.VMEM((halo_cols, width), F32),
-            pltpu.VMEM((points, width), BF16),
-            pltpu.VMEM((192, 256), F32),
-            pltpu.VMEM((points, width), BF16),
-        ],
-        us=22,
-    )(
-        lat, kept[0][1], kept[1][1], lat_swap(row), from_l, from_r, lat_swap(from_l),
-        lat_swap(from_r), query_key_value_weight, output_weight, cot,
+    halos = [lat_swap(row), from_l, from_r, lat_swap(from_l), lat_swap(from_r)]
+    dn1, dw1, brow, bleft, bright = run_second(
+        lat, [kept[0][1], kept[1][1]], halos, query_key_value_weight, output_weight, cot
     )
 
     from_l, from_r, brow = from_left(bright), from_right(bleft), lat_swap(brow)
@@ -631,39 +706,9 @@
     weights = None
     backs = []
     for c in range(CHUNKS):
-        q0, kv0, p0, mixed0, h1 = kept[c][0]
-        final = c == CHUNKS - 1
-        kernel = functools.partial(third_kernel, firsts[c])
-        extra = [] if weights is None else [weights]
-        if weights is None:
-            kernel = functools.partial(without, kernel, 18, 1)
-        dh1, d0, d1, d2, d3, d4, d5, weights = call(
-            kernel,
-            (
-                struct((size, width), F32),
-                struct((size, width), F32),
-                *[part] * 5,
-                struct((4 * width, width), BF16 if final else F32),
-            ),
-            grid=(steps,),
-            in_specs=[scalar()]
-            + [tok_spec] * 6
-            + [feat_spec, kv_spec, p_spec, feat_spec, tok_spec]
-            + [token_spec(tile, width, firsts[c])] * 2
-            + [fixed((RETURNED, width)), wt_spec, wo_spec, gain_spec]
-            + [fixed((4 * width, width))] * len(extra),
-            out_specs=(*[tok_spec] * 7, fixed((4 * width, width))),
-            scratch=[
-                pltpu.VMEM((4 * width, width), F32),
-                pltpu.VMEM((width, tile), F32),
-                pltpu.VMEM((6, 2 * width, tile), BF16),
-                pltpu.VMEM((width, tile), BF16),
-                pltpu.VMEM((8, tile), F32),
-            ],
-            us=13,
-        )(
-            lat, *blocks[c], q0, kv0, p0, mixed0, h1, dn1, cot, packs, wt, output_weight,
-            norm_gain_table, *extra,
+        dh1, d0, d1, d2, d3, d4, d5, weights = run_third(
+            firsts[c], lat, blocks[c], kept[c][0], dn1, cot, packs, wt, output_weight,
+            norm_gain_table, weights, c == CHUNKS - 1,
         )
         d3 = plus(d3, lat_swap(d5))
         d2 = plus(d2, lat_swap(d4))
@@ -695,7 +740,6 @@
         sums = spread(sums, *stage)
     sums, far_1 = chained(sums, far_1)
     sums = spread(sums, *stages[0])
-    other = lat_swap(sums)
     ends = [(*backs[0][:3], far_0), (*backs[1][:2], d1_1, far_1)]
 
     grad_tokens = None
@@ -715,6 +759,8 @@
             us=4,
         )(starts[c], visible, norm_gain_table, dh1, d0, far, near, *extra)
 
+    sums, grad_tokens = chained(sums, grad_tokens)
+    other = lat_swap(sums)
     factor = (points * lat_count * lon_count) ** (-0.5)
     g_qkv, g_out, g_gain = call(
         functools.partial(weights_kernel, factor, lon_count),

time: 208 us -> 238 us (1.14)
  local copies, waits for them, and re-layouts: 8.89 us -> 49.4 us
  Pallas kernels: 84.8 us -> 64.1 us
  starting transfers between devices: 46.7 us -> 53.9 us
  other arithmetic: 1.16 us -> 5.58 us
    unnamed x68 -> x150, local copies, waits for them, and re-layouts: 5.8 us -> 47 us
    pallas_call x5, Pallas kernels: 67.4 us -> 54 us  [the longest x2 20.3 us: run_third(): call(kernel if extra else functools.partial(without, kernel, 18, 1), (str...]
    ppermute x8, starting transfers between devices: 8.88 us -> 14.6 us  [exchanged(): moved.append(lax.ppermute(parts(digit ^ d), 'lon', pairs))]
    ppermute x4, waiting for transfers between devices: 16.1 us -> 11.5 us  [spread(): got = lax.ppermute(value, 'lon', pairs)]
    ppermute x33, waiting for transfers between devices: 36.3 us -> 40.6 us  [permuted(): lax.ppermute(value, axis, [(i, target(i) % count) for i in range(count)])]
    pallas_call x2, Pallas kernels: 6.4 us -> 3.36 us  [local(): call(kernel if extra else functools.partial(without, kernel, 7, 1), struc...]
    ppermute x33, starting transfers between devices: 30.5 us -> 33.5 us  [permuted(): lax.ppermute(value, axis, [(i, target(i) % count) for i in range(count)])]
  transfers between devices with their start and end apart: 45 -> 45, of which waited for: 22 -> 22; matrix products, arithmetic and copies ran while one was open for 2% -> 3% of each run, Pallas kernels for 22% -> 9%
where the time goes in v5:
time: 238 us; the launch traced here: 236 us
  Pallas kernels  64.1 us (27%)
  waiting for transfers between devices  61.9 us (26%)
  starting transfers between devices  53.9 us (23%)
  local copies, waits for them, and re-layouts  49.4 us (21%)
  other arithmetic  5.58 us (2%)
    unnamed x150, local copies, waits for them, and re-layouts  47 us
    ppermute x33, waiting for transfers between devices, permuted(): lax.ppermute(value, axis, [(i, target(i) % count) for i in range(count)])  40.6 us
    ppermute x33, starting transfers between devices, permuted(): lax.ppermute(value, axis, [(i, target(i) % count) for i in range(count)])  33.5 us
    pallas_call x2, Pallas kernels, run_third(): call(kernel if extra else functools.partial(without, kernel, 18, 1), (str...  20.3 us
    pallas_call x1, Pallas kernels, run_second(): call(second_kernel, (struct((points, width), F32), struct((4 * width, wid...  20.1 us
    ppermute x8, starting transfers between devices, exchanged(): moved.append(lax.ppermute(parts(digit ^ d), 'lon', pairs))  14.6 us
    pallas_call x2, Pallas kernels, run_first(): call(kernel if packs else functools.partial(without, kernel, 8, 3), (stru...  13.6 us
    ppermute x4, waiting for transfers between devices, spread(): got = lax.ppermute(value, 'lon', pairs)  11.5 us
  transfers between devices with their start and end apart: 45, of which 22 were waited for; matrix products, arithmetic and copies ran while one was open for 3% of the time, Pallas kernels for 9%

profile of v5, /device:TPU:0, one launch (start us, length us, event | category | flops | bytes accessed | tf_op | source)
XLA Modules:
  0.0 236.2 jit_solution(15687902187758002304)
XLA Ops:
  6.2 3.0 %collective-permute-start = (bf16[512,384]{1,0:T(8,128)(2,1)}, bf16[512,384]{1,0:T(8,128)(2,1)}, u32[]{:S(2)}, u32[]{:S(2)}) collective-permute-start(bf16[512,384]{1,0:T(8,128)(2,1)} %get-tuple-element.80.refs_1_), channel_id=1, source_target_pairs={{0,2},{2,0},{4,6},{6,4},{8,10},{10,8},{12,14},{14,12},{1,3},{3,1},... | collective-permute-start | bytes 1179656 | tf_op jit(solution)/shard_map/ppermute | solution.py:42
  11.6 7.1 %collective-permute-done.refs_3_ = bf16[512,384]{1,0:T(8,128)(2,1)} collective-permute-done((bf16[512,384]{1,0:T(8,128)(2,1)}, bf16[512,384]{1,0:T(8,128)(2,1)}, u32[]{:S(2)}, u32[]{:S(2)}) %collective-permute-start) | collective-permute-done | bytes 393248 | tf_op jit(solution)/shard_map/ppermute | solution.py:42
  20.4 3.5 %collective-permute-start.2 = (bf16[512,384]{1,0:T(8,128)(2,1)}, bf16[512,384]{1,0:T(8,128)(2,1)}, u32[]{:S(2)}, u32[]{:S(2)}) collective-permute-start(bf16[512,384]{1,0:T(8,128)(2,1)} %get-tuple-element.81.n0), channel_id=1, source_target_pairs={{0,2},{2,0},{4,6},{6,4},{8,10},{10,8},{12,14},{14,12},{1,3},{3,1},... | collective-permute-start | bytes 1179656 | tf_op jit(solution)/shard_map/ppermute | solution.py:42
  24.5 6.6 %collective-permute-done.5.refs_4_ = bf16[512,384]{1,0:T(8,128)(2,1)} collective-permute-done((bf16[512,384]{1,0:T(8,128)(2,1)}, bf16[512,384]{1,0:T(8,128)(2,1)}, u32[]{:S(2)}, u32[]{:S(2)}) %collective-permute-start.5) | collective-permute-done | bytes 393248 | tf_op jit(solution)/shard_map/ppermute | solution.py:42
  35.2 6.6 %shard_map.104 = (bf16[384,512]{1,0:T(8,128)(2,1)S(1)}, bf16[6,768,512]{2,1,0:T(8,128)(2,1)S(1)}, f32[6,8,512]{2,1,0:T(8,128)S(1)}, bf16[384,512]{1,0:T(8,128)(2...) custom-call(s32[1]{0:T(128)} %bitcast.refs_0_.lat_ref, ...), custom_call_target="tpu_custom_call" | custom-call | flops 6400000000 | bytes 8000000 | tf_op jit(solution)/shard_map/pallas_call | solution.py:505
  41.8 2.2 copy-done.44
  48.1 7.0 %shard_map.105 = (bf16[384,512]{1,0:T(8,128)(2,1)S(1)}, bf16[6,768,512]{2,1,0:T(8,128)(2,1)S(1)}, f32[6,8,512]{2,1,0:T(8,128)S(1)}, bf16[384,512]{1,0:T(8,128)(2...) custom-call(s32[1]{0:T(128)} %bitcast.refs_0_.lat_ref, ...), custom_call_target="tpu_custom_call" | custom-call | flops 6400000000 | bytes 8000000 | tf_op jit(solution)/shard_map/pallas_call | solution.py:505
  55.1 2.2 copy-done.42
  60.9 4.9 %collective-permute-start.11 = (bf16[32,384]{1,0:T(8,128)(2,1)S(1)}, bf16[32,384]{1,0:T(8,128)(2,1)}, u32[]{:S(2)}, u32[]{:S(2)}) collective-permute-start(bf16[32,384]{1,0:T(8,128)(2,1)S(1)} %get-tuple-element.100), channel_id=1, source_target_pairs={{0,2},{2,4},{4,6},{6,8},{8,10},{10,12},{12,14},{14,0},{1,3},{3,5},... | collective-permute-start | bytes 73736 | tf_op jit(solution)/shard_map/ppermute | solution.py:42
  67.6 2.2 collective-permute-done.12.right_ref
  75.8 20.1 %shard_map.106 = (f32[1024,384]{1,0:T(8,128)S(1)}, bf16[1536,384]{1,0:T(8,128)(2,1)S(1)}, bf16[32,384]{1,0:T(8,128)(2,1)}, bf16[48,384]{1,0:T(8,128)(2,1)S(1)}, bf16[48,384]{1,0:T(8,128)(2,1)S(1)}) custom-call(s32[1]{0:T(128)} %bitcast.refs_0_.lat_ref, bf16[512,384]{1,0:T(8,128)(2,1)S(1)} %copy-done.66, bf16[512,384]{1,0:T(8,128)(2,1)S(1)} %copy-done.58, ...), custom_call_target="tpu_custom_call" | custom-call | flops 17600000000 | bytes 22000000 | tf_op jit(solution)/shard_map/pallas_call | solution.py:544
  99.6 3.8 %collective-permute-start.17 = (bf16[48,384]{1,0:T(8,128)(2,1)}, bf16[48,384]{1,0:T(8,128)(2,1)S(1)}, u32[]{:S(2)}, u32[]{:S(2)}) collective-permute-start(bf16[48,384]{1,0:T(8,128)(2,1)} %copy-done.21), channel_id=1, source_target_pairs={{0,14},{2,0},{4,2},{6,4},{8,6},{10,8},{12,10},{14,12},{1,15},{3,1}... | collective-permute-start | bytes 110600 | tf_op jit(solution)/shard_map/ppermute | solution.py:42
  103.5 2.1 collective-permute-done.16
  109.5 2.3 copy-done.45
  116.2 10.7 %shard_map.107 = (f32[512,384]{1,0:T(8,128)S(1)}, f32[512,384]{1,0:T(8,128)S(1)}, bf16[512,384]{1,0:T(8,128)(2,1)S(1)}, bf16[512,384]{1,0:T(8,128)(2,1)S(1)}, bf...) custom-call(s32[1]{0:T(128)} %bitcast.refs_0_.lat_ref, ...), custom_call_target="tpu_custom_call" | custom-call | flops 10400000000 | bytes 13000000 | tf_op jit(solution)/shard_map/pallas_call | solution.py:587
  136.0 2.3 copy-done.43
  144.4 9.7 %shard_map.108 = (f32[512,384]{1,0:T(8,128)S(1)}, f32[512,384]{1,0:T(8,128)S(1)}, bf16[512,384]{1,0:T(8,128)(2,1)S(1)}, bf16[512,384]{1,0:T(8,128)(2,1)S(1)}, bf...) custom-call(s32[1]{0:T(128)} %bitcast.refs_0_.lat_ref, ...), custom_call_target="tpu_custom_call" | custom-call | flops 10400000000 | bytes 13000000 | tf_op jit(solution)/shard_map/pallas_call | solution.py:587
  154.7 6.1 %collective-permute-start.27 = (bf16[96,384]{1,0:T(8,128)(2,1)S(1)}, bf16[96,384]{1,0:T(8,128)(2,1)S(1)}, u32[]{:S(2)}, u32[]{:S(2)}) collective-permute-start(bf16[96,384]{1,0:T(8,128)(2,1)S(1)} %get-tuple-element.159), channel_id=1, source_target_pairs={{0,8},{2,10},{4,12},{6,14},{8,0},{10,2},{12,4},{14,6},{1,9},{3,11}... | collective-permute-start | bytes 221192 | tf_op jit(solution)/shard_map/ppermute | solution.py:79
  160.9 4.7 %collective-permute-start.29 = (bf16[512,384]{1,0:T(8,128)(2,1)S(1)}, bf16[512,384]{1,0:T(8,128)(2,1)S(1)}, u32[]{:S(2)}, u32[]{:S(2)}) collective-permute-start(bf16[512,384]{1,0:T(8,128)(2,1)S(1)} %add_convert_fusion.6), channel_id=1, source_target_pairs={{0,12},{2,6},{4,0},{6,10},{8,4},{10,14},{12,8},{14,2},{1,13},{3,7}... | collective-permute-start | bytes 1179656 | tf_op jit(solution)/shard_map/ppermute | solution.py:42
  168.1 5.5 %collective-permute-done.29 = bf16[512,384]{1,0:T(8,128)(2,1)S(1)} collective-permute-done((bf16[512,384]{1,0:T(8,128)(2,1)S(1)}, bf16[512,384]{1,0:T(8,128)(2,1)S(1)}, u32[]{:S(2)}, u32[]{:S(2)}) %collective-permute-start.29) | collective-permute-done | bytes 393248 | tf_op jit(solution)/shard_map/ppermute | solution.py:42
  174.0 3.5 %collective-permute-start.33 = (bf16[384,384]{1,0:T(8,128)(2,1)S(1)}, bf16[384,384]{1,0:T(8,128)(2,1)S(1)}, u32[]{:S(2)}, u32[]{:S(2)}) collective-permute-start(bf16[384,384]{1,0:T(8,128)(2,1)S(1)} %constant_dynamic-slice_fusion.3), channel_id=1, source_target_pairs={{0,2},{2,0},{4,6},{6,4},{8,10},{10,8},{12,14},{14,12},{1,3},{3,1},... | collective-permute-start | bytes 884744 | tf_op jit(solution)/shard_map/ppermute | solution.py:79
  177.5 3.5 %collective-permute-start.34 = (bf16[512,384]{1,0:T(8,128)(2,1)S(1)}, bf16[512,384]{1,0:T(8,128)(2,1)S(1)}, u32[]{:S(2)}, u32[]{:S(2)}) collective-permute-start(bf16[512,384]{1,0:T(8,128)(2,1)S(1)} %add_convert_fusion.3), channel_id=1, source_target_pairs={{0,12},{2,6},{4,0},{6,10},{8,4},{10,14},{12,8},{14,2},{1,13},{3,7}... | collective-permute-start | bytes 1179656 | tf_op jit(solution)/shard_map/ppermute | solution.py:42
  180.9 3.9 %collective-permute-done.33 = bf16[384,384]{1,0:T(8,128)(2,1)S(1)} collective-permute-done((bf16[384,384]{1,0:T(8,128)(2,1)S(1)}, bf16[384,384]{1,0:T(8,128)(2,1)S(1)}, u32[]{:S(2)}, u32[]{:S(2)}) %collective-permute-start.33) | collective-permute-done | bytes 294944 | tf_op jit(solution)/shard_map/ppermute | solution.py:79
  184.9 4.7 %collective-permute-done.34 = bf16[512,384]{1,0:T(8,128)(2,1)S(1)} collective-permute-done((bf16[512,384]{1,0:T(8,128)(2,1)S(1)}, bf16[512,384]{1,0:T(8,128)(2,1)S(1)}, u32[]{:S(2)}, u32[]{:S(2)}) %collective-permute-start.34) | collective-permute-done | bytes 393248 | tf_op jit(solution)/shard_map/ppermute | solution.py:42
  190.0 4.5 %collective-permute-start.36 = (bf16[96,384]{1,0:T(8,128)(2,1)S(1)}, bf16[96,384]{1,0:T(8,128)(2,1)S(1)}, u32[]{:S(2)}, u32[]{:S(2)}) collective-permute-start(bf16[96,384]{1,0:T(8,128)(2,1)S(1)} %get-tuple-element.156), channel_id=1, source_target_pairs={{0,8},{2,10},{4,12},{6,14},{8,0},{10,2},{12,4},{14,6},{1,9},{3,11}... | collective-permute-start | bytes 221192 | tf_op jit(solution)/shard_map/ppermute | solution.py:79
  197.1 2.1 collective-permute-done.36
  200.8 3.5 %collective-permute-done.38.refs_5_ = bf16[512,384]{1,0:T(8,128)(2,1)S(1)} collective-permute-done((bf16[512,384]{1,0:T(8,128)(2,1)S(1)}, bf16[512,384]{1,0:T(8,128)(2,1)S(1)}, u32[]{:S(2)}, u32[]{:S(2)}) %collective-permute-start.38) | collective-permute-done | bytes 393248 | tf_op jit(solution)/shard_map/ppermute | solution.py:42
  205.0 3.5 %collective-permute-start.40 = (bf16[192,384]{1,0:T(8,128)(2,1)S(1)}, bf16[192,384]{1,0:T(8,128)(2,1)S(1)}, u32[]{:S(2)}, u32[]{:S(2)}) collective-permute-start(bf16[192,384]{1,0:T(8,128)(2,1)S(1)} %constant_dynamic-update-slice_fusion.5), channel_id=1, source_target_pairs={{0,8},{2,10},{4,12},{6,14},{8,0},{10,2},{12,4},{14,6},{1,9},{3,11}... | collective-permute-start | bytes 442376 | tf_op jit(solution)/shard_map/ppermute | solution.py:99
  211.3 6.4 %collective-permute-done.40 = bf16[192,384]{1,0:T(8,128)(2,1)S(1)} collective-permute-done((bf16[192,384]{1,0:T(8,128)(2,1)S(1)}, bf16[192,384]{1,0:T(8,128)(2,1)S(1)}, u32[]{:S(2)}, u32[]{:S(2)}) %collective-permute-start.40) | collective-permute-done | bytes 147488 | tf_op jit(solution)/shard_map/ppermute | solution.py:99
  224.5 5.1 %collective-permute-done.43 = bf16[768,384]{1,0:T(8,128)(2,1)S(1)} collective-permute-done((bf16[768,384]{1,0:T(8,128)(2,1)S(1)}, bf16[768,384]{1,0:T(8,128)(2,1)S(1)}, u32[]{:S(2)}, u32[]{:S(2)}) %collective-permute-start.43) | collective-permute-done | bytes 589856 | tf_op jit(solution)/shard_map/ppermute | solution.py:99
  229.8 2.8 %collective-permute-done.44.other_ref = bf16[1536,384]{1,0:T(8,128)(2,1)S(1)} collective-permute-done((bf16[1536,384]{1,0:T(8,128)(2,1)S(1)}, bf16[1536,384]{1,0:T(8,128)(2,1)S(1)}, u32[]{:S(2)}, u32[]{:S(2)}) %collective-permute-start.44) | collective-permute-done | bytes 1179680 | tf_op jit(solution)/shard_map/ppermute | solution.py:42
  232.7 3.5 %shard_map.111 = (f32[2,384,1152]{2,1,0:T(8,128)}, f32[2,384,384]{2,1,0:T(8,128)}, f32[2,384]{1,0:T(2,128)}) custom-call(s32[1]{0:T(128)} %bitcast.refs_0_.lat_ref, bf16[1536,384]{1,0:T(8,128)(2,1)S(1)} %constant_dynamic-update-slice_fusion.7.mine_ref, bf16[1536,384]{1,0:T(8,128)(2,1)S(1)} %collective-permute-done.44.other_ref, ...), custom_call_target="tpu_custom_call" | custom-call | flops 4000000000 | bytes 5000000 | tf_op jit(solution)/shard_map/pallas_call | solution.py:765
  (246 shorter events, 75.4 us)
Async XLA Ops:
  6.2 12.4 %collective-permute-start = (bf16[512,384]{1,0:T(8,128)(2,1)}, bf16[512,384]{1,0:T(8,128)(2,1)}, u32[]{:S(2)}, u32[]{:S(2)}) collective-permute-start(bf16[512,384]{1,0:T(8,128)(2,1)} %get-tuple-element.80.refs_1_), channel_id=1, source_target_pairs={{0,2},{2,0},{4,6},{6,4},{8,10},{10,8},{12,14},{14,12},{1,3},{3,1},... | collective-permute-start | bytes 1179656 | tf_op jit(solution)/shard_map/ppermute | solution.py:42
  18.6 12.4 %collective-permute-start.5 = (bf16[512,384]{1,0:T(8,128)(2,1)}, bf16[512,384]{1,0:T(8,128)(2,1)}, u32[]{:S(2)}, u32[]{:S(2)}) collective-permute-start(bf16[512,384]{1,0:T(8,128)(2,1)} %collective-permute-done.refs_3_), channel_id=1, source_target_pairs={{0,4},{2,14},{4,8},{6,2},{8,12},{10,6},{12,0},{14,10},{1,5},{3,15}... | collective-permute-start | bytes 1179656 | tf_op jit(solution)/shard_map/ppermute | solution.py:42
  20.4 12.4 %collective-permute-start.2 = (bf16[512,384]{1,0:T(8,128)(2,1)}, bf16[512,384]{1,0:T(8,128)(2,1)}, u32[]{:S(2)}, u32[]{:S(2)}) collective-permute-start(bf16[512,384]{1,0:T(8,128)(2,1)} %get-tuple-element.81.n0), channel_id=1, source_target_pairs={{0,2},{2,0},{4,6},{6,4},{8,10},{10,8},{12,14},{14,12},{1,3},{3,1},... | collective-permute-start | bytes 1179656 | tf_op jit(solution)/shard_map/ppermute | solution.py:42
  24.0 8.8 %collective-permute-start.4 = (bf16[512,384]{1,0:T(8,128)(2,1)}, bf16[512,384]{1,0:T(8,128)(2,1)}, u32[]{:S(2)}, u32[]{:S(2)}) collective-permute-start(bf16[512,384]{1,0:T(8,128)(2,1)} %get-tuple-element.80.refs_1_), channel_id=1, source_target_pairs={{0,1},{1,0},{2,3},{3,2},{4,5},{5,4},{6,7},{7,6},{8,9},{9,8},{10,11... | collective-permute-start | bytes 1179656 | tf_op jit(solution)/shard_map/ppermute | solution.py:42
  24.0 9.0 %collective-permute-start.6 = (bf16[512,384]{1,0:T(8,128)(2,1)}, bf16[512,384]{1,0:T(8,128)(2,1)}, u32[]{:S(2)}, u32[]{:S(2)}) collective-permute-start(bf16[512,384]{1,0:T(8,128)(2,1)} %collective-permute-done.refs_3_), channel_id=1, source_target_pairs={{0,1},{1,0},{2,3},{3,2},{4,5},{5,4},{6,7},{7,6},{8,9},{9,8},{10,11... | collective-permute-start | bytes 1179656 | tf_op jit(solution)/shard_map/ppermute | solution.py:42
  32.2 14.4 %collective-permute-start.1 = (bf16[512,384]{1,0:T(8,128)(2,1)}, bf16[512,384]{1,0:T(8,128)(2,1)S(1)}, u32[]{:S(2)}, u32[]{:S(2)}) collective-permute-start(bf16[512,384]{1,0:T(8,128)(2,1)} %get-tuple-element.81.n0), channel_id=1, source_target_pairs={{0,1},{1,0},{2,3},{3,2},{4,5},{5,4},{6,7},{7,6},{8,9},{9,8},{10,11... | collective-permute-start | bytes 1179656 | tf_op jit(solution)/shard_map/ppermute | solution.py:42
  32.8 13.5 %collective-permute-start.3 = (bf16[512,384]{1,0:T(8,128)(2,1)}, bf16[512,384]{1,0:T(8,128)(2,1)S(1)}, u32[]{:S(2)}, u32[]{:S(2)}) collective-permute-start(bf16[512,384]{1,0:T(8,128)(2,1)} %collective-permute-done.2.n2), channel_id=1, source_target_pairs={{0,4},{2,14},{4,8},{6,2},{8,12},{10,6},{12,0},{14,10},{1,5},{3,15}... | collective-permute-start | bytes 1179656 | tf_op jit(solution)/shard_map/ppermute | solution.py:42
  32.8 13.9 %collective-permute-start.8 = (bf16[512,384]{1,0:T(8,128)(2,1)}, bf16[512,384]{1,0:T(8,128)(2,1)S(1)}, u32[]{:S(2)}, u32[]{:S(2)}) collective-permute-start(bf16[512,384]{1,0:T(8,128)(2,1)} %collective-permute-done.2.n2), channel_id=1, source_target_pairs={{0,1},{1,0},{2,3},{3,2},{4,5},{5,4},{6,7},{7,6},{8,9},{9,8},{10,11... | collective-permute-start | bytes 1179656 | tf_op jit(solution)/shard_map/ppermute | solution.py:42
  60.9 6.6 %collective-permute-start.11 = (bf16[32,384]{1,0:T(8,128)(2,1)S(1)}, bf16[32,384]{1,0:T(8,128)(2,1)}, u32[]{:S(2)}, u32[]{:S(2)}) collective-permute-start(bf16[32,384]{1,0:T(8,128)(2,1)S(1)} %get-tuple-element.100), channel_id=1, source_target_pairs={{0,2},{2,4},{4,6},{6,8},{8,10},{10,12},{12,14},{14,0},{1,3},{3,5},... | collective-permute-start | bytes 73736 | tf_op jit(solution)/shard_map/ppermute | solution.py:42
  98.1 8.9 %collective-permute-start.20 = (bf16[768,384]{1,0:T(8,128)(2,1)S(1)}, bf16[768,384]{1,0:T(8,128)(2,1)}, u32[]{:S(2)}, u32[]{:S(2)}) collective-permute-start(bf16[768,384]{1,0:T(8,128)(2,1)S(1)} %constant_dynamic-slice_fusion.9), channel_id=1, source_target_pairs={{0,1},{1,0},{2,3},{3,2},{4,5},{5,4},{6,7},{7,6},{8,9},{9,8},{10,11... | collective-permute-start | bytes 1769480 | tf_op jit(solution)/shard_map/ppermute | solution.py:42
  98.7 6.9 %collective-permute-start.16 = (bf16[48,384]{1,0:T(8,128)(2,1)}, bf16[48,384]{1,0:T(8,128)(2,1)S(1)}, u32[]{:S(2)}, u32[]{:S(2)}) collective-permute-start(bf16[48,384]{1,0:T(8,128)(2,1)} %copy-done.22), channel_id=1, source_target_pairs={{0,2},{2,4},{4,6},{6,8},{8,10},{10,12},{12,14},{14,0},{1,3},{3,5},... | collective-permute-start | bytes 110600 | tf_op jit(solution)/shard_map/ppermute | solution.py:42
  99.6 6.0 %collective-permute-start.17 = (bf16[48,384]{1,0:T(8,128)(2,1)}, bf16[48,384]{1,0:T(8,128)(2,1)S(1)}, u32[]{:S(2)}, u32[]{:S(2)}) collective-permute-start(bf16[48,384]{1,0:T(8,128)(2,1)} %copy-done.21), channel_id=1, source_target_pairs={{0,14},{2,0},{4,2},{6,4},{8,6},{10,8},{12,10},{14,12},{1,15},{3,1}... | collective-permute-start | bytes 110600 | tf_op jit(solution)/shard_map/ppermute | solution.py:42
  109.4 23.1 %collective-permute-start.21 = (bf16[384,384]{1,0:T(8,128)(2,1)}, bf16[384,384]{1,0:T(8,128)(2,1)}, u32[]{:S(2)}, u32[]{:S(2)}) collective-permute-start(bf16[384,384]{1,0:T(8,128)(2,1)} %constant_dynamic-slice_fusion.8), channel_id=1, source_target_pairs={{0,2},{2,0},{4,6},{6,4},{8,10},{10,8},{12,14},{14,12},{1,3},{3,1},... | collective-permute-start | bytes 884744 | tf_op jit(solution)/shard_map/ppermute | solution.py:79
  154.1 13.8 %collective-permute-start.32 = (bf16[512,384]{1,0:T(8,128)(2,1)S(1)}, bf16[512,384]{1,0:T(8,128)(2,1)S(1)}, u32[]{:S(2)}, u32[]{:S(2)}) collective-permute-start(bf16[512,384]{1,0:T(8,128)(2,1)S(1)} %get-tuple-element.129), channel_id=1, source_target_pairs={{0,1},{1,0},{2,3},{3,2},{4,5},{5,4},{6,7},{7,6},{8,9},{9,8},{10,11... | collective-permute-start | bytes 1179656 | tf_op jit(solution)/shard_map/ppermute | solution.py:42
  154.4 13.6 %collective-permute-start.31 = (bf16[512,384]{1,0:T(8,128)(2,1)S(1)}, bf16[512,384]{1,0:T(8,128)(2,1)S(1)}, u32[]{:S(2)}, u32[]{:S(2)}) collective-permute-start(bf16[512,384]{1,0:T(8,128)(2,1)S(1)} %get-tuple-element.127), channel_id=1, source_target_pairs={{0,1},{1,0},{2,3},{3,2},{4,5},{5,4},{6,7},{7,6},{8,9},{9,8},{10,11... | collective-permute-start | bytes 1179656 | tf_op jit(solution)/shard_map/ppermute | solution.py:42
  154.7 6.2 %collective-permute-start.26 = (bf16[96,384]{1,0:T(8,128)(2,1)S(1)}, bf16[96,384]{1,0:T(8,128)(2,1)S(1)}, u32[]{:S(2)}, u32[]{:S(2)}) collective-permute-start(bf16[96,384]{1,0:T(8,128)(2,1)S(1)} %get-tuple-element.157), channel_id=1, source_target_pairs={{0,4},{2,6},{4,0},{6,2},{8,12},{10,14},{12,8},{14,10},{1,5},{3,7},... | collective-permute-start | bytes 221192 | tf_op jit(solution)/shard_map/ppermute | solution.py:79
  154.7 11.4 %collective-permute-start.27 = (bf16[96,384]{1,0:T(8,128)(2,1)S(1)}, bf16[96,384]{1,0:T(8,128)(2,1)S(1)}, u32[]{:S(2)}, u32[]{:S(2)}) collective-permute-start(bf16[96,384]{1,0:T(8,128)(2,1)S(1)} %get-tuple-element.159), channel_id=1, source_target_pairs={{0,8},{2,10},{4,12},{6,14},{8,0},{10,2},{12,4},{14,6},{1,9},{3,11}... | collective-permute-start | bytes 221192 | tf_op jit(solution)/shard_map/ppermute | solution.py:79
  160.8 7.0 %collective-permute-start.28 = (bf16[96,384]{1,0:T(8,128)(2,1)S(1)}, bf16[96,384]{1,0:T(8,128)(2,1)S(1)}, u32[]{:S(2)}, u32[]{:S(2)}) collective-permute-start(bf16[96,384]{1,0:T(8,128)(2,1)S(1)} %get-tuple-element.158), channel_id=1, source_target_pairs={{0,12},{2,14},{4,8},{6,10},{8,4},{10,6},{12,0},{14,2},{1,13},{3,15... | collective-permute-start | bytes 221192 | tf_op jit(solution)/shard_map/ppermute | solution.py:79
  160.9 12.7 %collective-permute-start.29 = (bf16[512,384]{1,0:T(8,128)(2,1)S(1)}, bf16[512,384]{1,0:T(8,128)(2,1)S(1)}, u32[]{:S(2)}, u32[]{:S(2)}) collective-permute-start(bf16[512,384]{1,0:T(8,128)(2,1)S(1)} %add_convert_fusion.6), channel_id=1, source_target_pairs={{0,12},{2,6},{4,0},{6,10},{8,4},{10,14},{12,8},{14,2},{1,13},{3,7}... | collective-permute-start | bytes 1179656 | tf_op jit(solution)/shard_map/ppermute | solution.py:42
  166.1 7.6 %collective-permute-start.25 = (bf16[768,384]{1,0:T(8,128)(2,1)S(1)}, bf16[768,384]{1,0:T(8,128)(2,1)S(1)}, u32[]{:S(2)}, u32[]{:S(2)}) collective-permute-start(bf16[768,384]{1,0:T(8,128)(2,1)S(1)} %constant_dynamic-slice_fusion.7), channel_id=1, source_target_pairs={{0,1},{1,0},{2,3},{3,2},{4,5},{5,4},{6,7},{7,6},{8,9},{9,8},{10,11... | collective-permute-start | bytes 1769480 | tf_op jit(solution)/shard_map/ppermute | solution.py:42
  167.8 6.1 %collective-permute-start.30 = (bf16[512,384]{1,0:T(8,128)(2,1)S(1)}, bf16[512,384]{1,0:T(8,128)(2,1)S(1)}, u32[]{:S(2)}, u32[]{:S(2)}) collective-permute-start(bf16[512,384]{1,0:T(8,128)(2,1)S(1)} %get-tuple-element.125), channel_id=1, source_target_pairs={{0,1},{1,0},{2,3},{3,2},{4,5},{5,4},{6,7},{7,6},{8,9},{9,8},{10,11... | collective-permute-start | bytes 1179656 | tf_op jit(solution)/shard_map/ppermute | solution.py:42
  174.0 10.8 %collective-permute-start.33 = (bf16[384,384]{1,0:T(8,128)(2,1)S(1)}, bf16[384,384]{1,0:T(8,128)(2,1)S(1)}, u32[]{:S(2)}, u32[]{:S(2)}) collective-permute-start(bf16[384,384]{1,0:T(8,128)(2,1)S(1)} %constant_dynamic-slice_fusion.3), channel_id=1, source_target_pairs={{0,2},{2,0},{4,6},{6,4},{8,10},{10,8},{12,14},{14,12},{1,3},{3,1},... | collective-permute-start | bytes 884744 | tf_op jit(solution)/shard_map/ppermute | solution.py:79
  177.5 12.1 %collective-permute-start.34 = (bf16[512,384]{1,0:T(8,128)(2,1)S(1)}, bf16[512,384]{1,0:T(8,128)(2,1)S(1)}, u32[]{:S(2)}, u32[]{:S(2)}) collective-permute-start(bf16[512,384]{1,0:T(8,128)(2,1)S(1)} %add_convert_fusion.3), channel_id=1, source_target_pairs={{0,12},{2,6},{4,0},{6,10},{8,4},{10,14},{12,8},{14,2},{1,13},{3,7}... | collective-permute-start | bytes 1179656 | tf_op jit(solution)/shard_map/ppermute | solution.py:42
  189.6 7.5 %collective-permute-start.35 = (bf16[96,384]{1,0:T(8,128)(2,1)S(1)}, bf16[96,384]{1,0:T(8,128)(2,1)S(1)}, u32[]{:S(2)}, u32[]{:S(2)}) collective-permute-start(bf16[96,384]{1,0:T(8,128)(2,1)S(1)} %get-tuple-element.154), channel_id=1, source_target_pairs={{0,4},{2,6},{4,0},{6,2},{8,12},{10,14},{12,8},{14,10},{1,5},{3,7},... | collective-permute-start | bytes 221192 | tf_op jit(solution)/shard_map/ppermute | solution.py:79
  190.0 9.1 %collective-permute-start.36 = (bf16[96,384]{1,0:T(8,128)(2,1)S(1)}, bf16[96,384]{1,0:T(8,128)(2,1)S(1)}, u32[]{:S(2)}, u32[]{:S(2)}) collective-permute-start(bf16[96,384]{1,0:T(8,128)(2,1)S(1)} %get-tuple-element.156), channel_id=1, source_target_pairs={{0,8},{2,10},{4,12},{6,14},{8,0},{10,2},{12,4},{14,6},{1,9},{3,11}... | collective-permute-start | bytes 221192 | tf_op jit(solution)/shard_map/ppermute | solution.py:79
  194.5 6.2 %collective-permute-start.37 = (bf16[96,384]{1,0:T(8,128)(2,1)S(1)}, bf16[96,384]{1,0:T(8,128)(2,1)S(1)}, u32[]{:S(2)}, u32[]{:S(2)}) collective-permute-start(bf16[96,384]{1,0:T(8,128)(2,1)S(1)} %get-tuple-element.155), channel_id=1, source_target_pairs={{0,12},{2,14},{4,8},{6,10},{8,4},{10,6},{12,0},{14,2},{1,13},{3,15... | collective-permute-start | bytes 221192 | tf_op jit(solution)/shard_map/ppermute | solution.py:79
  194.5 9.8 %collective-permute-start.38 = (bf16[512,384]{1,0:T(8,128)(2,1)S(1)}, bf16[512,384]{1,0:T(8,128)(2,1)S(1)}, u32[]{:S(2)}, u32[]{:S(2)}) collective-permute-start(bf16[512,384]{1,0:T(8,128)(2,1)S(1)} %add_convert_fusion.5), channel_id=1, source_target_pairs={{0,2},{2,0},{4,6},{6,4},{8,10},{10,8},{12,14},{14,12},{1,3},{3,1},... | collective-permute-start | bytes 1179656 | tf_op jit(solution)/shard_map/ppermute | solution.py:42
  204.3 6.0 %collective-permute-start.39 = (bf16[192,384]{1,0:T(8,128)(2,1)S(1)}, bf16[192,384]{1,0:T(8,128)(2,1)}, u32[]{:S(2)}, u32[]{:S(2)}) collective-permute-start(bf16[192,384]{1,0:T(8,128)(2,1)S(1)} %constant_dynamic-update-slice_fusion.5), channel_id=1, source_target_pairs={{0,4},{2,6},{4,0},{6,2},{8,12},{10,14},{12,8},{14,10},{1,5},{3,7},... | collective-permute-start | bytes 442376 | tf_op jit(solution)/shard_map/ppermute | solution.py:99
  205.0 12.7 %collective-permute-start.40 = (bf16[192,384]{1,0:T(8,128)(2,1)S(1)}, bf16[192,384]{1,0:T(8,128)(2,1)S(1)}, u32[]{:S(2)}, u32[]{:S(2)}) collective-permute-start(bf16[192,384]{1,0:T(8,128)(2,1)S(1)} %constant_dynamic-update-slice_fusion.5), channel_id=1, source_target_pairs={{0,8},{2,10},{4,12},{6,14},{8,0},{10,2},{12,4},{14,6},{1,9},{3,11}... | collective-permute-start | bytes 442376 | tf_op jit(solution)/shard_map/ppermute | solution.py:99
  208.5 9.2 %collective-permute-start.41 = (bf16[192,384]{1,0:T(8,128)(2,1)S(1)}, bf16[192,384]{1,0:T(8,128)(2,1)S(1)}, u32[]{:S(2)}, u32[]{:S(2)}) collective-permute-start(bf16[192,384]{1,0:T(8,128)(2,1)S(1)} %constant_dynamic-update-slice_fusion.5), channel_id=1, source_target_pairs={{0,12},{2,14},{4,8},{6,10},{8,4},{10,6},{12,0},{14,2},{1,13},{3,15... | collective-permute-start | bytes 442376 | tf_op jit(solution)/shard_map/ppermute | solution.py:99
  208.8 9.5 %collective-permute-start.42 = (bf16[512,384]{1,0:T(8,128)(2,1)}, bf16[512,384]{1,0:T(8,128)(2,1)S(1)}, u32[]{:S(2)}, u32[]{:S(2)}) collective-permute-start(bf16[512,384]{1,0:T(8,128)(2,1)} %add_convert_fusion.2), channel_id=1, source_target_pairs={{0,2},{2,0},{4,6},{6,4},{8,10},{10,8},{12,14},{14,12},{1,3},{3,1},... | collective-permute-start | bytes 1179656 | tf_op jit(solution)/shard_map/ppermute | solution.py:42
  218.3 11.4 %collective-permute-start.43 = (bf16[768,384]{1,0:T(8,128)(2,1)S(1)}, bf16[768,384]{1,0:T(8,128)(2,1)S(1)}, u32[]{:S(2)}, u32[]{:S(2)}) collective-permute-start(bf16[768,384]{1,0:T(8,128)(2,1)S(1)} %constant_dynamic-update-slice_fusion.9), channel_id=1, source_target_pairs={{0,2},{2,0},{4,6},{6,4},{8,10},{10,8},{12,14},{14,12},{1,3},{3,1},... | collective-permute-start | bytes 1769480 | tf_op jit(solution)/shard_map/ppermute | solution.py:99
  (85 other events, 322.5 us)

commit v6 on v5

--- a/solution.py
+++ b/solution.py
@@ -11,9 +11,10 @@
 EPS = 1e-05
 F32 = jnp.float32
 BF16 = jnp.bfloat16
-VMEM_BYTES = 26 * 1024 * 1024
+LARGE_MIB = 56
 HALO = 112
 CORNER = 96
+KEYS = 208
 RETURNED = 224
 
 
@@ -27,6 +28,10 @@
 
 def tn(a, b):
     return lax.dot_general(a, b, (((0,), (0,)), ((), ())), preferred_element_type=F32)
+
+
+def tt(a, b):
+    return lax.dot_general(a, b, (((0,), (1,)), ((), ())), preferred_element_type=F32)
 
 
 def iota(shape, dim):
@@ -114,12 +119,8 @@
     return out
 
 
-def halves_summed(value):
-    lat = lax.axis_index("lat")
-    half = value.shape[0] // 2
-    mine = lax.dynamic_slice_in_dim(value, lat * half, half, 0)
-    other = lat_swap(lax.dynamic_slice_in_dim(value, (1 - lat) * half, half, 0))
-    return (mine.astype(F32) + other.astype(F32)).astype(BF16)
+def halves_summed(mine, other):
+    return (mine.astype(F32) + lat_swap(other).astype(F32)).astype(BF16)
 
 
 def stage_summed(value, stage):
@@ -223,6 +224,16 @@
             ref[...] = pack_s[i * 32 : i * 32 + 32, :].astype(BF16)
 
 
+def write_halves(lat, total_ref, mine_ref, other_ref):
+    half = mine_ref.shape[0]
+    for band in range(2):
+
+        @pl.when(lat == band)
+        def _():
+            mine_ref[...] = total_ref[band * half : (band + 1) * half, :].astype(BF16)
+            other_ref[...] = total_ref[(1 - band) * half : (2 - band) * half, :].astype(BF16)
+
+
 def second_kernel(
     lat_ref, na_ref, nb_ref, row_ref, left_ref, right_ref, dleft_ref, dright_ref,
     w_all, wo_all, cot_ref,
@@ -255,74 +266,69 @@
     for at in (0, 32 + points):
         k_s[at : at + 32, :] = kh[0:32]
         v_s[at : at + 32, :] = vh[0:32]
-    kc_s[...] = kh[32:HALO]
-    vc_s[...] = vh[32:HALO]
+    tiles = points // 128
+    slots = tiles * 16
+    a, b = iota((slots, HALO - 32), 0), iota((slots, HALO - 32), 1)
+    place, is_right = a % 16, jnp.where(a % 16 >= 6, 1, 0)
+    ext_row = 4 * (a // 16) + place - 6 * is_right
+    inner = (ext_row >= 1) & (ext_row <= 32)
+    source = jnp.where(inner, 32 * is_right + ext_row - 1, 64 + is_right)
+    spread_cols = one_hot((place < 12) & (b == source))
+    kc_s[...] = nn(spread_cols, kh[32:HALO]).astype(BF16)
+    vc_s[...] = nn(spread_cols, vh[32:HALO]).astype(BF16)
     dk_s[...] = jnp.zeros_like(dk_s)
     dv_s[...] = jnp.zeros_like(dv_s)
-    dkc_s[...] = jnp.zeros_like(dkc_s)
-    dvc_s[...] = jnp.zeros_like(dvc_s)
     cot = cot_ref[...].astype(BF16)
     do_s[...] = nt(cot, wo_ref[...]).astype(BF16)
 
-    key, query = iota((192, 256), 0), iota((192, 256), 1) % 128
-    drow = key // 32 - 1 - query // 32
-    dcol = key % 32 - query % 32
-    mask_s[...] = jnp.where((jnp.abs(drow) <= 1) & (jnp.abs(dcol) <= 1), 1.0, 0.0)
-
-    tiles = points // 128
+    key, query = iota((KEYS, 256), 0), iota((KEYS, 256), 1) % 128
+    place = key - 192
+    right = place >= 6
+    row = jnp.where(place < 0, key // 32, jnp.where(right, place - 6, place))
+    col = jnp.where(place < 0, key % 32, jnp.where(right, 32, -1))
+    near = (jnp.abs(row - 1 - query // 32) <= 1) & (jnp.abs(col - query % 32) <= 1)
+    mask_s[...] = jnp.where(near & (place < 12), row, 9)
 
     def tile_step(t, carry):
         base = pl.multiple_of(t * 128, 128)
-        key = iota((192, 256), 0)
-        first = jnp.where(upper & (t == 0), 32, 0)
-        last = jnp.where(jnp.logical_not(upper) & (t == tiles - 1), 160, 192)
-        mask1 = (mask_s[...] > 0.5) & (key >= first) & (key < last)
-        e, query = iota((HALO - 32, 256), 0), iota((HALO - 32, 256), 1) % 128
-        corner = e >= 64
-        key_row = jnp.where(corner, jnp.where(upper, 32, -1), e % 32)
-        is_left = (e < 32) | (e == 64)
-        near = jnp.abs(key_row - (4 * t + query // 32)) <= 1
-        side = query % 32 == jnp.where(is_left, 0, 31)
-        mask2 = near & side & (e < 66)
-        lane = iota((128, 128), 1)
-        even = lane < 64
+        first = jnp.where(upper & (t == 0), 1, 0)
+        last = jnp.where(jnp.logical_not(upper) & (t == tiles - 1), 4, 5)
+        mask = (mask_s[...] >= first) & (mask_s[...] <= last)
+        even = iota((128, 128), 1) < 64
+        top = iota((128, 128), 0) < 64
+        win, here = pl.ds(base, 192), pl.ds(base, 128)
+        side = pl.ds(pl.multiple_of(t * 16, 16), 16)
         for pair in range(HEADS // 2):
             lanes = slice(pair * 128, pair * 128 + 128)
-            win = pl.ds(base, 192)
-            here = pl.ds(base, 128)
             q = q_s[here, lanes]
             do = do_s[here, lanes]
             zero = jnp.zeros_like(q)
             qm = jnp.concatenate([jnp.where(even, q, zero), jnp.where(even, zero, q)], 0)
             dom = jnp.concatenate([jnp.where(even, do, zero), jnp.where(even, zero, do)], 0)
-            k1, v1 = k_s[win, lanes], v_s[win, lanes]
-            k2, v2 = kc_s[:, lanes], vc_s[:, lanes]
-            w1 = jnp.where(mask1, jnp.exp(nt(k1, qm)), 0.0)
-            w2 = jnp.where(mask2, jnp.exp(nt(k2, qm)), 0.0)
-            total = jnp.sum(w1, axis=0, keepdims=True) + jnp.sum(w2, axis=0, keepdims=True)
-            inverse = 1.0 / total
-            p1, p2 = w1 * inverse, w2 * inverse
-            dp1, dp2 = nt(v1, dom), nt(v2, dom)
-            delta = jnp.sum(p1 * dp1, axis=0, keepdims=True) + jnp.sum(
-                p2 * dp2, axis=0, keepdims=True
-            )
-            ds1, ds2 = (p1 * (dp1 - delta)).astype(BF16), (p2 * (dp2 - delta)).astype(BF16)
-            p1, p2 = p1.astype(BF16), p2.astype(BF16)
-            out = tn(p1, v1) + tn(p2, v2)
-            mixed_s[here, lanes] = jnp.where(even, out[0:128], out[128:256]).astype(BF16)
-            dq = (tn(ds1, k1) + tn(ds2, k2)) * scale
-            dq_ref[here, lanes] = jnp.where(even, dq[0:128], dq[128:256]).astype(BF16)
-            dk_s[win, lanes] += nn(ds1, qm)
-            dv_s[win, lanes] += nn(p1, dom)
-            dkc_s[:, lanes] += nn(ds2, qm)
-            dvc_s[:, lanes] += nn(p2, dom)
+            k = jnp.concatenate([k_s[win, lanes], kc_s[side, lanes]], 0)
+            v = jnp.concatenate([v_s[win, lanes], vc_s[side, lanes]], 0)
+            w = jnp.where(mask, jnp.exp(nt(k, qm)), 0.0)
+            p = w * (1.0 / jnp.sum(w, axis=0, keepdims=True))
+            dp = nt(v, dom)
+            delta = jnp.sum(p * dp, axis=0, keepdims=True)
+            ds = (p * (dp - delta)).astype(BF16)
+            p = p.astype(BF16)
+            out = tn(v, p)
+            mixed_s[lanes, here] = jnp.where(top, out[:, 0:128], out[:, 128:256]).astype(BF16)
+            dq = tn(k, ds) * scale
+            dq_ref[lanes, here] = jnp.where(top, dq[:, 0:128], dq[:, 128:256]).astype(BF16)
+            dk, dv = nn(ds, qm), nn(p, dom)
+            dk_s[win, lanes] += dk[0:192]
+            dv_s[win, lanes] += dv[0:192]
+            dkc_s[side, lanes] = dk[192:KEYS].astype(BF16)
+            dvc_s[side, lanes] = dv[192:KEYS].astype(BF16)
         return carry
 
     lax.fori_loop(0, tiles, tile_step, 0)
 
     row_at = pl.multiple_of(jnp.where(upper, 32 + points, 0), 32)
-    dkh = jnp.concatenate([dk_s[pl.ds(row_at, 32), :], dkc_s[...]], 0).astype(BF16)
-    dvh = jnp.concatenate([dv_s[pl.ds(row_at, 32), :], dvc_s[...]], 0).astype(BF16)
+    dkh = jnp.concatenate([dk_s[pl.ds(row_at, 32), :], tn(spread_cols, dkc_s[...])], 0).astype(BF16)
+    dvh = jnp.concatenate([dv_s[pl.ds(row_at, 32), :], tn(spread_cols, dvc_s[...])], 0).astype(BF16)
     dkh_ref[...] = dkh
     dvh_ref[...] = dvh
     dk_ref[...] = dk_s[32 : 32 + points, :].astype(BF16)
@@ -334,20 +340,20 @@
         ref[0:32, :] = back[at : at + 32]
         ref[32:48, :] = back[CORNER:HALO]
     wq, wk, wv = (w_all[1, :, i * width : (i + 1) * width] for i in range(3))
-    dw_ref[0:width, :] = tn(dq_ref[...], normal).astype(BF16)
+    dw_ref[0:width, :] = nn(dq_ref[...], normal).astype(BF16)
     dw_ref[width : 2 * width, :] = (tn(dk_ref[...], normal) + tn(dkh_ref[...], halo)).astype(BF16)
     dw_ref[2 * width : 3 * width, :] = (
         tn(dv_ref[...], normal) + tn(dvh_ref[...], halo)
     ).astype(BF16)
-    dw_ref[3 * width : 4 * width, :] = tn(mixed_s[...], cot).astype(BF16)
-    dn_ref[...] = nt(dq_ref[...], wq) + nt(dk_ref[...], wk) + nt(dv_ref[...], wv)
+    dw_ref[3 * width : 4 * width, :] = nn(mixed_s[...], cot).astype(BF16)
+    dn_ref[...] = tt(dq_ref[...], wq) + nt(dk_ref[...], wk) + nt(dv_ref[...], wv)
 
 
 def third_kernel(
     first, lat_ref, n0, n1, n2, n3, n4, n5, q_ref, kv_ref, p_ref, mixed_ref, h_ref, dn1_ref, cot_ref,
     packs_ref, wt_ref, wo_ref, gain_ref, dw_in,
-    dh_ref, d0, d1, d2, d3, d4, d5, dw_ref,
-    dw_s, dmix_s, dkv_s, dq_s, dp_s,
+    dh_ref, d0, d1, d2, d3, d4, d5, dw_ref, other_ref,
+    dw_s, dmix_s, dkv_s, dq_s, dp_s, n_s,
 ):
     width, tile = q_ref.shape
     head = width // HEADS
@@ -394,22 +400,26 @@
             p = p_ref[b, h : h + 1, :]
             ds = p * (dp_s[b : b + 1, :] - delta) * scale
             dq = dq + ds * kv_ref[b, lo:hi, :].astype(F32)
-            dkv_s[b, lo:hi, :] = (ds * q).astype(BF16)
-            dkv_s[b, width + lo : width + hi, :] = (p * dmix).astype(BF16)
+            here = slice(b * tile, (b + 1) * tile)
+            dkv_s[lo:hi, here] = (ds * q).astype(BF16)
+            dkv_s[width + lo : width + hi, here] = (p * dmix).astype(BF16)
         dq_s[lo:hi, :] = dq.astype(BF16)
     dq = dq_s[...]
     dw_s[0:width, :] += nn(dq, n0[...])
-    for b, (ref, out) in enumerate(zip(blocks, outs)):
-        dkv = dkv_s[b]
-        grad = tn(dkv, wt_ref[width : 3 * width])
-        if b == 0:
-            grad = grad + tn(dq, wt_ref[0:width])
-        out[...] = grad.astype(out.dtype)
-        dw_s[width : 3 * width, :] += nn(dkv, ref[...])
+    for b, ref in enumerate(blocks):
+        n_s[b * tile : (b + 1) * tile, :] = ref[...]
+    dw_s[width : 3 * width, :] += nn(dkv_s[...], n_s[...])
+    grads = tn(dkv_s[...], wt_ref[width : 3 * width])
+    outs[0][...] = grads[0:tile] + tn(dq, wt_ref[0:width])
+    for b in range(1, len(blocks)):
+        outs[b][...] = grads[b * tile : (b + 1) * tile].astype(BF16)
 
     @pl.when(step == pl.num_programs(0) - 1)
     def _():
-        dw_ref[...] = dw_s[...].astype(dw_ref.dtype)
+        if other_ref is None:
+            dw_ref[...] = dw_s[...]
+        else:
+            write_halves(lat_ref[0], dw_s, dw_ref, other_ref)
 
 
 def last_kernel(
@@ -448,7 +458,7 @@
 
 
 def call(
-    kernel, out_shape, scratch=(), grid=None, in_specs=None, out_specs=None, us=1, aliases=None
+    kernel, out_shape, scratch=(), grid=None, in_specs=None, out_specs=None, us=1, aliases=None, mib=12
 ):
     return pl.pallas_call(
         kernel,
@@ -464,7 +474,7 @@
         cost_estimate=pl.CostEstimate(
             flops=int(us * 1e6 * 800), bytes_accessed=int(us * 1e6), transcendentals=0
         ),
-        compiler_params=pltpu.CompilerParams(vmem_limit_bytes=VMEM_BYTES),
+        compiler_params=pltpu.CompilerParams(vmem_limit_bytes=mib * 1024 * 1024),
     )
 
 
@@ -532,6 +542,7 @@
             *[fixed((32, width))] * 3,
         ),
         scratch=[pltpu.VMEM((6, 8, tile), F32), pltpu.VMEM((96, width), F32)],
+        mib=LARGE_MIB,
         us=8,
     )(lat, *blocks, start, *packs, wt, output_weight, norm_gain_table)
 
@@ -539,7 +550,8 @@
 def run_second(lat, normals, halos, query_key_value_weight, output_weight, cot):
     points, width = cot.shape
     struct = jax.ShapeDtypeStruct
-    ext, halo_cols = points + 64, HALO - 32
+    ext, slots = points + 64, points // 8
+    across = pltpu.VMEM((width, points), BF16)
     every, halo = pltpu.VMEM((points, width), BF16), pltpu.VMEM((HALO, width), BF16)
     return call(
         second_kernel,
@@ -553,54 +565,58 @@
         in_specs=[scalar()] + [whole()] * 10,
         out_specs=(whole(),) * 5,
         scratch=[
-            *[every] * 4,
+            across, every, every, across,
             *[halo] * 3,
             every,
             pltpu.VMEM((ext, width), BF16),
             pltpu.VMEM((ext, width), BF16),
-            pltpu.VMEM((halo_cols, width), BF16),
-            pltpu.VMEM((halo_cols, width), BF16),
+            *[pltpu.VMEM((slots, width), BF16)] * 2,
             pltpu.VMEM((ext, width), F32),
             pltpu.VMEM((ext, width), F32),
-            pltpu.VMEM((halo_cols, width), F32),
-            pltpu.VMEM((halo_cols, width), F32),
+            *[pltpu.VMEM((slots, width), BF16)] * 2,
             every,
-            pltpu.VMEM((192, 256), F32),
+            pltpu.VMEM((KEYS, 256), jnp.int32),
             every,
         ],
+        mib=LARGE_MIB,
         us=22,
     )(lat, *normals, *halos, query_key_value_weight, output_weight, cot)
 
 
 def run_third(
-    first, lat, blocks, kept, dn1, cot, packs, wt, output_weight, norm_gain_table, weights, final
+    first, size, at, lat, blocks, kept, dn1, cot, packs, wt, output_weight, norm_gain_table, weights, final
 ):
     q0, kv0, p0, mixed0, h1 = kept
-    size, width = h1.shape
+    width = h1.shape[1]
     tile = min(BACKWARD_TILE, size)
     struct = jax.ShapeDtypeStruct
     part = struct((size, width), BF16)
-    tok_spec = token_spec(tile, width)
-    feat_spec = pl.BlockSpec((width, tile), lambda i: (0, i))
+    tok_spec, from_spec = token_spec(tile, width), token_spec(tile, width, at)
+    skip = at // tile
+    feat_spec = pl.BlockSpec((width, tile), lambda i: (0, i + skip))
     kernel = functools.partial(third_kernel, first)
     extra = [] if weights is None else [weights]
+    if not extra:
+        kernel = functools.partial(without, kernel, 18, 1)
+    if not final:
+        kernel = functools.partial(without, kernel, 26 + len(extra) , 1)
     return call(
-        kernel if extra else functools.partial(without, kernel, 18, 1),
+        kernel,
         (
             struct((size, width), F32),
             struct((size, width), F32),
             *[part] * 5,
-            struct((4 * width, width), BF16 if final else F32),
+            *([struct((2 * width, width), BF16)] * 2 if final else [struct((4 * width, width), F32)]),
         ),
         grid=(size // tile,),
         in_specs=[scalar()]
-        + [tok_spec] * 6
+        + [from_spec] * 6
         + [
             feat_spec,
-            pl.BlockSpec((6, 2 * width, tile), lambda i: (0, 0, i)),
-            pl.BlockSpec((6, 8, tile), lambda i: (0, 0, i)),
+            pl.BlockSpec((6, 2 * width, tile), lambda i: (0, 0, i + skip)),
+            pl.BlockSpec((6, 8, tile), lambda i: (0, 0, i + skip)),
             feat_spec,
-            tok_spec,
+            from_spec,
         ]
         + [token_spec(tile, width, first)] * 2
         + [
@@ -610,14 +626,19 @@
             fixed((2, width)),
         ]
         + [fixed((4 * width, width))] * len(extra),
-        out_specs=(*[tok_spec] * 7, fixed((4 * width, width))),
+        out_specs=(
+            *[tok_spec] * 7,
+            *([fixed((2 * width, width))] * 2 if final else [fixed((4 * width, width))]),
+        ),
         scratch=[
             pltpu.VMEM((4 * width, width), F32),
             pltpu.VMEM((width, tile), F32),
-            pltpu.VMEM((6, 2 * width, tile), BF16),
+            pltpu.VMEM((2 * width, 6 * tile), BF16),
             pltpu.VMEM((width, tile), BF16),
             pltpu.VMEM((8, tile), F32),
+            pltpu.VMEM((6 * tile, width), BF16),
         ],
+        mib=LARGE_MIB,
         us=13,
     )(
         lat, *blocks, q0, kv0, p0, mixed0, h1, dn1, cot, packs, wt, output_weight,
@@ -656,6 +677,7 @@
                 gain_spec,
             ],
             out_specs=(token_spec(small, width),) * 2,
+            mib=LARGE_MIB,
             us=2,
         )(tokens, visible, mask_token, norm_gain_table)
         starts.append(start)
@@ -697,64 +719,74 @@
         [brow, from_l, from_r, lat_swap(from_l), lat_swap(from_r)], 0
     )
     stages = lon_factors()
-    sum1 = halves_summed(dw1)
+    sum1 = halves_summed(
+        lax.dynamic_slice_in_dim(dw1, lat[0] * 2 * width, 2 * width, 0),
+        lax.dynamic_slice_in_dim(dw1, (1 - lat[0]) * 2 * width, 2 * width, 0),
+    )
     packs, sum1 = chained(packs, sum1)
 
     def plus(a, b):
         return (a.astype(F32) + b.astype(F32)).astype(BF16)
 
+    pieces = [(first, size) for first in firsts]
     weights = None
-    backs = []
-    for c in range(CHUNKS):
-        dh1, d0, d1, d2, d3, d4, d5, weights = run_third(
-            firsts[c], lat, blocks[c], kept[c][0], dn1, cot, packs, wt, output_weight,
-            norm_gain_table, weights, c == CHUNKS - 1,
+    sum_stages = list(stages)
+    ends = []
+    coming = returned = None
+    for n, (first, count) in enumerate(pieces):
+        c = first // size
+        dh1, d0, d1, d2, d3, d4, d5, *weights = run_third(
+            first, count, first - c * size, lat, blocks[c], kept[c][0], dn1, cot, packs, wt,
+            output_weight, norm_gain_table, weights, n == len(pieces) - 1,
+        )
+        if sum_stages:
+            sum1 = stage_summed(sum1, sum_stages.pop(0))
+        weights, sum1, d1, d2, d3, d4, d5, coming, returned = lax.optimization_barrier(
+            (weights, sum1, d1, d2, d3, d4, d5, coming, returned)
         )
         d3 = plus(d3, lat_swap(d5))
         d2 = plus(d2, lat_swap(d4))
         d1 = lat_swap(d1)
-        if c == 0:
-            sum1 = stage_summed(sum1, stages[0])
-            weights, sum1, d1, d2, d3 = lax.optimization_barrier((weights, sum1, d1, d2, d3))
-            for stage in stages[1:]:
-                sum1 = stage_summed(sum1, stage)
-            d2 = plus(d2, lon_backward(d3))
-        backs.append((dh1, d0, d1, d2, d3))
-
-    d2_0, (d1_1, d2_1, d3_1) = backs[0][3], backs[1][2:]
-    sum0 = halves_summed(weights)
-    sum0, sum1, d2_0, d1_1, d2_1, d3_1 = lax.optimization_barrier(
-        (sum0, sum1, d2_0, d1_1, d2_1, d3_1)
-    )
-    back_1 = lon_backward(d3_1)
-    sum0 = stage_summed(sum0, stages[0])
-    sum0, d2_0, back_1 = lax.optimization_barrier((sum0, d2_0, back_1))
-    far_0 = lon_swap(d2_0)
-    d2_1 = plus(d2_1, back_1)
-    for stage in stages[1:]:
+        if n == len(pieces) - 1:
+            weights = [halves_summed(*weights)]
+        weights, d1, d2, d3 = lax.optimization_barrier((weights, d1, d2, d3))
+        if returned is not None:
+            ends[-2][-1] = returned
+        returned = None
+        if coming is not None:
+            returned = lon_swap(coming)
+        coming = plus(d2, lon_backward(d3))
+        weights = weights[0]
+        ends.append([first, count, dh1, d0, d1, None])
+
+    sum0 = stage_summed(weights, stages[0])
+    for stage in sum_stages:
+        sum1 = stage_summed(sum1, stage)
+    sum0, sum1, coming, returned = lax.optimization_barrier((sum0, sum1, coming, returned))
+    ends[-2][-1] = returned
+    returned = lon_swap(coming)
+    sum0 = stage_summed(sum0, stages[1])
+    sum0, returned = lax.optimization_barrier((sum0, returned))
+    ends[-1][-1] = returned
+    for stage in stages[2:]:
         sum0 = stage_summed(sum0, stage)
-    sum0, d2_1, far_0 = lax.optimization_barrier((sum0, d2_1, far_0))
-    far_1 = lon_swap(d2_1)
     sums = jnp.concatenate([sum0, sum1], 0)
-    for stage in stages[:0:-1]:
+    for stage in stages[::-1]:
         sums = spread(sums, *stage)
-    sums, far_1 = chained(sums, far_1)
-    sums = spread(sums, *stages[0])
-    ends = [(*backs[0][:3], far_0), (*backs[1][:2], d1_1, far_1)]
 
     grad_tokens = None
-    for c in range(CHUNKS):
-        dh1, d0, near, far = ends[c]
+    for first, count, dh1, d0, near, far in ends:
+        c = first // size
         extra = [] if grad_tokens is None else [grad_tokens]
-        kernel = functools.partial(last_kernel, firsts[c])
+        kernel = functools.partial(last_kernel, first)
         grad_tokens = call(
             kernel if extra else functools.partial(without, kernel, 7, 1),
             struct((points, width), F32),
-            grid=(size // small,),
-            in_specs=[token_spec(small, width), fixed((rows, cols)), gain_spec]
+            grid=(count // small,),
+            in_specs=[token_spec(small, width, first - c * size), fixed((rows, cols)), gain_spec]
             + [token_spec(small, width)] * 4
             + [pl.BlockSpec(memory_space=pl.ANY)] * len(extra),
-            out_specs=token_spec(small, width, firsts[c]),
+            out_specs=token_spec(small, width, first),
             aliases={7: 0} if extra else {},
             us=4,
         )(starts[c], visible, norm_gain_table, dh1, d0, far, near, *extra)
@@ -772,6 +804,7 @@
         in_specs=[scalar()] + [whole()] * 4,
         out_specs=(whole(),) * 3,
         scratch=[pltpu.VMEM((2, 4 * width, width), F32)],
+        mib=20,
         us=5,
     )(lat, sums, other, wt, norm_gain_table)
     return grad_tokens.reshape(rows, cols, width), g_qkv, g_out, g_gain

time: 238 us -> 202 us (0.85)
  local copies, waits for them, and re-layouts: 49.4 us -> 6.19 us
  Pallas kernels: 64.1 us -> 77 us
  starting transfers between devices: 53.9 us -> 42.9 us
  waiting for transfers between devices: 61.9 us -> 71.1 us
  other arithmetic: 5.58 us -> 1.16 us
    unnamed x150 -> x76, local copies, waits for them, and re-layouts: 47 us -> 4.35 us
    ppermute x8, waiting for transfers between devices: 9.71 us -> 17.7 us  [exchanged(): moved.append(lax.ppermute(parts(digit ^ d), 'lon', pairs))]
    pallas_call x2, Pallas kernels: 20.3 us -> 28 us  [run_third(): call(kernel, (struct((size, width), F32), struct((size, width), F32), *[p...]
    ppermute x33, starting transfers between devices: 33.5 us -> 27.3 us  [permuted(): lax.ppermute(value, axis, [(i, target(i) % count) for i in range(count)])]
    ppermute x8, starting transfers between devices: 14.6 us -> 10.1 us  [exchanged(): moved.append(lax.ppermute(parts(digit ^ d), 'lon', pairs))]
    pallas_call x2, Pallas kernels: 13.6 us -> 17.1 us  [run_first(): call(kernel if packs else functools.partial(without, kernel, 8, 3), (stru...]
    ppermute x4, waiting for transfers between devices: 11.5 us -> 14.6 us  [spread(): got = lax.ppermute(value, 'lon', pairs)]
  transfers between devices with their start and end apart: 45 -> 45, of which waited for: 22 -> 24; matrix products, arithmetic and copies ran while one was open for 3% -> 2% of each run, Pallas kernels for 9% -> 21%
where the time goes in v6:
time: 202 us; the launch traced here: 200 us
  Pallas kernels  77 us (38%)
  waiting for transfers between devices  71.1 us (35%)
  starting transfers between devices  42.9 us (21%)
  local copies, waits for them, and re-layouts  6.19 us (3%)
    ppermute x33, waiting for transfers between devices, permuted(): lax.ppermute(value, axis, [(i, target(i) % count) for i in range(count)])  38.8 us
    pallas_call x2, Pallas kernels, run_third(): call(kernel, (struct((size, width), F32), struct((size, width), F32), *[p...  28 us
    ppermute x33, starting transfers between devices, permuted(): lax.ppermute(value, axis, [(i, target(i) % count) for i in range(count)])  27.3 us
    pallas_call x1, Pallas kernels, run_second(): call(second_kernel, (struct((points, width), F32), struct((4 * width, wid...  19.6 us
    ppermute x8, waiting for transfers between devices, exchanged(): moved.append(lax.ppermute(parts(digit ^ d), 'lon', pairs))  17.7 us
    pallas_call x2, Pallas kernels, run_first(): call(kernel if packs else functools.partial(without, kernel, 8, 3), (stru...  17.1 us
    ppermute x4, waiting for transfers between devices, spread(): got = lax.ppermute(value, 'lon', pairs)  14.6 us
    ppermute x8, starting transfers between devices, exchanged(): moved.append(lax.ppermute(parts(digit ^ d), 'lon', pairs))  10.1 us
  transfers between devices with their start and end apart: 45, of which 24 were waited for; matrix products, arithmetic and copies ran while one was open for 2% of the time, Pallas kernels for 21%

profile of v6, /device:TPU:0, one launch (start us, length us, event | category | flops | bytes accessed | tf_op | source)
XLA Modules:
  0.0 199.5 jit_solution(3752178821638240510)
XLA Ops:
  0.6 2.6 %shard_map.103 = (bf16[512,384]{1,0:T(8,128)(2,1)}, bf16[512,384]{1,0:T(8,128)(2,1)}) custom-call(bf16[1024,384]{1,0:T(8,128)(2,1)} %bitcast.13, s32[32,32]{1,0:T(8,128)} %vis_ref.5, bf16[384]{0:T(512)(128)(2,1)} %mask_ref.3, f32[2,384]{1,0:T(2,128)} %gain_ref.11), custom_call_target="tpu_custom_call" | custom-call | flops 1600000000 | bytes 2000000 | tf_op jit(solution)/shard_map/pallas_call | solution.py:669
  3.2 3.0 %collective-permute-start = (bf16[512,384]{1,0:T(8,128)(2,1)}, bf16[512,384]{1,0:T(8,128)(2,1)S(1)}, u32[]{:S(2)}, u32[]{:S(2)}) collective-permute-start(bf16[512,384]{1,0:T(8,128)(2,1)} %get-tuple-element.92.refs_1_), channel_id=1, source_target_pairs={{0,2},{2,0},{4,6},{6,4},{8,10},{10,8},{12,14},{14,12},{1,3},{3,1},... | collective-permute-start | bytes 1179656 | tf_op jit(solution)/shard_map/ppermute | solution.py:47
  6.2 2.7 %shard_map.102 = (bf16[512,384]{1,0:T(8,128)(2,1)}, bf16[512,384]{1,0:T(8,128)(2,1)}) custom-call(bf16[1024,384]{1,0:T(8,128)(2,1)} %bitcast.14, s32[32,32]{1,0:T(8,128)} %vis_ref.5, bf16[384]{0:T(512)(128)(2,1)} %mask_ref.3, f32[2,384]{1,0:T(2,128)} %gain_ref.11), custom_call_target="tpu_custom_call" | custom-call | flops 1600000000 | bytes 2000000 | tf_op jit(solution)/shard_map/pallas_call | solution.py:669
  8.9 6.7 %collective-permute-done.refs_3_ = bf16[512,384]{1,0:T(8,128)(2,1)S(1)} collective-permute-done((bf16[512,384]{1,0:T(8,128)(2,1)}, bf16[512,384]{1,0:T(8,128)(2,1)S(1)}, u32[]{:S(2)}, u32[]{:S(2)}) %collective-permute-start) | collective-permute-done | bytes 393248 | tf_op jit(solution)/shard_map/ppermute | solution.py:47
  17.3 3.5 %collective-permute-start.2 = (bf16[512,384]{1,0:T(8,128)(2,1)}, bf16[512,384]{1,0:T(8,128)(2,1)S(1)}, u32[]{:S(2)}, u32[]{:S(2)}) collective-permute-start(bf16[512,384]{1,0:T(8,128)(2,1)} %get-tuple-element.93.n0), channel_id=1, source_target_pairs={{0,2},{2,0},{4,6},{6,4},{8,10},{10,8},{12,14},{14,12},{1,3},{3,1},... | collective-permute-start | bytes 1179656 | tf_op jit(solution)/shard_map/ppermute | solution.py:47
  21.4 6.4 %collective-permute-done.5.refs_4_ = bf16[512,384]{1,0:T(8,128)(2,1)} collective-permute-done((bf16[512,384]{1,0:T(8,128)(2,1)S(1)}, bf16[512,384]{1,0:T(8,128)(2,1)}, u32[]{:S(2)}, u32[]{:S(2)}) %collective-permute-start.5) | collective-permute-done | bytes 393248 | tf_op jit(solution)/shard_map/ppermute | solution.py:47
  27.8 2.3 %copy.12 = bf16[2,384,1152]{1,2,0:T(8,128)(2,1)} copy(bf16[2,384,1152]{2,1,0:T(8,128)(2,1)S(1)} %copy-done.9) | data formatting | bytes 3538944 | tf_op args[4]
  30.7 8.5 %shard_map.104 = (bf16[384,512]{1,0:T(8,128)(2,1)}, bf16[6,768,512]{2,1,0:T(8,128)(2,1)}, f32[6,8,512]{2,1,0:T(8,128)}, bf16[384,512]{1,0:T(8,128)(2,1)}, bf16[5...) custom-call(s32[1]{0:T(128)} %bitcast.refs_0_.lat_ref, ...), custom_call_target="tpu_custom_call" | custom-call | flops 6400000000 | bytes 8000000 | tf_op jit(solution)/shard_map/pallas_call | solution.py:515
  39.2 4.2 %collective-permute-done.3.n3 = bf16[512,384]{1,0:T(8,128)(2,1)S(1)} collective-permute-done((bf16[512,384]{1,0:T(8,128)(2,1)S(1)}, bf16[512,384]{1,0:T(8,128)(2,1)S(1)}, u32[]{:S(2)}, u32[]{:S(2)}) %collective-permute-start.3) | collective-permute-done | bytes 393248 | tf_op jit(solution)/shard_map/ppermute | solution.py:47
  45.9 8.6 %shard_map.105 = (bf16[384,512]{1,0:T(8,128)(2,1)}, bf16[6,768,512]{2,1,0:T(8,128)(2,1)}, f32[6,8,512]{2,1,0:T(8,128)}, bf16[384,512]{1,0:T(8,128)(2,1)}, bf16[5...) custom-call(s32[1]{0:T(128)} %bitcast.refs_0_.lat_ref, ...), custom_call_target="tpu_custom_call" | custom-call | flops 6400000000 | bytes 8000000 | tf_op jit(solution)/shard_map/pallas_call | solution.py:515
  55.4 3.9 %collective-permute-start.12 = (bf16[32,384]{1,0:T(8,128)(2,1)}, bf16[32,384]{1,0:T(8,128)(2,1)S(1)}, u32[]{:S(2)}, u32[]{:S(2)}) collective-permute-start(bf16[32,384]{1,0:T(8,128)(2,1)} %get-tuple-element.113), channel_id=1, source_target_pairs={{0,14},{2,0},{4,2},{6,4},{8,6},{10,8},{12,10},{14,12},{1,15},{3,1}... | collective-permute-start | bytes 73736 | tf_op jit(solution)/shard_map/ppermute | solution.py:47
  59.3 2.0 %collective-permute-done.11.left_ref = bf16[32,384]{1,0:T(8,128)(2,1)S(1)} collective-permute-done((bf16[32,384]{1,0:T(8,128)(2,1)}, bf16[32,384]{1,0:T(8,128)(2,1)S(1)}, u32[]{:S(2)}, u32[]{:S(2)}) %collective-permute-start.11) | collective-permute-done | bytes 24608 | tf_op jit(solution)/shard_map/ppermute | solution.py:47
  63.3 19.6 %shard_map.106 = (f32[1024,384]{1,0:T(8,128)}, bf16[1536,384]{1,0:T(8,128)(2,1)}, bf16[32,384]{1,0:T(8,128)(2,1)}, bf16[48,384]{1,0:T(8,128)(2,1)}, bf16[48,384]{1,0:T(8,128)(2,1)}) custom-call(s32[1]{0:T(128)} %bitcast.refs_0_.lat_ref, bf16[512,384]{1,0:T(8,128)(2,1)} %get-tuple-element.109.na_ref, bf16[512,384]{1,0:T(8,128)(2,1)} %get-tuple-element.110.nb_ref, ...), custom_call_target="tpu_custom_call" | custom-call | flops 17600000000 | bytes 22000000 | tf_op jit(solution)/shard_map/pallas_call | solution.py:556
  84.7 4.8 %collective-permute-start.17 = (bf16[48,384]{1,0:T(8,128)(2,1)S(1)}, bf16[48,384]{1,0:T(8,128)(2,1)S(1)}, u32[]{:S(2)}, u32[]{:S(2)}) collective-permute-start(bf16[48,384]{1,0:T(8,128)(2,1)S(1)} %copy-done.28), channel_id=1, source_target_pairs={{0,14},{2,0},{4,2},{6,4},{8,6},{10,8},{12,10},{14,12},{1,15},{3,1}... | collective-permute-start | bytes 110600 | tf_op jit(solution)/shard_map/ppermute | solution.py:47
  89.5 1.8 collective-permute-done.16
  93.4 13.7 %shard_map.107 = (f32[512,384]{1,0:T(8,128)}, f32[512,384]{1,0:T(8,128)}, bf16[512,384]{1,0:T(8,128)(2,1)}, bf16[512,384]{1,0:T(8,128)(2,1)}, bf16[512,384]{1,0:...) custom-call(s32[1]{0:T(128)} %bitcast.refs_0_.lat_ref, ...), custom_call_target="tpu_custom_call" | custom-call | flops 10400000000 | bytes 13000000 | tf_op jit(solution)/shard_map/pallas_call | solution.py:603
  107.8 5.5 %collective-permute-start.26 = (bf16[96,384]{1,0:T(8,128)(2,1)S(1)}, bf16[96,384]{1,0:T(8,128)(2,1)S(1)}, u32[]{:S(2)}, u32[]{:S(2)}) collective-permute-start(bf16[96,384]{1,0:T(8,128)(2,1)S(1)} %get-tuple-element.183), channel_id=1, source_target_pairs={{0,8},{2,10},{4,12},{6,14},{8,0},{10,2},{12,4},{14,6},{1,9},{3,11}... | collective-permute-start | bytes 221192 | tf_op jit(solution)/shard_map/ppermute | solution.py:84
  113.8 5.7 %collective-permute-done.26 = bf16[96,384]{1,0:T(8,128)(2,1)S(1)} collective-permute-done((bf16[96,384]{1,0:T(8,128)(2,1)S(1)}, bf16[96,384]{1,0:T(8,128)(2,1)S(1)}, u32[]{:S(2)}, u32[]{:S(2)}) %collective-permute-start.26) | collective-permute-done | bytes 73760 | tf_op jit(solution)/shard_map/ppermute | solution.py:84
  119.8 2.5 %collective-permute-start.28 = (bf16[512,384]{1,0:T(8,128)(2,1)S(1)}, bf16[512,384]{1,0:T(8,128)(2,1)S(1)}, u32[]{:S(2)}, u32[]{:S(2)}) collective-permute-start(bf16[512,384]{1,0:T(8,128)(2,1)S(1)} %add_convert_fusion.6), channel_id=1, source_target_pairs={{0,12},{2,6},{4,0},{6,10},{8,4},{10,14},{12,8},{14,2},{1,13},{3,7}... | collective-permute-start | bytes 1179656 | tf_op jit(solution)/shard_map/ppermute | solution.py:47
  122.3 14.3 %shard_map.108 = (f32[512,384]{1,0:T(8,128)}, f32[512,384]{1,0:T(8,128)}, bf16[512,384]{1,0:T(8,128)(2,1)}, bf16[512,384]{1,0:T(8,128)(2,1)}, bf16[512,384]{1,0:...) custom-call(s32[1]{0:T(128)} %bitcast.refs_0_.lat_ref, ...), custom_call_target="tpu_custom_call" | custom-call | flops 10400000000 | bytes 13000000 | tf_op jit(solution)/shard_map/pallas_call | solution.py:603
  141.1 2.0 %collective-permute-start.34 = (bf16[512,384]{1,0:T(8,128)(2,1)S(1)}, bf16[512,384]{1,0:T(8,128)(2,1)S(1)}, u32[]{:S(2)}, u32[]{:S(2)}) collective-permute-start(bf16[512,384]{1,0:T(8,128)(2,1)S(1)} %add_convert_fusion.3), channel_id=1, source_target_pairs={{0,12},{2,6},{4,0},{6,10},{8,4},{10,14},{12,8},{14,2},{1,13},{3,7}... | collective-permute-start | bytes 1179656 | tf_op jit(solution)/shard_map/ppermute | solution.py:47
  143.1 7.8 %collective-permute-done.33 = bf16[384,384]{1,0:T(8,128)(2,1)S(1)} collective-permute-done((bf16[384,384]{1,0:T(8,128)(2,1)S(1)}, bf16[384,384]{1,0:T(8,128)(2,1)S(1)}, u32[]{:S(2)}, u32[]{:S(2)}) %collective-permute-start.33) | collective-permute-done | bytes 294944 | tf_op jit(solution)/shard_map/ppermute | solution.py:84
  152.6 5.9 %collective-permute-done.35.refs_5_ = bf16[512,384]{1,0:T(8,128)(2,1)S(1)} collective-permute-done((bf16[512,384]{1,0:T(8,128)(2,1)S(1)}, bf16[512,384]{1,0:T(8,128)(2,1)S(1)}, u32[]{:S(2)}, u32[]{:S(2)}) %collective-permute-start.35) | collective-permute-done | bytes 393248 | tf_op jit(solution)/shard_map/ppermute | solution.py:47
  161.2 2.2 %collective-permute-start.38 = (bf16[96,384]{1,0:T(8,128)(2,1)S(1)}, bf16[96,384]{1,0:T(8,128)(2,1)S(1)}, u32[]{:S(2)}, u32[]{:S(2)}) collective-permute-start(bf16[96,384]{1,0:T(8,128)(2,1)S(1)} %get-tuple-element.179), channel_id=1, source_target_pairs={{0,12},{2,14},{4,8},{6,10},{8,4},{10,6},{12,0},{14,2},{1,13},{3,15... | collective-permute-start | bytes 221192 | tf_op jit(solution)/shard_map/ppermute | solution.py:84
  163.4 3.2 %collective-permute-done.37 = bf16[96,384]{1,0:T(8,128)(2,1)S(1)} collective-permute-done((bf16[96,384]{1,0:T(8,128)(2,1)S(1)}, bf16[96,384]{1,0:T(8,128)(2,1)S(1)}, u32[]{:S(2)}, u32[]{:S(2)}) %collective-permute-start.37) | collective-permute-done | bytes 73760 | tf_op jit(solution)/shard_map/ppermute | solution.py:84
  169.0 2.2 %collective-permute-start.41 = (bf16[192,384]{1,0:T(8,128)(2,1)S(1)}, bf16[192,384]{1,0:T(8,128)(2,1)S(1)}, u32[]{:S(2)}, u32[]{:S(2)}) collective-permute-start(bf16[192,384]{1,0:T(8,128)(2,1)S(1)} %constant_dynamic-update-slice_fusion.5), channel_id=1, source_target_pairs={{0,8},{2,10},{4,12},{6,14},{8,0},{10,2},{12,4},{14,6},{1,9},{3,11}... | collective-permute-start | bytes 442376 | tf_op jit(solution)/shard_map/ppermute | solution.py:104
  171.2 2.1 %collective-permute-start.42 = (bf16[192,384]{1,0:T(8,128)(2,1)S(1)}, bf16[192,384]{1,0:T(8,128)(2,1)S(1)}, u32[]{:S(2)}, u32[]{:S(2)}) collective-permute-start(bf16[192,384]{1,0:T(8,128)(2,1)S(1)} %constant_dynamic-update-slice_fusion.5), channel_id=1, source_target_pairs={{0,12},{2,14},{4,8},{6,10},{8,4},{10,6},{12,0},{14,2},{1,13},{3,15... | collective-permute-start | bytes 442376 | tf_op jit(solution)/shard_map/ppermute | solution.py:104
  173.4 2.3 %collective-permute-done.40 = bf16[192,384]{1,0:T(8,128)(2,1)S(1)} collective-permute-done((bf16[192,384]{1,0:T(8,128)(2,1)S(1)}, bf16[192,384]{1,0:T(8,128)(2,1)S(1)}, u32[]{:S(2)}, u32[]{:S(2)}) %collective-permute-start.40) | collective-permute-done | bytes 147488 | tf_op jit(solution)/shard_map/ppermute | solution.py:104
  175.8 6.2 %collective-permute-done.41 = bf16[192,384]{1,0:T(8,128)(2,1)S(1)} collective-permute-done((bf16[192,384]{1,0:T(8,128)(2,1)S(1)}, bf16[192,384]{1,0:T(8,128)(2,1)S(1)}, u32[]{:S(2)}, u32[]{:S(2)}) %collective-permute-start.41) | collective-permute-done | bytes 147488 | tf_op jit(solution)/shard_map/ppermute | solution.py:104
  186.8 6.1 %collective-permute-done.43 = bf16[768,384]{1,0:T(8,128)(2,1)S(1)} collective-permute-done((bf16[768,384]{1,0:T(8,128)(2,1)S(1)}, bf16[768,384]{1,0:T(8,128)(2,1)S(1)}, u32[]{:S(2)}, u32[]{:S(2)}) %collective-permute-start.43) | collective-permute-done | bytes 589856 | tf_op jit(solution)/shard_map/ppermute | solution.py:104
  193.1 2.8 %collective-permute-done.44.other_ref = bf16[1536,384]{1,0:T(8,128)(2,1)S(1)} collective-permute-done((bf16[1536,384]{1,0:T(8,128)(2,1)S(1)}, bf16[1536,384]{1,0:T(8,128)(2,1)S(1)}, u32[]{:S(2)}, u32[]{:S(2)}) %collective-permute-start.44) | collective-permute-done | bytes 1179680 | tf_op jit(solution)/shard_map/ppermute | solution.py:47
  195.9 3.6 %shard_map.111 = (f32[2,384,1152]{2,1,0:T(8,128)}, f32[2,384,384]{2,1,0:T(8,128)}, f32[2,384]{1,0:T(2,128)}) custom-call(s32[1]{0:T(128)} %bitcast.refs_0_.lat_ref, bf16[1536,384]{1,0:T(8,128)(2,1)S(1)} %constant_dynamic-update-slice_fusion.7.mine_ref, bf16[1536,384]{1,0:T(8,128)(2,1)S(1)} %collective-permute-done.44.other_ref, ...), custom_call_target="tpu_custom_call" | custom-call | flops 4000000000 | bytes 5000000 | tf_op jit(solution)/shard_map/pallas_call | solution.py:797
  (171 shorter events, 29.5 us)
Async XLA Ops:
  3.2 12.4 %collective-permute-start = (bf16[512,384]{1,0:T(8,128)(2,1)}, bf16[512,384]{1,0:T(8,128)(2,1)S(1)}, u32[]{:S(2)}, u32[]{:S(2)}) collective-permute-start(bf16[512,384]{1,0:T(8,128)(2,1)} %get-tuple-element.92.refs_1_), channel_id=1, source_target_pairs={{0,2},{2,0},{4,6},{6,4},{8,10},{10,8},{12,14},{14,12},{1,3},{3,1},... | collective-permute-start | bytes 1179656 | tf_op jit(solution)/shard_map/ppermute | solution.py:47
  15.6 12.2 %collective-permute-start.5 = (bf16[512,384]{1,0:T(8,128)(2,1)S(1)}, bf16[512,384]{1,0:T(8,128)(2,1)}, u32[]{:S(2)}, u32[]{:S(2)}) collective-permute-start(bf16[512,384]{1,0:T(8,128)(2,1)S(1)} %collective-permute-done.refs_3_), channel_id=1, source_target_pairs={{0,4},{2,14},{4,8},{6,2},{8,12},{10,6},{12,0},{14,10},{1,5},{3,15}... | collective-permute-start | bytes 1179656 | tf_op jit(solution)/shard_map/ppermute | solution.py:47
  17.3 13.2 %collective-permute-start.2 = (bf16[512,384]{1,0:T(8,128)(2,1)}, bf16[512,384]{1,0:T(8,128)(2,1)S(1)}, u32[]{:S(2)}, u32[]{:S(2)}) collective-permute-start(bf16[512,384]{1,0:T(8,128)(2,1)} %get-tuple-element.93.n0), channel_id=1, source_target_pairs={{0,2},{2,0},{4,6},{6,4},{8,10},{10,8},{12,14},{14,12},{1,3},{3,1},... | collective-permute-start | bytes 1179656 | tf_op jit(solution)/shard_map/ppermute | solution.py:47
  20.9 9.7 %collective-permute-start.4 = (bf16[512,384]{1,0:T(8,128)(2,1)S(1)}, bf16[512,384]{1,0:T(8,128)(2,1)}, u32[]{:S(2)}, u32[]{:S(2)}) collective-permute-start(bf16[512,384]{1,0:T(8,128)(2,1)S(1)} %copy-done.23), channel_id=1, source_target_pairs={{0,1},{1,0},{2,3},{3,2},{4,5},{5,4},{6,7},{7,6},{8,9},{9,8},{10,11... | collective-permute-start | bytes 1179656 | tf_op jit(solution)/shard_map/ppermute | solution.py:47
  20.9 9.9 %collective-permute-start.6 = (bf16[512,384]{1,0:T(8,128)(2,1)S(1)}, bf16[512,384]{1,0:T(8,128)(2,1)}, u32[]{:S(2)}, u32[]{:S(2)}) collective-permute-start(bf16[512,384]{1,0:T(8,128)(2,1)S(1)} %collective-permute-done.refs_3_), channel_id=1, source_target_pairs={{0,1},{1,0},{2,3},{3,2},{4,5},{5,4},{6,7},{7,6},{8,9},{9,8},{10,11... | collective-permute-start | bytes 1179656 | tf_op jit(solution)/shard_map/ppermute | solution.py:47
  30.1 13.4 %collective-permute-start.1 = (bf16[512,384]{1,0:T(8,128)(2,1)S(1)}, bf16[512,384]{1,0:T(8,128)(2,1)S(1)}, u32[]{:S(2)}, u32[]{:S(2)}) collective-permute-start(bf16[512,384]{1,0:T(8,128)(2,1)S(1)} %copy-done.17), channel_id=1, source_target_pairs={{0,1},{1,0},{2,3},{3,2},{4,5},{5,4},{6,7},{7,6},{8,9},{9,8},{10,11... | collective-permute-start | bytes 1179656 | tf_op jit(solution)/shard_map/ppermute | solution.py:47
  30.6 12.9 %collective-permute-start.3 = (bf16[512,384]{1,0:T(8,128)(2,1)S(1)}, bf16[512,384]{1,0:T(8,128)(2,1)S(1)}, u32[]{:S(2)}, u32[]{:S(2)}) collective-permute-start(bf16[512,384]{1,0:T(8,128)(2,1)S(1)} %collective-permute-done.2.n2), channel_id=1, source_target_pairs={{0,4},{2,14},{4,8},{6,2},{8,12},{10,6},{12,0},{14,10},{1,5},{3,15}... | collective-permute-start | bytes 1179656 | tf_op jit(solution)/shard_map/ppermute | solution.py:47
  30.6 12.9 %collective-permute-start.8 = (bf16[512,384]{1,0:T(8,128)(2,1)S(1)}, bf16[512,384]{1,0:T(8,128)(2,1)S(1)}, u32[]{:S(2)}, u32[]{:S(2)}) collective-permute-start(bf16[512,384]{1,0:T(8,128)(2,1)S(1)} %collective-permute-done.2.n2), channel_id=1, source_target_pairs={{0,1},{1,0},{2,3},{3,2},{4,5},{5,4},{6,7},{7,6},{8,9},{9,8},{10,11... | collective-permute-start | bytes 1179656 | tf_op jit(solution)/shard_map/ppermute | solution.py:47
  54.5 6.8 %collective-permute-start.11 = (bf16[32,384]{1,0:T(8,128)(2,1)}, bf16[32,384]{1,0:T(8,128)(2,1)S(1)}, u32[]{:S(2)}, u32[]{:S(2)}) collective-permute-start(bf16[32,384]{1,0:T(8,128)(2,1)} %get-tuple-element.112), channel_id=1, source_target_pairs={{0,2},{2,4},{4,6},{6,8},{8,10},{10,12},{12,14},{14,0},{1,3},{3,5},... | collective-permute-start | bytes 73736 | tf_op jit(solution)/shard_map/ppermute | solution.py:47
  55.4 6.0 %collective-permute-start.12 = (bf16[32,384]{1,0:T(8,128)(2,1)}, bf16[32,384]{1,0:T(8,128)(2,1)S(1)}, u32[]{:S(2)}, u32[]{:S(2)}) collective-permute-start(bf16[32,384]{1,0:T(8,128)(2,1)} %get-tuple-element.113), channel_id=1, source_target_pairs={{0,14},{2,0},{4,2},{6,4},{8,6},{10,8},{12,10},{14,12},{1,15},{3,1}... | collective-permute-start | bytes 73736 | tf_op jit(solution)/shard_map/ppermute | solution.py:47
  84.1 8.6 %collective-permute-start.20 = (bf16[768,384]{1,0:T(8,128)(2,1)S(1)}, bf16[768,384]{1,0:T(8,128)(2,1)S(1)}, u32[]{:S(2)}, u32[]{:S(2)}) collective-permute-start(bf16[768,384]{1,0:T(8,128)(2,1)S(1)} %constant_dynamic-slice_fusion.8), channel_id=1, source_target_pairs={{0,1},{1,0},{2,3},{3,2},{4,5},{5,4},{6,7},{7,6},{8,9},{9,8},{10,11... | collective-permute-start | bytes 1769480 | tf_op jit(solution)/shard_map/ppermute | solution.py:47
  84.5 5.0 %collective-permute-start.15 = (bf16[32,384]{1,0:T(8,128)(2,1)}, bf16[32,384]{1,0:T(8,128)(2,1)S(1)}, u32[]{:S(2)}, u32[]{:S(2)}) collective-permute-start(bf16[32,384]{1,0:T(8,128)(2,1)} %get-tuple-element.115), channel_id=1, source_target_pairs={{0,1},{1,0},{2,3},{3,2},{4,5},{5,4},{6,7},{7,6},{8,9},{9,8},{10,11... | collective-permute-start | bytes 73736 | tf_op jit(solution)/shard_map/ppermute | solution.py:47
  84.7 6.7 %collective-permute-start.16 = (bf16[48,384]{1,0:T(8,128)(2,1)S(1)}, bf16[48,384]{1,0:T(8,128)(2,1)S(1)}, u32[]{:S(2)}, u32[]{:S(2)}) collective-permute-start(bf16[48,384]{1,0:T(8,128)(2,1)S(1)} %copy-done.29), channel_id=1, source_target_pairs={{0,2},{2,4},{4,6},{6,8},{8,10},{10,12},{12,14},{14,0},{1,3},{3,5},... | collective-permute-start | bytes 110600 | tf_op jit(solution)/shard_map/ppermute | solution.py:47
  84.7 6.7 %collective-permute-start.17 = (bf16[48,384]{1,0:T(8,128)(2,1)S(1)}, bf16[48,384]{1,0:T(8,128)(2,1)S(1)}, u32[]{:S(2)}, u32[]{:S(2)}) collective-permute-start(bf16[48,384]{1,0:T(8,128)(2,1)S(1)} %copy-done.28), channel_id=1, source_target_pairs={{0,14},{2,0},{4,2},{6,4},{8,6},{10,8},{12,10},{14,12},{1,15},{3,1}... | collective-permute-start | bytes 110600 | tf_op jit(solution)/shard_map/ppermute | solution.py:47
  93.4 13.8 %collective-permute-start.21 = (bf16[384,384]{1,0:T(8,128)(2,1)S(1)}, bf16[384,384]{1,0:T(8,128)(2,1)S(1)}, u32[]{:S(2)}, u32[]{:S(2)}) collective-permute-start(bf16[384,384]{1,0:T(8,128)(2,1)S(1)} %constant_dynamic-slice_fusion.7), channel_id=1, source_target_pairs={{0,2},{2,0},{4,6},{6,4},{8,10},{10,8},{12,14},{14,12},{1,3},{3,1},... | collective-permute-start | bytes 884744 | tf_op jit(solution)/shard_map/ppermute | solution.py:84
  107.3 12.3 %collective-permute-start.24 = (bf16[512,384]{1,0:T(8,128)(2,1)}, bf16[512,384]{1,0:T(8,128)(2,1)S(1)}, u32[]{:S(2)}, u32[]{:S(2)}) collective-permute-start(bf16[512,384]{1,0:T(8,128)(2,1)} %get-tuple-element.137), channel_id=1, source_target_pairs={{0,1},{1,0},{2,3},{3,2},{4,5},{5,4},{6,7},{7,6},{8,9},{9,8},{10,11... | collective-permute-start | bytes 1179656 | tf_op jit(solution)/shard_map/ppermute | solution.py:47
  107.7 5.6 %collective-permute-start.25 = (bf16[96,384]{1,0:T(8,128)(2,1)S(1)}, bf16[96,384]{1,0:T(8,128)(2,1)S(1)}, u32[]{:S(2)}, u32[]{:S(2)}) collective-permute-start(bf16[96,384]{1,0:T(8,128)(2,1)S(1)} %get-tuple-element.181), channel_id=1, source_target_pairs={{0,4},{2,6},{4,0},{6,2},{8,12},{10,14},{12,8},{14,10},{1,5},{3,7},... | collective-permute-start | bytes 221192 | tf_op jit(solution)/shard_map/ppermute | solution.py:84
  107.8 11.7 %collective-permute-start.26 = (bf16[96,384]{1,0:T(8,128)(2,1)S(1)}, bf16[96,384]{1,0:T(8,128)(2,1)S(1)}, u32[]{:S(2)}, u32[]{:S(2)}) collective-permute-start(bf16[96,384]{1,0:T(8,128)(2,1)S(1)} %get-tuple-element.183), channel_id=1, source_target_pairs={{0,8},{2,10},{4,12},{6,14},{8,0},{10,2},{12,4},{14,6},{1,9},{3,11}... | collective-permute-start | bytes 221192 | tf_op jit(solution)/shard_map/ppermute | solution.py:84
  113.3 6.2 %collective-permute-start.27 = (bf16[96,384]{1,0:T(8,128)(2,1)S(1)}, bf16[96,384]{1,0:T(8,128)(2,1)S(1)}, u32[]{:S(2)}, u32[]{:S(2)}) collective-permute-start(bf16[96,384]{1,0:T(8,128)(2,1)S(1)} %get-tuple-element.182), channel_id=1, source_target_pairs={{0,12},{2,14},{4,8},{6,10},{8,4},{10,6},{12,0},{14,2},{1,13},{3,15... | collective-permute-start | bytes 221192 | tf_op jit(solution)/shard_map/ppermute | solution.py:84
  113.3 6.4 %collective-permute-start.23 = (bf16[512,384]{1,0:T(8,128)(2,1)S(1)}, bf16[512,384]{1,0:T(8,128)(2,1)S(1)}, u32[]{:S(2)}, u32[]{:S(2)}) collective-permute-start(bf16[512,384]{1,0:T(8,128)(2,1)S(1)} %copy-done.26), channel_id=1, source_target_pairs={{0,1},{1,0},{2,3},{3,2},{4,5},{5,4},{6,7},{7,6},{8,9},{9,8},{10,11... | collective-permute-start | bytes 1179656 | tf_op jit(solution)/shard_map/ppermute | solution.py:47
  113.3 6.5 %collective-permute-start.22 = (bf16[512,384]{1,0:T(8,128)(2,1)S(1)}, bf16[512,384]{1,0:T(8,128)(2,1)S(1)}, u32[]{:S(2)}, u32[]{:S(2)}) collective-permute-start(bf16[512,384]{1,0:T(8,128)(2,1)S(1)} %copy-done.25), channel_id=1, source_target_pairs={{0,1},{1,0},{2,3},{3,2},{4,5},{5,4},{6,7},{7,6},{8,9},{9,8},{10,11... | collective-permute-start | bytes 1179656 | tf_op jit(solution)/shard_map/ppermute | solution.py:47
  119.8 16.9 %collective-permute-start.28 = (bf16[512,384]{1,0:T(8,128)(2,1)S(1)}, bf16[512,384]{1,0:T(8,128)(2,1)S(1)}, u32[]{:S(2)}, u32[]{:S(2)}) collective-permute-start(bf16[512,384]{1,0:T(8,128)(2,1)S(1)} %add_convert_fusion.6), channel_id=1, source_target_pairs={{0,12},{2,6},{4,0},{6,10},{8,4},{10,14},{12,8},{14,2},{1,13},{3,7}... | collective-permute-start | bytes 1179656 | tf_op jit(solution)/shard_map/ppermute | solution.py:47
  141.0 9.9 %collective-permute-start.33 = (bf16[384,384]{1,0:T(8,128)(2,1)S(1)}, bf16[384,384]{1,0:T(8,128)(2,1)S(1)}, u32[]{:S(2)}, u32[]{:S(2)}) collective-permute-start(bf16[384,384]{1,0:T(8,128)(2,1)S(1)} %constant_dynamic-slice_fusion.3), channel_id=1, source_target_pairs={{0,2},{2,0},{4,6},{6,4},{8,10},{10,8},{12,14},{14,12},{1,3},{3,1},... | collective-permute-start | bytes 884744 | tf_op jit(solution)/shard_map/ppermute | solution.py:84
  141.1 11.5 %collective-permute-start.34 = (bf16[512,384]{1,0:T(8,128)(2,1)S(1)}, bf16[512,384]{1,0:T(8,128)(2,1)S(1)}, u32[]{:S(2)}, u32[]{:S(2)}) collective-permute-start(bf16[512,384]{1,0:T(8,128)(2,1)S(1)} %add_convert_fusion.3), channel_id=1, source_target_pairs={{0,12},{2,6},{4,0},{6,10},{8,4},{10,14},{12,8},{14,2},{1,13},{3,7}... | collective-permute-start | bytes 1179656 | tf_op jit(solution)/shard_map/ppermute | solution.py:47
  143.1 15.4 %collective-permute-start.35 = (bf16[512,384]{1,0:T(8,128)(2,1)S(1)}, bf16[512,384]{1,0:T(8,128)(2,1)S(1)}, u32[]{:S(2)}, u32[]{:S(2)}) collective-permute-start(bf16[512,384]{1,0:T(8,128)(2,1)S(1)} %add_convert_fusion.5), channel_id=1, source_target_pairs={{0,2},{2,0},{4,6},{6,4},{8,10},{10,8},{12,14},{14,12},{1,3},{3,1},... | collective-permute-start | bytes 1179656 | tf_op jit(solution)/shard_map/ppermute | solution.py:47
  158.5 10.3 %collective-permute-start.39 = (bf16[512,384]{1,0:T(8,128)(2,1)S(1)}, bf16[512,384]{1,0:T(8,128)(2,1)S(1)}, u32[]{:S(2)}, u32[]{:S(2)}) collective-permute-start(bf16[512,384]{1,0:T(8,128)(2,1)S(1)} %add_convert_fusion.2), channel_id=1, source_target_pairs={{0,2},{2,0},{4,6},{6,4},{8,10},{10,8},{12,14},{14,12},{1,3},{3,1},... | collective-permute-start | bytes 1179656 | tf_op jit(solution)/shard_map/ppermute | solution.py:47
  159.4 7.1 %collective-permute-start.37 = (bf16[96,384]{1,0:T(8,128)(2,1)S(1)}, bf16[96,384]{1,0:T(8,128)(2,1)S(1)}, u32[]{:S(2)}, u32[]{:S(2)}) collective-permute-start(bf16[96,384]{1,0:T(8,128)(2,1)S(1)} %get-tuple-element.180), channel_id=1, source_target_pairs={{0,8},{2,10},{4,12},{6,14},{8,0},{10,2},{12,4},{14,6},{1,9},{3,11}... | collective-permute-start | bytes 221192 | tf_op jit(solution)/shard_map/ppermute | solution.py:84
  161.2 6.3 %collective-permute-start.38 = (bf16[96,384]{1,0:T(8,128)(2,1)S(1)}, bf16[96,384]{1,0:T(8,128)(2,1)S(1)}, u32[]{:S(2)}, u32[]{:S(2)}) collective-permute-start(bf16[96,384]{1,0:T(8,128)(2,1)S(1)} %get-tuple-element.179), channel_id=1, source_target_pairs={{0,12},{2,14},{4,8},{6,10},{8,4},{10,6},{12,0},{14,2},{1,13},{3,15... | collective-permute-start | bytes 221192 | tf_op jit(solution)/shard_map/ppermute | solution.py:84
  168.9 6.9 %collective-permute-start.40 = (bf16[192,384]{1,0:T(8,128)(2,1)S(1)}, bf16[192,384]{1,0:T(8,128)(2,1)S(1)}, u32[]{:S(2)}, u32[]{:S(2)}) collective-permute-start(bf16[192,384]{1,0:T(8,128)(2,1)S(1)} %constant_dynamic-update-slice_fusion.5), channel_id=1, source_target_pairs={{0,4},{2,6},{4,0},{6,2},{8,12},{10,14},{12,8},{14,10},{1,5},{3,7},... | collective-permute-start | bytes 442376 | tf_op jit(solution)/shard_map/ppermute | solution.py:104
  169.0 13.0 %collective-permute-start.41 = (bf16[192,384]{1,0:T(8,128)(2,1)S(1)}, bf16[192,384]{1,0:T(8,128)(2,1)S(1)}, u32[]{:S(2)}, u32[]{:S(2)}) collective-permute-start(bf16[192,384]{1,0:T(8,128)(2,1)S(1)} %constant_dynamic-update-slice_fusion.5), channel_id=1, source_target_pairs={{0,8},{2,10},{4,12},{6,14},{8,0},{10,2},{12,4},{14,6},{1,9},{3,11}... | collective-permute-start | bytes 442376 | tf_op jit(solution)/shard_map/ppermute | solution.py:104
  171.2 10.8 %collective-permute-start.42 = (bf16[192,384]{1,0:T(8,128)(2,1)S(1)}, bf16[192,384]{1,0:T(8,128)(2,1)S(1)}, u32[]{:S(2)}, u32[]{:S(2)}) collective-permute-start(bf16[192,384]{1,0:T(8,128)(2,1)S(1)} %constant_dynamic-update-slice_fusion.5), channel_id=1, source_target_pairs={{0,12},{2,14},{4,8},{6,10},{8,4},{10,6},{12,0},{14,2},{1,13},{3,15... | collective-permute-start | bytes 442376 | tf_op jit(solution)/shard_map/ppermute | solution.py:104
  182.1 10.8 %collective-permute-start.43 = (bf16[768,384]{1,0:T(8,128)(2,1)S(1)}, bf16[768,384]{1,0:T(8,128)(2,1)S(1)}, u32[]{:S(2)}, u32[]{:S(2)}) collective-permute-start(bf16[768,384]{1,0:T(8,128)(2,1)S(1)} %constant_dynamic-update-slice_fusion.9), channel_id=1, source_target_pairs={{0,2},{2,0},{4,6},{6,4},{8,10},{10,8},{12,14},{14,12},{1,3},{3,1},... | collective-permute-start | bytes 1769480 | tf_op jit(solution)/shard_map/ppermute | solution.py:104
  (48 other events, 283.8 us)

commit v7 on v6

--- a/solution.py
+++ b/solution.py
@@ -2,6 +2,7 @@
 
 import jax
 import jax.numpy as jnp
+import numpy as np
 from jax import lax
 from jax.experimental import pallas as pl
 from jax.experimental.pallas import tpu as pltpu
@@ -147,27 +148,40 @@
     )
 
 
-def shown_column(visible, base, tile):
+def shown_column(visible, token):
     rows, cols = visible.shape
-    token = base + iota((tile, rows), 0)
+    tile = token.shape[0]
     of_row = nn(one_hot(token // cols == iota((tile, rows), 1)), visible.astype(F32).astype(BF16))
-    token = base + iota((tile, cols), 0)
     mine = token % cols == iota((tile, cols), 1)
     return jnp.sum(jnp.where(mine, of_row, 0.0), axis=1, keepdims=True)
 
 
-def start_kernel(first, tok_ref, vis_ref, mask_ref, gain_ref, start_ref, normal_ref):
-    tile, width = tok_ref.shape
-    base = first + pl.program_id(0) * tile
-    shown = shown_column(vis_ref[...], base, tile)
-    x = jnp.where(shown > 0.5, tok_ref[...].astype(F32), mask_ref[...].astype(F32).reshape(1, width))
+def token_order(rows, cols):
+    row, col = np.divmod(np.arange(rows * cols), cols)
+    border = (row == 0) | (row == rows - 1) | (col == 0) | (col == cols - 1)
+    order = np.argsort(~border, kind="stable").astype(np.int32)
+    return order, np.argsort(order, kind="stable").astype(np.int32)
+
+
+def picked(places, values):
+    count = values.shape[0]
+    return nn(one_hot(places == iota((places.shape[0], count), 1)), values)
+
+
+def start_kernel(order_ref, tok_ref, vis_ref, mask_ref, gain_ref, start_ref, normal_ref):
+    width = tok_ref.shape[1]
+    token = order_ref[...]
+    shown = shown_column(vis_ref[...], token)
+    x = jnp.where(
+        shown > 0.5, picked(token, tok_ref[...]), mask_ref[...].astype(F32).reshape(1, width)
+    )
     start_ref[...] = x.astype(BF16)
     xhat, _ = norm_parts(x)
     normal_ref[...] = (xhat * gain_ref[0:1, :]).astype(BF16)
 
 
 def first_kernel(
-    first, lat_ref, n0, n1, n2, n3, n4, n5, start_ref, row_in, left_in, right_in,
+    lat_ref, order_ref, n0, n1, n2, n3, n4, n5, start_ref,
     wt_ref, wo_ref, gain_ref,
     q_ref, kv_ref, p_ref, mixed_ref, h_ref, normal_ref, row_ref, left_ref, right_ref,
     w_s, pack_s,
@@ -202,8 +216,7 @@
     step = pl.program_id(0)
     brow = jnp.where(lat_ref[0] == 0, 31, 0)
     slot = iota((96, tile), 0)
-    token = first + step * tile + iota((96, tile), 1)
-    r, c = token // 32, token % 32
+    r, c = order_ref[...] // 32, order_ref[...] % 32
     pick = one_hot(
         ((slot < 32) & (r == brow) & (c == slot))
         | ((slot >= 32) & (slot < 64) & (c == 0) & (r == slot - 32))
@@ -212,9 +225,7 @@
 
     @pl.when(step == 0)
     def _():
-        for i, ref in enumerate((row_in, left_in, right_in)):
-            known = jnp.zeros((32, width), F32) if ref is None else ref[...].astype(F32)
-            pack_s[i * 32 : i * 32 + 32, :] = known
+        pack_s[...] = jnp.zeros_like(pack_s)
 
     pack_s[...] += nn(pick, normal)
 
@@ -235,9 +246,9 @@
 
 
 def second_kernel(
-    lat_ref, na_ref, nb_ref, row_ref, left_ref, right_ref, dleft_ref, dright_ref,
+    lat_ref, place_ref, na_ref, nb_ref, row_ref, left_ref, right_ref, dleft_ref, dright_ref,
     w_all, wo_all, cot_ref,
-    dn_ref, dw_ref, brow_ref, bleft_ref, bright_ref,
+    both_ref, dw_ref, brow_ref, bleft_ref, bright_ref,
     dq_ref, dk_ref, dv_ref, mixed_s, dkh_ref, dvh_ref, halo_s,
     q_s, k_s, v_s, kc_s, vc_s, dk_s, dv_s, dkc_s, dvc_s, do_s, mask_s, normal_s,
 ):
@@ -254,8 +265,10 @@
     corners += nn(one_hot(sent & (a == 1)), dright_ref[...])
     halo_s[CORNER:HALO, :] = corners.astype(BF16)
     halo = halo_s[...]
-    normal_s[0 : points // 2, :] = na_ref[...]
-    normal_s[points // 2 : points, :] = nb_ref[...]
+    ordered = jnp.concatenate([na_ref[...], nb_ref[...]], 0)
+    for at in range(0, points, 256):
+        rows = slice(at, at + 256)
+        normal_s[rows, :] = picked(place_ref[rows, :], ordered).astype(BF16)
     normal = normal_s[...]
     scale = head**-0.5
     q_s[...] = (nn(normal, w_ref[:, 0:width]).astype(BF16).astype(F32) * scale).astype(BF16)
@@ -279,6 +292,7 @@
     dk_s[...] = jnp.zeros_like(dk_s)
     dv_s[...] = jnp.zeros_like(dv_s)
     cot = cot_ref[...].astype(BF16)
+    both_ref[:, width : 2 * width] = cot
     do_s[...] = nt(cot, wo_ref[...]).astype(BF16)
 
     key, query = iota((KEYS, 256), 0), iota((KEYS, 256), 1) % 128
@@ -346,11 +360,11 @@
         tn(dv_ref[...], normal) + tn(dvh_ref[...], halo)
     ).astype(BF16)
     dw_ref[3 * width : 4 * width, :] = nn(mixed_s[...], cot).astype(BF16)
-    dn_ref[...] = tt(dq_ref[...], wq) + nt(dk_ref[...], wk) + nt(dv_ref[...], wv)
+    both_ref[:, 0:width] = (tt(dq_ref[...], wq) + nt(dk_ref[...], wk) + nt(dv_ref[...], wv)).astype(BF16)
 
 
 def third_kernel(
-    first, lat_ref, n0, n1, n2, n3, n4, n5, q_ref, kv_ref, p_ref, mixed_ref, h_ref, dn1_ref, cot_ref,
+    lat_ref, order_ref, n0, n1, n2, n3, n4, n5, q_ref, kv_ref, p_ref, mixed_ref, h_ref, both_ref,
     packs_ref, wt_ref, wo_ref, gain_ref, dw_in,
     dh_ref, d0, d1, d2, d3, d4, d5, dw_ref, other_ref,
     dw_s, dmix_s, dkv_s, dq_s, dp_s, n_s,
@@ -366,21 +380,24 @@
     def _():
         dw_s[...] = jnp.zeros_like(dw_s) if dw_in is None else dw_in[...]
 
-    brow = jnp.where(lat_ref[0] == 0, 31, 0)
-    shape = (tile, RETURNED)
-    token = first + step * tile + iota(shape, 0)
-    r, c, slot = token // 32, token % 32, iota(shape, 1)
-    border = r == brow
-    place = one_hot(
-        (border & (slot < 32) & (slot == c))
-        | ((c == 0) & (slot < 64) & (slot == 32 + r))
-        | ((c == 31) & (slot < 112) & (slot == 80 + r))
-        | (border & (c == 0) & (slot == 128 + 33))
-        | (border & (c == 31) & (slot == 176 + 32))
-    )
-    dn = dn1_ref[...] + nn(place, packs_ref[...])
-    dh = cot_ref[...] + norm_back(h_ref[...].astype(F32), gain_ref[1:2, :], dn)
+    token = order_ref[...]
+    both = picked(token, both_ref[...])
+    dn = both[:, 0:width]
+    if packs_ref is not None:
+        brow = jnp.where(lat_ref[0] == 0, 31, 0)
+        r, c, slot = token // 32, token % 32, iota((tile, RETURNED), 1)
+        border = r == brow
+        place = one_hot(
+            (border & (slot < 32) & (slot == c))
+            | ((c == 0) & (slot < 64) & (slot == 32 + r))
+            | ((c == 31) & (slot < 112) & (slot == 80 + r))
+            | (border & (c == 0) & (slot == 128 + 33))
+            | (border & (c == 31) & (slot == 176 + 32))
+        )
+        dn = dn + nn(place, packs_ref[...])
+    dh = norm_back(h_ref[...].astype(F32), gain_ref[1:2, :], dn)
     dh_ref[...] = dh
+    dh = dh + both[:, width : 2 * width]
     dhb = dh.astype(BF16)
     dmix_s[...] = nt(wo_ref[...], dhb)
     dw_s[3 * width : 4 * width, :] += nn(mixed_ref[...], dhb)
@@ -422,14 +439,29 @@
             write_halves(lat_ref[0], dw_s, dw_ref, other_ref)
 
 
-def last_kernel(
-    first, start_ref, vis_ref, gain_ref, dh_ref, own_ref, far_ref, near_ref, prev_ref, out_ref
-):
-    tile, width = start_ref.shape
-    shown = shown_column(vis_ref[...], first + pl.program_id(0) * tile, tile)
-    dn = own_ref[...] + far_ref[...].astype(F32) + near_ref[...].astype(F32)
-    grad = dh_ref[...] + norm_back(start_ref[...].astype(F32), gain_ref[0:1, :], dn)
-    out_ref[...] = jnp.where(shown > 0.5, grad, 0.0)
+def last_kernel(place_ref, vis_ref, gain_ref, cot_ref, *refs):
+    inputs, out_ref, high_s, low_s = refs[:-3], refs[-3], refs[-2], refs[-1]
+    points, width = cot_ref.shape
+    tile = 256
+    at = 0
+    while inputs:
+        start_ref, dh_ref, own_ref, far_ref, near_ref = inputs[:5]
+        for lo in range(0, start_ref.shape[0], tile):
+            rows = slice(lo, lo + tile)
+            dn = own_ref[rows] + far_ref[rows].astype(F32) + near_ref[rows].astype(F32)
+            back = norm_back(start_ref[rows].astype(F32), gain_ref[0:1, :], dn)
+            grad = dh_ref[rows] + back
+            high = grad.astype(BF16)
+            high_s[at : at + tile, :] = high
+            low_s[at : at + tile, :] = (grad - high.astype(F32)).astype(BF16)
+            at += tile
+        inputs = inputs[5:]
+    for lo in range(0, points, tile):
+        rows = slice(lo, lo + tile)
+        place = place_ref[rows, :]
+        shown = shown_column(vis_ref[...], lo + iota((tile, 1), 0))
+        grad = picked(place, high_s[...]) + picked(place, low_s[...]) + cot_ref[rows]
+        out_ref[rows] = jnp.where(shown > 0.5, grad, 0.0)
 
 
 def weights_kernel(
@@ -504,16 +536,16 @@
 BACKWARD_TILE = 256
 
 
-def run_first(first, lat, blocks, start, packs, wt, output_weight, norm_gain_table):
+def run_first(first, lat, order, blocks, start, wt, output_weight, norm_gain_table):
     size, width = start.shape
     tile = min(FORWARD_TILE, size)
     struct = jax.ShapeDtypeStruct
     part = struct((size, width), BF16)
     tok_spec = token_spec(tile, width)
     feat_spec = pl.BlockSpec((width, tile), lambda i: (0, i))
-    kernel = functools.partial(first_kernel, first)
+    at = first // tile
     return call(
-        kernel if packs else functools.partial(without, kernel, 8, 3),
+        first_kernel,
         (
             struct((width, size), BF16),
             struct((6, 2 * width, size), BF16),
@@ -524,9 +556,8 @@
             *[struct((32, width), BF16)] * 3,
         ),
         grid=(size // tile,),
-        in_specs=[scalar()]
+        in_specs=[scalar(), pl.BlockSpec((1, tile), lambda i: (0, i + at))]
         + [tok_spec] * 7
-        + [fixed((32, width))] * len(packs)
         + [
             layer_spec(0, 3 * width, width),
             layer_spec(0, width, width),
@@ -544,10 +575,10 @@
         scratch=[pltpu.VMEM((6, 8, tile), F32), pltpu.VMEM((96, width), F32)],
         mib=LARGE_MIB,
         us=8,
-    )(lat, *blocks, start, *packs, wt, output_weight, norm_gain_table)
-
-
-def run_second(lat, normals, halos, query_key_value_weight, output_weight, cot):
+    )(lat, order, *blocks, start, wt, output_weight, norm_gain_table)
+
+
+def run_second(lat, places, normals, halos, query_key_value_weight, output_weight, cot):
     points, width = cot.shape
     struct = jax.ShapeDtypeStruct
     ext, slots = points + 64, points // 8
@@ -556,13 +587,13 @@
     return call(
         second_kernel,
         (
-            struct((points, width), F32),
+            struct((points, 2 * width), BF16),
             struct((4 * width, width), BF16),
             struct((32, width), BF16),
             struct((48, width), BF16),
             struct((48, width), BF16),
         ),
-        in_specs=[scalar()] + [whole()] * 10,
+        in_specs=[scalar()] + [whole()] * 11,
         out_specs=(whole(),) * 5,
         scratch=[
             across, every, every, across,
@@ -580,58 +611,55 @@
         ],
         mib=LARGE_MIB,
         us=22,
-    )(lat, *normals, *halos, query_key_value_weight, output_weight, cot)
+    )(lat, places, *normals, *halos, query_key_value_weight, output_weight, cot)
+
+
+def inner_third_kernel(*refs):
+    third_kernel(*refs[:14], None, *refs[14:17], None, *refs[17:25], None, *refs[25:])
 
 
 def run_third(
-    first, size, at, lat, blocks, kept, dn1, cot, packs, wt, output_weight, norm_gain_table, weights, final
+    first, lat, order, blocks, kept, both, packs, wt, output_weight, norm_gain_table, weights
 ):
     q0, kv0, p0, mixed0, h1 = kept
-    width = h1.shape[1]
+    size, width = h1.shape
+    points = both.shape[0]
     tile = min(BACKWARD_TILE, size)
     struct = jax.ShapeDtypeStruct
     part = struct((size, width), BF16)
-    tok_spec, from_spec = token_spec(tile, width), token_spec(tile, width, at)
-    skip = at // tile
-    feat_spec = pl.BlockSpec((width, tile), lambda i: (0, i + skip))
-    kernel = functools.partial(third_kernel, first)
-    extra = [] if weights is None else [weights]
-    if not extra:
-        kernel = functools.partial(without, kernel, 18, 1)
-    if not final:
-        kernel = functools.partial(without, kernel, 26 + len(extra) , 1)
+    tok_spec = token_spec(tile, width)
+    feat_spec = pl.BlockSpec((width, tile), lambda i: (0, i))
+    final = packs is not None
+    whole_dw, half_dw = (4 * width, width), (2 * width, width)
     return call(
-        kernel,
+        third_kernel if final else inner_third_kernel,
         (
             struct((size, width), F32),
             struct((size, width), F32),
             *[part] * 5,
-            *([struct((2 * width, width), BF16)] * 2 if final else [struct((4 * width, width), F32)]),
+            *([struct(half_dw, BF16)] * 2 if final else [struct(whole_dw, F32)]),
         ),
         grid=(size // tile,),
-        in_specs=[scalar()]
-        + [from_spec] * 6
+        in_specs=[scalar(), token_spec(tile, 1, first)]
+        + [tok_spec] * 6
         + [
             feat_spec,
-            pl.BlockSpec((6, 2 * width, tile), lambda i: (0, 0, i + skip)),
-            pl.BlockSpec((6, 8, tile), lambda i: (0, 0, i + skip)),
+            pl.BlockSpec((6, 2 * width, tile), lambda i: (0, 0, i)),
+            pl.BlockSpec((6, 8, tile), lambda i: (0, 0, i)),
             feat_spec,
-            from_spec,
+            tok_spec,
         ]
-        + [token_spec(tile, width, first)] * 2
+        + [fixed((points, 2 * width))]
+        + [fixed((RETURNED, width))] * final
         + [
-            fixed((RETURNED, width)),
             layer_spec(0, 3 * width, width),
             layer_spec(0, width, width),
             fixed((2, width)),
         ]
-        + [fixed((4 * width, width))] * len(extra),
-        out_specs=(
-            *[tok_spec] * 7,
-            *([fixed((2 * width, width))] * 2 if final else [fixed((4 * width, width))]),
-        ),
+        + [fixed(whole_dw)] * final,
+        out_specs=(*[tok_spec] * 7, *([fixed(half_dw)] * 2 if final else [fixed(whole_dw)])),
         scratch=[
-            pltpu.VMEM((4 * width, width), F32),
+            pltpu.VMEM(whole_dw, F32),
             pltpu.VMEM((width, tile), F32),
             pltpu.VMEM((2 * width, 6 * tile), BF16),
             pltpu.VMEM((width, tile), BF16),
@@ -641,8 +669,8 @@
         mib=LARGE_MIB,
         us=13,
     )(
-        lat, *blocks, q0, kv0, p0, mixed0, h1, dn1, cot, packs, wt, output_weight,
-        norm_gain_table, *extra,
+        lat, order, *blocks, q0, kv0, p0, mixed0, h1, both, *([packs] if final else []), wt,
+        output_weight, norm_gain_table, *([weights] if final else []),
     )
 
 
@@ -663,15 +691,20 @@
     gain_spec = fixed((2, width))
     wt_spec, wo_spec = layer_spec(0, 3 * width, width), layer_spec(0, width, width)
 
+    order, places = token_order(rows, cols)
+    order_row = jnp.asarray(order.reshape(1, points))
+    order, places = jnp.asarray(order.reshape(points, 1)), jnp.asarray(places.reshape(points, 1))
+
     small = 256
     starts, normals = [], []
     for first in firsts:
         start, normal = call(
-            functools.partial(start_kernel, first),
+            start_kernel,
             (part, part),
             grid=(size // small,),
             in_specs=[
-                token_spec(small, width, first),
+                token_spec(small, 1, first),
+                fixed((points, width)),
                 fixed((rows, cols)),
                 fixed((width,)),
                 gain_spec,
@@ -679,7 +712,7 @@
             out_specs=(token_spec(small, width),) * 2,
             mib=LARGE_MIB,
             us=2,
-        )(tokens, visible, mask_token, norm_gain_table)
+        )(order, tokens, visible, mask_token, norm_gain_table)
         starts.append(start)
         normals.append(normal)
 
@@ -694,60 +727,57 @@
 
     blocks = [blocks_of(normals[0], near0, swapped0, beyond0), None]
 
-    packs = []
     kept = []
     for c in range(CHUNKS):
         *keep, normal1, row, left, right = run_first(
-            firsts[c], lat, blocks[c], starts[c], packs, wt, output_weight, norm_gain_table
+            firsts[c], lat, order_row, blocks[c], starts[c], wt, output_weight, norm_gain_table
         )
-        packs = [row, left, right]
+        if c == 1:
+            keep, normal1, halos = lax.optimization_barrier((keep, normal1, halos))
+            halos = [*halos, lat_swap(halos[1]), lat_swap(halos[2])]
         kept.append((keep, normal1))
         if c == 0:
-            beyond1, row, left, right = lax.optimization_barrier((beyond1, *packs))
-            packs = [row, left, right]
+            beyond1, row, left, right = lax.optimization_barrier((beyond1, row, left, right))
+            halos = [lat_swap(row), from_left(right), from_right(left)]
             blocks[1] = blocks_of(own1, near1, swapped1, beyond1)
 
-    row, left, right = packs
-    from_l, from_r = from_left(right), from_right(left)
-    halos = [lat_swap(row), from_l, from_r, lat_swap(from_l), lat_swap(from_r)]
-    dn1, dw1, brow, bleft, bright = run_second(
-        lat, [kept[0][1], kept[1][1]], halos, query_key_value_weight, output_weight, cot
+    both1, dw1, brow, bleft, bright = run_second(
+        lat, places, [kept[0][1], kept[1][1]], halos, query_key_value_weight, output_weight, cot
     )
 
     from_l, from_r, brow = from_left(bright), from_right(bleft), lat_swap(brow)
-    packs = jnp.concatenate(
-        [brow, from_l, from_r, lat_swap(from_l), lat_swap(from_r)], 0
-    )
     stages = lon_factors()
     sum1 = halves_summed(
         lax.dynamic_slice_in_dim(dw1, lat[0] * 2 * width, 2 * width, 0),
         lax.dynamic_slice_in_dim(dw1, (1 - lat[0]) * 2 * width, 2 * width, 0),
     )
-    packs, sum1 = chained(packs, sum1)
+    both1, sum1 = chained(both1, sum1)
+    border = (brow, from_l, from_r)
 
     def plus(a, b):
         return (a.astype(F32) + b.astype(F32)).astype(BF16)
 
-    pieces = [(first, size) for first in firsts]
-    weights = None
+    weights = packs = None
     sum_stages = list(stages)
     ends = []
     coming = returned = None
-    for n, (first, count) in enumerate(pieces):
-        c = first // size
+    for n, c in enumerate(range(CHUNKS)[::-1]):
         dh1, d0, d1, d2, d3, d4, d5, *weights = run_third(
-            first, count, first - c * size, lat, blocks[c], kept[c][0], dn1, cot, packs, wt,
-            output_weight, norm_gain_table, weights, n == len(pieces) - 1,
+            firsts[c], lat, order, blocks[c], kept[c][0], both1, packs, wt,
+            output_weight, norm_gain_table, weights,
         )
-        if sum_stages:
+        if n == 0:
             sum1 = stage_summed(sum1, sum_stages.pop(0))
-        weights, sum1, d1, d2, d3, d4, d5, coming, returned = lax.optimization_barrier(
-            (weights, sum1, d1, d2, d3, d4, d5, coming, returned)
+        border, weights, sum1, d1, d2, d3, d4, d5, coming, returned = lax.optimization_barrier(
+            (border, weights, sum1, d1, d2, d3, d4, d5, coming, returned)
         )
+        if n == 0:
+            brow, from_l, from_r = border
+            packs = jnp.concatenate([brow, from_l, from_r, lat_swap(from_l), lat_swap(from_r)], 0)
         d3 = plus(d3, lat_swap(d5))
         d2 = plus(d2, lat_swap(d4))
         d1 = lat_swap(d1)
-        if n == len(pieces) - 1:
+        if n == CHUNKS - 1:
             weights = [halves_summed(*weights)]
         weights, d1, d2, d3 = lax.optimization_barrier((weights, d1, d2, d3))
         if returned is not None:
@@ -757,7 +787,7 @@
             returned = lon_swap(coming)
         coming = plus(d2, lon_backward(d3))
         weights = weights[0]
-        ends.append([first, count, dh1, d0, d1, None])
+        ends.append([c, dh1, d0, d1, None])
 
     sum0 = stage_summed(weights, stages[0])
     for stage in sum_stages:
@@ -774,23 +804,19 @@
     for stage in stages[::-1]:
         sums = spread(sums, *stage)
 
-    grad_tokens = None
-    for first, count, dh1, d0, near, far in ends:
-        c = first // size
-        extra = [] if grad_tokens is None else [grad_tokens]
-        kernel = functools.partial(last_kernel, first)
-        grad_tokens = call(
-            kernel if extra else functools.partial(without, kernel, 7, 1),
-            struct((points, width), F32),
-            grid=(count // small,),
-            in_specs=[token_spec(small, width, first - c * size), fixed((rows, cols)), gain_spec]
-            + [token_spec(small, width)] * 4
-            + [pl.BlockSpec(memory_space=pl.ANY)] * len(extra),
-            out_specs=token_spec(small, width, first),
-            aliases={7: 0} if extra else {},
-            us=4,
-        )(starts[c], visible, norm_gain_table, dh1, d0, far, near, *extra)
-
+    pieces = []
+    for c, dh1, d0, near, far in ends:
+        pieces.append((c, [starts[c], dh1, d0, far, near]))
+    pieces = [array for _, arrays in sorted(pieces, key=lambda p: p[0]) for array in arrays]
+    grad_tokens = call(
+        last_kernel,
+        struct((points, width), F32),
+        in_specs=[whole()] * (4 + len(pieces)),
+        out_specs=whole(),
+        scratch=[pltpu.VMEM((points, width), BF16)] * 2,
+        mib=LARGE_MIB,
+        us=6,
+    )(places, visible, norm_gain_table, cot, *pieces)
     sums, grad_tokens = chained(sums, grad_tokens)
     other = lat_swap(sums)
     factor = (points * lat_count * lon_count) ** (-0.5)

time: 202 us -> 192 us (0.950)
  waiting for transfers between devices: 71.1 us -> 44.7 us
  Pallas kernels: 77 us -> 87.5 us
  starting transfers between devices: 42.9 us -> 45.4 us
    pallas_call x9 -> x8, Pallas kernels: 73.4 us -> 84 us  [the longest x2 30.9 us: run_third(): call(third_kernel if final else inner_third_kernel, (struct((size, width)...]
    ppermute x33, waiting for transfers between devices: 38.8 us -> 28.2 us  [permuted(): lax.ppermute(value, axis, [(i, target(i) % count) for i in range(count)])]
    ppermute x8, waiting for transfers between devices: 17.7 us -> 9.14 us  [exchanged(): moved.append(lax.ppermute(parts(digit ^ d), 'lon', pairs))]
    ppermute x4, waiting for transfers between devices: 14.6 us -> 7.41 us  [spread(): got = lax.ppermute(value, 'lon', pairs)]
    unnamed x76 -> x64, local copies, waits for them, and re-layouts: 4.35 us -> 5.4 us
  transfers between devices with their start and end apart: 45 -> 45, of which waited for: 24 -> 17; matrix products, arithmetic and copies ran while one was open for 2% -> 3% of each run, Pallas kernels for 21% -> 32%
where the time goes in v7:
time: 192 us; the launch traced here: 188 us
  Pallas kernels  87.5 us (46%)
  starting transfers between devices  45.4 us (24%)
  waiting for transfers between devices  44.7 us (23%)
  local copies, waits for them, and re-layouts  7.23 us (4%)
  other arithmetic  2.05 us (1%)
    pallas_call x2, Pallas kernels, run_third(): call(third_kernel if final else inner_third_kernel, (struct((size, width)...  30.9 us
    ppermute x33, starting transfers between devices, permuted(): lax.ppermute(value, axis, [(i, target(i) % count) for i in range(count)])  28.4 us
    ppermute x33, waiting for transfers between devices, permuted(): lax.ppermute(value, axis, [(i, target(i) % count) for i in range(count)])  28.2 us
    pallas_call x1, Pallas kernels, run_second(): call(second_kernel, (struct((points, 2 * width), BF16), struct((4 * width...  20.9 us
    pallas_call x2, Pallas kernels, run_first(): call(first_kernel, (struct((width, size), BF16), struct((6, 2 * width, si...  17.2 us
    ppermute x8, starting transfers between devices, exchanged(): moved.append(lax.ppermute(parts(digit ^ d), 'lon', pairs))  11.2 us
    ppermute x8, waiting for transfers between devices, exchanged(): moved.append(lax.ppermute(parts(digit ^ d), 'lon', pairs))  9.14 us
    pallas_call x1, Pallas kernels, local(): call(last_kernel, struct((points, width), F32), in_specs=[whole()] * (4 +...  7.99 us
  transfers between devices with their start and end apart: 45, of which 17 were waited for; matrix products, arithmetic and copies ran while one was open for 3% of the time, Pallas kernels for 32%

profile of v7, /device:TPU:0, one launch (start us, length us, event | category | flops | bytes accessed | tf_op | source)
XLA Modules:
  0.0 188.1 jit_solution(2253952175219251266)
XLA Ops:
  0.6 3.4 %shard_map.129 = (bf16[512,384]{1,0:T(8,128)(2,1)}, bf16[512,384]{1,0:T(8,128)(2,1)}) custom-call(s32[1024,1]{1,0:T(8,128)} %constant.91.clone.order_ref.refs_1_, bf16[1024,384]{1,0:T(8,128)(2,1)} %bitcast.12, s32[32,32]{1,0:T(8,128)} %vis_ref.5, bf16[384]{0:T(512)(128)(2,1)} %mask_ref.3, f32[2,384]{1,0:T(2,128)} %gain_ref.13), custom_call_target="tpu_custom_call" | custom-call | flops 1600000000 | bytes 2000000 | tf_op jit(solution)/shard_map/pallas_call | solution.py:701
  4.1 3.0 %collective-permute-start.1 = (bf16[512,384]{1,0:T(8,128)(2,1)}, bf16[512,384]{1,0:T(8,128)(2,1)S(1)}, u32[]{:S(2)}, u32[]{:S(2)}) collective-permute-start(bf16[512,384]{1,0:T(8,128)(2,1)} %get-tuple-element.100.n0), channel_id=1, source_target_pairs={{0,2},{2,0},{4,6},{6,4},{8,10},{10,8},{12,14},{14,12},{1,3},{3,1},... | collective-permute-start | bytes 1179656 | tf_op jit(solution)/shard_map/ppermute | solution.py:48
  7.0 3.5 %shard_map.130 = (bf16[512,384]{1,0:T(8,128)(2,1)}, bf16[512,384]{1,0:T(8,128)(2,1)}) custom-call(s32[1024,1]{1,0:T(8,128)} %constant.91.clone.order_ref.refs_1_, bf16[1024,384]{1,0:T(8,128)(2,1)} %bitcast.13, s32[32,32]{1,0:T(8,128)} %vis_ref.5, bf16[384]{0:T(512)(128)(2,1)} %mask_ref.3, f32[2,384]{1,0:T(2,128)} %gain_ref.13), custom_call_target="tpu_custom_call" | custom-call | flops 1600000000 | bytes 2000000 | tf_op jit(solution)/shard_map/pallas_call | solution.py:701
  10.6 5.8 %collective-permute-done.1.n2 = bf16[512,384]{1,0:T(8,128)(2,1)S(1)} collective-permute-done((bf16[512,384]{1,0:T(8,128)(2,1)}, bf16[512,384]{1,0:T(8,128)(2,1)S(1)}, u32[]{:S(2)}, u32[]{:S(2)}) %collective-permute-start.1) | collective-permute-done | bytes 393248 | tf_op jit(solution)/shard_map/ppermute | solution.py:48
  16.4 1.7 collective-permute-start.2
  18.2 3.5 %collective-permute-start.6 = (bf16[512,384]{1,0:T(8,128)(2,1)}, bf16[512,384]{1,0:T(8,128)(2,1)}, u32[]{:S(2)}, u32[]{:S(2)}) collective-permute-start(bf16[512,384]{1,0:T(8,128)(2,1)} %get-tuple-element.105.n0.refs_2_), channel_id=1, source_target_pairs={{0,2},{2,0},{4,6},{6,4},{8,10},{10,8},{12,14},{14,12},{1,3},{3,1},... | collective-permute-start | bytes 1179656 | tf_op jit(solution)/shard_map/ppermute | solution.py:48
  22.2 6.3 %collective-permute-done.2.n3 = bf16[512,384]{1,0:T(8,128)(2,1)S(1)} collective-permute-done((bf16[512,384]{1,0:T(8,128)(2,1)S(1)}, bf16[512,384]{1,0:T(8,128)(2,1)S(1)}, u32[]{:S(2)}, u32[]{:S(2)}) %collective-permute-start.2) | collective-permute-done | bytes 393248 | tf_op jit(solution)/shard_map/ppermute | solution.py:48
  28.5 2.3 %copy.14 = bf16[2,384,1152]{1,2,0:T(8,128)(2,1)} copy(bf16[2,384,1152]{2,1,0:T(8,128)(2,1)S(1)} %copy-done.2) | data formatting | bytes 3538944 | tf_op args[4]
  32.1 8.5 %shard_map.131 = (bf16[384,512]{1,0:T(8,128)(2,1)}, bf16[6,768,512]{2,1,0:T(8,128)(2,1)}, f32[6,8,512]{2,1,0:T(8,128)}, bf16[384,512]{1,0:T(8,128)(2,1)}, bf16[5...) custom-call(s32[1]{0:T(128)} %bitcast.lat_ref.refs_0_, ...), custom_call_target="tpu_custom_call" | custom-call | flops 6400000000 | bytes 8000000 | tf_op jit(solution)/shard_map/pallas_call | solution.py:547
  40.6 3.8 %collective-permute-done.7.n3.refs_5_ = bf16[512,384]{1,0:T(8,128)(2,1)S(1)} collective-permute-done((bf16[512,384]{1,0:T(8,128)(2,1)}, bf16[512,384]{1,0:T(8,128)(2,1)S(1)}, u32[]{:S(2)}, u32[]{:S(2)}) %collective-permute-start.7) | collective-permute-done | bytes 393248 | tf_op jit(solution)/shard_map/ppermute | solution.py:48
  46.1 3.5 %collective-permute-start.12 = (bf16[32,384]{1,0:T(8,128)(2,1)}, bf16[32,384]{1,0:T(8,128)(2,1)S(1)}, u32[]{:S(2)}, u32[]{:S(2)}) collective-permute-start(bf16[32,384]{1,0:T(8,128)(2,1)} %get-tuple-element.119), channel_id=1, source_target_pairs={{0,14},{2,0},{4,2},{6,4},{8,6},{10,8},{12,10},{14,12},{1,15},{3,1}... | collective-permute-start | bytes 73736 | tf_op jit(solution)/shard_map/ppermute | solution.py:48
  50.5 8.7 %shard_map.132 = (bf16[384,512]{1,0:T(8,128)(2,1)}, bf16[6,768,512]{2,1,0:T(8,128)(2,1)}, f32[6,8,512]{2,1,0:T(8,128)}, bf16[384,512]{1,0:T(8,128)(2,1)}, bf16[5...) custom-call(s32[1]{0:T(128)} %bitcast.lat_ref.refs_0_, ...), custom_call_target="tpu_custom_call" | custom-call | flops 6400000000 | bytes 8000000 | tf_op jit(solution)/shard_map/pallas_call | solution.py:547
  61.3 20.9 %shard_map.133 = (bf16[1024,768]{1,0:T(8,128)(2,1)}, bf16[1536,384]{1,0:T(8,128)(2,1)}, bf16[32,384]{1,0:T(8,128)(2,1)}, bf16[48,384]{1,0:T(8,128)(2,1)}, bf16[48,384]{1,0:T(8,128)(2,1)}) custom-call(s32[1]{0:T(128)} %bitcast.lat_ref.refs_0_, s32[1024,1]{1,0:T(8,128)} %constant.92.clone.place_ref, bf16[512,384]{1,0:T(8,128)(2,1)} %get-tuple-element.104.na_ref, ...), custom_call_target="tpu_custom_call" | custom-call | flops 17600000000 | bytes 22000000 | tf_op jit(solution)/shard_map/pallas_call | solution.py:587
  83.9 4.7 %collective-permute-start.17 = (bf16[48,384]{1,0:T(8,128)(2,1)S(1)}, bf16[48,384]{1,0:T(8,128)(2,1)S(1)}, u32[]{:S(2)}, u32[]{:S(2)}) collective-permute-start(bf16[48,384]{1,0:T(8,128)(2,1)S(1)} %copy-done.23), channel_id=1, source_target_pairs={{0,14},{2,0},{4,2},{6,4},{8,6},{10,8},{12,10},{14,12},{1,15},{3,1}... | collective-permute-start | bytes 110600 | tf_op jit(solution)/shard_map/ppermute | solution.py:48
  88.9 15.0 %shard_map.134 = (f32[512,384]{1,0:T(8,128)}, f32[512,384]{1,0:T(8,128)}, bf16[512,384]{1,0:T(8,128)(2,1)}, bf16[512,384]{1,0:T(8,128)(2,1)}, bf16[512,384]{1,0:...) custom-call(s32[1]{0:T(128)} %bitcast.lat_ref.refs_0_, ...), custom_call_target="tpu_custom_call" | custom-call | flops 10400000000 | bytes 13000000 | tf_op jit(solution)/shard_map/pallas_call | solution.py:634
  107.9 16.0 %shard_map.135 = (f32[512,384]{1,0:T(8,128)}, f32[512,384]{1,0:T(8,128)}, bf16[512,384]{1,0:T(8,128)(2,1)}, bf16[512,384]{1,0:T(8,128)(2,1)}, bf16[512,384]{1,0:...) custom-call(s32[1]{0:T(128)} %bitcast.lat_ref.refs_0_, ...), custom_call_target="tpu_custom_call" | custom-call | flops 10400000000 | bytes 13000000 | tf_op jit(solution)/shard_map/pallas_call | solution.py:634
  126.9 3.2 %collective-permute-start.33 = (bf16[96,384]{1,0:T(8,128)(2,1)S(1)}, bf16[96,384]{1,0:T(8,128)(2,1)}, u32[]{:S(2)}, u32[]{:S(2)}) collective-permute-start(bf16[96,384]{1,0:T(8,128)(2,1)S(1)} %get-tuple-element.200), channel_id=1, source_target_pairs={{0,12},{2,14},{4,8},{6,10},{8,4},{10,6},{12,0},{14,2},{1,13},{3,15... | collective-permute-start | bytes 221192 | tf_op jit(solution)/shard_map/ppermute | solution.py:85
  131.2 1.7 collective-permute-start.30
  133.3 2.9 %collective-permute-start.34 = (bf16[512,384]{1,0:T(8,128)(2,1)S(1)}, bf16[512,384]{1,0:T(8,128)(2,1)S(1)}, u32[]{:S(2)}, u32[]{:S(2)}) collective-permute-start(bf16[512,384]{1,0:T(8,128)(2,1)S(1)} %add_convert_fusion.3), channel_id=1, source_target_pairs={{0,12},{2,6},{4,0},{6,10},{8,4},{10,14},{12,8},{14,2},{1,13},{3,7}... | collective-permute-start | bytes 1179656 | tf_op jit(solution)/shard_map/ppermute | solution.py:48
  137.2 4.0 %collective-permute-done.30 = bf16[384,384]{1,0:T(8,128)(2,1)S(1)} collective-permute-done((bf16[384,384]{1,0:T(8,128)(2,1)S(1)}, bf16[384,384]{1,0:T(8,128)(2,1)S(1)}, u32[]{:S(2)}, u32[]{:S(2)}) %collective-permute-start.30) | collective-permute-done | bytes 294944 | tf_op jit(solution)/shard_map/ppermute | solution.py:85
  141.3 2.7 %collective-permute-done.34 = bf16[512,384]{1,0:T(8,128)(2,1)S(1)} collective-permute-done((bf16[512,384]{1,0:T(8,128)(2,1)S(1)}, bf16[512,384]{1,0:T(8,128)(2,1)S(1)}, u32[]{:S(2)}, u32[]{:S(2)}) %collective-permute-start.34) | collective-permute-done | bytes 393248 | tf_op jit(solution)/shard_map/ppermute | solution.py:48
  144.0 4.4 %collective-permute-done.35.refs_8_ = bf16[512,384]{1,0:T(8,128)(2,1)S(1)} collective-permute-done((bf16[512,384]{1,0:T(8,128)(2,1)S(1)}, bf16[512,384]{1,0:T(8,128)(2,1)S(1)}, u32[]{:S(2)}, u32[]{:S(2)}) %collective-permute-start.35) | collective-permute-done | bytes 393248 | tf_op jit(solution)/shard_map/ppermute | solution.py:48
  148.4 1.7 collective-permute-start.39
  150.4 3.1 %collective-permute-start.37 = (bf16[96,384]{1,0:T(8,128)(2,1)S(1)}, bf16[96,384]{1,0:T(8,128)(2,1)S(1)}, u32[]{:S(2)}, u32[]{:S(2)}) collective-permute-start(bf16[96,384]{1,0:T(8,128)(2,1)S(1)} %get-tuple-element.198), channel_id=1, source_target_pairs={{0,8},{2,10},{4,12},{6,14},{8,0},{10,2},{12,4},{14,6},{1,9},{3,11}... | collective-permute-start | bytes 221192 | tf_op jit(solution)/shard_map/ppermute | solution.py:85
  154.6 2.9 %collective-permute-done.37 = bf16[96,384]{1,0:T(8,128)(2,1)S(1)} collective-permute-done((bf16[96,384]{1,0:T(8,128)(2,1)S(1)}, bf16[96,384]{1,0:T(8,128)(2,1)S(1)}, u32[]{:S(2)}, u32[]{:S(2)}) %collective-permute-start.37) | collective-permute-done | bytes 73760 | tf_op jit(solution)/shard_map/ppermute | solution.py:85
  157.6 2.2 %collective-permute-done.38 = bf16[96,384]{1,0:T(8,128)(2,1)S(1)} collective-permute-done((bf16[96,384]{1,0:T(8,128)(2,1)S(1)}, bf16[96,384]{1,0:T(8,128)(2,1)S(1)}, u32[]{:S(2)}, u32[]{:S(2)}) %collective-permute-start.38) | collective-permute-done | bytes 73760 | tf_op jit(solution)/shard_map/ppermute | solution.py:85
  161.7 2.6 %collective-permute-start.42 = (bf16[192,384]{1,0:T(8,128)(2,1)S(1)}, bf16[192,384]{1,0:T(8,128)(2,1)S(1)}, u32[]{:S(2)}, u32[]{:S(2)}) collective-permute-start(bf16[192,384]{1,0:T(8,128)(2,1)S(1)} %constant_dynamic-update-slice_fusion.5), channel_id=1, source_target_pairs={{0,12},{2,14},{4,8},{6,10},{8,4},{10,6},{12,0},{14,2},{1,13},{3,15... | collective-permute-start | bytes 442376 | tf_op jit(solution)/shard_map/ppermute | solution.py:105
  164.4 2.9 %collective-permute-done.40 = bf16[192,384]{1,0:T(8,128)(2,1)S(1)} collective-permute-done((bf16[192,384]{1,0:T(8,128)(2,1)S(1)}, bf16[192,384]{1,0:T(8,128)(2,1)S(1)}, u32[]{:S(2)}, u32[]{:S(2)}) %collective-permute-start.40) | collective-permute-done | bytes 147488 | tf_op jit(solution)/shard_map/ppermute | solution.py:105
  167.4 4.2 %collective-permute-done.41 = bf16[192,384]{1,0:T(8,128)(2,1)S(1)} collective-permute-done((bf16[192,384]{1,0:T(8,128)(2,1)S(1)}, bf16[192,384]{1,0:T(8,128)(2,1)S(1)}, u32[]{:S(2)}, u32[]{:S(2)}) %collective-permute-start.41) | collective-permute-done | bytes 147488 | tf_op jit(solution)/shard_map/ppermute | solution.py:105
  173.0 8.0 %shard_map.136 = f32[1024,384]{1,0:T(8,128)} custom-call(s32[1024,1]{1,0:T(8,128)} %constant.92.clone.place_ref, s32[32,32]{1,0:T(8,128)} %vis_ref.5, f32[2,384]{1,0:T(2,128)} %gain_ref.13, f32[1024,384]{1,0:T(8,128)} %bitcast.11, bf16[512,384]{1,0:T(8,128)(2,1)} %get-tuple-element.103.start_ref.refs_0_, f32[512,384]{1,0:T(8,128)} %get-tuple-element.183.refs_1_, ...), custom_call_target="tpu_custom_call" | custom-call | flops 4800000000 | bytes 6000000 | tf_op jit(solution)/shard_map/pallas_call | solution.py:811
  181.7 2.8 %collective-permute-done.44.other_ref = bf16[1536,384]{1,0:T(8,128)(2,1)S(1)} collective-permute-done((bf16[1536,384]{1,0:T(8,128)(2,1)S(1)}, bf16[1536,384]{1,0:T(8,128)(2,1)S(1)}, u32[]{:S(2)}, u32[]{:S(2)}) %collective-permute-start.44) | collective-permute-done | bytes 1179680 | tf_op jit(solution)/shard_map/ppermute | solution.py:48
  184.6 3.5 %shard_map.137 = (f32[2,384,1152]{2,1,0:T(8,128)}, f32[2,384,384]{2,1,0:T(8,128)}, f32[2,384]{1,0:T(2,128)}) custom-call(s32[1]{0:T(128)} %bitcast.lat_ref.refs_0_, bf16[1536,384]{1,0:T(8,128)(2,1)S(1)} %constant_dynamic-update-slice_fusion.7.mine_ref, bf16[1536,384]{1,0:T(8,128)(2,1)S(1)} %collective-permute-done.44.other_ref, ...), custom_call_target="tpu_custom_call" | custom-call | flops 4000000000 | bytes 5000000 | tf_op jit(solution)/shard_map/pallas_call | solution.py:823
  (158 shorter events, 23.2 us)
Async XLA Ops:
  4.1 12.4 %collective-permute-start.1 = (bf16[512,384]{1,0:T(8,128)(2,1)}, bf16[512,384]{1,0:T(8,128)(2,1)S(1)}, u32[]{:S(2)}, u32[]{:S(2)}) collective-permute-start(bf16[512,384]{1,0:T(8,128)(2,1)} %get-tuple-element.100.n0), channel_id=1, source_target_pairs={{0,2},{2,0},{4,6},{6,4},{8,10},{10,8},{12,14},{14,12},{1,3},{3,1},... | collective-permute-start | bytes 1179656 | tf_op jit(solution)/shard_map/ppermute | solution.py:48
  16.4 12.1 %collective-permute-start.2 = (bf16[512,384]{1,0:T(8,128)(2,1)S(1)}, bf16[512,384]{1,0:T(8,128)(2,1)S(1)}, u32[]{:S(2)}, u32[]{:S(2)}) collective-permute-start(bf16[512,384]{1,0:T(8,128)(2,1)S(1)} %collective-permute-done.1.n2), channel_id=1, source_target_pairs={{0,4},{2,14},{4,8},{6,2},{8,12},{10,6},{12,0},{14,10},{1,5},{3,15}... | collective-permute-start | bytes 1179656 | tf_op jit(solution)/shard_map/ppermute | solution.py:48
  18.2 13.1 %collective-permute-start.6 = (bf16[512,384]{1,0:T(8,128)(2,1)}, bf16[512,384]{1,0:T(8,128)(2,1)}, u32[]{:S(2)}, u32[]{:S(2)}) collective-permute-start(bf16[512,384]{1,0:T(8,128)(2,1)} %get-tuple-element.105.n0.refs_2_), channel_id=1, source_target_pairs={{0,2},{2,0},{4,6},{6,4},{8,10},{10,8},{12,14},{14,12},{1,3},{3,1},... | collective-permute-start | bytes 1179656 | tf_op jit(solution)/shard_map/ppermute | solution.py:48
  21.7 9.6 %collective-permute-start = (bf16[512,384]{1,0:T(8,128)(2,1)S(1)}, bf16[512,384]{1,0:T(8,128)(2,1)S(1)}, u32[]{:S(2)}, u32[]{:S(2)}) collective-permute-start(bf16[512,384]{1,0:T(8,128)(2,1)S(1)} %copy-done.11), channel_id=1, source_target_pairs={{0,1},{1,0},{2,3},{3,2},{4,5},{5,4},{6,7},{7,6},{8,9},{9,8},{10,11... | collective-permute-start | bytes 1179656 | tf_op jit(solution)/shard_map/ppermute | solution.py:48
  21.7 9.8 %collective-permute-start.3 = (bf16[512,384]{1,0:T(8,128)(2,1)S(1)}, bf16[512,384]{1,0:T(8,128)(2,1)}, u32[]{:S(2)}, u32[]{:S(2)}) collective-permute-start(bf16[512,384]{1,0:T(8,128)(2,1)S(1)} %collective-permute-done.1.n2), channel_id=1, source_target_pairs={{0,1},{1,0},{2,3},{3,2},{4,5},{5,4},{6,7},{7,6},{8,9},{9,8},{10,11... | collective-permute-start | bytes 1179656 | tf_op jit(solution)/shard_map/ppermute | solution.py:48
  30.8 15.3 %collective-permute-start.5 = (bf16[512,384]{1,0:T(8,128)(2,1)}, bf16[512,384]{1,0:T(8,128)(2,1)S(1)}, u32[]{:S(2)}, u32[]{:S(2)}) collective-permute-start(bf16[512,384]{1,0:T(8,128)(2,1)} %get-tuple-element.105.n0.refs_2_), channel_id=1, source_target_pairs={{0,1},{1,0},{2,3},{3,2},{4,5},{5,4},{6,7},{7,6},{8,9},{9,8},{10,11... | collective-permute-start | bytes 1179656 | tf_op jit(solution)/shard_map/ppermute | solution.py:48
  31.3 13.1 %collective-permute-start.7 = (bf16[512,384]{1,0:T(8,128)(2,1)}, bf16[512,384]{1,0:T(8,128)(2,1)S(1)}, u32[]{:S(2)}, u32[]{:S(2)}) collective-permute-start(bf16[512,384]{1,0:T(8,128)(2,1)} %collective-permute-done.6.n2.refs_4_), channel_id=1, source_target_pairs={{0,4},{2,14},{4,8},{6,2},{8,12},{10,6},{12,0},{14,10},{1,5},{3,15}... | collective-permute-start | bytes 1179656 | tf_op jit(solution)/shard_map/ppermute | solution.py:48
  31.3 18.3 %collective-permute-start.8 = (bf16[512,384]{1,0:T(8,128)(2,1)}, bf16[512,384]{1,0:T(8,128)(2,1)S(1)}, u32[]{:S(2)}, u32[]{:S(2)}) collective-permute-start(bf16[512,384]{1,0:T(8,128)(2,1)} %collective-permute-done.6.n2.refs_4_), channel_id=1, source_target_pairs={{0,1},{1,0},{2,3},{3,2},{4,5},{5,4},{6,7},{7,6},{8,9},{9,8},{10,11... | collective-permute-start | bytes 1179656 | tf_op jit(solution)/shard_map/ppermute | solution.py:48
  44.4 5.2 %collective-permute-start.9 = (bf16[512,384]{1,0:T(8,128)(2,1)S(1)}, bf16[512,384]{1,0:T(8,128)(2,1)S(1)}, u32[]{:S(2)}, u32[]{:S(2)}) collective-permute-start(bf16[512,384]{1,0:T(8,128)(2,1)S(1)} %collective-permute-done.7.n3.refs_5_), channel_id=1, source_target_pairs={{0,1},{1,0},{2,3},{3,2},{4,5},{5,4},{6,7},{7,6},{8,9},{9,8},{10,11... | collective-permute-start | bytes 1179656 | tf_op jit(solution)/shard_map/ppermute | solution.py:48
  44.4 14.8 %collective-permute-start.10 = (bf16[32,384]{1,0:T(8,128)(2,1)}, bf16[32,384]{1,0:T(8,128)(2,1)S(1)}, u32[]{:S(2)}, u32[]{:S(2)}) collective-permute-start(bf16[32,384]{1,0:T(8,128)(2,1)} %get-tuple-element.117), channel_id=1, source_target_pairs={{0,1},{1,0},{2,3},{3,2},{4,5},{5,4},{6,7},{7,6},{8,9},{9,8},{10,11... | collective-permute-start | bytes 73736 | tf_op jit(solution)/shard_map/ppermute | solution.py:48
  44.9 14.4 %collective-permute-start.11 = (bf16[32,384]{1,0:T(8,128)(2,1)}, bf16[32,384]{1,0:T(8,128)(2,1)S(1)}, u32[]{:S(2)}, u32[]{:S(2)}) collective-permute-start(bf16[32,384]{1,0:T(8,128)(2,1)} %get-tuple-element.118), channel_id=1, source_target_pairs={{0,2},{2,4},{4,6},{6,8},{8,10},{10,12},{12,14},{14,0},{1,3},{3,5},... | collective-permute-start | bytes 73736 | tf_op jit(solution)/shard_map/ppermute | solution.py:48
  46.1 13.2 %collective-permute-start.12 = (bf16[32,384]{1,0:T(8,128)(2,1)}, bf16[32,384]{1,0:T(8,128)(2,1)S(1)}, u32[]{:S(2)}, u32[]{:S(2)}) collective-permute-start(bf16[32,384]{1,0:T(8,128)(2,1)} %get-tuple-element.119), channel_id=1, source_target_pairs={{0,14},{2,0},{4,2},{6,4},{8,6},{10,8},{12,10},{14,12},{1,15},{3,1}... | collective-permute-start | bytes 73736 | tf_op jit(solution)/shard_map/ppermute | solution.py:48
  83.9 20.1 %collective-permute-start.16 = (bf16[48,384]{1,0:T(8,128)(2,1)}, bf16[48,384]{1,0:T(8,128)(2,1)S(1)}, u32[]{:S(2)}, u32[]{:S(2)}) collective-permute-start(bf16[48,384]{1,0:T(8,128)(2,1)} %get-tuple-element.125), channel_id=1, source_target_pairs={{0,2},{2,4},{4,6},{6,8},{8,10},{10,12},{12,14},{14,0},{1,3},{3,5},... | collective-permute-start | bytes 110600 | tf_op jit(solution)/shard_map/ppermute | solution.py:48
  83.9 20.1 %collective-permute-start.17 = (bf16[48,384]{1,0:T(8,128)(2,1)S(1)}, bf16[48,384]{1,0:T(8,128)(2,1)S(1)}, u32[]{:S(2)}, u32[]{:S(2)}) collective-permute-start(bf16[48,384]{1,0:T(8,128)(2,1)S(1)} %copy-done.23), channel_id=1, source_target_pairs={{0,14},{2,0},{4,2},{6,4},{8,6},{10,8},{12,10},{14,12},{1,15},{3,1}... | collective-permute-start | bytes 110600 | tf_op jit(solution)/shard_map/ppermute | solution.py:48
  88.6 15.4 %collective-permute-start.15 = (bf16[32,384]{1,0:T(8,128)(2,1)}, bf16[32,384]{1,0:T(8,128)(2,1)S(1)}, u32[]{:S(2)}, u32[]{:S(2)}) collective-permute-start(bf16[32,384]{1,0:T(8,128)(2,1)} %get-tuple-element.124), channel_id=1, source_target_pairs={{0,1},{1,0},{2,3},{3,2},{4,5},{5,4},{6,7},{7,6},{8,9},{9,8},{10,11... | collective-permute-start | bytes 73736 | tf_op jit(solution)/shard_map/ppermute | solution.py:48
  88.9 15.1 %collective-permute-start.19 = (bf16[384,384]{1,0:T(8,128)(2,1)S(1)}, bf16[384,384]{1,0:T(8,128)(2,1)S(1)}, u32[]{:S(2)}, u32[]{:S(2)}) collective-permute-start(bf16[384,384]{1,0:T(8,128)(2,1)S(1)} %constant_dynamic-slice_fusion.7), channel_id=1, source_target_pairs={{0,2},{2,0},{4,6},{6,4},{8,10},{10,8},{12,14},{14,12},{1,3},{3,1},... | collective-permute-start | bytes 884744 | tf_op jit(solution)/shard_map/ppermute | solution.py:85
  107.4 16.4 %collective-permute-start.25 = (bf16[512,384]{1,0:T(8,128)(2,1)S(1)}, bf16[512,384]{1,0:T(8,128)(2,1)S(1)}, u32[]{:S(2)}, u32[]{:S(2)}) collective-permute-start(bf16[512,384]{1,0:T(8,128)(2,1)S(1)} %add_convert_fusion.6), channel_id=1, source_target_pairs={{0,12},{2,6},{4,0},{6,10},{8,4},{10,14},{12,8},{14,2},{1,13},{3,7}... | collective-permute-start | bytes 1179656 | tf_op jit(solution)/shard_map/ppermute | solution.py:48
  124.5 5.7 %collective-permute-start.26 = (bf16[768,384]{1,0:T(8,128)(2,1)}, bf16[768,384]{1,0:T(8,128)(2,1)S(1)}, u32[]{:S(2)}, u32[]{:S(2)}) collective-permute-start(bf16[768,384]{1,0:T(8,128)(2,1)} %get-tuple-element.168), channel_id=1, source_target_pairs={{0,1},{1,0},{2,3},{3,2},{4,5},{5,4},{6,7},{7,6},{8,9},{9,8},{10,11... | collective-permute-start | bytes 1769480 | tf_op jit(solution)/shard_map/ppermute | solution.py:48
  124.8 5.6 %collective-permute-start.27 = (bf16[512,384]{1,0:T(8,128)(2,1)S(1)}, bf16[512,384]{1,0:T(8,128)(2,1)S(1)}, u32[]{:S(2)}, u32[]{:S(2)}) collective-permute-start(bf16[512,384]{1,0:T(8,128)(2,1)S(1)} %copy-done.22), channel_id=1, source_target_pairs={{0,1},{1,0},{2,3},{3,2},{4,5},{5,4},{6,7},{7,6},{8,9},{9,8},{10,11... | collective-permute-start | bytes 1179656 | tf_op jit(solution)/shard_map/ppermute | solution.py:48
  125.1 8.2 %collective-permute-start.31 = (bf16[96,384]{1,0:T(8,128)(2,1)S(1)}, bf16[96,384]{1,0:T(8,128)(2,1)S(1)}, u32[]{:S(2)}, u32[]{:S(2)}) collective-permute-start(bf16[96,384]{1,0:T(8,128)(2,1)S(1)} %get-tuple-element.199), channel_id=1, source_target_pairs={{0,4},{2,6},{4,0},{6,2},{8,12},{10,14},{12,8},{14,10},{1,5},{3,7},... | collective-permute-start | bytes 221192 | tf_op jit(solution)/shard_map/ppermute | solution.py:85
  126.8 9.5 %collective-permute-start.32 = (bf16[96,384]{1,0:T(8,128)(2,1)S(1)}, bf16[96,384]{1,0:T(8,128)(2,1)S(1)}, u32[]{:S(2)}, u32[]{:S(2)}) collective-permute-start(bf16[96,384]{1,0:T(8,128)(2,1)S(1)} %get-tuple-element.201), channel_id=1, source_target_pairs={{0,8},{2,10},{4,12},{6,14},{8,0},{10,2},{12,4},{14,6},{1,9},{3,11}... | collective-permute-start | bytes 221192 | tf_op jit(solution)/shard_map/ppermute | solution.py:85
  126.9 9.3 %collective-permute-start.33 = (bf16[96,384]{1,0:T(8,128)(2,1)S(1)}, bf16[96,384]{1,0:T(8,128)(2,1)}, u32[]{:S(2)}, u32[]{:S(2)}) collective-permute-start(bf16[96,384]{1,0:T(8,128)(2,1)S(1)} %get-tuple-element.200), channel_id=1, source_target_pairs={{0,12},{2,14},{4,8},{6,10},{8,4},{10,6},{12,0},{14,2},{1,13},{3,15... | collective-permute-start | bytes 221192 | tf_op jit(solution)/shard_map/ppermute | solution.py:85
  131.2 10.0 %collective-permute-start.30 = (bf16[384,384]{1,0:T(8,128)(2,1)S(1)}, bf16[384,384]{1,0:T(8,128)(2,1)S(1)}, u32[]{:S(2)}, u32[]{:S(2)}) collective-permute-start(bf16[384,384]{1,0:T(8,128)(2,1)S(1)} %constant_dynamic-slice_fusion.6), channel_id=1, source_target_pairs={{0,2},{2,0},{4,6},{6,4},{8,10},{10,8},{12,14},{14,12},{1,3},{3,1},... | collective-permute-start | bytes 884744 | tf_op jit(solution)/shard_map/ppermute | solution.py:85
  132.9 15.5 %collective-permute-start.35 = (bf16[512,384]{1,0:T(8,128)(2,1)S(1)}, bf16[512,384]{1,0:T(8,128)(2,1)S(1)}, u32[]{:S(2)}, u32[]{:S(2)}) collective-permute-start(bf16[512,384]{1,0:T(8,128)(2,1)S(1)} %add_convert_fusion.5), channel_id=1, source_target_pairs={{0,2},{2,0},{4,6},{6,4},{8,10},{10,8},{12,14},{14,12},{1,3},{3,1},... | collective-permute-start | bytes 1179656 | tf_op jit(solution)/shard_map/ppermute | solution.py:48
  133.3 10.6 %collective-permute-start.34 = (bf16[512,384]{1,0:T(8,128)(2,1)S(1)}, bf16[512,384]{1,0:T(8,128)(2,1)S(1)}, u32[]{:S(2)}, u32[]{:S(2)}) collective-permute-start(bf16[512,384]{1,0:T(8,128)(2,1)S(1)} %add_convert_fusion.3), channel_id=1, source_target_pairs={{0,12},{2,6},{4,0},{6,10},{8,4},{10,14},{12,8},{14,2},{1,13},{3,7}... | collective-permute-start | bytes 1179656 | tf_op jit(solution)/shard_map/ppermute | solution.py:48
  148.4 11.4 %collective-permute-start.39 = (bf16[512,384]{1,0:T(8,128)(2,1)S(1)}, bf16[512,384]{1,0:T(8,128)(2,1)S(1)}, u32[]{:S(2)}, u32[]{:S(2)}) collective-permute-start(bf16[512,384]{1,0:T(8,128)(2,1)S(1)} %add_convert_fusion.2), channel_id=1, source_target_pairs={{0,2},{2,0},{4,6},{6,4},{8,10},{10,8},{12,14},{14,12},{1,3},{3,1},... | collective-permute-start | bytes 1179656 | tf_op jit(solution)/shard_map/ppermute | solution.py:48
  150.4 7.1 %collective-permute-start.37 = (bf16[96,384]{1,0:T(8,128)(2,1)S(1)}, bf16[96,384]{1,0:T(8,128)(2,1)S(1)}, u32[]{:S(2)}, u32[]{:S(2)}) collective-permute-start(bf16[96,384]{1,0:T(8,128)(2,1)S(1)} %get-tuple-element.198), channel_id=1, source_target_pairs={{0,8},{2,10},{4,12},{6,14},{8,0},{10,2},{12,4},{14,6},{1,9},{3,11}... | collective-permute-start | bytes 221192 | tf_op jit(solution)/shard_map/ppermute | solution.py:85
  153.6 6.2 %collective-permute-start.38 = (bf16[96,384]{1,0:T(8,128)(2,1)S(1)}, bf16[96,384]{1,0:T(8,128)(2,1)S(1)}, u32[]{:S(2)}, u32[]{:S(2)}) collective-permute-start(bf16[96,384]{1,0:T(8,128)(2,1)S(1)} %get-tuple-element.197), channel_id=1, source_target_pairs={{0,12},{2,14},{4,8},{6,10},{8,4},{10,6},{12,0},{14,2},{1,13},{3,15... | collective-permute-start | bytes 221192 | tf_op jit(solution)/shard_map/ppermute | solution.py:85
  159.9 7.5 %collective-permute-start.40 = (bf16[192,384]{1,0:T(8,128)(2,1)S(1)}, bf16[192,384]{1,0:T(8,128)(2,1)S(1)}, u32[]{:S(2)}, u32[]{:S(2)}) collective-permute-start(bf16[192,384]{1,0:T(8,128)(2,1)S(1)} %constant_dynamic-update-slice_fusion.5), channel_id=1, source_target_pairs={{0,4},{2,6},{4,0},{6,2},{8,12},{10,14},{12,8},{14,10},{1,5},{3,7},... | collective-permute-start | bytes 442376 | tf_op jit(solution)/shard_map/ppermute | solution.py:105
  160.0 11.6 %collective-permute-start.41 = (bf16[192,384]{1,0:T(8,128)(2,1)S(1)}, bf16[192,384]{1,0:T(8,128)(2,1)S(1)}, u32[]{:S(2)}, u32[]{:S(2)}) collective-permute-start(bf16[192,384]{1,0:T(8,128)(2,1)S(1)} %constant_dynamic-update-slice_fusion.5), channel_id=1, source_target_pairs={{0,8},{2,10},{4,12},{6,14},{8,0},{10,2},{12,4},{14,6},{1,9},{3,11}... | collective-permute-start | bytes 442376 | tf_op jit(solution)/shard_map/ppermute | solution.py:105
  161.7 9.9 %collective-permute-start.42 = (bf16[192,384]{1,0:T(8,128)(2,1)S(1)}, bf16[192,384]{1,0:T(8,128)(2,1)S(1)}, u32[]{:S(2)}, u32[]{:S(2)}) collective-permute-start(bf16[192,384]{1,0:T(8,128)(2,1)S(1)} %constant_dynamic-update-slice_fusion.5), channel_id=1, source_target_pairs={{0,12},{2,14},{4,8},{6,10},{8,4},{10,6},{12,0},{14,2},{1,13},{3,15... | collective-permute-start | bytes 442376 | tf_op jit(solution)/shard_map/ppermute | solution.py:105
  171.6 9.9 %collective-permute-start.43 = (bf16[768,384]{1,0:T(8,128)(2,1)S(1)}, bf16[768,384]{1,0:T(8,128)(2,1)S(1)}, u32[]{:S(2)}, u32[]{:S(2)}) collective-permute-start(bf16[768,384]{1,0:T(8,128)(2,1)S(1)} %constant_dynamic-update-slice_fusion.9), channel_id=1, source_target_pairs={{0,2},{2,0},{4,6},{6,4},{8,10},{10,8},{12,14},{14,12},{1,3},{3,1},... | collective-permute-start | bytes 1769480 | tf_op jit(solution)/shard_map/ppermute | solution.py:105
  (42 other events, 184.4 us)
